TPU v7x, 32 devices: a whole 2x2x4 slice. The times are simulated.
32 devices in a mesh: fsdp: 4 (over y, core), ctx: 2 (over x), tp: 4 (over z).
Axes of the slice: x: 2, y: 2, z: 4, core: 2. Of those that a mesh axis runs over, the one named last changes fastest.
Arguments:
- tokens: bfloat16 [8192, 768], P(('fsdp', 'ctx')), may hold values from -6 to 6
- encoder: bfloat16 [16384, 768], P(('fsdp', 'ctx')), may hold values from -6 to 6
- cotangent: bfloat16 [8192, 768], P(('fsdp', 'ctx')), may hold values from -6 to 6
- parents: int32 [8, 8], P('fsdp'), may hold values from 0 to 6, as said below
- targets: int32 [8192], P(('fsdp', 'ctx')), may hold values from 0 to 32127
- w_query: bfloat16 [768, 768], P(('fsdp', 'ctx'), 'tp'), may hold values from -0.0546875 to 0.0546875
- w_key: bfloat16 [768, 768], P(('fsdp', 'ctx'), 'tp'), may hold values from -0.21875 to 0.21875
- w_value: bfloat16 [768, 768], P(('fsdp', 'ctx'), 'tp'), may hold values from -0.21875 to 0.21875
- w_out: bfloat16 [768, 768], P('tp', ('fsdp', 'ctx')), may hold values from -0.875 to 0.875
- c_query: bfloat16 [768, 768], P(('fsdp', 'ctx'), 'tp'), may hold values from -0.0546875 to 0.0546875
- c_key: bfloat16 [768, 768], P(('fsdp', 'ctx'), 'tp'), may hold values from -0.21875 to 0.21875
- c_value: bfloat16 [768, 768], P(('fsdp', 'ctx'), 'tp'), may hold values from -0.21875 to 0.21875
- c_out: bfloat16 [768, 768], P('tp', ('fsdp', 'ctx')), may hold values from -0.875 to 0.875
- w_gate: bfloat16 [768, 2048], P(('fsdp', 'ctx'), 'tp'), may hold values from -0.21875 to 0.21875
- w_up: bfloat16 [768, 2048], P(('fsdp', 'ctx'), 'tp'), may hold values from -0.21875 to 0.21875
- w_down: bfloat16 [2048, 768], P('tp', ('fsdp', 'ctx')), may hold values from -0.125 to 0.125
- embedding: bfloat16 [32128, 768], P('tp', ('fsdp', 'ctx')), may hold values from -12 to 12
- norm_self: bfloat16 [768], P(('fsdp', 'ctx')), may hold values from 0.5 to 1.5
- norm_cross: bfloat16 [768], P(('fsdp', 'ctx')), may hold values from 0.5 to 1.5
- norm_ff: bfloat16 [768], P(('fsdp', 'ctx')), may hold values from 0.5 to 1.5
- norm_exit: bfloat16 [768], P(('fsdp', 'ctx')), may hold values from 0.5 to 1.5
Outputs:
- mixed: bfloat16 [8192, 768], P(('fsdp', 'ctx'))
- exit_loss: float32 [8192], P(('fsdp', 'ctx'))
- exit_score: float32 [8192], P(('fsdp', 'ctx'))
- grad_tokens: float32 [8192, 768], P(('fsdp', 'ctx'))
- grad_encoder: float32 [16384, 768], P(('fsdp', 'ctx'))
- grad_w_query: float32 [768, 768], P(('fsdp', 'ctx'), 'tp')
- grad_w_key: float32 [768, 768], P(('fsdp', 'ctx'), 'tp')
- grad_w_value: float32 [768, 768], P(('fsdp', 'ctx'), 'tp')
- grad_w_out: float32 [768, 768], P('tp', ('fsdp', 'ctx'))
- grad_c_query: float32 [768, 768], P(('fsdp', 'ctx'), 'tp')
- grad_c_key: float32 [768, 768], P(('fsdp', 'ctx'), 'tp')
- grad_c_value: float32 [768, 768], P(('fsdp', 'ctx'), 'tp')
- grad_c_out: float32 [768, 768], P('tp', ('fsdp', 'ctx'))
- grad_w_gate: float32 [768, 2048], P(('fsdp', 'ctx'), 'tp')
- grad_w_up: float32 [768, 2048], P(('fsdp', 'ctx'), 'tp')
- grad_w_down: float32 [2048, 768], P('tp', ('fsdp', 'ctx'))
- grad_embedding: float32 [32128, 768], P('tp', ('fsdp', 'ctx'))
- grad_norm_self: float32 [768], P(('fsdp', 'ctx'))
- grad_norm_cross: float32 [768], P(('fsdp', 'ctx'))
- grad_norm_ff: float32 [768], P(('fsdp', 'ctx'))
- grad_norm_exit: float32 [768], P(('fsdp', 'ctx'))
Inputs may be any that keep to these rules, and one draw needn't show every extreme that they name: parents[t, 0] = 0; blocks 1 to 3 each name the block before them; every later block names a block at index 3 or later that comes before it; the last block names the one before it.
All inputs are finite; a program needn't handle non-finite values.
Results may differ from a plain program's by a relative error of at most 0.03.
The roundings to bfloat16 on the way count: a program that leaves them out, or rounds other values in their place, can miss the bound.
Values may be sent and summed in bfloat16 or wider, within the bound.
A program may use at most 256 MiB of HBM per device.

v0:
```python
import math

import jax
import jax.numpy as jnp
from jax import lax
from jax.sharding import PartitionSpec as P

D = 768
HD = 64
BLK = 128
MB = 2


EPSILON = 1e-06
MASKED = -1000000000.0
HIGH = lax.Precision.HIGHEST


def merged(part, axis, combine):
    gathered = jax.tree.map(lambda a: lax.all_gather(a, axis), part)

    def take(source):
        return jax.tree.map(lambda a: lax.dynamic_index_in_dim(a, source, 0, False), gathered)

    return lax.fori_loop(
        1, lax.axis_size(axis), lambda source, state: combine(state, take(source)), take(0)
    )


def rms_scale(values):
    return lax.rsqrt(jnp.mean(values * values, axis=-1, keepdims=True) + EPSILON)


def rms_back(grad_normed, normed, scale):
    return scale * (grad_normed - normed * jnp.mean(grad_normed * normed, axis=-1, keepdims=True))


def ancestry(parent_row):
    block_count = parent_row.shape[0]
    blocks = jnp.arange(block_count, dtype=jnp.int32)
    reachable = (parent_row[:, None] == blocks[None, :]).astype(jnp.float32)
    reachable = jnp.maximum(reachable, (blocks[:, None] == blocks[None, :]).astype(jnp.float32))
    for doubling in range(max(1, (block_count - 1).bit_length())):
        reachable = jnp.minimum(jnp.dot(reachable, reachable, precision=HIGH), 1.0)
    return reachable


def local_mask(parent_row, ctx_index, row_count, group_count):
    reachable = ancestry(parent_row)
    tree_blocks = jnp.arange(parent_row.shape[0], dtype=jnp.int32)
    query_pos = ctx_index * row_count + jnp.arange(row_count, dtype=jnp.int32)
    key_pos = jnp.arange(group_count, dtype=jnp.int32)
    query_onehot = (query_pos[:, None] // BLK == tree_blocks[None, :]).astype(jnp.float32)
    key_onehot = (key_pos[:, None] // BLK == tree_blocks[None, :]).astype(jnp.float32)
    linked = (
        jnp.dot(jnp.dot(query_onehot, reachable, precision=HIGH), key_onehot.T, precision=HIGH)
        > 0.5
    )
    causal = (query_pos[:, None] // BLK != key_pos[None, :] // BLK) | (
        key_pos[None, :] <= query_pos[:, None]
    )
    return linked & causal


def split_heads(values):
    return jnp.moveaxis(values.reshape(values.shape[0], -1, HD), 1, 0)


def join_heads(values):
    moved = jnp.moveaxis(values, 0, 1)
    return moved.reshape(moved.shape[0], -1)


def head_scores(queries, keys_part, allowed):
    scores = jnp.einsum("qd,kd->qk", queries, keys_part, preferred_element_type=jnp.float32)
    if allowed is None:
        return scores
    return jnp.where(allowed, scores, MASKED)


def head_forward(queries, keys_part, values_part, allowed):
    scores = head_scores(queries, keys_part, allowed)
    highest = jnp.max(scores, axis=-1, keepdims=True)
    exponent = jnp.exp(scores - highest)
    denominator = jnp.sum(exponent, axis=-1, keepdims=True)
    probs = (exponent / denominator).astype(jnp.bfloat16)
    output = jnp.einsum("qk,kd->qd", probs, values_part, preferred_element_type=jnp.float32)
    return (output.astype(jnp.bfloat16), (highest + jnp.log(denominator))[:, 0])


def head_backward(queries, keys_part, values_part, log_total, grad_out, allowed):
    scores = head_scores(queries, keys_part, allowed)
    probs = jnp.exp(scores - log_total[:, None])
    grad_values = jnp.einsum(
        "qk,qd->kd", probs.astype(jnp.bfloat16), grad_out, preferred_element_type=jnp.float32
    )
    grad_probs = jnp.einsum("qd,kd->qk", grad_out, values_part, preferred_element_type=jnp.float32)
    inner_sum = jnp.sum(probs * grad_probs, axis=-1, keepdims=True)
    grad_scores = (probs * (grad_probs - inner_sum)).astype(jnp.bfloat16)
    grad_queries = jnp.einsum(
        "qk,kd->qd", grad_scores, keys_part, preferred_element_type=jnp.float32
    )
    grad_keys = jnp.einsum("qk,qd->kd", grad_scores, queries, preferred_element_type=jnp.float32)
    return (grad_queries, grad_keys, grad_values)


def attend(queries, keys_all, values_all, allowed):
    outputs, totals = lax.map(
        lambda element: head_forward(element[0], element[1], element[2], allowed),
        (split_heads(queries), split_heads(keys_all), split_heads(values_all)),
    )
    return (join_heads(outputs), totals)


def attend_back(queries, keys_all, values_all, totals, grad_out, allowed):
    grad_parts = lax.map(
        lambda element: head_backward(
            element[0], element[1], element[2], element[3], element[4], allowed
        ),
        (
            split_heads(queries),
            split_heads(keys_all),
            split_heads(values_all),
            totals,
            split_heads(grad_out),
        ),
    )
    return (join_heads(grad_parts[0]), join_heads(grad_parts[1]), join_heads(grad_parts[2]))


def head_total(partial_value):
    shares = lax.psum_scatter(partial_value, "tp", scatter_dimension=0, tiled=True)
    return lax.all_gather(shares, "tp", axis=0, tiled=True)


def combine_stats(earlier, later):
    highest = jnp.maximum(earlier[0], later[0])
    scaled = earlier[1] * jnp.exp(earlier[0] - highest) + later[1] * jnp.exp(later[0] - highest)
    return (highest, scaled, earlier[2] + later[2])


def mat(left, right):
    return jnp.dot(left, right, preferred_element_type=jnp.float32)


def micro_batch(tokens, encoder, cotangent, parent_row, targets, gathered, ctx_index, vocab_index):
    (
        w_query,
        w_key,
        w_value,
        w_out,
        c_query,
        c_key,
        c_value,
        c_out,
        w_gate,
        w_up,
        w_down,
        embedding,
        norm_self,
        norm_cross,
        norm_ff,
        norm_exit,
    ) = gathered
    gain_self = norm_self.astype(jnp.float32)
    gain_cross = norm_cross.astype(jnp.float32)
    gain_ff = norm_ff.astype(jnp.float32)
    gain_exit = norm_exit.astype(jnp.float32)
    row_count = tokens.shape[0]
    tok_float = tokens.astype(jnp.float32)
    scale_one = rms_scale(tok_float)
    normed_one = tok_float * scale_one
    hidden_one = (normed_one * gain_self).astype(jnp.bfloat16)
    queries = mat(hidden_one, w_query).astype(jnp.bfloat16)
    keys_self = mat(hidden_one, w_key).astype(jnp.bfloat16)
    values_self = mat(hidden_one, w_value).astype(jnp.bfloat16)
    keys_cross = mat(encoder, c_key).astype(jnp.bfloat16)
    values_cross = mat(encoder, c_value).astype(jnp.bfloat16)
    keys_group, values_group, keys_enc, values_enc = (
        lax.all_gather(keys_self, "ctx", axis=0, tiled=True),
        lax.all_gather(values_self, "ctx", axis=0, tiled=True),
        lax.all_gather(keys_cross, "ctx", axis=0, tiled=True),
        lax.all_gather(values_cross, "ctx", axis=0, tiled=True),
    )
    allowed = local_mask(parent_row, ctx_index, row_count, keys_group.shape[0])
    attended, totals_self = attend(queries, keys_group, values_group, allowed)
    after_self = tok_float + head_total(mat(attended, w_out))
    scale_two = rms_scale(after_self)
    normed_two = after_self * scale_two
    hidden_two = (normed_two * gain_cross).astype(jnp.bfloat16)
    cross_queries = mat(hidden_two, c_query).astype(jnp.bfloat16)
    crossed, totals_cross = attend(cross_queries, keys_enc, values_enc, None)
    after_cross = after_self + head_total(mat(crossed, c_out))
    scale_three = rms_scale(after_cross)
    normed_three = after_cross * scale_three
    hidden_three = (normed_three * gain_ff).astype(jnp.bfloat16)
    gate_pre = mat(hidden_three, w_gate)
    up_pre = mat(hidden_three, w_up)
    activated = (jax.nn.gelu(gate_pre, approximate=True) * up_pre).astype(jnp.bfloat16)
    mixed = after_cross + head_total(mat(activated, w_down))
    scale_four = rms_scale(mixed)
    normed_four = mixed * scale_four
    shrink = 1.0 / math.sqrt(D)
    exit_in = (normed_four * gain_exit * shrink).astype(jnp.bfloat16)
    logits = jnp.einsum("td,vd->tv", exit_in, embedding, preferred_element_type=jnp.float32)
    vocab_local = embedding.shape[0]
    columns = vocab_index * vocab_local + jnp.arange(vocab_local, dtype=jnp.int32)
    hits = columns[None, :] == targets[:, None]
    highest = jnp.max(logits, axis=-1)
    summed = jnp.sum(jnp.exp(logits - highest[:, None]), axis=-1)
    picked = jnp.sum(jnp.where(hits, logits, 0.0), axis=-1)
    top_all, total_all, picked_all = merged((highest, summed, picked), "tp", combine_stats)
    log_total = top_all + jnp.log(total_all)
    losses = log_total - picked_all
    scores = top_all - log_total
    grad_logits = (jnp.exp(logits - log_total[:, None]) - hits.astype(jnp.float32)).astype(
        jnp.bfloat16
    )
    grad_embed = jnp.einsum("tv,td->vd", grad_logits, exit_in, preferred_element_type=jnp.float32)
    grad_exit = head_total(mat(grad_logits, embedding)) * shrink
    grad_norm_exit = jnp.sum(grad_exit * normed_four, axis=0)
    grad_mixed = cotangent.astype(jnp.float32) + rms_back(
        grad_exit * gain_exit, normed_four, scale_four
    )
    grad_mixed_low = grad_mixed.astype(jnp.bfloat16)
    grad_down = jnp.einsum(
        "tf,td->fd", activated, grad_mixed_low, preferred_element_type=jnp.float32
    )
    grad_act = jnp.einsum("td,fd->tf", grad_mixed_low, w_down, preferred_element_type=jnp.float32)
    pull_back = jax.vjp(
        lambda gate_in, up_in: jax.nn.gelu(gate_in, approximate=True) * up_in, gate_pre, up_pre
    )[1]
    grad_gate_float, grad_up_float = pull_back(grad_act)
    grad_gate_low = grad_gate_float.astype(jnp.bfloat16)
    grad_up_low = grad_up_float.astype(jnp.bfloat16)
    grad_gate_w = jnp.einsum(
        "td,tf->df", hidden_three, grad_gate_low, preferred_element_type=jnp.float32
    )
    grad_up_w = jnp.einsum(
        "td,tf->df", hidden_three, grad_up_low, preferred_element_type=jnp.float32
    )
    grad_hidden_three = head_total(
        jnp.einsum("tf,df->td", grad_gate_low, w_gate, preferred_element_type=jnp.float32)
        + jnp.einsum("tf,df->td", grad_up_low, w_up, preferred_element_type=jnp.float32)
    )
    grad_norm_ff = jnp.sum(grad_hidden_three * normed_three, axis=0)
    grad_after_cross = grad_mixed + rms_back(grad_hidden_three * gain_ff, normed_three, scale_three)
    grad_cross_low = grad_after_cross.astype(jnp.bfloat16)
    grad_c_out = jnp.einsum(
        "ti,td->id", crossed, grad_cross_low, preferred_element_type=jnp.float32
    )
    grad_crossed = jnp.einsum(
        "td,id->ti", grad_cross_low, c_out, preferred_element_type=jnp.float32
    ).astype(jnp.bfloat16)
    grad_cq, grad_keys_enc, grad_values_enc = attend_back(
        cross_queries, keys_enc, values_enc, totals_cross, grad_crossed, None
    )
    grad_cq_low = grad_cq.astype(jnp.bfloat16)
    grad_c_query = jnp.einsum(
        "td,ti->di", hidden_two, grad_cq_low, preferred_element_type=jnp.float32
    )
    grad_hidden_two = head_total(
        jnp.einsum("ti,di->td", grad_cq_low, c_query, preferred_element_type=jnp.float32)
    )
    grad_norm_cross = jnp.sum(grad_hidden_two * normed_two, axis=0)
    grad_after_self = grad_after_cross + rms_back(
        grad_hidden_two * gain_cross, normed_two, scale_two
    )
    grad_self_low = grad_after_self.astype(jnp.bfloat16)
    grad_w_out = jnp.einsum(
        "ti,td->id", attended, grad_self_low, preferred_element_type=jnp.float32
    )
    grad_attended = jnp.einsum(
        "td,id->ti", grad_self_low, w_out, preferred_element_type=jnp.float32
    ).astype(jnp.bfloat16)
    grad_q, grad_keys_group, grad_values_group = attend_back(
        queries, keys_group, values_group, totals_self, grad_attended, allowed
    )
    grad_keys_own, grad_values_own, grad_keys_mine, grad_values_mine = (
        lax.psum_scatter(
            grad_keys_group.astype(jnp.bfloat16), "ctx", scatter_dimension=0, tiled=True
        ).astype(jnp.float32),
        lax.psum_scatter(
            grad_values_group.astype(jnp.bfloat16), "ctx", scatter_dimension=0, tiled=True
        ).astype(jnp.float32),
        lax.psum_scatter(
            grad_keys_enc.astype(jnp.bfloat16), "ctx", scatter_dimension=0, tiled=True
        ).astype(jnp.float32),
        lax.psum_scatter(
            grad_values_enc.astype(jnp.bfloat16), "ctx", scatter_dimension=0, tiled=True
        ).astype(jnp.float32),
    )
    grad_q_low = grad_q.astype(jnp.bfloat16)
    grad_k_low = grad_keys_own.astype(jnp.bfloat16)
    grad_v_low = grad_values_own.astype(jnp.bfloat16)
    grad_kc_low = grad_keys_mine.astype(jnp.bfloat16)
    grad_vc_low = grad_values_mine.astype(jnp.bfloat16)
    grad_w_query = jnp.einsum(
        "td,ti->di", hidden_one, grad_q_low, preferred_element_type=jnp.float32
    )
    grad_w_key = jnp.einsum("td,ti->di", hidden_one, grad_k_low, preferred_element_type=jnp.float32)
    grad_w_value = jnp.einsum(
        "td,ti->di", hidden_one, grad_v_low, preferred_element_type=jnp.float32
    )
    grad_hidden_one = head_total(
        jnp.einsum("ti,di->td", grad_q_low, w_query, preferred_element_type=jnp.float32)
        + jnp.einsum("ti,di->td", grad_k_low, w_key, preferred_element_type=jnp.float32)
        + jnp.einsum("ti,di->td", grad_v_low, w_value, preferred_element_type=jnp.float32)
    )
    grad_norm_self = jnp.sum(grad_hidden_one * normed_one, axis=0)
    grad_tokens = grad_after_self + rms_back(grad_hidden_one * gain_self, normed_one, scale_one)
    grad_c_key = jnp.einsum("ed,ei->di", encoder, grad_kc_low, preferred_element_type=jnp.float32)
    grad_c_value = jnp.einsum("ed,ei->di", encoder, grad_vc_low, preferred_element_type=jnp.float32)
    grad_encoder = lax.psum(
        (
            jnp.einsum("ei,di->ed", grad_kc_low, c_key, preferred_element_type=jnp.float32)
            + jnp.einsum("ei,di->ed", grad_vc_low, c_value, preferred_element_type=jnp.float32)
        ).astype(jnp.bfloat16),
        "tp",
    ).astype(jnp.float32)
    outputs = (mixed.astype(jnp.bfloat16), losses, scores, grad_tokens, grad_encoder)
    grad_terms = (
        grad_w_query,
        grad_w_key,
        grad_w_value,
        grad_w_out,
        grad_c_query,
        grad_c_key,
        grad_c_value,
        grad_c_out,
        grad_gate_w,
        grad_up_w,
        grad_down,
        grad_embed,
        grad_norm_self,
        grad_norm_cross,
        grad_norm_ff,
        grad_norm_exit,
    )
    return (outputs, grad_terms)


def local(
    tokens,
    encoder,
    cotangent,
    parents,
    targets,
    w_query,
    w_key,
    w_value,
    w_out,
    c_query,
    c_key,
    c_value,
    c_out,
    w_gate,
    w_up,
    w_down,
    embedding,
    norm_self,
    norm_cross,
    norm_ff,
    norm_exit,
):
    ctx_index = lax.axis_index("ctx")
    vocab_index = lax.axis_index("tp")
    row_count = tokens.shape[0] // MB
    enc_count = encoder.shape[0] // MB
    results = []
    reduced = None
    for micro_index in range(MB):
        gathered = (
            lax.all_gather(w_query, ("fsdp", "ctx"), axis=0, tiled=True),
            lax.all_gather(w_key, ("fsdp", "ctx"), axis=0, tiled=True),
            lax.all_gather(w_value, ("fsdp", "ctx"), axis=0, tiled=True),
            lax.all_gather(w_out, ("fsdp", "ctx"), axis=1, tiled=True),
            lax.all_gather(c_query, ("fsdp", "ctx"), axis=0, tiled=True),
            lax.all_gather(c_key, ("fsdp", "ctx"), axis=0, tiled=True),
            lax.all_gather(c_value, ("fsdp", "ctx"), axis=0, tiled=True),
            lax.all_gather(c_out, ("fsdp", "ctx"), axis=1, tiled=True),
            lax.all_gather(w_gate, ("fsdp", "ctx"), axis=0, tiled=True),
            lax.all_gather(w_up, ("fsdp", "ctx"), axis=0, tiled=True),
            lax.all_gather(w_down, ("fsdp", "ctx"), axis=1, tiled=True),
            lax.all_gather(embedding, ("fsdp", "ctx"), axis=1, tiled=True),
            lax.all_gather(norm_self, ("fsdp", "ctx"), axis=0, tiled=True),
            lax.all_gather(norm_cross, ("fsdp", "ctx"), axis=0, tiled=True),
            lax.all_gather(norm_ff, ("fsdp", "ctx"), axis=0, tiled=True),
            lax.all_gather(norm_exit, ("fsdp", "ctx"), axis=0, tiled=True),
        )
        first_row = micro_index * row_count
        first_enc = micro_index * enc_count
        outputs, grad_terms = micro_batch(
            tokens[first_row : first_row + row_count],
            encoder[first_enc : first_enc + enc_count],
            cotangent[first_row : first_row + row_count],
            parents[micro_index],
            targets[first_row : first_row + row_count],
            gathered,
            ctx_index,
            vocab_index,
        )
        results.append(outputs)
        shares = (
            lax.psum_scatter(grad_terms[0], ("fsdp", "ctx"), scatter_dimension=0, tiled=True),
            lax.psum_scatter(grad_terms[1], ("fsdp", "ctx"), scatter_dimension=0, tiled=True),
            lax.psum_scatter(grad_terms[2], ("fsdp", "ctx"), scatter_dimension=0, tiled=True),
            lax.psum_scatter(grad_terms[3], ("fsdp", "ctx"), scatter_dimension=1, tiled=True),
            lax.psum_scatter(grad_terms[4], ("fsdp", "ctx"), scatter_dimension=0, tiled=True),
            lax.psum_scatter(grad_terms[5], ("fsdp", "ctx"), scatter_dimension=0, tiled=True),
            lax.psum_scatter(grad_terms[6], ("fsdp", "ctx"), scatter_dimension=0, tiled=True),
            lax.psum_scatter(grad_terms[7], ("fsdp", "ctx"), scatter_dimension=1, tiled=True),
            lax.psum_scatter(grad_terms[8], ("fsdp", "ctx"), scatter_dimension=0, tiled=True),
            lax.psum_scatter(grad_terms[9], ("fsdp", "ctx"), scatter_dimension=0, tiled=True),
            lax.psum_scatter(grad_terms[10], ("fsdp", "ctx"), scatter_dimension=1, tiled=True),
            lax.psum_scatter(grad_terms[11], ("fsdp", "ctx"), scatter_dimension=1, tiled=True),
            lax.psum_scatter(grad_terms[12], ("fsdp", "ctx"), scatter_dimension=0, tiled=True),
            lax.psum_scatter(grad_terms[13], ("fsdp", "ctx"), scatter_dimension=0, tiled=True),
            lax.psum_scatter(grad_terms[14], ("fsdp", "ctx"), scatter_dimension=0, tiled=True),
            lax.psum_scatter(grad_terms[15], ("fsdp", "ctx"), scatter_dimension=0, tiled=True),
        )
        reduced = shares if reduced is None else jax.tree.map(jnp.add, reduced, shares)
    joined = tuple(
        (
            jnp.concatenate([result_part[slot_index] for result_part in results], axis=0)
            for slot_index in range(5)
        )
    )
    return (
        joined[0],
        joined[1],
        joined[2],
        joined[3],
        joined[4],
        reduced[0],
        reduced[1],
        reduced[2],
        reduced[3],
        reduced[4],
        reduced[5],
        reduced[6],
        reduced[7],
        reduced[8],
        reduced[9],
        reduced[10],
        reduced[11],
        reduced[12],
        reduced[13],
        reduced[14],
        reduced[15],
    )


def solution(mesh):
    return jax.shard_map(
        local,
        mesh=mesh,
        in_specs=(
            P(("fsdp", "ctx"), None),
            P(("fsdp", "ctx"), None),
            P(("fsdp", "ctx"), None),
            P("fsdp", None),
            P(("fsdp", "ctx")),
            P(("fsdp", "ctx"), "tp"),
            P(("fsdp", "ctx"), "tp"),
            P(("fsdp", "ctx"), "tp"),
            P("tp", ("fsdp", "ctx")),
            P(("fsdp", "ctx"), "tp"),
            P(("fsdp", "ctx"), "tp"),
            P(("fsdp", "ctx"), "tp"),
            P("tp", ("fsdp", "ctx")),
            P(("fsdp", "ctx"), "tp"),
            P(("fsdp", "ctx"), "tp"),
            P("tp", ("fsdp", "ctx")),
            P("tp", ("fsdp", "ctx")),
            P(("fsdp", "ctx")),
            P(("fsdp", "ctx")),
            P(("fsdp", "ctx")),
            P(("fsdp", "ctx")),
        ),
        out_specs=(
            P(("fsdp", "ctx"), None),
            P(("fsdp", "ctx")),
            P(("fsdp", "ctx")),
            P(("fsdp", "ctx"), None),
            P(("fsdp", "ctx"), None),
            P(("fsdp", "ctx"), "tp"),
            P(("fsdp", "ctx"), "tp"),
            P(("fsdp", "ctx"), "tp"),
            P("tp", ("fsdp", "ctx")),
            P(("fsdp", "ctx"), "tp"),
            P(("fsdp", "ctx"), "tp"),
            P(("fsdp", "ctx"), "tp"),
            P("tp", ("fsdp", "ctx")),
            P(("fsdp", "ctx"), "tp"),
            P(("fsdp", "ctx"), "tp"),
            P("tp", ("fsdp", "ctx")),
            P("tp", ("fsdp", "ctx")),
            P(("fsdp", "ctx")),
            P(("fsdp", "ctx")),
            P(("fsdp", "ctx")),
            P(("fsdp", "ctx")),
        ),
        check_vma=False,
    )
```

profile of v0, /device:TPU:0, one launch (start us, length us, event | category | flops | bytes accessed | tf_op | source)
XLA Modules:
  0.0 2407.5 jit_solution(15336680293357638272)
XLA Ops:
  7.3 17.9 all_gather.167
  115.6 16.8 all_gather.172
  170.5 37.1 %reduce-scatter.49.cloned.1.call-done = f32[128,768]{1,0:T(8,128)} async-done(((f32[512,768]{1,0:T(8,128)}), f32[128,768]{1,0:T(8,128)}) %reduce-scatter.49.cloned.1.call-update) | async-done | bytes 393232 | tf_op jit(solution)/shard_map/reduce_scatter | solution.py:132
  207.7 17.1 all_gather.176
  322.0 18.8 all_gather.180
  398.3 36.4 %reduce-scatter.51.cloned.1.call-done = f32[128,768]{1,0:T(8,128)} async-done(((f32[512,768]{1,0:T(8,128)}), f32[128,768]{1,0:T(8,128)}) %reduce-scatter.51.cloned.1.call-update) | async-done | bytes 393232 | tf_op jit(solution)/shard_map/reduce_scatter | solution.py:132
  434.7 20.2 all_gather.183
  455.0 20.5 all_gather.184
  475.5 19.3 all_gather.185
  525.5 27.9 %reduce-scatter.47.cloned.1.call-done = f32[128,768]{1,0:T(8,128)} async-done(((f32[512,768]{1,0:T(8,128)}), f32[128,768]{1,0:T(8,128)}) %reduce-scatter.47.cloned.1.call-update) | async-done | bytes 393232 | tf_op jit(solution)/shard_map/reduce_scatter | solution.py:132
  553.5 36.4 %reduce-scatter.53.cloned.1.call-done = f32[128,768]{1,0:T(8,128)} async-done(((f32[512,768]{1,0:T(8,128)}), f32[128,768]{1,0:T(8,128)}) %reduce-scatter.53.cloned.1.call-update) | async-done | bytes 393232 | tf_op jit(solution)/shard_map/reduce_scatter | solution.py:132
  590.8 36.8 %all-gather.32.cloned.1.call-done = f32[512,768]{1,0:T(8,128)} async-done(((f32[128,768]{1,0:T(8,128)}), f32[512,768]{1,0:T(8,128)}) %all-gather.32.cloned.1.call-update) | async-done | bytes 1572880 | tf_op jit(solution)/shard_map/all_gather | solution.py:133
  630.3 34.7 %all-gather.38.cloned.1.call-done = f32[512,768]{1,0:T(8,128)} async-done(((f32[128,768]{1,0:T(8,128)}), f32[512,768]{1,0:T(8,128)}) %all-gather.38.cloned.1.call-update) | async-done | bytes 1572880 | tf_op jit(solution)/shard_map/all_gather | solution.py:133
  668.1 68.9 %all-gather.40.cloned.1.call-done = bf16[8032,768]{0,1:T(8,128)(2,1)} async-done(((bf16[8032,96]{0,1:T(8,128)(2,1)}), bf16[8032,768]{0,1:T(8,128)(2,1)}) %all-gather.40.cloned.1.call-update) | async-done | bytes 12337168 | tf_op jit(solution)/shard_map/all_gather | solution.py:385
  737.0 18.3 fusion.267
  767.5 18.4 fusion.268
  908.0 36.4 %reduce-scatter.67.cloned.1.call-done = f32[128,768]{1,0:T(8,128)} async-done(((f32[512,768]{1,0:T(8,128)}), f32[128,768]{1,0:T(8,128)}) %reduce-scatter.67.cloned.1.call-update) | async-done | bytes 393232 | tf_op jit(solution)/shard_map/reduce_scatter | solution.py:132
  944.5 37.4 %all-gather.42.cloned.1.call-done = f32[512,768]{1,0:T(8,128)} async-done(((f32[128,768]{1,0:T(8,128)}), f32[512,768]{1,0:T(8,128)}) %all-gather.42.cloned.1.call-update) | async-done | bytes 1572880 | tf_op jit(solution)/shard_map/all_gather | solution.py:133
  982.0 37.4 %all-gather.50.cloned.1.call-done = f32[512,768]{1,0:T(8,128)} async-done(((f32[128,768]{1,0:T(8,128)}), f32[512,768]{1,0:T(8,128)}) %all-gather.50.cloned.1.call-update) | async-done | bytes 1572880 | tf_op jit(solution)/shard_map/all_gather | solution.py:133
  1039.3 27.3 %reduce-scatter.57.cloned.1.call-done = f32[128,768]{1,0:T(8,128)} async-done(((f32[512,768]{1,0:T(8,128)}), f32[128,768]{1,0:T(8,128)}) %reduce-scatter.57.cloned.1.call-update) | async-done | bytes 393232 | tf_op jit(solution)/shard_map/reduce_scatter | solution.py:132
  1066.7 37.1 %reduce-scatter.69.cloned.1.call-done = f32[128,768]{1,0:T(8,128)} async-done(((f32[512,768]{1,0:T(8,128)}), f32[128,768]{1,0:T(8,128)}) %reduce-scatter.69.cloned.1.call-update) | async-done | bytes 393232 | tf_op jit(solution)/shard_map/reduce_scatter | solution.py:132
  1104.0 37.3 %all-gather.44.cloned.1.call-done = f32[512,768]{1,0:T(8,128)} async-done(((f32[128,768]{1,0:T(8,128)}), f32[512,768]{1,0:T(8,128)}) %all-gather.44.cloned.1.call-update) | async-done | bytes 1572880 | tf_op jit(solution)/shard_map/all_gather | solution.py:133
  1143.7 35.1 %all-gather.52.cloned.1.call-done = f32[512,768]{1,0:T(8,128)} async-done(((f32[128,768]{1,0:T(8,128)}), f32[512,768]{1,0:T(8,128)}) %all-gather.52.cloned.1.call-update) | async-done | bytes 1572880 | tf_op jit(solution)/shard_map/all_gather | solution.py:133
  1193.7 21.8 while.148
  1220.1 23.9 while.150
  1252.6 37.1 %reduce-scatter.71.cloned.1.call-done = f32[128,768]{1,0:T(8,128)} async-done(((f32[512,768]{1,0:T(8,128)}), f32[128,768]{1,0:T(8,128)}) %reduce-scatter.71.cloned.1.call-update) | async-done | bytes 393232 | tf_op jit(solution)/shard_map/reduce_scatter | solution.py:132
  1290.1 37.2 %all-gather.46.cloned.1.call-done = f32[512,768]{1,0:T(8,128)} async-done(((f32[128,768]{1,0:T(8,128)}), f32[512,768]{1,0:T(8,128)}) %all-gather.46.cloned.1.call-update) | async-done | bytes 1572880 | tf_op jit(solution)/shard_map/all_gather | solution.py:133
  1329.2 35.6 %all-gather.54.cloned.1.call-done = f32[512,768]{1,0:T(8,128)} async-done(((f32[128,768]{1,0:T(8,128)}), f32[512,768]{1,0:T(8,128)}) %all-gather.54.cloned.1.call-update) | async-done | bytes 1572880 | tf_op jit(solution)/shard_map/all_gather | solution.py:133
  1375.0 21.3 while.149
  1405.9 21.3 while.151
  1544.1 28.1 %reduce-scatter.65.cloned.1.call-done = f32[128,768]{1,0:T(8,128)} async-done(((f32[512,768]{1,0:T(8,128)}), f32[128,768]{1,0:T(8,128)}) %reduce-scatter.65.cloned.1.call-update) | async-done | bytes 393232 | tf_op jit(solution)/shard_map/reduce_scatter | solution.py:132
  1572.2 37.1 %reduce-scatter.77.cloned.1.call-done = f32[128,768]{1,0:T(8,128)} async-done(((f32[512,768]{1,0:T(8,128)}), f32[128,768]{1,0:T(8,128)}) %reduce-scatter.77.cloned.1.call-update) | async-done | bytes 393232 | tf_op jit(solution)/shard_map/reduce_scatter | solution.py:132
  1641.5 18.6 fusion.235
  1662.6 25.8 %convolution_add_fusion = f32[8032,768]{0,1:T(8,128)} fusion(f32[8032,768]{0,1:T(8,128)} %fusion.235, f32[512,768]{1,0:T(8,128)S(1)} %copy-done.27, f32[512]{0:T(512)S(1)} %copy-done.161, f32[768]{0:T(1024)S(1)} %copy-done.173, f32[512,8032]{0,1:T(8,128)} %get-tuple-element.1056, f32[512]{0:T(512)S(1)} %copy-done.164, s32[512]{0:T(512)S(1)} %copy-done.159, ...), kind=kOutput, calls=%fused_computation.210 | convolution fusion | flops 6344925184 | bytes 67412352 | tf_op jit(solution)/shard_map/tv,td->vd/dot_general | solution.py:219
  1693.4 77.2 %all-reduce.13.cloned.1.call-done = (bf16[1024,768]{1,0:T(8,128)(2,1)}, bf16[1024,768]{1,0:T(8,128)(2,1)}) async-done(((bf16[1024,768]{1,0:T(8,128)(2,1)}, bf16[1024,768]{1,0:T(8,128)(2,1)}), (bf16[1024,768]{1,0:T(8,128)(2,1)}, bf16[1024,768]{1,0:T(8,128)(2,1)})) %all-reduce.13.cloned.1.call-update) | async-done | bytes 3145744 | tf_op jit(solution)/shard_map/psum | solution.py:314
  1775.7 32.1 %reduce-scatter.103.cloned.1.call-done = f32[96,192]{1,0:T(8,128)} async-done(((f32[768,192]{1,0:T(8,128)}), f32[96,192]{1,0:T(8,128)}) %reduce-scatter.103.cloned.1.call-update) | async-done | bytes 73744
  1809.5 36.9 %all-gather.48.cloned.1.call-done = f32[512,768]{1,0:T(8,128)} async-done(((f32[128,768]{1,0:T(8,128)}), f32[512,768]{1,0:T(8,128)}) %all-gather.48.cloned.1.call-update) | async-done | bytes 1572880 | tf_op jit(solution)/shard_map/all_gather | solution.py:133
  1846.4 37.6 %all-gather.56.cloned.1.call-done = f32[512,768]{1,0:T(8,128)} async-done(((f32[128,768]{1,0:T(8,128)}), f32[512,768]{1,0:T(8,128)}) %all-gather.56.cloned.1.call-update) | async-done | bytes 1572880 | tf_op jit(solution)/shard_map/all_gather | solution.py:133
  1886.8 24.1 %all-reduce.8 = (f32[768]{0:T(1024)S(1)}, f32[768]{0:T(1024)S(1)}, f32[768]{0:T(1024)S(1)}, f32[768]{0:T(1024)S(1)}) all-reduce(f32[768]{0:T(1024)S(1)} %add.628, f32[768]{0:T(1024)S(1)} %add.629, f32[768]{0:T(1024)S(1)} %add.630, f32[768]{0:T(1024)S(1)} %add.631), channel_id=58, replica_groups=mesh['fsdp'=4,'ctx'=2,'tp'=4] {'fsdp','ctx'}, use_global_device_ids=true, to_apply=%region_103.104.clone | all-reduce | flops 3072 | bytes 24576
  1925.2 42.4 %reduce-scatter.97.cloned.1.call-done = f32[96,512]{1,0:T(8,128)} async-done(((f32[768,512]{1,0:T(8,128)}), f32[96,512]{1,0:T(8,128)}) %reduce-scatter.97.cloned.1.call-update) | async-done | bytes 196624 | tf_op jit(solution)/shard_map/reduce_scatter | solution.py:414
  1967.6 42.2 %reduce-scatter.99.cloned.1.call-done = f32[512,96]{0,1:T(8,128)} async-done(((f32[512,768]{0,1:T(8,128)}), f32[512,96]{0,1:T(8,128)}) %reduce-scatter.99.cloned.1.call-update) | async-done | bytes 196624 | tf_op jit(solution)/shard_map/reduce_scatter | solution.py:415
  2009.8 38.7 %reduce-scatter.93.cloned.1.call-done = f32[96,192]{1,0:T(8,128)} async-done(((f32[768,192]{1,0:T(8,128)}), f32[96,192]{1,0:T(8,128)}) %reduce-scatter.93.cloned.1.call-update) | async-done | bytes 73744 | tf_op jit(solution)/shard_map/reduce_scatter | solution.py:409
  2048.5 38.6 %reduce-scatter.105.cloned.1.call-done = f32[96,192]{1,0:T(8,128)} async-done(((f32[768,192]{1,0:T(8,128)}), f32[96,192]{1,0:T(8,128)}) %reduce-scatter.105.cloned.1.call-update) | async-done | bytes 73744
  2087.2 38.6 %reduce-scatter.107.cloned.1.call-done = f32[96,192]{1,0:T(8,128)} async-done(((f32[768,192]{1,0:T(8,128)}), f32[96,192]{1,0:T(8,128)}) %reduce-scatter.107.cloned.1.call-update) | async-done | bytes 73744
  2125.7 38.6 %reduce-scatter.87.cloned.1.call-done = f32[96,192]{1,0:T(8,128)} async-done(((f32[768,192]{1,0:T(8,128)}), f32[96,192]{1,0:T(8,128)}) %reduce-scatter.87.cloned.1.call-update) | async-done | bytes 73744 | tf_op jit(solution)/shard_map/reduce_scatter | solution.py:405
  2164.3 38.6 %reduce-scatter.89.cloned.1.call-done = f32[96,192]{1,0:T(8,128)} async-done(((f32[768,192]{1,0:T(8,128)}), f32[96,192]{1,0:T(8,128)}) %reduce-scatter.89.cloned.1.call-update) | async-done | bytes 73744 | tf_op jit(solution)/shard_map/reduce_scatter | solution.py:406
  2202.9 38.6 %reduce-scatter.91.cloned.1.call-done = f32[96,192]{1,0:T(8,128)} async-done(((f32[768,192]{1,0:T(8,128)}), f32[96,192]{1,0:T(8,128)}) %reduce-scatter.91.cloned.1.call-update) | async-done | bytes 73744 | tf_op jit(solution)/shard_map/reduce_scatter | solution.py:407
  2241.5 159.2 %reduce-scatter.101.cloned.1.call-done = f32[8032,96]{0,1:T(8,128)} async-done(((f32[8032,768]{0,1:T(8,128)}), f32[8032,96]{0,1:T(8,128)}) %reduce-scatter.101.cloned.1.call-update) | async-done | bytes 3084304 | tf_op jit(solution)/shard_map/reduce_scatter | solution.py:416
  (991 shorter events, 839.0 us)
Async XLA Ops:
  7.2 163.2 %reduce-scatter.43.cloned.1.call-start = ((), (), s32[]{:S(2)}) async-start(), calls=%async_computation.34 | async-start | bytes 1966080 | tf_op jit(solution)/shard_map/reduce_scatter | solution.py:132
  134.8 72.9 %reduce-scatter.49.cloned.1.call-start = ((), (), s32[]{:S(2)}) async-start(), calls=%async_computation.40 | async-start | bytes 1966080 | tf_op jit(solution)/shard_map/reduce_scatter | solution.py:132
  164.2 176.6 %all-gather.28.cloned.1.call-start = ((), (), s32[]{:S(2)}) async-start(), calls=%async_computation.35 | async-start | bytes 1966080 | tf_op jit(solution)/shard_map/all_gather | solution.py:133
  170.5 170.4 %all-gather.34.cloned.1.call-start = ((), (), s32[]{:S(2)}) async-start(), calls=%async_computation.41 | async-start | bytes 1966080 | tf_op jit(solution)/shard_map/all_gather | solution.py:133
  207.7 190.5 %reduce-scatter.45.cloned.1.call-start = ((), (), s32[]{:S(2)}) async-start(), calls=%async_computation.36 | async-start | bytes 1966080 | tf_op jit(solution)/shard_map/reduce_scatter | solution.py:132
  365.3 69.4 %reduce-scatter.51.cloned.1.call-start = ((), (), s32[]{:S(2)}) async-start(), calls=%async_computation.42 | async-start | bytes 1966080 | tf_op jit(solution)/shard_map/reduce_scatter | solution.py:132
  390.6 104.1 %all-gather.30.cloned.1.call-start = ((), (), s32[]{:S(2)}) async-start(), calls=%async_computation.37 | async-start | bytes 1966080 | tf_op jit(solution)/shard_map/all_gather | solution.py:133
  398.2 111.6 %all-gather.36.cloned.1.call-start = ((), (), s32[]{:S(2)}) async-start(), calls=%async_computation.43 | async-start | bytes 1966080 | tf_op jit(solution)/shard_map/all_gather | solution.py:133
  434.7 118.7 %reduce-scatter.47.cloned.1.call-start = ((), (), s32[]{:S(2)}) async-start(), calls=%async_computation.38 | async-start | bytes 1966080 | tf_op jit(solution)/shard_map/reduce_scatter | solution.py:132
  519.1 70.7 %reduce-scatter.53.cloned.1.call-start = ((), (), s32[]{:S(2)}) async-start(), calls=%async_computation.44 | async-start | bytes 1966080 | tf_op jit(solution)/shard_map/reduce_scatter | solution.py:132
  525.4 102.1 %all-gather.32.cloned.1.call-start = ((), (), s32[]{:S(2)}) async-start(), calls=%async_computation.39 | async-start | bytes 1966080 | tf_op jit(solution)/shard_map/all_gather | solution.py:133
  553.4 111.5 %all-gather.38.cloned.1.call-start = ((), (), s32[]{:S(2)}) async-start(), calls=%async_computation.45 | async-start | bytes 1966080 | tf_op jit(solution)/shard_map/all_gather | solution.py:133
  589.9 147.1 %all-gather.40.cloned.1.call-start = ((), (), s32[]{:S(2)}) async-start(), calls=%async_computation.46 | async-start | bytes 13934592 | tf_op jit(solution)/shard_map/all_gather | solution.py:385
  590.6 317.4 %reduce-scatter.55.cloned.1.call-start = ((), (), s32[]{:S(2)}) async-start(), calls=%async_computation.47 | async-start | bytes 1966080 | tf_op jit(solution)/shard_map/reduce_scatter | solution.py:132
  874.9 69.5 %reduce-scatter.67.cloned.1.call-start = ((), (), s32[]{:S(2)}) async-start(), calls=%async_computation.57 | async-start | bytes 1966080 | tf_op jit(solution)/shard_map/reduce_scatter | solution.py:132
  891.5 90.4 %all-gather.42.cloned.1.call-start = ((), (), s32[]{:S(2)}) async-start(), calls=%async_computation.48 | async-start | bytes 1966080 | tf_op jit(solution)/shard_map/all_gather | solution.py:133
  908.0 111.4 %all-gather.50.cloned.1.call-start = ((), (), s32[]{:S(2)}) async-start(), calls=%async_computation.58 | async-start | bytes 1966080 | tf_op jit(solution)/shard_map/all_gather | solution.py:133
  944.5 122.1 %reduce-scatter.57.cloned.1.call-start = ((), (), s32[]{:S(2)}) async-start(), calls=%async_computation.49 | async-start | bytes 1966080 | tf_op jit(solution)/shard_map/reduce_scatter | solution.py:132
  1032.3 71.5 %reduce-scatter.69.cloned.1.call-start = ((), (), s32[]{:S(2)}) async-start(), calls=%async_computation.59 | async-start | bytes 1966080 | tf_op jit(solution)/shard_map/reduce_scatter | solution.py:132
  1039.3 102.0 %all-gather.44.cloned.1.call-start = ((), (), s32[]{:S(2)}) async-start(), calls=%async_computation.50 | async-start | bytes 1966080 | tf_op jit(solution)/shard_map/all_gather | solution.py:133
  1066.6 112.2 %all-gather.52.cloned.1.call-start = ((), (), s32[]{:S(2)}) async-start(), calls=%async_computation.60 | async-start | bytes 1966080 | tf_op jit(solution)/shard_map/all_gather | solution.py:133
  1103.8 148.8 %reduce-scatter.59.cloned.1.call-start = ((), (), s32[]{:S(2)}) async-start(), calls=%async_computation.51 | async-start | bytes 1966080 | tf_op jit(solution)/shard_map/reduce_scatter | solution.py:132
  1218.3 71.5 %reduce-scatter.71.cloned.1.call-start = ((), (), s32[]{:S(2)}) async-start(), calls=%async_computation.61 | async-start | bytes 1966080 | tf_op jit(solution)/shard_map/reduce_scatter | solution.py:132
  1246.7 80.6 %all-gather.46.cloned.1.call-start = ((), (), s32[]{:S(2)}) async-start(), calls=%async_computation.52 | async-start | bytes 1966080 | tf_op jit(solution)/shard_map/all_gather | solution.py:133
  1252.6 112.2 %all-gather.54.cloned.1.call-start = ((), (), s32[]{:S(2)}) async-start(), calls=%async_computation.62 | async-start | bytes 1966080 | tf_op jit(solution)/shard_map/all_gather | solution.py:133
  1289.8 143.3 %reduce-scatter.61.cloned.1.call-start = ((), (), s32[]{:S(2)}) async-start(), calls=%async_computation.53 | async-start | bytes 589824 | tf_op jit(solution)/shard_map/reduce_scatter | solution.py:280
  1396.3 39.5 %reduce-scatter.63.cloned.1.call-start = ((), (), s32[]{:S(2)}) async-start(), calls=%async_computation.54 | async-start | bytes 589824 | tf_op jit(solution)/shard_map/reduce_scatter | solution.py:283
  1427.9 46.8 %reduce-scatter.83.cloned.1.call-start = ((), (), s32[]{:S(2)}) async-start(), calls=%async_computation.69 | async-start | bytes 1179648 | tf_op jit(solution)/shard_map/reduce_scatter | solution.py:286
  1428.5 66.0 %reduce-scatter.79.cloned.1.call-start = ((), (), s32[]{:S(2)}) async-start(), calls=%async_computation.67 | async-start | bytes 1179648 | tf_op jit(solution)/shard_map/reduce_scatter | solution.py:286
  1429.3 85.0 %reduce-scatter.85.cloned.1.call-start = ((), (), s32[]{:S(2)}) async-start(), calls=%async_computation.70 | async-start | bytes 1179648 | tf_op jit(solution)/shard_map/reduce_scatter | solution.py:289
  1430.0 103.9 %reduce-scatter.81.cloned.1.call-start = ((), (), s32[]{:S(2)}) async-start(), calls=%async_computation.68 | async-start | bytes 1179648 | tf_op jit(solution)/shard_map/reduce_scatter | solution.py:289
  1430.6 141.6 %reduce-scatter.65.cloned.1.call-start = ((), (), s32[]{:S(2)}) async-start(), calls=%async_computation.55 | async-start | bytes 1966080 | tf_op jit(solution)/shard_map/reduce_scatter | solution.py:132
  1439.5 169.8 %reduce-scatter.77.cloned.1.call-start = ((), (), s32[]{:S(2)}) async-start(), calls=%async_computation.65 | async-start | bytes 1966080 | tf_op jit(solution)/shard_map/reduce_scatter | solution.py:132
  1458.8 233.0 %reduce-scatter.109.cloned.1.call-start = ((), (), s32[]{:S(2)}) async-start(), calls=%async_computation.82 | async-start | bytes 884736
  1465.1 305.6 %all-reduce.13.cloned.1.call-start = ((), (), s32[]{:S(2)}) async-start(), calls=%async_computation.83 | async-start | bytes 6291456 | tf_op jit(solution)/shard_map/psum | solution.py:314
  1537.8 270.1 %reduce-scatter.103.cloned.1.call-start = ((), (), s32[]{:S(2)}) async-start(), calls=%async_computation.79 | async-start | bytes 884736
  1544.1 302.3 %all-gather.48.cloned.1.call-start = ((), (), s32[]{:S(2)}) async-start(), calls=%async_computation.56 | async-start | bytes 1966080 | tf_op jit(solution)/shard_map/all_gather | solution.py:133
  1572.2 311.8 %all-gather.56.cloned.1.call-start = ((), (), s32[]{:S(2)}) async-start(), calls=%async_computation.66 | async-start | bytes 1966080 | tf_op jit(solution)/shard_map/all_gather | solution.py:133
  1609.4 315.8 %reduce-scatter.95.cloned.1.call-start = ((), (), s32[]{:S(2)}) async-start(), calls=%async_computation.75 | async-start | bytes 1769472 | tf_op jit(solution)/shard_map/reduce_scatter | solution.py:413
  1613.2 354.4 %reduce-scatter.97.cloned.1.call-start = ((), (), s32[]{:S(2)}) async-start(), calls=%async_computation.76 | async-start | bytes 1769472 | tf_op jit(solution)/shard_map/reduce_scatter | solution.py:414
  1617.1 392.7 %reduce-scatter.99.cloned.1.call-start = ((), (), s32[]{:S(2)}) async-start(), calls=%async_computation.77 | async-start | bytes 1769472 | tf_op jit(solution)/shard_map/reduce_scatter | solution.py:415
  1621.4 427.1 %reduce-scatter.93.cloned.1.call-start = ((), (), s32[]{:S(2)}) async-start(), calls=%async_computation.74 | async-start | bytes 884736 | tf_op jit(solution)/shard_map/reduce_scatter | solution.py:409
  1624.2 463.0 %reduce-scatter.105.cloned.1.call-start = ((), (), s32[]{:S(2)}) async-start(), calls=%async_computation.80 | async-start | bytes 884736
  1631.2 494.5 %reduce-scatter.107.cloned.1.call-start = ((), (), s32[]{:S(2)}) async-start(), calls=%async_computation.81 | async-start | bytes 884736
  1636.5 527.9 %reduce-scatter.87.cloned.1.call-start = ((), (), s32[]{:S(2)}) async-start(), calls=%async_computation.71 | async-start | bytes 884736 | tf_op jit(solution)/shard_map/reduce_scatter | solution.py:405
  1638.8 564.1 %reduce-scatter.89.cloned.1.call-start = ((), (), s32[]{:S(2)}) async-start(), calls=%async_computation.72 | async-start | bytes 884736 | tf_op jit(solution)/shard_map/reduce_scatter | solution.py:406
  1641.2 600.3 %reduce-scatter.91.cloned.1.call-start = ((), (), s32[]{:S(2)}) async-start(), calls=%async_computation.73 | async-start | bytes 884736 | tf_op jit(solution)/shard_map/reduce_scatter | solution.py:407
  1662.5 738.2 %reduce-scatter.101.cloned.1.call-start = ((), (), s32[]{:S(2)}) async-start(), calls=%async_computation.78 | async-start | bytes 27869184 | tf_op jit(solution)/shard_map/reduce_scatter | solution.py:416
  (242 other events, 4749.9 us)
Sparse Core Ops, SparseCore 0:
  134.8 35.5 reduce-scatter.42
  173.3 34.2 reduce-scatter.48
  209.2 36.0 all-gather.27
  246.7 35.9 all-gather.33
  365.4 32.7 reduce-scatter.44
  400.3 34.2 reduce-scatter.50
  436.2 36.0 all-gather.29
  473.9 35.9 all-gather.35
  519.2 34.1 reduce-scatter.46
  555.5 34.2 reduce-scatter.52
  591.4 36.0 all-gather.31
  628.9 35.9 all-gather.37
  666.8 70.1 all-gather.39
  875.1 32.8 reduce-scatter.54
  910.1 34.2 reduce-scatter.66
  945.9 36.0 all-gather.41
  983.4 35.9 all-gather.49
  1032.4 34.1 reduce-scatter.56
  1069.5 34.2 reduce-scatter.68
  1105.2 36.0 all-gather.43
  1142.8 35.9 all-gather.51
  1218.4 34.1 reduce-scatter.58
  1255.4 34.2 reduce-scatter.70
  1291.2 36.0 all-gather.45
  1328.8 35.9 all-gather.53
  1411.2 13.1 reduce-scatter.62
  1442.1 13.1 reduce-scatter.74
  1457.3 17.4 reduce-scatter.82
  1477.1 17.4 reduce-scatter.78
  1496.8 17.4 reduce-scatter.84
  1516.5 17.4 reduce-scatter.80
  1536.8 35.3 reduce-scatter.64
  1575.0 34.2 reduce-scatter.76
  1612.3 33.9 reduce-scatter.108
  1649.2 121.4 all-reduce.12
  1773.8 33.9 reduce-scatter.102
  1809.3 37.0 all-gather.47
  1848.0 35.9 all-gather.55
  1887.8 37.3 reduce-scatter.94
  1929.1 38.4 reduce-scatter.96
  1971.3 38.4 reduce-scatter.98
  2013.5 34.9 reduce-scatter.92
  2052.1 35.0 reduce-scatter.104
  2090.7 34.9 reduce-scatter.106
  2129.3 34.9 reduce-scatter.86
  2167.9 34.9 reduce-scatter.88
  2206.5 34.9 reduce-scatter.90
  2245.9 154.8 reduce-scatter.100
  (2 shorter events, 24.2 us)
where the time goes:
time: 2420 us; the launch traced here: 2410 us
  waiting for transfers between devices  1490 us (62%)
  blocking collectives  386 us (16%)
  matrix products  321 us (13%)
  local copies, waits for them, and re-layouts  103 us (4%)
  other arithmetic  86.2 us (4%)
    all_gather x14, waiting for transfers between devices, head_total(): return lax.all_gather(shares, 'tp', axis=0, tiled=True)  378 us
    reduce_scatter x14, waiting for transfers between devices, head_total(): lax.psum_scatter(partial_value, 'tp', scatter_dimension=0, tiled=True)  377 us
    reduce_scatter x1, waiting for transfers between devices, local(): lax.psum_scatter(grad_terms[11], ('fsdp', 'ctx'), scatter_dimension=1, ti...  159 us
    unnamed x54, waiting for transfers between devices  114 us
    psum x1, waiting for transfers between devices, micro_batch(): lax.psum((jnp.einsum('ei,di->ed', grad_kc_low, c_key, preferred_element_t...  77.2 us
    all_gather x6, blocking collectives, merged(): gathered = jax.tree.map(lambda a: lax.all_gather(a, axis), part)  71.5 us
    all_gather x1, waiting for transfers between devices, local(): lax.all_gather(embedding, ('fsdp', 'ctx'), axis=1, tiled=True)  68.9 us
    dot_general x24, matrix products, mat(): return jnp.dot(left, right, preferred_element_type=jnp.float32)  65.1 us
  transfers between devices with their start and end apart: 50, of which 43 were waited for; matrix products, arithmetic and copies ran while one was open for 12% of the time, Pallas kernels for 0%

commit v1 on v0

v1 whole, which is shorter than its diff:
```python
import functools
import math

import jax
import jax.numpy as jnp
from jax import lax
from jax.experimental import pallas as pl
from jax.experimental.pallas import tpu as pltpu
from jax.sharding import PartitionSpec as P

HD = 64
BLK = 128
MB = 2
EPSILON = 1e-06
MASKED = -1000000000.0
F32 = jnp.float32
BF16 = jnp.bfloat16
PLANE = ("fsdp", "ctx")
VMEM_LIMIT = 48 * 1024 * 1024


def mat(left, right):
    return jnp.dot(left, right, preferred_element_type=F32)


def mat_nt(left, right):
    return lax.dot_general(left, right, (((1,), (1,)), ((), ())), preferred_element_type=F32)


def mat_tn(left, right):
    return lax.dot_general(left, right, (((0,), (0,)), ((), ())), preferred_element_type=F32)


def swap(value, axis, bit):
    count = lax.axis_size(axis)
    return lax.ppermute(value, axis, [(i, i ^ bit) for i in range(count)])


def core_swap(value):
    return swap(value, "fsdp", 1)


def small_plane():
    return lax.axis_size("fsdp") == 4 and lax.axis_size("ctx") == 2


def coords():
    f = lax.axis_index("fsdp")
    return f // 2, f % 2, lax.axis_index("ctx")


def ordered(pieces, y, core, x):
    rows, columns = pieces[0][0][0].shape
    out = jnp.zeros((8 * rows, columns), pieces[0][0][0].dtype)
    for dy in range(2):
        for dc in range(2):
            for dx in range(2):
                index = ((y ^ dy) * 2 + (core ^ dc)) * 2 + (x ^ dx)
                out = lax.dynamic_update_slice(out, pieces[dy][dc][dx], (index * rows, 0))
    return out


def chips_gather(first, second):
    first_x = swap(first, "ctx", 1)
    second_y = swap(second, "fsdp", 2)
    first_pair = jnp.stack([first, first_x])
    second_pair = jnp.stack([second, second_y])
    first_far = swap(first_pair, "fsdp", 2)
    second_far = swap(second_pair, "ctx", 1)
    firsts = [[first, first_x], [first_far[0], first_far[1]]]
    seconds = [[second, second_far[0]], [second_y, second_far[1]]]
    return firsts, seconds


def plane_gather(shard):
    if not small_plane():
        return lax.all_gather(shard, PLANE, axis=0, tiled=True)
    y, core, x = coords()
    half = shard.shape[1] // 2
    firsts, seconds = chips_gather(shard[:, :half], shard[:, half:])
    mine = [
        [jnp.concatenate([firsts[dy][dx], seconds[dy][dx]], axis=1) for dx in range(2)]
        for dy in range(2)
    ]
    other = core_swap(jnp.stack([mine[0][0], mine[0][1], mine[1][0], mine[1][1]]))
    pieces = [[mine[dy], [other[dy * 2], other[dy * 2 + 1]]] for dy in range(2)]
    return ordered(pieces, y, core, x)


def embed_gather(shard):
    half = shard.shape[1] // 2
    y, core, x = coords()
    if not small_plane():
        whole = lax.all_gather(shard, PLANE, axis=0, tiled=True)
        return lax.dynamic_slice_in_dim(whole, core * half, half, 1)
    firsts, seconds = chips_gather(shard[:, :half], shard[:, half:])
    flat_first = jnp.stack([firsts[0][0], firsts[0][1], firsts[1][0], firsts[1][1]])
    flat_second = jnp.stack([seconds[0][0], seconds[0][1], seconds[1][0], seconds[1][1]])
    is_first = core == 0
    keep = jnp.where(is_first, flat_first, flat_second)
    give = jnp.where(is_first, flat_second, flat_first)
    other = core_swap(give)
    pieces = [
        [[keep[dy * 2], keep[dy * 2 + 1]], [other[dy * 2], other[dy * 2 + 1]]] for dy in range(2)
    ]
    return ordered(pieces, y, core, x)


def pick(value, index):
    return lax.dynamic_index_in_dim(value, index, 0, False)


def low_sum(left, right):
    return (left.astype(F32) + right.astype(F32)).astype(BF16)


def chips_scatter(first, second, y, x):
    first_mid = low_sum(pick(first, y), swap(pick(first, 1 - y), "fsdp", 2))
    moved = jnp.moveaxis(second, 1, 0)
    second_mid = low_sum(pick(moved, x), swap(pick(moved, 1 - x), "ctx", 1))
    first_out = pick(first_mid, x).astype(F32) + swap(pick(first_mid, 1 - x), "ctx", 1).astype(F32)
    second_out = pick(second_mid, y).astype(F32) + swap(pick(second_mid, 1 - y), "fsdp", 2).astype(
        F32
    )
    return first_out, second_out


def plane_scatter(total):
    if not small_plane():
        return lax.psum_scatter(total.astype(F32), PLANE, scatter_dimension=0, tiled=True)
    y, core, x = coords()
    rows, columns = total.shape[0] // 8, total.shape[1]
    blocks = total.reshape(2, 2, 2, rows, columns)
    keep = lax.dynamic_index_in_dim(blocks, core, 1, False)
    give = lax.dynamic_index_in_dim(blocks, 1 - core, 1, False)
    chip = low_sum(keep, core_swap(give))
    half = columns // 2
    first, second = chips_scatter(chip[..., :half], chip[..., half:], y, x)
    return jnp.concatenate([first, second], axis=1)


def embed_scatter(total):
    y, core, x = coords()
    rows, half = total.shape[0] // 8, total.shape[1]
    if not small_plane():
        n_plane = lax.axis_size("fsdp") * lax.axis_size("ctx")
        whole = jnp.zeros((total.shape[0], 2 * half), F32)
        whole = lax.dynamic_update_slice(whole, total.astype(F32), (0, core * half))
        return lax.psum_scatter(whole, PLANE, scatter_dimension=0, tiled=True)
    blocks = jnp.moveaxis(total.reshape(2, 2, 2, rows, half), 1, 2)
    first, second = chips_scatter(blocks[:, :, 0], blocks[:, :, 1], y, x)
    is_first = core == 0
    keep = jnp.where(is_first, first, second)
    give = jnp.where(is_first, second, first)
    other = core_swap(give.astype(BF16)).astype(F32)
    return jnp.concatenate(
        [jnp.where(is_first, keep, other), jnp.where(is_first, other, keep)], axis=1
    )


def tp_list(value):
    count = lax.axis_size("tp")
    return [value] + [
        lax.ppermute(value, "tp", [(i, (i + k) % count) for i in range(count)])
        for k in range(1, count)
    ]


def tp_sum(partial):
    count = lax.axis_size("tp")
    t = lax.axis_index("tp")
    rows = partial.shape[0] // count
    low = partial.astype(BF16)

    def block(k):
        return lax.dynamic_slice_in_dim(low, ((t + k) % count) * rows, rows, 0)

    total = lax.dynamic_slice_in_dim(partial, t * rows, rows, 0)
    for k in range(1, count):
        got = lax.ppermute(block(k), "tp", [(i, (i + k) % count) for i in range(count)])
        total = total + got.astype(F32)
    shares = tp_list(total.astype(BF16))
    ring = jnp.concatenate(shares[::-1] * 2, axis=0)
    return lax.dynamic_slice_in_dim(ring, ((count - 1 - t) % count) * rows, count * rows, 0).astype(
        F32
    )


def ctx_gather(value):
    if lax.axis_size("ctx") == 2:
        return jnp.concatenate([value, swap(value, "ctx", 1)], axis=0)
    return lax.all_gather(value, "ctx", axis=0, tiled=True)


def ctx_positions(rows):
    c, count = lax.axis_index("ctx"), lax.axis_size("ctx")
    if count == 2:
        return jnp.concatenate(
            [c * rows + jnp.arange(rows), (1 - c) * rows + jnp.arange(rows)]
        ).astype(jnp.int32)
    return jnp.arange(rows * count, dtype=jnp.int32)


def ctx_scatter(value):
    if lax.axis_size("ctx") == 2:
        rows = value.shape[0] // 2
        return low_sum(value[:rows], swap(value[rows:], "ctx", 1))
    return lax.psum_scatter(value.astype(F32), "ctx", scatter_dimension=0, tiled=True).astype(BF16)


def forward_kernel(heads, q_ref, kv_ref, bias_ref, out_ref, total_ref):
    width = heads * HD
    for h in range(heads):
        cols = slice(h * HD, (h + 1) * HD)
        keys = kv_ref[:, cols]
        values = kv_ref[:, width + h * HD : width + (h + 1) * HD]
        scores = mat_nt(keys, q_ref[:, cols])
        if bias_ref is not None:
            scores = scores + bias_ref[...]
        highest = jnp.max(scores, axis=0, keepdims=True)
        exponent = jnp.exp(scores - highest)
        denominator = jnp.sum(exponent, axis=0, keepdims=True)
        outcome = mat_tn(values, exponent.astype(BF16)) / denominator
        out_ref[:, cols] = outcome.T.astype(BF16)
        total_ref[h : h + 1, :] = highest + jnp.log(denominator)


def backward_kernel(
    heads, q_ref, kv_ref, bias_ref, total_ref, go_ref, dq_ref, dkv_ref, acc_ref
):
    width = heads * HD
    step = pl.program_id(0)

    @pl.when(step == 0)
    def _():
        acc_ref[...] = jnp.zeros_like(acc_ref)

    for h in range(heads):
        cols = slice(h * HD, (h + 1) * HD)
        vcols = slice(width + h * HD, width + (h + 1) * HD)
        keys, values = kv_ref[:, cols], kv_ref[:, vcols]
        queries, go = q_ref[:, cols], go_ref[:, cols]
        scores = mat_nt(keys, queries)
        if bias_ref is not None:
            scores = scores + bias_ref[...]
        probs = jnp.exp(scores - total_ref[h : h + 1, :])
        grad_probs = mat_nt(values, go)
        inner = jnp.sum(probs * grad_probs, axis=0, keepdims=True)
        grad_scores = (probs * (grad_probs - inner)).astype(BF16)
        acc_ref[:, vcols] += mat(probs.astype(BF16), go)
        acc_ref[:, cols] += mat(grad_scores, queries)
        dq_ref[:, cols] = mat_tn(keys, grad_scores).T.astype(BF16)

    @pl.when(step == pl.num_programs(0) - 1)
    def _():
        dkv_ref[...] = acc_ref[...].astype(BF16)


def attention_specs(rows, width, keys, tile, masked):
    specs = [
        pl.BlockSpec((tile, width), lambda i: (i, 0)),
        pl.BlockSpec((keys, 2 * width), lambda i: (0, 0)),
    ]
    if masked:
        specs.append(pl.BlockSpec((keys, tile), lambda i: (0, i)))
    return specs


def attend(queries, kv, bias):
    rows, width = queries.shape
    keys, heads = kv.shape[0], width // HD
    tile = min(rows, 256)
    masked = bias is not None
    body = functools.partial(forward_kernel, heads)
    if not masked:
        plain = body
        body = lambda q, k, o, t: plain(q, k, None, o, t)
    return pl.pallas_call(
        body,
        grid=(rows // tile,),
        in_specs=attention_specs(rows, width, keys, tile, masked),
        out_specs=[
            pl.BlockSpec((tile, width), lambda i: (i, 0)),
            pl.BlockSpec((heads, tile), lambda i: (0, i)),
        ],
        out_shape=[
            jax.ShapeDtypeStruct((rows, width), BF16),
            jax.ShapeDtypeStruct((heads, rows), F32),
        ],
        compiler_params=pltpu.CompilerParams(vmem_limit_bytes=VMEM_LIMIT),
        cost_estimate=pl.CostEstimate(
            flops=16 * rows * keys * width,
            bytes_accessed=4 * keys * width + 8 * rows * width,
            transcendentals=rows * keys * heads,
        ),
        name="attend_masked" if masked else "attend",
    )(*([queries, kv, bias] if masked else [queries, kv]))


def attend_back(queries, kv, bias, totals, go):
    rows, width = queries.shape
    keys, heads = kv.shape[0], width // HD
    tile = min(rows, 256)
    masked = bias is not None
    body = functools.partial(backward_kernel, heads)
    if not masked:
        plain = body
        body = lambda q, k, *rest: plain(q, k, None, *rest)
    specs = attention_specs(rows, width, keys, tile, masked) + [
        pl.BlockSpec((heads, tile), lambda i: (0, i)),
        pl.BlockSpec((tile, width), lambda i: (i, 0)),
    ]
    operands = ([queries, kv, bias] if masked else [queries, kv]) + [totals, go]
    return pl.pallas_call(
        body,
        grid=(rows // tile,),
        in_specs=specs,
        out_specs=[
            pl.BlockSpec((tile, width), lambda i: (i, 0)),
            pl.BlockSpec((keys, 2 * width), lambda i: (0, 0)),
        ],
        out_shape=[
            jax.ShapeDtypeStruct((rows, width), BF16),
            jax.ShapeDtypeStruct((keys, 2 * width), BF16),
        ],
        scratch_shapes=[pltpu.VMEM((keys, 2 * width), F32)],
        compiler_params=pltpu.CompilerParams(vmem_limit_bytes=VMEM_LIMIT),
        cost_estimate=pl.CostEstimate(
            flops=40 * rows * keys * width,
            bytes_accessed=8 * keys * width + 10 * rows * width,
            transcendentals=rows * keys * heads,
        ),
        name="attend_back_masked" if masked else "attend_back",
    )(*operands)


def rms_scale(values):
    return lax.rsqrt(jnp.mean(values * values, axis=-1, keepdims=True) + EPSILON)


def rms_back(grad_normed, normed, scale):
    return scale * (grad_normed - normed * jnp.mean(grad_normed * normed, axis=-1, keepdims=True))


def mask_bias(parent_row, row_count):
    block_count = parent_row.shape[0]
    blocks = jnp.arange(block_count, dtype=jnp.int32)
    current = blocks
    reachable = blocks[:, None] == blocks[None, :]
    for _ in range(block_count - 1):
        current = jnp.sum(
            jnp.where(current[:, None] == blocks[None, :], parent_row[None, :], 0), axis=1
        )
        reachable = reachable | (current[:, None] == blocks[None, :])
    query_pos = lax.axis_index("ctx") * row_count + jnp.arange(row_count, dtype=jnp.int32)
    key_pos = ctx_positions(row_count)
    query_onehot = (query_pos[:, None] // BLK == blocks[None, :]).astype(F32)
    key_onehot = (key_pos[:, None] // BLK == blocks[None, :]).astype(F32)
    linked = mat_nt(key_onehot, mat(query_onehot, reachable.astype(F32))) > 0.5
    causal = (query_pos[None, :] // BLK != key_pos[:, None] // BLK) | (
        key_pos[:, None] <= query_pos[None, :]
    )
    return jnp.where(linked & causal, 0.0, MASKED)


def gelu_parts(gate):
    root = math.sqrt(2.0 / math.pi)
    inner = jnp.tanh(root * (gate + 0.044715 * gate * gate * gate))
    value = 0.5 * gate * (1.0 + inner)
    slope = 0.5 * (1.0 + inner) + 0.5 * gate * (1.0 - inner * inner) * root * (
        1.0 + 3.0 * 0.044715 * gate * gate
    )
    return value, slope


def head_stats(stats):
    tp_count, f_count = lax.axis_size("tp"), lax.axis_size("fsdp")
    rows = stats.shape[1] // 2
    parts = []
    for dc in range(2):
        for k in range(tp_count):
            if dc == 0 and k == 0:
                parts.append(stats)
                continue
            perm = [
                (f * tp_count + t, (f ^ dc) * tp_count + (t + k) % tp_count)
                for f in range(f_count)
                for t in range(tp_count)
            ]
            got = lax.ppermute(stats, ("fsdp", "tp"), perm)
            if dc == 1:
                got = jnp.concatenate([got[:, rows:], got[:, :rows]], axis=1)
            parts.append(got)
    highest = functools.reduce(jnp.maximum, [part[0] for part in parts])
    total = sum(part[1] * jnp.exp(part[0] - highest) for part in parts)
    picked = sum(part[2] for part in parts)
    return highest, highest + jnp.log(total), picked


def local(
    tokens,
    encoder,
    cotangent,
    parents,
    targets,
    w_query,
    w_key,
    w_value,
    w_out,
    c_query,
    c_key,
    c_value,
    c_out,
    w_gate,
    w_up,
    w_down,
    embedding,
    norm_self,
    norm_cross,
    norm_ff,
    norm_exit,
):
    t = lax.axis_index("tp")
    core = lax.axis_index("fsdp") % 2
    rows = tokens.shape[0] // MB
    enc_rows = encoder.shape[0] // MB
    features = tokens.shape[1]
    width = w_query.shape[1]
    hidden_units = w_gate.shape[1]
    tp_count = lax.axis_size("tp")
    trees = range(MB)

    def tree_rows(value, i):
        count = value.shape[0] // MB
        return value[i * count : (i + 1) * count]

    w_heads = plane_gather(
        jnp.concatenate([w_query, w_key, w_value, c_key, c_value, c_query], axis=1)
    )
    w_qkv = w_heads[:, : 3 * width]
    c_kv = w_heads[:, 3 * width : 5 * width]
    c_q = w_heads[:, 5 * width :]
    gains = plane_gather(
        jnp.pad(
            jnp.stack([norm_self, norm_cross, norm_ff, norm_exit], axis=1), ((0, 0), (0, 252))
        )
    )[:, :4].astype(F32)
    gain_self, gain_cross, gain_ff, gain_exit = (gains[:, j][None, :] for j in range(4))
    pieces = tp_list(
        jnp.concatenate([w_out.T, c_out.T, c_query, w_gate, w_up, w_down.T], axis=1)
    )
    spans = [0, width, 2 * width, 3 * width]
    spans += [spans[-1] + hidden_units * j for j in (1, 2, 3)]
    ordered_pieces = [
        jnp.concatenate([piece[:, spans[j] : spans[j + 1]] for piece in pieces], axis=1)
        for j in range(6)
    ]
    whole = plane_gather(jnp.concatenate(ordered_pieces, axis=1))
    cuts = [tp_count * s for s in spans]
    w_out_t, c_out_t, c_query_all, gate_all, up_all, down_t = (
        whole[:, cuts[j] : cuts[j + 1]] for j in range(6)
    )
    embed_t = embed_gather(embedding.T)
    vocab_half = embed_t.shape[1]

    tok = tokens.astype(F32)
    scale_one = rms_scale(tok)
    normed_one = tok * scale_one
    hidden_one = (normed_one * gain_self).astype(BF16)
    qkv = mat(hidden_one, w_qkv).astype(BF16)
    enc_kv = mat(encoder, c_kv).astype(BF16)
    queries = [tree_rows(qkv, i)[:, :width] for i in trees]
    kv_self = [ctx_gather(tree_rows(qkv, i)[:, width:]) for i in trees]
    kv_cross = [ctx_gather(tree_rows(enc_kv, i)) for i in trees]
    biases = [mask_bias(parents[i], rows) for i in trees]
    targets_all = [
        jnp.concatenate([tree_rows(targets, i), core_swap(tree_rows(targets, i))]) for i in trees
    ]
    shrink = 1.0 / math.sqrt(features)

    saved = []
    for i in trees:
        attended, totals_self = attend(queries[i], kv_self[i], biases[i])
        attended_all = jnp.concatenate(tp_list(attended), axis=1)
        after_self = tree_rows(tok, i) + mat_nt(attended_all, w_out_t)
        scale_two = rms_scale(after_self)
        normed_two = after_self * scale_two
        hidden_two = (normed_two * gain_cross).astype(BF16)
        cross_q = mat(hidden_two, c_q).astype(BF16)
        crossed, totals_cross = attend(cross_q, kv_cross[i], None)
        crossed_all = jnp.concatenate(tp_list(crossed), axis=1)
        after_cross = after_self + mat_nt(crossed_all, c_out_t)
        scale_three = rms_scale(after_cross)
        normed_three = after_cross * scale_three
        hidden_three = (normed_three * gain_ff).astype(BF16)
        gate_pre = mat(hidden_three, gate_all)
        up_pre = mat(hidden_three, up_all)
        activated = (gelu_parts(gate_pre)[0] * up_pre).astype(BF16)
        mixed = after_cross + mat_nt(activated, down_t)
        scale_four = rms_scale(mixed)
        normed_four = mixed * scale_four
        exit_own = (normed_four * gain_exit * shrink).astype(BF16)
        exit_in = jnp.concatenate([exit_own, core_swap(exit_own)], axis=0)
        saved.append(
            dict(
                attended=attended,
                totals_self=totals_self,
                scale_two=scale_two,
                normed_two=normed_two,
                hidden_two=hidden_two,
                cross_q=cross_q,
                crossed=crossed,
                totals_cross=totals_cross,
                scale_three=scale_three,
                normed_three=normed_three,
                hidden_three=hidden_three,
                gate_pre=gate_pre,
                up_pre=up_pre,
                activated=activated,
                mixed=mixed,
                scale_four=scale_four,
                normed_four=normed_four,
                exit_in=exit_in,
            )
        )

    columns = (t * 2 + core) * vocab_half + jnp.arange(vocab_half, dtype=jnp.int32)
    losses, scores, grad_embed = [], [], None
    for i in trees:
        s = saved[i]
        logits = mat(s["exit_in"], embed_t)
        hits = columns[None, :] == targets_all[i][:, None]
        highest = jnp.max(logits, axis=-1)
        summed = jnp.sum(jnp.exp(logits - highest[:, None]), axis=-1)
        picked = jnp.sum(jnp.where(hits, logits, 0.0), axis=-1)
        top, log_total, picked = head_stats(jnp.stack([highest, summed, picked]))
        losses.append((log_total - picked)[:rows])
        scores.append((top - log_total)[:rows])
        grad_logits = (jnp.exp(logits - log_total[:, None]) - hits.astype(F32)).astype(BF16)
        grad_exit_part = mat_nt(grad_logits, embed_t)
        s["grad_exit_part"] = grad_exit_part[:rows] + core_swap(
            grad_exit_part[rows:].astype(BF16)
        ).astype(F32)
        s["grad_exit"] = tp_sum(s["grad_exit_part"]) * shrink
        term = mat_tn(s["exit_in"], grad_logits)
        grad_embed = term if grad_embed is None else grad_embed + term
    grad_embed_own = embed_scatter(grad_embed.astype(BF16))

    norm_terms = [0.0, 0.0, 0.0, 0.0]
    grads = [None] * 7

    def add(j, term):
        grads[j] = term if grads[j] is None else grads[j] + term

    def norm_add(j, grad, normed):
        norm_terms[j] = norm_terms[j] + jnp.sum(grad * normed, axis=0)

    grad_tokens, grad_encoder = [], []
    for i in trees:
        s = saved[i]
        grad_exit = s["grad_exit"]
        norm_add(3, grad_exit, s["normed_four"])
        grad_mixed = tree_rows(cotangent, i).astype(F32) + rms_back(
            grad_exit * gain_exit, s["normed_four"], s["scale_four"]
        )
        grad_mixed_low = grad_mixed.astype(BF16)
        add(6, mat_tn(grad_mixed_low, s["activated"][:, :hidden_units]))
        grad_act = mat(grad_mixed_low, down_t)
        value, slope = gelu_parts(s["gate_pre"])
        grad_gate = (grad_act * slope * s["up_pre"]).astype(BF16)
        grad_up = (grad_act * value).astype(BF16)
        add(4, mat_tn(s["hidden_three"], grad_gate[:, :hidden_units]))
        add(5, mat_tn(s["hidden_three"], grad_up[:, :hidden_units]))
        grad_three = mat_nt(grad_gate, gate_all) + mat_nt(grad_up, up_all)
        norm_add(2, grad_three, s["normed_three"])
        grad_after_cross = grad_mixed + rms_back(
            grad_three * gain_ff, s["normed_three"], s["scale_three"]
        )
        grad_cross_low = grad_after_cross.astype(BF16)
        add(3, mat_tn(grad_cross_low, s["crossed"]))
        grad_crossed = mat(grad_cross_low, c_out_t[:, :width]).astype(BF16)
        grad_cq, grad_kv = attend_back(
            s["cross_q"], kv_cross[i], None, s["totals_cross"], grad_crossed
        )
        grad_kv = ctx_scatter(grad_kv)
        s["grad_kv_cross"] = grad_kv
        grad_encoder.append(tp_sum(mat_nt(grad_kv, c_kv)))
        s["grad_cq"] = grad_cq
        grad_cq_all = jnp.concatenate(tp_list(grad_cq), axis=1)
        grad_two = mat_nt(grad_cq_all, c_query_all)
        norm_add(1, grad_two, s["normed_two"])
        grad_after_self = grad_after_cross + rms_back(
            grad_two * gain_cross, s["normed_two"], s["scale_two"]
        )
        grad_self_low = grad_after_self.astype(BF16)
        add(2, mat_tn(grad_self_low, s["attended"]))
        grad_attended = mat(grad_self_low, w_out_t[:, :width]).astype(BF16)
        grad_q, grad_kv = attend_back(
            queries[i], kv_self[i], biases[i], s["totals_self"], grad_attended
        )
        grad_qkv = jnp.concatenate([grad_q, ctx_scatter(grad_kv)], axis=1)
        add(0, mat_tn(tree_rows(hidden_one, i), grad_qkv))
        grad_one = tp_sum(mat_nt(grad_qkv, w_qkv))
        norm_add(0, grad_one, tree_rows(normed_one, i))
        grad_tokens.append(
            grad_after_self
            + rms_back(grad_one * gain_self, tree_rows(normed_one, i), tree_rows(scale_one, i))
        )
        add(
            1,
            jnp.concatenate(
                [
                    mat_tn(tree_rows(encoder, i), grad_kv_part)
                    for grad_kv_part in (s["grad_kv_cross"],)
                ]
                + [mat_tn(s["hidden_two"], grad_cq)],
                axis=1,
            ),
        )

    ff_own = plane_scatter(
        jnp.concatenate([grads[3], grads[4], grads[5], grads[6]], axis=1).astype(BF16)
    )
    norm_block = jnp.pad(jnp.stack(norm_terms, axis=1), ((0, 0), (0, 60)))
    own = plane_scatter(
        jnp.concatenate([grads[0], grads[1], grads[2], norm_block], axis=1).astype(BF16)
    )

    def part(value, start, size):
        return value[:, start : start + size]

    base = 7 * width
    return (
        jnp.concatenate([s["mixed"].astype(BF16) for s in saved], axis=0),
        jnp.concatenate(losses),
        jnp.concatenate(scores),
        jnp.concatenate(grad_tokens, axis=0),
        jnp.concatenate(grad_encoder, axis=0),
        part(own, 0, width),
        part(own, width, width),
        part(own, 2 * width, width),
        part(own, 6 * width, width).T,
        part(own, 5 * width, width),
        part(own, 3 * width, width),
        part(own, 4 * width, width),
        part(ff_own, 0, width).T,
        part(ff_own, width, hidden_units),
        part(ff_own, width + hidden_units, hidden_units),
        part(ff_own, width + 2 * hidden_units, hidden_units).T,
        grad_embed_own.T,
        own[:, base],
        own[:, base + 1],
        own[:, base + 2],
        own[:, base + 3],
    )


def solution(mesh):
    rows_cols = P(PLANE, "tp")
    cols_rows = P("tp", PLANE)
    data = P(PLANE, None)
    flat = P(PLANE)
    weights = (rows_cols,) * 3 + (cols_rows,) + (rows_cols,) * 3 + (cols_rows,)
    weights += (rows_cols,) * 2 + (cols_rows,) * 2 + (flat,) * 4
    return jax.shard_map(
        local,
        mesh=mesh,
        in_specs=(data, data, data, P("fsdp", None), flat) + weights,
        out_specs=(data, flat, flat, data, data) + weights,
        check_vma=False,
    )
```

time: 2420 us -> 1040 us (0.43)
  waiting for transfers between devices: 1490 us -> 309 us
  blocking collectives: 386 us -> 0 us
  starting transfers between devices: 3.54 us -> 173 us
  matrix products: 321 us -> 215 us
  Pallas kernels: 0 us -> 59.4 us
  local copies, waits for them, and re-layouts: 103 us -> 162 us
    reduce_scatter x30 -> x0, waiting for transfers between devices: 850 us -> none  [the longest x14 377 us: head_total(): lax.psum_scatter(partial_value, 'tp', scatter_dimension=0, tiled=True)]
    all_gather x15 -> x0, waiting for transfers between devices: 447 us -> none  [the longest x14 378 us: head_total(): return lax.all_gather(shares, 'tp', axis=0, tiled=True)]
    all_gather x25 -> x0, blocking collectives: 347 us -> none  [the longest x6 71.5 us: merged(): gathered = jax.tree.map(lambda a: lax.all_gather(a, axis), part)]
    ppermute x0 -> x120, waiting for transfers between devices: none -> 309 us  [the longest x49 132 us: swap(): return lax.ppermute(value, axis, [(i, i ^ bit) for i in range(count)])]
    ppermute x0 -> x120, starting transfers between devices: none -> 173 us  [the longest x39 82.9 us: tp_list(): lax.ppermute(value, 'tp', [(i, (i + k) % count) for i in range(count)])]
    unnamed x54 -> x0, waiting for transfers between devices: 114 us -> none
    dot_general x166 -> x52, matrix products: 321 us -> 212 us  [the longest x20 79.7 us: mat_nt(): lax.dot_general(left, right, (((1,), (1,)), ((), ())), preferred_element_...]
    psum x1 -> x0, waiting for transfers between devices: 77.2 us -> none  [micro_batch(): lax.psum((jnp.einsum('ei,di->ed', grad_kc_low, c_key, preferred_element_t...]
  transfers between devices with their start and end apart: 50 -> 120, of which waited for: 43 -> 44; matrix products, arithmetic and copies ran while one was open for 12% -> 39% of each run, Pallas kernels for 0% -> 6%
where the time goes in v1:
time: 1040 us; the launch traced here: 1020 us
  waiting for transfers between devices  309 us (30%)
  matrix products  215 us (21%)
  starting transfers between devices  173 us (17%)
  local copies, waits for them, and re-layouts  162 us (16%)
  other arithmetic  101 us (10%)
  Pallas kernels  59.4 us (6%)
    ppermute x49, waiting for transfers between devices, swap(): return lax.ppermute(value, axis, [(i, i ^ bit) for i in range(count)])  132 us
    ppermute x39, waiting for transfers between devices, tp_list(): lax.ppermute(value, 'tp', [(i, (i + k) % count) for i in range(count)])  109 us
    ppermute x39, starting transfers between devices, tp_list(): lax.ppermute(value, 'tp', [(i, (i + k) % count) for i in range(count)])  82.9 us
    dot_general x20, matrix products, mat_nt(): lax.dot_general(left, right, (((1,), (1,)), ((), ())), preferred_element_...  79.7 us
    dot_general x16, matrix products, mat(): return jnp.dot(left, right, preferred_element_type=F32)  69.8 us
    ppermute x18, waiting for transfers between devices, tp_sum(): lax.ppermute(block(k), 'tp', [(i, (i + k) % count) for i in range(count)])  63 us
    dot_general x16, matrix products, mat_tn(): lax.dot_general(left, right, (((0,), (0,)), ((), ())), preferred_element_...  62.2 us
    ppermute x49, starting transfers between devices, swap(): return lax.ppermute(value, axis, [(i, i ^ bit) for i in range(count)])  38.9 us
  transfers between devices with their start and end apart: 120, of which 44 were waited for; matrix products, arithmetic and copies ran while one was open for 39% of the time, Pallas kernels for 6%

profile of v1, /device:TPU:0, one launch (start us, length us, event | category | flops | bytes accessed | tf_op | source)
XLA Modules:
  0.0 1023.9 jit_solution(13978457188296557515)
XLA Ops:
  72.4 6.5 collective-permute-done.7
  80.3 6.1 collective-permute-done.8
  110.6 5.4 broadcast_in_dim.99
  149.9 23.9 %collective-permute-done.10 = bf16[512,384]{1,0:T(8,128)(2,1)S(1)} collective-permute-done((bf16[512,384]{1,0:T(8,128)(2,1)S(1)}, bf16[512,384]{1,0:T(8,128)(2,1)S(1)}, u32[]{:S(2)}, u32[]{:S(2)}) %collective-permute-start.10) | collective-permute-done | bytes 393248 | tf_op jit(solution)/shard_map/ppermute | solution.py:36
  173.9 8.3 collective-permute-done.26
  191.6 7.7 collective-permute-done.22
  201.0 15.1 %collective-permute-done.30 = bf16[1024,384]{1,0:T(8,128)(2,1)} collective-permute-done((bf16[1024,384]{1,0:T(8,128)(2,1)S(1)}, bf16[1024,384]{1,0:T(8,128)(2,1)}, u32[]{:S(2)}, u32[]{:S(2)}) %collective-permute-start.30) | collective-permute-done | bytes 786464 | tf_op jit(solution)/shard_map/ppermute | solution.py:36
  225.4 24.8 %collective-permute-done.19 = bf16[2,96,4224]{2,1,0:T(8,128)(2,1)} collective-permute-done((bf16[2,96,4224]{2,1,0:T(8,128)(2,1)}, bf16[2,96,4224]{2,1,0:T(8,128)(2,1)}, u32[]{:S(2)}, u32[]{:S(2)}) %collective-permute-start.19) | collective-permute-done | bytes 1622048 | tf_op jit(solution)/shard_map/ppermute | solution.py:36
  261.5 5.6 collective-permute-done.21
  280.4 7.7 attend.2
  297.6 8.1 attend.3
  308.3 7.0 collective-permute-done.24
  320.1 16.9 %collective-permute-done.32 = bf16[512,192]{1,0:T(8,128)(2,1)S(1)} collective-permute-done((bf16[512,192]{1,0:T(8,128)(2,1)S(1)}, bf16[512,192]{1,0:T(8,128)(2,1)S(1)}, u32[]{:S(2)}, u32[]{:S(2)}) %collective-permute-start.32) | collective-permute-done | bytes 196640 | tf_op jit(solution)/shard_map/ppermute | solution.py:164
  340.0 5.0 fusion.49
  361.8 9.5 fusion.361
  371.4 18.2 %fusion.362 = (f32[1024]{0:T(1024)S(1)}, f32[1024,4016]{0,1:T(8,128)}) fusion(bf16[768,4016]{1,0:T(8,128)(2,1)} %fusion.133, bf16[512,768]{1,0:T(8,128)(2,1)} %collective-permute-done.48, bf16[512,768]{1,0:T(8,128)(2,1)S(1)} %get-tuple-element.357), kind=kOutput, calls=%fused_computation.715 | convolution fusion | flops 6323878912 | bytes 24195072 | tf_op jit(solution)/shard_map/dot_general | solution.py:23
  389.5 11.4 %exponential_reduce_fusion.1 = (f32[1024]{0:T(1024)S(1)}, f32[1024]{0:T(1024)S(1)}, f32[1024]{0:T(1024)S(1)}, f32[1024]{0:T(1024)S(1)}) fusion(f32[1024,4016]{0,1:T(8,128)S(1)} %get-tuple-element.381, f32[1024]{0:T(1024)S(1)} %get-tuple-element.380, s32[1024]{0:T(1024)S(1)} %pad_add_fusion.1, s32[4016]{0:T(1024)S(1)} %iota_add_fusion, ...), kind=kLoop, calls=%fused_computation.11 | loop fusion | flops 41119744 | bytes 32947904 | tf_op jit(solution)/shard_map/reduce_sum | solution.py:534
  415.9 15.9 %fusion.326 = f32[1024,768]{1,0:T(8,128)S(1)} fusion(bf16[768,4016]{1,0:T(8,128)(2,1)} %fusion.133, f32[1024,4016]{0,1:T(8,128)} %copy-done.51, f32[1024]{0:T(1024)S(1)} %get-tuple-element.172, s32[1024]{0:T(1024)S(1)} %pad_add_fusion.1, s32[4016]{0:T(1024)S(1)} %iota_add_fusion), kind=kOutput, calls=%fused_computation.681 | convolution fusion | flops 6337183744 | bytes 25788096 | tf_op jit(solution)/shard_map/dot_general | solution.py:27
  438.0 17.7 %fusion.323 = f32[1024,768]{1,0:T(8,128)} fusion(bf16[768,4016]{1,0:T(8,128)(2,1)} %fusion.133, f32[1024,4016]{0,1:T(8,128)} %get-tuple-element.383, f32[1024]{0:T(1024)S(1)} %get-tuple-element.174, s32[1024]{0:T(1024)S(1)} %pad_add_fusion.2, s32[4016]{0:T(1024)S(1)} %iota_add_fusion), kind=kOutput, calls=%fused_computation.680 | convolution fusion | flops 6337183744 | bytes 25788096 | tf_op jit(solution)/shard_map/dot_general | solution.py:27
  458.1 15.7 %fusion.127 = f32[768,4016]{0,1:T(8,128)} fusion(bf16[512,768]{1,0:T(8,128)(2,1)} %collective-permute-done.48, bf16[512,768]{1,0:T(8,128)(2,1)S(1)} %get-tuple-element.357, f32[1024,4016]{0,1:T(8,128)} %get-tuple-element.383, f32[1024]{0:T(1024)S(1)} %get-tuple-element.174, s32[1024]{0:T(1024)S(1)} %pad_add_fusion.2, s32[4016]{0:T(1024)S(1)} %iota_add_fusion), kind=kOutput, calls=%fused_computation.231 | convolution fusion | flops 6340329472 | bytes 30383808 | tf_op jit(solution)/shard_map/dot_general | solution.py:31
  473.8 16.2 %add_convert_fusion = bf16[768,4016]{0,1:T(8,128)(2,1)} fusion(f32[768,4016]{0,1:T(8,128)} %fusion.127, bf16[512,768]{1,0:T(8,128)(2,1)S(1)} %copy-done.155, bf16[512,768]{1,0:T(8,128)(2,1)S(1)} %get-tuple-element.356, f32[1024,4016]{0,1:T(8,128)} %copy-done.51, f32[1024]{0:T(1024)S(1)} %get-tuple-element.172, s32[1024]{0:T(1024)S(1)} %pad_add_fusion.1, ...), kind=kOutput, calls=%fused_computation.12 | convolution fusion | flops 6346498048 | bytes 36552384 | tf_op jit(solution)/shard_map/dot_general | solution.py:31
  490.0 8.6 copy.134
  518.6 9.4 collective-permute-done.59
  528.0 8.4 collective-permute-start.75
  536.6 8.4 collective-permute-done.76
  545.0 8.3 collective-permute-start.63
  553.7 8.6 collective-permute-done.62
  562.4 7.9 collective-permute-start.80
  570.4 8.0 collective-permute-done.79
  583.7 5.9 fusion.15
  594.4 5.9 fusion.21
  610.5 11.7 %attend_back.2 = (bf16[512,192]{1,0:T(8,128)(2,1)}, bf16[2048,384]{1,0:T(8,128)(2,1)S(1)}) custom-call(bf16[512,192]{1,0:T(8,128)(2,1)S(1)} %copy-done.21, bf16[2048,384]{1,0:T(8,128)(2,1)S(1)} %copy-done.3, f32[3,512]{1,0:T(4,128)S(1)} %get-tuple-element.41.rest_0_, bf16[512,192]{1,0:T(8,128)(2,1)S(1)} %copy-done.26), custom_call_target="tpu_custom_call" | custom-call | flops 8053063680 | bytes 4128768 | tf_op jit(solution)/shard_map/attend_back/pallas_call | solution.py:314
  643.5 10.8 %attend_back.3 = (bf16[512,192]{1,0:T(8,128)(2,1)S(1)}, bf16[2048,384]{1,0:T(8,128)(2,1)S(1)}) custom-call(bf16[512,192]{1,0:T(8,128)(2,1)S(1)} %copy-done.19, bf16[2048,384]{1,0:T(8,128)(2,1)S(1)} %copy-done.1, f32[3,512]{1,0:T(4,128)S(1)} %get-tuple-element.46.rest_0_, bf16[512,192]{1,0:T(8,128)(2,1)S(1)} %copy-done.27), custom_call_target="tpu_custom_call" | custom-call | flops 8053063680 | bytes 4128768 | tf_op jit(solution)/shard_map/attend_back/pallas_call | solution.py:314
  671.7 5.5 concatenate.297
  694.4 15.3 %collective-permute-done.82 = bf16[512,192]{1,0:T(8,128)(2,1)S(1)} collective-permute-done((bf16[512,192]{1,0:T(8,128)(2,1)S(1)}, bf16[512,192]{1,0:T(8,128)(2,1)S(1)}, u32[]{:S(2)}, u32[]{:S(2)}) %collective-permute-start.82) | collective-permute-done | bytes 196640 | tf_op jit(solution)/shard_map/ppermute | solution.py:164
  730.5 6.3 attend_back_masked.2
  736.9 5.9 attend_back_masked.3
  803.0 11.3 %collective-permute-done.86 = bf16[128,768]{1,0:T(8,128)(2,1)S(1)} collective-permute-done((bf16[128,768]{1,0:T(8,128)(2,1)}, bf16[128,768]{1,0:T(8,128)(2,1)S(1)}, u32[]{:S(2)}, u32[]{:S(2)}) %collective-permute-start.86) | collective-permute-done | bytes 196640 | tf_op jit(solution)/shard_map/ppermute | solution.py:180
  832.0 7.5 collective-permute-start.89
  845.5 5.6 collective-permute-done.90
  851.1 11.4 %collective-permute-start.100 = (bf16[256,768]{1,0:T(8,128)(2,1)}, bf16[256,768]{1,0:T(8,128)(2,1)}, u32[]{:S(2)}, u32[]{:S(2)}) collective-permute-start(bf16[256,768]{1,0:T(8,128)(2,1)} %get-tuple-element.207), channel_id=1, source_target_pairs={{0,2},{1,3},{2,0},{3,1},{4,6},{5,7},{6,4},{7,5},{8,10},{9,11},{10,... | collective-permute-start | bytes 1179656 | tf_op jit(solution)/shard_map/ppermute | solution.py:180
  867.6 5.0 concatenate.291
  883.3 10.7 %collective-permute-done.100 = bf16[256,768]{1,0:T(8,128)(2,1)} collective-permute-done((bf16[256,768]{1,0:T(8,128)(2,1)}, bf16[256,768]{1,0:T(8,128)(2,1)}, u32[]{:S(2)}, u32[]{:S(2)}) %collective-permute-start.100) | collective-permute-done | bytes 393248 | tf_op jit(solution)/shard_map/ppermute | solution.py:180
  899.0 17.5 %collective-permute-done.93 = bf16[256,768]{1,0:T(8,128)(2,1)S(1)} collective-permute-done((bf16[256,768]{1,0:T(8,128)(2,1)S(1)}, bf16[256,768]{1,0:T(8,128)(2,1)S(1)}, u32[]{:S(2)}, u32[]{:S(2)}) %collective-permute-start.93) | collective-permute-done | bytes 393248 | tf_op jit(solution)/shard_map/ppermute | solution.py:180
  916.5 14.6 %collective-permute-start.103 = (bf16[256,768]{1,0:T(8,128)(2,1)S(1)}, bf16[256,768]{1,0:T(8,128)(2,1)S(1)}, u32[]{:S(2)}, u32[]{:S(2)}) collective-permute-start(bf16[256,768]{1,0:T(8,128)(2,1)S(1)} %add_convert_fusion.7), channel_id=1, source_target_pairs={{0,2},{1,3},{2,0},{3,1},{4,6},{5,7},{6,4},{7,5},{8,10},{9,11},{10,... | collective-permute-start | bytes 1179656 | tf_op jit(solution)/shard_map/ppermute | solution.py:164
  938.6 20.9 %collective-permute-done.103 = bf16[256,768]{1,0:T(8,128)(2,1)S(1)} collective-permute-done((bf16[256,768]{1,0:T(8,128)(2,1)S(1)}, bf16[256,768]{1,0:T(8,128)(2,1)S(1)}, u32[]{:S(2)}, u32[]{:S(2)}) %collective-permute-start.103) | collective-permute-done | bytes 393248 | tf_op jit(solution)/shard_map/ppermute | solution.py:164
  959.5 6.2 collective-permute-start.97
  967.3 15.4 %collective-permute-done.96 = bf16[256,768]{1,0:T(8,128)(2,1)S(1)} collective-permute-done((bf16[256,768]{1,0:T(8,128)(2,1)S(1)}, bf16[256,768]{1,0:T(8,128)(2,1)S(1)}, u32[]{:S(2)}, u32[]{:S(2)}) %collective-permute-start.96) | collective-permute-done | bytes 393248 | tf_op jit(solution)/shard_map/ppermute | solution.py:164
  (927 shorter events, 506.0 us)
Async XLA Ops:
  4.7 87.1 %collective-permute-start.15 = (bf16[96,2112]{1,0:T(8,128)(2,1)}, bf16[96,2112]{1,0:T(8,128)(2,1)}, u32[]{:S(2)}, u32[]{:S(2)}) collective-permute-start(bf16[96,2112]{1,0:T(8,128)(2,1)} %concatenate.241), channel_id=1, source_target_pairs={{0,2},{1,3},{2,0},{3,1},{4,6},{5,7},{6,4},{7,5},{8,10},{9,11},{10,... | collective-permute-start | bytes 1216520 | tf_op jit(solution)/shard_map/ppermute | solution.py:164
  8.7 82.0 %collective-permute-start.14 = (bf16[96,2112]{1,0:T(8,128)(2,1)}, bf16[96,2112]{1,0:T(8,128)(2,1)}, u32[]{:S(2)}, u32[]{:S(2)}) collective-permute-start(bf16[96,2112]{1,0:T(8,128)(2,1)} %concatenate.241), channel_id=1, source_target_pairs={{0,1},{1,2},{2,3},{3,0},{4,5},{5,6},{6,7},{7,4},{8,9},{9,10},{10,1... | collective-permute-start | bytes 1216520 | tf_op jit(solution)/shard_map/ppermute | solution.py:164
  10.3 78.8 %collective-permute-start.16 = (bf16[96,2112]{1,0:T(8,128)(2,1)}, bf16[96,2112]{1,0:T(8,128)(2,1)}, u32[]{:S(2)}, u32[]{:S(2)}) collective-permute-start(bf16[96,2112]{1,0:T(8,128)(2,1)} %concatenate.241), channel_id=1, source_target_pairs={{0,3},{1,0},{2,1},{3,2},{4,7},{5,4},{6,5},{7,6},{8,11},{9,8},{10,9... | collective-permute-start | bytes 1216520 | tf_op jit(solution)/shard_map/ppermute | solution.py:164
  12.6 24.7 %collective-permute-start.1 = (bf16[96,128]{0,1:T(8,128)(2,1)S(1)}, bf16[96,128]{0,1:T(8,128)(2,1)S(1)}, u32[]{:S(2)}, u32[]{:S(2)}) collective-permute-start(bf16[96,128]{0,1:T(8,128)(2,1)S(1)} %slice.637), channel_id=1, source_target_pairs={{0,16},{8,24},{16,0},{24,8},{1,17},{9,25},{17,1},{25,9},{2,18},{10... | collective-permute-start | bytes 73736 | tf_op jit(solution)/shard_map/ppermute | solution.py:36
  53.4 65.5 %collective-permute-start.35 = (bf16[96,4016]{1,0:T(8,128)(2,1)}, bf16[96,4016]{1,0:T(8,128)(2,1)}, u32[]{:S(2)}, u32[]{:S(2)}) collective-permute-start(bf16[96,4016]{1,0:T(8,128)(2,1)} %get-tuple-element.216), channel_id=1, source_target_pairs={{0,4},{4,0},{1,5},{5,1},{2,6},{6,2},{3,7},{7,3},{8,12},{12,8},{9,1... | collective-permute-start | bytes 2313224 | tf_op jit(solution)/shard_map/ppermute | solution.py:36
  86.5 35.3 %collective-permute-start.37 = (bf16[96,4016]{1,0:T(8,128)(2,1)}, bf16[96,4016]{1,0:T(8,128)(2,1)}, u32[]{:S(2)}, u32[]{:S(2)}) collective-permute-start(bf16[96,4016]{1,0:T(8,128)(2,1)} %get-tuple-element.215), channel_id=1, source_target_pairs={{0,16},{8,24},{16,0},{24,8},{1,17},{9,25},{17,1},{25,9},{2,18},{10... | collective-permute-start | bytes 2313224 | tf_op jit(solution)/shard_map/ppermute | solution.py:36
  89.1 43.9 %collective-permute-start.9 = (bf16[4,96,1152]{2,1,0:T(8,128)(2,1)}, bf16[4,96,1152]{2,1,0:T(8,128)(2,1)}, u32[]{:S(2)}, u32[]{:S(2)}) collective-permute-start(bf16[4,96,1152]{2,1,0:T(8,128)(2,1)} %pad_maximum_fusion.21), channel_id=1, source_target_pairs={{0,8},{8,0},{16,24},{24,16},{1,9},{9,1},{17,25},{25,17},{2,10},{10... | collective-permute-start | bytes 2654216 | tf_op jit(solution)/shard_map/ppermute | solution.py:36
  99.5 26.8 %collective-permute-start.18 = (bf16[96,4224]{1,0:T(8,128)(2,1)}, bf16[96,4224]{1,0:T(8,128)(2,1)S(1)}, u32[]{:S(2)}, u32[]{:S(2)}) collective-permute-start(bf16[96,4224]{1,0:T(8,128)(2,1)} %get-tuple-element.226), channel_id=1, source_target_pairs={{0,16},{8,24},{16,0},{24,8},{1,17},{9,25},{17,1},{25,9},{2,18},{10... | collective-permute-start | bytes 2433032 | tf_op jit(solution)/shard_map/ppermute | solution.py:36
  121.4 98.9 %collective-permute-start.36 = (bf16[2,96,4016]{2,1,0:T(8,128)(2,1)}, bf16[2,96,4016]{2,1,0:T(8,128)(2,1)S(1)}, u32[]{:S(2)}, u32[]{:S(2)}) collective-permute-start(bf16[2,96,4016]{2,1,0:T(8,128)(2,1)} %pad_maximum_fusion.14), channel_id=1, source_target_pairs={{0,16},{8,24},{16,0},{24,8},{1,17},{9,25},{17,1},{25,9},{2,18},{10... | collective-permute-start | bytes 4626440 | tf_op jit(solution)/shard_map/ppermute | solution.py:36
  124.2 93.2 %collective-permute-start.38 = (bf16[2,96,4016]{2,1,0:T(8,128)(2,1)}, bf16[2,96,4016]{2,1,0:T(8,128)(2,1)}, u32[]{:S(2)}, u32[]{:S(2)}) collective-permute-start(bf16[2,96,4016]{2,1,0:T(8,128)(2,1)} %pad_maximum_fusion.15), channel_id=1, source_target_pairs={{0,4},{4,0},{1,5},{5,1},{2,6},{6,2},{3,7},{7,3},{8,12},{12,8},{9,1... | collective-permute-start | bytes 4626440 | tf_op jit(solution)/shard_map/ppermute | solution.py:36
  144.4 29.4 %collective-permute-start.10 = (bf16[512,384]{1,0:T(8,128)(2,1)S(1)}, bf16[512,384]{1,0:T(8,128)(2,1)S(1)}, u32[]{:S(2)}, u32[]{:S(2)}) collective-permute-start(bf16[512,384]{1,0:T(8,128)(2,1)S(1)} %get-tuple-element.219), channel_id=1, source_target_pairs={{0,4},{4,0},{1,5},{5,1},{2,6},{6,2},{3,7},{7,3},{8,12},{12,8},{9,1... | collective-permute-start | bytes 1179656 | tf_op jit(solution)/shard_map/ppermute | solution.py:36
  147.5 34.7 %collective-permute-start.26 = (bf16[512,384]{1,0:T(8,128)(2,1)S(1)}, bf16[512,384]{1,0:T(8,128)(2,1)S(1)}, u32[]{:S(2)}, u32[]{:S(2)}) collective-permute-start(bf16[512,384]{1,0:T(8,128)(2,1)S(1)} %get-tuple-element.220), channel_id=1, source_target_pairs={{0,4},{4,0},{1,5},{5,1},{2,6},{6,2},{3,7},{7,3},{8,12},{12,8},{9,1... | collective-permute-start | bytes 1179656 | tf_op jit(solution)/shard_map/ppermute | solution.py:36
  149.8 49.5 %collective-permute-start.22 = (bf16[1024,384]{1,0:T(8,128)(2,1)S(1)}, bf16[1024,384]{1,0:T(8,128)(2,1)}, u32[]{:S(2)}, u32[]{:S(2)}) collective-permute-start(bf16[1024,384]{1,0:T(8,128)(2,1)S(1)} %get-tuple-element.211), channel_id=1, source_target_pairs={{0,4},{4,0},{1,5},{5,1},{2,6},{6,2},{3,7},{7,3},{8,12},{12,8},{9,1... | collective-permute-start | bytes 2359304 | tf_op jit(solution)/shard_map/ppermute | solution.py:36
  173.9 42.2 %collective-permute-start.30 = (bf16[1024,384]{1,0:T(8,128)(2,1)S(1)}, bf16[1024,384]{1,0:T(8,128)(2,1)}, u32[]{:S(2)}, u32[]{:S(2)}) collective-permute-start(bf16[1024,384]{1,0:T(8,128)(2,1)S(1)} %get-tuple-element.212), channel_id=1, source_target_pairs={{0,4},{4,0},{1,5},{5,1},{2,6},{6,2},{3,7},{7,3},{8,12},{12,8},{9,1... | collective-permute-start | bytes 2359304 | tf_op jit(solution)/shard_map/ppermute | solution.py:36
  182.3 67.9 %collective-permute-start.19 = (bf16[2,96,4224]{2,1,0:T(8,128)(2,1)}, bf16[2,96,4224]{2,1,0:T(8,128)(2,1)}, u32[]{:S(2)}, u32[]{:S(2)}) collective-permute-start(bf16[2,96,4224]{2,1,0:T(8,128)(2,1)} %pad_maximum_fusion.5), channel_id=1, source_target_pairs={{0,4},{4,0},{1,5},{5,1},{2,6},{6,2},{3,7},{7,3},{8,12},{12,8},{9,1... | collective-permute-start | bytes 4866056 | tf_op jit(solution)/shard_map/ppermute | solution.py:36
  199.2 52.4 %collective-permute-start.20 = (bf16[2,96,4224]{2,1,0:T(8,128)(2,1)}, bf16[2,96,4224]{2,1,0:T(8,128)(2,1)S(1)}, u32[]{:S(2)}, u32[]{:S(2)}) collective-permute-start(bf16[2,96,4224]{2,1,0:T(8,128)(2,1)} %pad_maximum_fusion.7), channel_id=1, source_target_pairs={{0,16},{8,24},{16,0},{24,8},{1,17},{9,25},{17,1},{25,9},{2,18},{10... | collective-permute-start | bytes 4866056 | tf_op jit(solution)/shard_map/ppermute | solution.py:36
  216.1 57.9 %collective-permute-start.13 = (bf16[512,192]{1,0:T(8,128)(2,1)S(1)}, bf16[512,192]{1,0:T(8,128)(2,1)S(1)}, u32[]{:S(2)}, u32[]{:S(2)}) collective-permute-start(bf16[512,192]{1,0:T(8,128)(2,1)S(1)} %get-tuple-element.37), channel_id=1, source_target_pairs={{0,3},{1,0},{2,1},{3,2},{4,7},{5,4},{6,5},{7,6},{8,11},{9,8},{10,9... | collective-permute-start | bytes 589832 | tf_op jit(solution)/shard_map/ppermute | solution.py:164
  217.5 57.2 %collective-permute-start.12 = (bf16[512,192]{1,0:T(8,128)(2,1)S(1)}, bf16[512,192]{1,0:T(8,128)(2,1)}, u32[]{:S(2)}, u32[]{:S(2)}) collective-permute-start(bf16[512,192]{1,0:T(8,128)(2,1)S(1)} %get-tuple-element.37), channel_id=1, source_target_pairs={{0,2},{1,3},{2,0},{3,1},{4,6},{5,7},{6,4},{7,5},{8,10},{9,11},{10,... | collective-permute-start | bytes 589832 | tf_op jit(solution)/shard_map/ppermute | solution.py:164
  220.4 54.4 %collective-permute-start.11 = (bf16[512,192]{1,0:T(8,128)(2,1)S(1)}, bf16[512,192]{1,0:T(8,128)(2,1)}, u32[]{:S(2)}, u32[]{:S(2)}) collective-permute-start(bf16[512,192]{1,0:T(8,128)(2,1)S(1)} %get-tuple-element.37), channel_id=1, source_target_pairs={{0,1},{1,2},{2,3},{3,0},{4,5},{5,6},{6,7},{7,4},{8,9},{9,10},{10,1... | collective-permute-start | bytes 589832 | tf_op jit(solution)/shard_map/ppermute | solution.py:164
  257.6 33.6 %collective-permute-start.29 = (bf16[512,192]{1,0:T(8,128)(2,1)S(1)}, bf16[512,192]{1,0:T(8,128)(2,1)}, u32[]{:S(2)}, u32[]{:S(2)}) collective-permute-start(bf16[512,192]{1,0:T(8,128)(2,1)S(1)} %get-tuple-element.39), channel_id=1, source_target_pairs={{0,3},{1,0},{2,1},{3,2},{4,7},{5,4},{6,5},{7,6},{8,11},{9,8},{10,9... | collective-permute-start | bytes 589832 | tf_op jit(solution)/shard_map/ppermute | solution.py:164
  267.0 26.1 %collective-permute-start.28 = (bf16[512,192]{1,0:T(8,128)(2,1)S(1)}, bf16[512,192]{1,0:T(8,128)(2,1)S(1)}, u32[]{:S(2)}, u32[]{:S(2)}) collective-permute-start(bf16[512,192]{1,0:T(8,128)(2,1)S(1)} %get-tuple-element.39), channel_id=1, source_target_pairs={{0,2},{1,3},{2,0},{3,1},{4,6},{5,7},{6,4},{7,5},{8,10},{9,11},{10,... | collective-permute-start | bytes 589832 | tf_op jit(solution)/shard_map/ppermute | solution.py:164
  290.3 25.0 %collective-permute-start.24 = (bf16[512,192]{1,0:T(8,128)(2,1)S(1)}, bf16[512,192]{1,0:T(8,128)(2,1)S(1)}, u32[]{:S(2)}, u32[]{:S(2)}) collective-permute-start(bf16[512,192]{1,0:T(8,128)(2,1)S(1)} %get-tuple-element.38), channel_id=1, source_target_pairs={{0,2},{1,3},{2,0},{3,1},{4,6},{5,7},{6,4},{7,5},{8,10},{9,11},{10,... | collective-permute-start | bytes 589832 | tf_op jit(solution)/shard_map/ppermute | solution.py:164
  291.2 24.2 %collective-permute-start.23 = (bf16[512,192]{1,0:T(8,128)(2,1)S(1)}, bf16[512,192]{1,0:T(8,128)(2,1)S(1)}, u32[]{:S(2)}, u32[]{:S(2)}) collective-permute-start(bf16[512,192]{1,0:T(8,128)(2,1)S(1)} %get-tuple-element.38), channel_id=1, source_target_pairs={{0,1},{1,2},{2,3},{3,0},{4,5},{5,6},{6,7},{7,4},{8,9},{9,10},{10,1... | collective-permute-start | bytes 589832 | tf_op jit(solution)/shard_map/ppermute | solution.py:164
  307.6 29.4 %collective-permute-start.32 = (bf16[512,192]{1,0:T(8,128)(2,1)S(1)}, bf16[512,192]{1,0:T(8,128)(2,1)S(1)}, u32[]{:S(2)}, u32[]{:S(2)}) collective-permute-start(bf16[512,192]{1,0:T(8,128)(2,1)S(1)} %get-tuple-element.40), channel_id=1, source_target_pairs={{0,2},{1,3},{2,0},{3,1},{4,6},{5,7},{6,4},{7,5},{8,10},{9,11},{10,... | collective-permute-start | bytes 589832 | tf_op jit(solution)/shard_map/ppermute | solution.py:164
  307.9 29.1 %collective-permute-start.31 = (bf16[512,192]{1,0:T(8,128)(2,1)S(1)}, bf16[512,192]{1,0:T(8,128)(2,1)S(1)}, u32[]{:S(2)}, u32[]{:S(2)}) collective-permute-start(bf16[512,192]{1,0:T(8,128)(2,1)S(1)} %get-tuple-element.40), channel_id=1, source_target_pairs={{0,1},{1,2},{2,3},{3,0},{4,5},{5,6},{6,7},{7,4},{8,9},{9,10},{10,1... | collective-permute-start | bytes 589832 | tf_op jit(solution)/shard_map/ppermute | solution.py:164
  407.9 23.9 %collective-permute-start.56 = (f32[3,1024]{1,0:T(4,128)S(1)}, f32[3,1024]{1,0:T(4,128)S(1)}, u32[]{:S(2)}, u32[]{:S(2)}) collective-permute-start(f32[3,1024]{1,0:T(4,128)S(1)} %pad_maximum_fusion.45), channel_id=1, source_target_pairs={{0,11},{1,8},{2,9},{3,10},{8,3},{9,0},{10,1},{11,2},{16,27},{17,24... | collective-permute-start | bytes 36872 | tf_op jit(solution)/shard_map/ppermute | solution.py:390
  433.9 72.9 %collective-permute-start.57 = (bf16[512,768]{1,0:T(8,128)(2,1)}, bf16[512,768]{1,0:T(8,128)(2,1)}, u32[]{:S(2)}, u32[]{:S(2)}) collective-permute-start(bf16[512,768]{1,0:T(8,128)(2,1)} %slice.1185), channel_id=1, source_target_pairs={{0,8},{8,0},{16,24},{24,16},{1,9},{9,1},{17,25},{25,17},{2,10},{10... | collective-permute-start | bytes 2359304 | tf_op jit(solution)/shard_map/ppermute | solution.py:36
  458.1 51.5 %collective-permute-start.74 = (bf16[512,768]{1,0:T(8,128)(2,1)}, bf16[512,768]{1,0:T(8,128)(2,1)}, u32[]{:S(2)}, u32[]{:S(2)}) collective-permute-start(bf16[512,768]{1,0:T(8,128)(2,1)} %slice.1184), channel_id=1, source_target_pairs={{0,8},{8,0},{16,24},{24,16},{1,9},{9,1},{17,25},{25,17},{2,10},{10... | collective-permute-start | bytes 2359304 | tf_op jit(solution)/shard_map/ppermute | solution.py:36
  503.4 243.6 %collective-permute-start.115 = (bf16[2,96,4016]{2,1,0:T(8,128)(2,1)}, bf16[2,96,4016]{2,1,0:T(8,128)(2,1)}, u32[]{:S(2)}, u32[]{:S(2)}) collective-permute-start(bf16[2,96,4016]{2,1,0:T(8,128)(2,1)} %dynamic-slice_bitcast_fusion.1), channel_id=1, source_target_pairs={{0,16},{8,24},{16,0},{24,8},{1,17},{9,25},{17,1},{25,9},{2,18},{10... | collective-permute-start | bytes 4626440 | tf_op jit(solution)/shard_map/ppermute | solution.py:36
  505.3 246.1 %collective-permute-start.117 = (bf16[2,96,4016]{2,1,0:T(8,128)(2,1)}, bf16[2,96,4016]{2,1,0:T(8,128)(2,1)}, u32[]{:S(2)}, u32[]{:S(2)}) collective-permute-start(bf16[2,96,4016]{2,1,0:T(8,128)(2,1)} %dynamic-slice_bitcast_fusion), channel_id=1, source_target_pairs={{0,4},{4,0},{1,5},{5,1},{2,6},{6,2},{3,7},{7,3},{8,12},{12,8},{9,1... | collective-permute-start | bytes 4626440 | tf_op jit(solution)/shard_map/ppermute | solution.py:36
  622.1 61.5 %collective-permute-start.66 = (bf16[512,192]{1,0:T(8,128)(2,1)}, bf16[512,192]{1,0:T(8,128)(2,1)}, u32[]{:S(2)}, u32[]{:S(2)}) collective-permute-start(bf16[512,192]{1,0:T(8,128)(2,1)} %get-tuple-element.42), channel_id=1, source_target_pairs={{0,3},{1,0},{2,1},{3,2},{4,7},{5,4},{6,5},{7,6},{8,11},{9,8},{10,9... | collective-permute-start | bytes 589832 | tf_op jit(solution)/shard_map/ppermute | solution.py:164
  625.1 61.3 %collective-permute-start.65 = (bf16[512,192]{1,0:T(8,128)(2,1)}, bf16[512,192]{1,0:T(8,128)(2,1)}, u32[]{:S(2)}, u32[]{:S(2)}) collective-permute-start(bf16[512,192]{1,0:T(8,128)(2,1)} %get-tuple-element.42), channel_id=1, source_target_pairs={{0,2},{1,3},{2,0},{3,1},{4,6},{5,7},{6,4},{7,5},{8,10},{9,11},{10,... | collective-permute-start | bytes 589832 | tf_op jit(solution)/shard_map/ppermute | solution.py:164
  625.1 62.4 %collective-permute-start.64 = (bf16[512,192]{1,0:T(8,128)(2,1)}, bf16[512,192]{1,0:T(8,128)(2,1)}, u32[]{:S(2)}, u32[]{:S(2)}) collective-permute-start(bf16[512,192]{1,0:T(8,128)(2,1)} %get-tuple-element.42), channel_id=1, source_target_pairs={{0,1},{1,2},{2,3},{3,0},{4,5},{5,6},{6,7},{7,4},{8,9},{9,10},{10,1... | collective-permute-start | bytes 589832 | tf_op jit(solution)/shard_map/ppermute | solution.py:164
  693.2 90.7 %collective-permute-start.98 = (bf16[1024,384]{1,0:T(8,128)(2,1)}, bf16[1024,384]{1,0:T(8,128)(2,1)}, u32[]{:S(2)}, u32[]{:S(2)}) collective-permute-start(bf16[1024,384]{1,0:T(8,128)(2,1)} %slice.800), channel_id=1, source_target_pairs={{0,4},{4,0},{1,5},{5,1},{2,6},{6,2},{3,7},{7,3},{8,12},{12,8},{9,1... | collective-permute-start | bytes 2359304 | tf_op jit(solution)/shard_map/ppermute | solution.py:36
  709.7 66.2 %collective-permute-start.91 = (bf16[1024,384]{1,0:T(8,128)(2,1)}, bf16[1024,384]{1,0:T(8,128)(2,1)}, u32[]{:S(2)}, u32[]{:S(2)}) collective-permute-start(bf16[1024,384]{1,0:T(8,128)(2,1)} %slice.798), channel_id=1, source_target_pairs={{0,4},{4,0},{1,5},{5,1},{2,6},{6,2},{3,7},{7,3},{8,12},{12,8},{9,1... | collective-permute-start | bytes 2359304 | tf_op jit(solution)/shard_map/ppermute | solution.py:36
  711.0 221.5 %collective-permute-start.110 = (bf16[2,2,96,1728]{3,2,1,0:T(8,128)(2,1)}, bf16[2,2,96,1728]{3,2,1,0:T(8,128)(2,1)}, u32[]{:S(2)}, u32[]{:S(2)}) collective-permute-start(bf16[2,2,96,1728]{3,2,1,0:T(8,128)(2,1)} %dynamic-slice_bitcast_fusion.2), channel_id=1, source_target_pairs={{0,8},{8,0},{16,24},{24,16},{1,9},{9,1},{17,25},{25,17},{2,10},{10... | collective-permute-start | bytes 3981320 | tf_op jit(solution)/shard_map/ppermute | solution.py:36
  759.1 120.2 %collective-permute-start.116 = (bf16[96,4016]{1,0:T(8,128)(2,1)}, bf16[96,4016]{1,0:T(8,128)(2,1)}, u32[]{:S(2)}, u32[]{:S(2)}) collective-permute-start(bf16[96,4016]{1,0:T(8,128)(2,1)} %dynamic-slice_bitcast_fusion.5), channel_id=1, source_target_pairs={{0,4},{4,0},{1,5},{5,1},{2,6},{6,2},{3,7},{7,3},{8,12},{12,8},{9,1... | collective-permute-start | bytes 2313224 | tf_op jit(solution)/shard_map/ppermute | solution.py:36
  767.6 26.6 %collective-permute-start.70 = (bf16[128,768]{1,0:T(8,128)(2,1)}, bf16[128,768]{1,0:T(8,128)(2,1)}, u32[]{:S(2)}, u32[]{:S(2)}) collective-permute-start(bf16[128,768]{1,0:T(8,128)(2,1)} %get-tuple-element.233), channel_id=1, source_target_pairs={{0,3},{1,0},{2,1},{3,2},{4,7},{5,4},{6,5},{7,6},{8,11},{9,8},{10,9... | collective-permute-start | bytes 589832 | tf_op jit(solution)/shard_map/ppermute | solution.py:180
  801.9 77.6 %collective-permute-start.118 = (bf16[96,4016]{1,0:T(8,128)(2,1)}, bf16[96,4016]{1,0:T(8,128)(2,1)}, u32[]{:S(2)}, u32[]{:S(2)}) collective-permute-start(bf16[96,4016]{1,0:T(8,128)(2,1)} %dynamic-slice_bitcast_fusion.4), channel_id=1, source_target_pairs={{0,16},{8,24},{16,0},{24,8},{1,17},{9,25},{17,1},{25,9},{2,18},{10... | collective-permute-start | bytes 2313224 | tf_op jit(solution)/shard_map/ppermute | solution.py:36
  845.5 37.8 %collective-permute-start.101 = (bf16[256,768]{1,0:T(8,128)(2,1)}, bf16[256,768]{1,0:T(8,128)(2,1)}, u32[]{:S(2)}, u32[]{:S(2)}) collective-permute-start(bf16[256,768]{1,0:T(8,128)(2,1)} %get-tuple-element.206), channel_id=1, source_target_pairs={{0,3},{1,0},{2,1},{3,2},{4,7},{5,4},{6,5},{7,6},{8,11},{9,8},{10,9... | collective-permute-start | bytes 1179656 | tf_op jit(solution)/shard_map/ppermute | solution.py:180
  851.1 42.9 %collective-permute-start.100 = (bf16[256,768]{1,0:T(8,128)(2,1)}, bf16[256,768]{1,0:T(8,128)(2,1)}, u32[]{:S(2)}, u32[]{:S(2)}) collective-permute-start(bf16[256,768]{1,0:T(8,128)(2,1)} %get-tuple-element.207), channel_id=1, source_target_pairs={{0,2},{1,3},{2,0},{3,1},{4,6},{5,7},{6,4},{7,5},{8,10},{9,11},{10,... | collective-permute-start | bytes 1179656 | tf_op jit(solution)/shard_map/ppermute | solution.py:180
  883.3 33.2 %collective-permute-start.93 = (bf16[256,768]{1,0:T(8,128)(2,1)S(1)}, bf16[256,768]{1,0:T(8,128)(2,1)S(1)}, u32[]{:S(2)}, u32[]{:S(2)}) collective-permute-start(bf16[256,768]{1,0:T(8,128)(2,1)S(1)} %copy-done.117), channel_id=1, source_target_pairs={{0,2},{1,3},{2,0},{3,1},{4,6},{5,7},{6,4},{7,5},{8,10},{9,11},{10,... | collective-permute-start | bytes 1179656 | tf_op jit(solution)/shard_map/ppermute | solution.py:180
  896.7 106.0 %collective-permute-start.105 = (bf16[2,2,96,1408]{3,2,1,0:T(8,128)(2,1)}, bf16[2,2,96,1408]{3,2,1,0:T(8,128)(2,1)}, u32[]{:S(2)}, u32[]{:S(2)}) collective-permute-start(bf16[2,2,96,1408]{3,2,1,0:T(8,128)(2,1)} %dynamic-slice_bitcast_fusion.3), channel_id=1, source_target_pairs={{0,8},{8,0},{16,24},{24,16},{1,9},{9,1},{17,25},{25,17},{2,10},{10... | collective-permute-start | bytes 3244040 | tf_op jit(solution)/shard_map/ppermute | solution.py:36
  898.5 101.8 %collective-permute-start.119 = (bf16[96,4016]{1,0:T(8,128)(2,1)}, bf16[96,4016]{1,0:T(8,128)(2,1)}, u32[]{:S(2)}, u32[]{:S(2)}) collective-permute-start(bf16[96,4016]{1,0:T(8,128)(2,1)} %select_convert_fusion), channel_id=1, source_target_pairs={{0,8},{8,0},{16,24},{24,16},{1,9},{9,1},{17,25},{25,17},{2,10},{10... | collective-permute-start | bytes 2313224 | tf_op jit(solution)/shard_map/ppermute | solution.py:36
  916.5 43.0 %collective-permute-start.103 = (bf16[256,768]{1,0:T(8,128)(2,1)S(1)}, bf16[256,768]{1,0:T(8,128)(2,1)S(1)}, u32[]{:S(2)}, u32[]{:S(2)}) collective-permute-start(bf16[256,768]{1,0:T(8,128)(2,1)S(1)} %add_convert_fusion.7), channel_id=1, source_target_pairs={{0,2},{1,3},{2,0},{3,1},{4,6},{5,7},{6,4},{7,5},{8,10},{9,11},{10,... | collective-permute-start | bytes 1179656 | tf_op jit(solution)/shard_map/ppermute | solution.py:164
  932.5 27.0 %collective-permute-start.104 = (bf16[256,768]{1,0:T(8,128)(2,1)S(1)}, bf16[256,768]{1,0:T(8,128)(2,1)S(1)}, u32[]{:S(2)}, u32[]{:S(2)}) collective-permute-start(bf16[256,768]{1,0:T(8,128)(2,1)S(1)} %add_convert_fusion.7), channel_id=1, source_target_pairs={{0,1},{1,2},{2,3},{3,0},{4,5},{5,6},{6,7},{7,4},{8,9},{9,10},{10,1... | collective-permute-start | bytes 1179656 | tf_op jit(solution)/shard_map/ppermute | solution.py:164
  934.7 31.3 %collective-permute-start.95 = (bf16[256,768]{1,0:T(8,128)(2,1)S(1)}, bf16[256,768]{1,0:T(8,128)(2,1)S(1)}, u32[]{:S(2)}, u32[]{:S(2)}) collective-permute-start(bf16[256,768]{1,0:T(8,128)(2,1)S(1)} %add_convert_fusion.8), channel_id=1, source_target_pairs={{0,3},{1,0},{2,1},{3,2},{4,7},{5,4},{6,5},{7,6},{8,11},{9,8},{10,9... | collective-permute-start | bytes 1179656 | tf_op jit(solution)/shard_map/ppermute | solution.py:164
  959.5 24.1 %collective-permute-start.97 = (bf16[256,768]{1,0:T(8,128)(2,1)S(1)}, bf16[256,768]{1,0:T(8,128)(2,1)S(1)}, u32[]{:S(2)}, u32[]{:S(2)}) collective-permute-start(bf16[256,768]{1,0:T(8,128)(2,1)S(1)} %add_convert_fusion.8), channel_id=1, source_target_pairs={{0,1},{1,2},{2,3},{3,0},{4,5},{5,6},{6,7},{7,4},{8,9},{9,10},{10,1... | collective-permute-start | bytes 1179656 | tf_op jit(solution)/shard_map/ppermute | solution.py:164
  (244 other events, 3563.7 us)

commit v2 on v1

v2 whole, which is shorter than its diff:
```python
import functools
import math

import jax
import jax.numpy as jnp
from jax import lax
from jax.experimental import pallas as pl
from jax.experimental.pallas import tpu as pltpu
from jax.sharding import PartitionSpec as P

HD = 64
BLK = 128
MB = 2
EPSILON = 1e-06
MASKED = -1000000000.0
F32 = jnp.float32
BF16 = jnp.bfloat16
PLANE = ("fsdp", "ctx")
VMEM_LIMIT = 48 * 1024 * 1024
MESH = pl.DeviceIdType.MESH
TILE = 1024
LOWEST = -3.0e38


def mat(left, right):
    return jnp.dot(left, right, preferred_element_type=F32)


def mat_nt(left, right):
    return lax.dot_general(left, right, (((1,), (1,)), ((), ())), preferred_element_type=F32)


def mat_tn(left, right):
    return lax.dot_general(left, right, (((0,), (0,)), ((), ())), preferred_element_type=F32)


def small_plane():
    return lax.axis_size("fsdp") == 4 and lax.axis_size("ctx") == 2


def swap(value, axis, bit):
    count = lax.axis_size(axis)
    return lax.ppermute(value, axis, [(i, i ^ bit) for i in range(count)])


def low_sum(left, right):
    return (left.astype(F32) + right.astype(F32)).astype(BF16)


def here():
    return lax.axis_index("fsdp"), lax.axis_index("ctx"), lax.axis_index("tp")


def greet(peers):
    barrier = pltpu.get_barrier_semaphore()
    for peer in peers:
        pl.semaphore_signal(barrier, inc=1, device_id=peer, device_id_type=MESH)
    pl.semaphore_wait(barrier, len(peers))


def greet_line(t, count, left, right):
    barrier = pltpu.get_barrier_semaphore()

    @pl.when(t > 0)
    def _():
        pl.semaphore_signal(barrier, inc=1, device_id=left, device_id_type=MESH)

    @pl.when(t < count - 1)
    def _():
        pl.semaphore_signal(barrier, inc=1, device_id=right, device_id_type=MESH)

    at_end = (t == 0) | (t == count - 1)
    pl.semaphore_wait(barrier, jnp.where(at_end, 1, 2).astype(jnp.int32))


def remote(src, dst, send, recv, peer):
    return pltpu.make_async_remote_copy(
        src_ref=src, dst_ref=dst, send_sem=send, recv_sem=recv, device_id=peer, device_id_type=MESH
    )


def plane_gather_kernel(x_ref, out_ref, send, recv, core_send, core_recv):
    f, c, t = here()
    core = f % 2
    chips = [(0, 1), (2, 0), (2, 1)]
    peers = [(f ^ df, c ^ dc, t) for df, dc in chips]
    partner = (f ^ 1, c, t)
    greet(peers + [partner])

    def slot(df, dc):
        return (f ^ df) * 2 + (c ^ dc)

    own = slot(0, 0)
    copies = []
    for j, peer in enumerate(peers):
        copy = remote(x_ref, out_ref.at[own], send.at[j], recv.at[j], peer)
        copy.start()
        copies.append(copy)
    passes = [remote(x_ref, out_ref.at[own], core_send.at[3], core_recv.at[3], partner)]
    passes[0].start()
    out_ref[own] = x_ref[...]
    for j, (df, dc) in enumerate(chips):
        copies[j].wait_recv()
        there = slot(df, dc)
        copy = remote(
            out_ref.at[there], out_ref.at[there], core_send.at[j], core_recv.at[j], partner
        )
        copy.start()
        passes.append(copy)
    for copy in copies:
        copy.wait_send()
    for copy in passes:
        copy.wait()


def plane_gather(shard, collective_id):
    if not small_plane():
        return lax.all_gather(shard, PLANE, axis=0, tiled=True)
    rows, columns = shard.shape
    out = pl.pallas_call(
        plane_gather_kernel,
        in_specs=[pl.BlockSpec(memory_space=pltpu.VMEM)],
        out_specs=pl.BlockSpec(memory_space=pltpu.VMEM),
        out_shape=jax.ShapeDtypeStruct((8, rows, columns), shard.dtype),
        scratch_shapes=[
            pltpu.SemaphoreType.DMA((3,)),
            pltpu.SemaphoreType.DMA((3,)),
            pltpu.SemaphoreType.DMA((4,)),
            pltpu.SemaphoreType.DMA((4,)),
        ],
        compiler_params=pltpu.CompilerParams(
            collective_id=collective_id, has_side_effects=True, vmem_limit_bytes=VMEM_LIMIT
        ),
        name="plane_gather",
    )(shard)
    return out.reshape(8 * rows, columns)


def plane_scatter_kernel(
    x_ref, out_ref, chip, core_in, chip_in, send, recv, core_send, core_recv
):
    f, c, t = here()
    core = f % 2
    chips = [(2, 1), (0, 1), (2, 0)]
    peers = [(f ^ df, c ^ dc, t) for df, dc in chips]
    partner = (f ^ 1, c, t)
    greet(peers + [partner])
    order = chips + [(0, 0)]
    swaps = []
    for j, (df, dc) in enumerate(order):
        block = (f ^ df ^ 1) * 2 + (c ^ dc)
        copy = remote(x_ref.at[block], core_in.at[j], core_send.at[j], core_recv.at[j], partner)
        copy.start()
        swaps.append(copy)
    copies = []
    for j, (df, dc) in enumerate(order):
        swaps[j].wait_recv()
        block = (f ^ df) * 2 + (c ^ dc)
        total = x_ref[block].astype(F32) + core_in[j].astype(F32)
        if j < 3:
            chip[j] = total.astype(BF16)
            copy = remote(chip.at[j], chip_in.at[j], send.at[j], recv.at[j], peers[j])
            copy.start()
            copies.append(copy)
        else:
            out_ref[...] = total
    for copy in swaps:
        copy.wait_send()
    for j in range(3):
        copies[j].wait()
        out_ref[...] += chip_in[j].astype(F32)


def plane_scatter(total, collective_id):
    if not small_plane():
        return lax.psum_scatter(total.astype(F32), PLANE, scatter_dimension=0, tiled=True)
    rows, columns = total.shape[0] // 8, total.shape[1]
    return pl.pallas_call(
        plane_scatter_kernel,
        in_specs=[pl.BlockSpec(memory_space=pltpu.VMEM)],
        out_specs=pl.BlockSpec(memory_space=pltpu.VMEM),
        out_shape=jax.ShapeDtypeStruct((rows, columns), F32),
        scratch_shapes=[
            pltpu.VMEM((3, rows, columns), BF16),
            pltpu.VMEM((4, rows, columns), BF16),
            pltpu.VMEM((3, rows, columns), BF16),
            pltpu.SemaphoreType.DMA((3,)),
            pltpu.SemaphoreType.DMA((3,)),
            pltpu.SemaphoreType.DMA((4,)),
            pltpu.SemaphoreType.DMA((4,)),
        ],
        compiler_params=pltpu.CompilerParams(
            collective_id=collective_id, has_side_effects=True, vmem_limit_bytes=VMEM_LIMIT
        ),
        name="plane_scatter",
    )(total.reshape(8, rows, columns))


def line_project_kernel(
    count, chunks, x_ref, w_ref, base_ref, out_ref, held, send_right, send_left, recv
):
    f, c, t = here()
    right, left = (f, c, t + 1), (f, c, t - 1)
    greet_line(t, count, left, right)
    rows = x_ref.shape[0] // chunks

    def part(j):
        return pl.ds(j * rows, rows)

    def go(j, d, peer, origin, sems):
        src = x_ref.at[part(j)] if d == 0 else held.at[origin, part(j)]
        return remote(src, held.at[origin, part(j)], sems.at[d, j], recv.at[origin, j], peer)

    def go_right(j, d):
        return go(j, d, right, t - d, send_right)

    def go_left(j, d):
        return go(j, d, left, t + d, send_left)

    def arrived(j, origin):
        return remote(x_ref.at[part(j)], held.at[origin, part(j)], send_right.at[0, j], recv.at[origin, j], right)

    @pl.when(t < count - 1)
    def _():
        for j in range(chunks):
            go_right(j, 0).start()

    @pl.when(t > 0)
    def _():
        for j in range(chunks):
            go_left(j, 0).start()

    held[t] = x_ref[...]
    for d in range(1, count):
        for j in range(chunks):

            @pl.when(t - d >= 0)
            def _():
                arrived(j, t - d).wait_recv()
                if d < count - 1:

                    @pl.when(t < count - 1)
                    def _():
                        go_right(j, d).start()

            @pl.when(t + d < count)
            def _():
                arrived(j, t + d).wait_recv()
                if d < count - 1:

                    @pl.when(t > 0)
                    def _():
                        go_left(j, d).start()

            if d == count - 1:
                total = base_ref[part(j)]
                for origin in range(count):
                    total = total + mat_nt(held[origin, part(j)], w_ref[origin])
                out_ref[part(j)] = total

    for d in range(count - 1):
        for j in range(chunks):

            @pl.when((t - d >= 0) & (t < count - 1))
            def _():
                go_right(j, d).wait_send()

            @pl.when((t + d < count) & (t > 0))
            def _():
                go_left(j, d).wait_send()


def line_project(value, weights, base, collective_id):
    rows, width = value.shape
    count, features = weights.shape[0], weights.shape[1]
    chunks = 4
    return pl.pallas_call(
        functools.partial(line_project_kernel, count, chunks),
        in_specs=[pl.BlockSpec(memory_space=pltpu.VMEM)] * 3,
        out_specs=pl.BlockSpec(memory_space=pltpu.VMEM),
        out_shape=jax.ShapeDtypeStruct((rows, features), F32),
        scratch_shapes=[
            pltpu.VMEM((count, rows, width), BF16),
            pltpu.SemaphoreType.DMA((count, chunks)),
            pltpu.SemaphoreType.DMA((count, chunks)),
            pltpu.SemaphoreType.DMA((count, chunks)),
        ],
        compiler_params=pltpu.CompilerParams(
            collective_id=collective_id, has_side_effects=True, vmem_limit_bytes=VMEM_LIMIT
        ),
        name="line_project",
    )(value, weights, base)


def line_sum_kernel(
    count,
    chunks,
    window,
    lag,
    x_ref,
    out_ref,
    from_right,
    from_left,
    to_left,
    to_right,
    up_send,
    up_recv,
    down_send,
    down_recv,
    low_send,
    low_recv,
    high_send,
    high_recv,
):
    f, c, t = here()
    right, left = (f, c, t + 1), (f, c, t - 1)
    last = count - 1
    greet_line(t, count, left, right)
    half = x_ref.shape[0] // 2
    rows = half // chunks

    def low(j):
        return pl.ds(j * rows, rows)

    def high(j):
        return pl.ds(half + j * rows, rows)

    def down(j, own):
        src = x_ref.at[low(j)] if own else to_left.at[low(j)]
        return remote(src, from_right.at[low(j)], down_send.at[j], down_recv.at[j], left)

    def up(j, own):
        src = x_ref.at[high(j)] if own else to_right.at[low(j)]
        return remote(src, from_left.at[low(j)], up_send.at[j], up_recv.at[j], right)

    def low_back(j):
        return remote(out_ref.at[low(j)], out_ref.at[low(j)], low_send.at[j], low_recv.at[j], right)

    def high_back(j):
        return remote(
            out_ref.at[high(j)], out_ref.at[high(j)], high_send.at[j], high_recv.at[j], left
        )

    def pace(j, copy):
        if j == 0:
            for k in range(min(window, chunks)):
                copy(k, True).start()
        copy(j, True).wait_send()
        if j + window < chunks:
            copy(j + window, True).start()

    def low_step(j):
        @pl.when(t == last)
        def _():
            pace(j, down)

        @pl.when(t < last)
        def _():
            down(j, False).wait_recv()
            total = from_right[low(j)].astype(F32) + x_ref[low(j)].astype(F32)

            @pl.when(t > 0)
            def _():
                to_left[low(j)] = total.astype(BF16)
                down(j, False).start()

            @pl.when(t == 0)
            def _():
                out_ref[low(j)] = total.astype(BF16)
                low_back(j).start()

    def high_step(j):
        @pl.when(t == 0)
        def _():
            pace(j, up)

        @pl.when(t > 0)
        def _():
            up(j, False).wait_recv()
            total = from_left[low(j)].astype(F32) + x_ref[high(j)].astype(F32)

            @pl.when(t < last)
            def _():
                to_right[low(j)] = total.astype(BF16)
                up(j, False).start()

            @pl.when(t == last)
            def _():
                out_ref[high(j)] = total.astype(BF16)
                high_back(j).start()

    def low_forward(j):
        @pl.when(t > 0)
        def _():
            low_back(j).wait_recv()

            @pl.when(t < last)
            def _():
                low_back(j).start()

    def high_forward(j):
        @pl.when(t < last)
        def _():
            high_back(j).wait_recv()

            @pl.when(t > 0)
            def _():
                high_back(j).start()

    for j in range(chunks + lag):

        @pl.when(t < count // 2)
        def _():
            if j < chunks:
                high_step(j)
            if 0 <= j - 1 < chunks:
                low_step(j - 1)

        @pl.when(t >= count // 2)
        def _():
            if j < chunks:
                low_step(j)
            if 0 <= j - 1 < chunks:
                high_step(j - 1)

        if j >= lag:

            @pl.when(t < count // 2)
            def _():
                low_forward(j - lag)
                high_forward(j - lag)

            @pl.when(t >= count // 2)
            def _():
                high_forward(j - lag)
                low_forward(j - lag)

    for j in range(chunks):

        @pl.when(t > 0)
        def _():
            high_back(j).wait_send()

            @pl.when(t < last)
            def _():
                down(j, False).wait_send()

        @pl.when(t < last)
        def _():
            low_back(j).wait_send()

            @pl.when(t > 0)
            def _():
                up(j, False).wait_send()


def line_sum(partial, collective_id, chunks=4, window=2, lag=4):
    count = lax.axis_size("tp")
    rows, columns = partial.shape
    while (rows // 2) % (chunks * 16):
        chunks -= 1
    half = rows // 2
    return pl.pallas_call(
        functools.partial(line_sum_kernel, count, chunks, window, lag),
        in_specs=[pl.BlockSpec(memory_space=pltpu.VMEM)],
        out_specs=pl.BlockSpec(memory_space=pltpu.VMEM),
        out_shape=jax.ShapeDtypeStruct((rows, columns), BF16),
        scratch_shapes=[pltpu.VMEM((half, columns), BF16)] * 4
        + [pltpu.SemaphoreType.DMA((chunks,))] * 8,
        compiler_params=pltpu.CompilerParams(
            collective_id=collective_id, has_side_effects=True, vmem_limit_bytes=VMEM_LIMIT
        ),
        name="line_sum",
    )(partial)


def share_stats_kernel(count, x_ref, top_ref, log_ref, picked_ref, held, send, recv):
    f, c, t = here()
    peers = [(f, c, lax.rem(t + k, count)) for k in range(1, count)]
    greet(peers)
    copies = []
    for k in range(1, count):
        copy = remote(x_ref, held.at[t], send.at[k], recv.at[k], peers[k - 1])
        copy.start()
        copies.append(copy)
    held[t] = x_ref[...]
    for copy in copies:
        copy.wait()
    highest = functools.reduce(jnp.maximum, [held[k, 0] for k in range(count)])
    total = sum(held[k, 1] * jnp.exp(held[k, 0] - highest) for k in range(count))
    top_ref[...] = highest
    log_ref[...] = highest + jnp.log(total)
    picked_ref[...] = sum(held[k, 2] for k in range(count))


def share_stats(stats, collective_id):
    count = lax.axis_size("tp")
    shape = jax.ShapeDtypeStruct(stats.shape[1:], F32)
    return pl.pallas_call(
        functools.partial(share_stats_kernel, count),
        in_specs=[pl.BlockSpec(memory_space=pltpu.VMEM)],
        out_specs=[pl.BlockSpec(memory_space=pltpu.VMEM)] * 3,
        out_shape=[shape] * 3,
        scratch_shapes=[
            pltpu.VMEM((count,) + stats.shape, F32),
            pltpu.SemaphoreType.DMA((count,)),
            pltpu.SemaphoreType.DMA((count,)),
        ],
        compiler_params=pltpu.CompilerParams(collective_id=collective_id, has_side_effects=True),
        name="share_stats",
    )(stats)


def after(value, earlier):
    return lax.optimization_barrier((value, earlier))[0]


def tp_list(value):
    count = lax.axis_size("tp")
    return [value] + [
        lax.ppermute(value, "tp", [(i, (i + k) % count) for i in range(count)])
        for k in range(1, count)
    ]


def ctx_gather(value):
    if lax.axis_size("ctx") == 2:
        return jnp.concatenate([value, swap(value, "ctx", 1)], axis=0)
    return lax.all_gather(value, "ctx", axis=0, tiled=True)


def ctx_pair(value):
    if lax.axis_size("ctx") == 2:
        return [value, swap(value, "ctx", 1)]
    return [lax.all_gather(value, "ctx", axis=0, tiled=True)]


def ctx_join(parts):
    return jnp.concatenate(parts, axis=0)


def ctx_positions(rows):
    c, count = lax.axis_index("ctx"), lax.axis_size("ctx")
    if count == 2:
        return jnp.concatenate(
            [c * rows + jnp.arange(rows), (1 - c) * rows + jnp.arange(rows)]
        ).astype(jnp.int32)
    return jnp.arange(rows * count, dtype=jnp.int32)


def ctx_scatter(value):
    if lax.axis_size("ctx") == 2:
        rows = value.shape[0] // 2
        return low_sum(value[:rows], swap(value[rows:], "ctx", 1))
    return lax.psum_scatter(value.astype(F32), "ctx", scatter_dimension=0, tiled=True).astype(BF16)


def exit_forward_kernel(
    valid, x_ref, e_ref, target_ref, logits_ref, top_ref, sum_ref, picked_ref, m_acc, l_acc, p_acc
):
    step = pl.program_id(0)
    rows, tile = logits_ref.shape

    @pl.when(step == 0)
    def _():
        m_acc[...] = jnp.full_like(m_acc, LOWEST)
        l_acc[...] = jnp.zeros_like(l_acc)
        p_acc[...] = jnp.zeros_like(p_acc)

    lanes = lax.broadcasted_iota(jnp.int32, (rows, 128), 1)
    logits_ref[...] = mat(x_ref[...], e_ref[...])
    relative = target_ref[...] - step * tile
    limit = valid - step * tile
    groups = tile // 128
    highest = m_acc[...]
    for g in range(groups):
        cols = slice(g * 128, (g + 1) * 128)
        part = jnp.where(lanes < limit - g * 128, logits_ref[:, cols], LOWEST)
        highest = jnp.maximum(highest, part)
    total = l_acc[...] * jnp.exp(m_acc[...] - highest)
    picked = p_acc[...]
    for g in range(groups):
        cols = slice(g * 128, (g + 1) * 128)
        part = jnp.where(lanes < limit - g * 128, logits_ref[:, cols], LOWEST)
        total += jnp.exp(part - highest)
        picked += jnp.where(lanes == relative - g * 128, part, 0.0)
    m_acc[...] = highest
    l_acc[...] = total
    p_acc[...] = picked

    @pl.when(step == pl.num_programs(0) - 1)
    def _():
        top = jnp.max(m_acc[...], axis=1, keepdims=True)
        top_ref[...] = top
        sum_ref[...] = jnp.sum(l_acc[...] * jnp.exp(m_acc[...] - top), axis=1, keepdims=True)
        picked_ref[...] = jnp.sum(p_acc[...], axis=1, keepdims=True)


def exit_forward(exit_in, embed_t, targets_local, valid):
    rows, features = exit_in.shape
    padded = embed_t.shape[1]
    column = pl.BlockSpec((rows, 1), lambda i: (0, 0))
    stat = jax.ShapeDtypeStruct((rows, 1), F32)
    return pl.pallas_call(
        functools.partial(exit_forward_kernel, valid),
        grid=(padded // TILE,),
        in_specs=[
            pl.BlockSpec((rows, features), lambda i: (0, 0)),
            pl.BlockSpec((features, TILE), lambda i: (0, i)),
            column,
        ],
        out_specs=[pl.BlockSpec((rows, TILE), lambda i: (0, i)), column, column, column],
        out_shape=[jax.ShapeDtypeStruct((rows, padded), F32), stat, stat, stat],
        scratch_shapes=[pltpu.VMEM((rows, 128), F32)] * 3,
        compiler_params=pltpu.CompilerParams(vmem_limit_bytes=VMEM_LIMIT),
        cost_estimate=pl.CostEstimate(
            flops=2 * rows * features * padded,
            bytes_accessed=4 * rows * padded + 2 * features * padded,
            transcendentals=rows * padded,
        ),
        name="exit_forward",
    )(exit_in, embed_t, targets_local)


def exit_backward_kernel(
    valid, logits_ref, e_ref, x_t_ref, target_ref, log_ref, embed_ref, exit_ref, acc
):
    step = pl.program_id(0)
    rows, tile = logits_ref.shape

    @pl.when(step == 0)
    def _():
        acc[...] = jnp.zeros_like(acc)

    lanes = lax.broadcasted_iota(jnp.int32, (rows, tile), 1)
    relative = target_ref[...] - step * tile
    probs = jnp.exp(logits_ref[...] - log_ref[...])
    probs = jnp.where(lanes < valid - step * tile, probs, 0.0)
    grad = (probs - jnp.where(lanes == relative, 1.0, 0.0)).astype(BF16)
    acc[...] += mat_nt(grad, e_ref[...])
    embed_ref[...] = mat(x_t_ref[...], grad).astype(BF16)

    @pl.when(step == pl.num_programs(0) - 1)
    def _():
        exit_ref[...] = acc[...].astype(BF16)


def exit_backward(logits, embed_t, exit_in_t, targets_local, log_total, valid):
    rows, padded = logits.shape
    features = embed_t.shape[0]
    column = pl.BlockSpec((rows, 1), lambda i: (0, 0))
    return pl.pallas_call(
        functools.partial(exit_backward_kernel, valid),
        grid=(padded // TILE,),
        in_specs=[
            pl.BlockSpec((rows, TILE), lambda i: (0, i)),
            pl.BlockSpec((features, TILE), lambda i: (0, i)),
            pl.BlockSpec((features, rows), lambda i: (0, 0)),
            column,
            column,
        ],
        out_specs=[
            pl.BlockSpec((features, TILE), lambda i: (0, i)),
            pl.BlockSpec((rows, features), lambda i: (0, 0)),
        ],
        out_shape=[
            jax.ShapeDtypeStruct((features, padded), BF16),
            jax.ShapeDtypeStruct((rows, features), BF16),
        ],
        scratch_shapes=[pltpu.VMEM((rows, features), F32)],
        compiler_params=pltpu.CompilerParams(vmem_limit_bytes=VMEM_LIMIT),
        cost_estimate=pl.CostEstimate(
            flops=4 * rows * features * padded,
            bytes_accessed=4 * rows * padded + 4 * features * padded,
            transcendentals=rows * padded,
        ),
        name="exit_backward",
    )(logits, embed_t, exit_in_t, targets_local, log_total)


def forward_kernel(heads, q_ref, kv_ref, bias_ref, out_ref, total_ref):
    width = heads * HD
    for h in range(heads):
        cols = slice(h * HD, (h + 1) * HD)
        keys = kv_ref[:, cols]
        values = kv_ref[:, width + h * HD : width + (h + 1) * HD]
        scores = mat_nt(keys, q_ref[:, cols])
        if bias_ref is not None:
            scores = scores + bias_ref[...]
        highest = jnp.max(scores, axis=0, keepdims=True)
        exponent = jnp.exp(scores - highest)
        denominator = jnp.sum(exponent, axis=0, keepdims=True)
        outcome = mat_tn(values, exponent.astype(BF16)) / denominator
        out_ref[:, cols] = outcome.T.astype(BF16)
        total_ref[h : h + 1, :] = highest + jnp.log(denominator)


def backward_kernel(
    heads, q_ref, kv_ref, bias_ref, total_ref, go_ref, dq_ref, dkv_ref, acc_ref
):
    width = heads * HD
    step = pl.program_id(0)

    @pl.when(step == 0)
    def _():
        acc_ref[...] = jnp.zeros_like(acc_ref)

    for h in range(heads):
        cols = slice(h * HD, (h + 1) * HD)
        vcols = slice(width + h * HD, width + (h + 1) * HD)
        keys, values = kv_ref[:, cols], kv_ref[:, vcols]
        queries, go = q_ref[:, cols], go_ref[:, cols]
        scores = mat_nt(keys, queries)
        if bias_ref is not None:
            scores = scores + bias_ref[...]
        probs = jnp.exp(scores - total_ref[h : h + 1, :])
        grad_probs = mat_nt(values, go)
        inner = jnp.sum(probs * grad_probs, axis=0, keepdims=True)
        grad_scores = (probs * (grad_probs - inner)).astype(BF16)
        acc_ref[:, vcols] += mat(probs.astype(BF16), go)
        acc_ref[:, cols] += mat(grad_scores, queries)
        dq_ref[:, cols] = mat_tn(keys, grad_scores).T.astype(BF16)

    @pl.when(step == pl.num_programs(0) - 1)
    def _():
        dkv_ref[...] = acc_ref[...].astype(BF16)


def attention_specs(rows, width, keys, tile, masked):
    specs = [
        pl.BlockSpec((tile, width), lambda i: (i, 0)),
        pl.BlockSpec((keys, 2 * width), lambda i: (0, 0)),
    ]
    if masked:
        specs.append(pl.BlockSpec((keys, tile), lambda i: (0, i)))
    return specs


def attend(queries, kv, bias):
    rows, width = queries.shape
    keys, heads = kv.shape[0], width // HD
    tile = min(rows, 256)
    masked = bias is not None
    body = functools.partial(forward_kernel, heads)
    if not masked:
        plain = body
        body = lambda q, k, o, t: plain(q, k, None, o, t)
    return pl.pallas_call(
        body,
        grid=(rows // tile,),
        in_specs=attention_specs(rows, width, keys, tile, masked),
        out_specs=[
            pl.BlockSpec((tile, width), lambda i: (i, 0)),
            pl.BlockSpec((heads, tile), lambda i: (0, i)),
        ],
        out_shape=[
            jax.ShapeDtypeStruct((rows, width), BF16),
            jax.ShapeDtypeStruct((heads, rows), F32),
        ],
        compiler_params=pltpu.CompilerParams(vmem_limit_bytes=VMEM_LIMIT),
        cost_estimate=pl.CostEstimate(
            flops=16 * rows * keys * width,
            bytes_accessed=4 * keys * width + 8 * rows * width,
            transcendentals=rows * keys * heads,
        ),
        name="attend_masked" if masked else "attend",
    )(*([queries, kv, bias] if masked else [queries, kv]))


def attend_back(queries, kv, bias, totals, go):
    rows, width = queries.shape
    keys, heads = kv.shape[0], width // HD
    tile = min(rows, 256)
    masked = bias is not None
    body = functools.partial(backward_kernel, heads)
    if not masked:
        plain = body
        body = lambda q, k, *rest: plain(q, k, None, *rest)
    specs = attention_specs(rows, width, keys, tile, masked) + [
        pl.BlockSpec((heads, tile), lambda i: (0, i)),
        pl.BlockSpec((tile, width), lambda i: (i, 0)),
    ]
    operands = ([queries, kv, bias] if masked else [queries, kv]) + [totals, go]
    return pl.pallas_call(
        body,
        grid=(rows // tile,),
        in_specs=specs,
        out_specs=[
            pl.BlockSpec((tile, width), lambda i: (i, 0)),
            pl.BlockSpec((keys, 2 * width), lambda i: (0, 0)),
        ],
        out_shape=[
            jax.ShapeDtypeStruct((rows, width), BF16),
            jax.ShapeDtypeStruct((keys, 2 * width), BF16),
        ],
        scratch_shapes=[pltpu.VMEM((keys, 2 * width), F32)],
        compiler_params=pltpu.CompilerParams(vmem_limit_bytes=VMEM_LIMIT),
        cost_estimate=pl.CostEstimate(
            flops=40 * rows * keys * width,
            bytes_accessed=8 * keys * width + 10 * rows * width,
            transcendentals=rows * keys * heads,
        ),
        name="attend_back_masked" if masked else "attend_back",
    )(*operands)


def rms_scale(values):
    return lax.rsqrt(jnp.mean(values * values, axis=-1, keepdims=True) + EPSILON)


def rms_back(grad_normed, normed, scale):
    return scale * (grad_normed - normed * jnp.mean(grad_normed * normed, axis=-1, keepdims=True))


def mask_bias(parent_row, row_count):
    block_count = parent_row.shape[0]
    blocks = jnp.arange(block_count, dtype=jnp.int32)
    current = blocks
    reachable = blocks[:, None] == blocks[None, :]
    for _ in range(block_count - 1):
        current = jnp.sum(
            jnp.where(current[:, None] == blocks[None, :], parent_row[None, :], 0), axis=1
        )
        reachable = reachable | (current[:, None] == blocks[None, :])
    query_pos = lax.axis_index("ctx") * row_count + jnp.arange(row_count, dtype=jnp.int32)
    key_pos = ctx_positions(row_count)
    query_onehot = (query_pos[:, None] // BLK == blocks[None, :]).astype(F32)
    key_onehot = (key_pos[:, None] // BLK == blocks[None, :]).astype(F32)
    linked = mat_nt(key_onehot, mat(query_onehot, reachable.astype(F32))) > 0.5
    causal = (query_pos[None, :] // BLK != key_pos[:, None] // BLK) | (
        key_pos[:, None] <= query_pos[None, :]
    )
    return jnp.where(linked & causal, 0.0, MASKED)


def gelu_parts(gate):
    root = math.sqrt(2.0 / math.pi)
    inner = jnp.tanh(root * (gate + 0.044715 * gate * gate * gate))
    value = 0.5 * gate * (1.0 + inner)
    slope = 0.5 * (1.0 + inner) + 0.5 * gate * (1.0 - inner * inner) * root * (
        1.0 + 3.0 * 0.044715 * gate * gate
    )
    return value, slope


def local(
    tokens,
    encoder,
    cotangent,
    parents,
    targets,
    w_query,
    w_key,
    w_value,
    w_out,
    c_query,
    c_key,
    c_value,
    c_out,
    w_gate,
    w_up,
    w_down,
    embedding,
    norm_self,
    norm_cross,
    norm_ff,
    norm_exit,
):
    t = lax.axis_index("tp")
    rows = tokens.shape[0] // MB
    features = tokens.shape[1]
    width = w_query.shape[1]
    hidden_units = w_gate.shape[1]
    vocab = embedding.shape[0]
    tp_count = lax.axis_size("tp")
    trees = range(MB)

    def tree_rows(value, i):
        count = value.shape[0] // MB
        return value[i * count : (i + 1) * count]

    gains_in = jnp.pad(
        jnp.stack([norm_self, norm_cross, norm_ff, norm_exit], axis=1), ((0, 0), (0, 124))
    )
    w_heads = plane_gather(
        jnp.concatenate([w_query, w_key, w_value, c_key, c_value, c_query, gains_in], axis=1), 1
    )
    w_qkv = w_heads[:, : 3 * width]
    c_kv = w_heads[:, 3 * width : 5 * width]
    c_q = w_heads[:, 5 * width : 6 * width]
    gains = w_heads[:, 6 * width : 6 * width + 4].astype(F32).T
    gain_self, gain_cross, gain_ff, gain_exit = (gains[j][None, :] for j in range(4))

    pieces = tp_list(
        jnp.concatenate([w_out.T, c_out.T, c_query, w_gate, w_up, w_down.T], axis=1)
    )
    pieces = after(pieces, w_heads)
    pieces = lax.dynamic_slice_in_dim(jnp.stack(pieces[::-1] * 2), tp_count - 1 - t, tp_count, 0)
    spans = [0, width, 2 * width, 3 * width]
    spans += [spans[-1] + hidden_units * j for j in (1, 2, 3)]
    packed = jnp.concatenate(
        [
            jnp.concatenate([pieces[k, :, spans[j] : spans[j + 1]] for k in range(tp_count)], axis=1)
            for j in range(6)
        ],
        axis=1,
    )
    whole = lax.all_gather(packed, PLANE, axis=0, tiled=True)
    cuts = [tp_count * s for s in spans]
    gate_all, up_all, down_t = (whole[:, cuts[j] : cuts[j + 1]] for j in range(3, 6))

    def own_units(value):
        return lax.dynamic_slice_in_dim(value, t * hidden_units, hidden_units, 1)

    def own_heads(value):
        return lax.dynamic_index_in_dim(value, t, 0, False)

    def stacked(j):
        return jnp.stack(
            [whole[:, cuts[j] + k * width : cuts[j] + (k + 1) * width] for k in range(tp_count)]
        )

    w_out_4, c_out_4, c_query_4 = stacked(0), stacked(1), stacked(2)
    padded = -(-vocab // TILE) * TILE
    embed_t = lax.all_gather(
        jnp.pad(after(embedding, packed).T, ((0, 0), (0, padded - vocab))),
        PLANE,
        axis=0,
        tiled=True,
    )

    tok = tokens.astype(F32)
    scale_one = rms_scale(tok)
    normed_one = tok * scale_one
    hidden_one = (normed_one * gain_self).astype(BF16)
    qkv = mat(hidden_one, w_qkv).astype(BF16)
    enc_kv = mat(encoder, c_kv).astype(BF16)
    queries = [tree_rows(qkv, i)[:, :width] for i in trees]
    kv_self = [ctx_gather(tree_rows(qkv, i)[:, width:]) for i in trees]
    kv_cross = [ctx_pair(tree_rows(enc_kv, i)) for i in trees]
    biases = [mask_bias(parents[i], rows) for i in trees]
    shrink = 1.0 / math.sqrt(features)

    outcome = [attend(queries[i], kv_self[i], biases[i]) for i in trees]
    attended = jnp.concatenate([o[0] for o in outcome], axis=0)
    totals_self = [o[1] for o in outcome]
    after_self = line_project(attended, w_out_4, tok, 2)
    scale_two = rms_scale(after_self)
    normed_two = after_self * scale_two
    hidden_two = (normed_two * gain_cross).astype(BF16)
    cross_q = mat(hidden_two, c_q).astype(BF16)
    kv_cross = [ctx_join(after(kv_cross[i], after_self)) for i in trees]
    outcome = [attend(tree_rows(cross_q, i), kv_cross[i], None) for i in trees]
    crossed = jnp.concatenate([o[0] for o in outcome], axis=0)
    totals_cross = [o[1] for o in outcome]
    after_cross = line_project(crossed, c_out_4, after_self, 3)
    scale_three = rms_scale(after_cross)
    normed_three = after_cross * scale_three
    hidden_three = (normed_three * gain_ff).astype(BF16)
    gate_pre = mat(hidden_three, gate_all)
    up_pre = mat(hidden_three, up_all)
    activated = (gelu_parts(gate_pre)[0] * up_pre).astype(BF16)
    mixed = after_cross + mat_nt(activated, down_t)
    scale_four = rms_scale(mixed)
    normed_four = mixed * scale_four
    exit_in = (normed_four * gain_exit * shrink).astype(BF16)

    targets_local = targets - t * vocab
    inside = (targets_local >= 0) & (targets_local < vocab)
    targets_local = jnp.where(inside, targets_local, -1)[:, None]
    logits, top, summed, picked = exit_forward(exit_in, embed_t, targets_local, vocab)
    stats = jnp.stack([top, summed, picked]).reshape(3, MB * rows // 128, 128)
    top, log_total, picked = share_stats(stats, 4)
    losses = (log_total - picked).reshape(-1)
    scores = (top - log_total).reshape(-1)
    grad_embed, grad_exit_part = exit_backward(
        logits, embed_t, exit_in.T, targets_local, log_total.reshape(-1, 1), vocab
    )
    grad_embed_own = lax.optimization_barrier(
        lax.psum_scatter(grad_embed, PLANE, scatter_dimension=0, tiled=True)
    )
    grad_exit = line_sum(grad_exit_part, 5).astype(F32) * shrink

    def norm_grad(grad, normed):
        return jnp.sum(grad * normed, axis=0)

    norm_exit_grad = norm_grad(grad_exit, normed_four)
    grad_mixed = cotangent.astype(F32) + rms_back(grad_exit * gain_exit, normed_four, scale_four)
    grad_mixed_low = grad_mixed.astype(BF16)
    grad_down = mat_tn(grad_mixed_low, own_units(activated))
    grad_act = mat(grad_mixed_low, down_t)
    value, slope = gelu_parts(gate_pre)
    grad_gate = (grad_act * slope * up_pre).astype(BF16)
    grad_up = (grad_act * value).astype(BF16)
    grad_gate_w = mat_tn(hidden_three, own_units(grad_gate))
    grad_up_w = mat_tn(hidden_three, own_units(grad_up))
    grad_three = mat_nt(grad_gate, gate_all) + mat_nt(grad_up, up_all)
    norm_ff_grad = norm_grad(grad_three, normed_three)
    grad_after_cross = grad_mixed + rms_back(grad_three * gain_ff, normed_three, scale_three)
    grad_cross_low = grad_after_cross.astype(BF16)
    grad_c_out = mat_tn(grad_cross_low, crossed)
    ff_grads = jnp.concatenate([grad_c_out, grad_gate_w, grad_up_w, grad_down], axis=1).astype(BF16)
    grad_crossed = mat(grad_cross_low, own_heads(c_out_4)).astype(BF16)
    outcome = [
        attend_back(
            tree_rows(cross_q, i), kv_cross[i], None, totals_cross[i], tree_rows(grad_crossed, i)
        )
        for i in trees
    ]
    grad_cq = jnp.concatenate([o[0] for o in outcome], axis=0)
    grad_kv_cross = jnp.concatenate([ctx_scatter(o[1]) for o in outcome], axis=0)
    grad_c_kv = mat_tn(encoder, grad_kv_cross)
    grad_c_query = mat_tn(hidden_two, grad_cq)
    encoder_part = mat_nt(grad_kv_cross, c_kv).astype(BF16)
    grad_two = line_project(grad_cq, c_query_4, jnp.zeros_like(tok), 6)
    ff_own = lax.psum_scatter(after(ff_grads, grad_two), PLANE, scatter_dimension=0, tiled=True)
    norm_cross_grad = norm_grad(grad_two, normed_two)
    grad_after_self = grad_after_cross + rms_back(grad_two * gain_cross, normed_two, scale_two)
    grad_self_low = grad_after_self.astype(BF16)
    grad_w_out = mat_tn(grad_self_low, attended)
    grad_attended = mat(grad_self_low, own_heads(w_out_4)).astype(BF16)
    outcome = [
        attend_back(
            queries[i], kv_self[i], biases[i], totals_self[i], tree_rows(grad_attended, i)
        )
        for i in trees
    ]
    grad_qkv = jnp.concatenate(
        [
            jnp.concatenate([o[0] for o in outcome], axis=0),
            jnp.concatenate([ctx_scatter(o[1]) for o in outcome], axis=0),
        ],
        axis=1,
    )
    both = jnp.concatenate([mat_nt(grad_qkv, w_qkv).astype(BF16), encoder_part], axis=0)
    both = line_sum(both, 7, 12)
    grad_encoder = both[MB * rows :].astype(F32)
    grad_w_qkv = mat_tn(hidden_one, grad_qkv)
    grad_one = both[: MB * rows].astype(F32)
    norm_self_grad = norm_grad(grad_one, normed_one)
    grad_tokens = grad_after_self + rms_back(grad_one * gain_self, normed_one, scale_one)
    norm_block = jnp.pad(
        jnp.stack([norm_self_grad, norm_cross_grad, norm_ff_grad, norm_exit_grad], axis=1),
        ((0, 0), (0, 60)),
    )
    own = plane_scatter(
        jnp.concatenate(
            [grad_w_qkv, grad_c_kv, grad_c_query, grad_w_out, norm_block], axis=1
        ).astype(BF16),
        9,
    )

    def part(value, start, size):
        return value[:, start : start + size].astype(F32)

    base = 7 * width
    return (
        mixed.astype(BF16),
        losses,
        scores,
        grad_tokens,
        grad_encoder,
        part(own, 0, width),
        part(own, width, width),
        part(own, 2 * width, width),
        part(own, 6 * width, width).T,
        part(own, 5 * width, width),
        part(own, 3 * width, width),
        part(own, 4 * width, width),
        part(ff_own, 0, width).T,
        part(ff_own, width, hidden_units),
        part(ff_own, width + hidden_units, hidden_units),
        part(ff_own, width + 2 * hidden_units, hidden_units).T,
        grad_embed_own[:, :vocab].astype(F32).T,
        own[:, base],
        own[:, base + 1],
        own[:, base + 2],
        own[:, base + 3],
    )


def solution(mesh):
    rows_cols = P(PLANE, "tp")
    cols_rows = P("tp", PLANE)
    data = P(PLANE, None)
    flat = P(PLANE)
    weights = (rows_cols,) * 3 + (cols_rows,) + (rows_cols,) * 3 + (cols_rows,)
    weights += (rows_cols,) * 2 + (cols_rows,) * 2 + (flat,) * 4
    return jax.shard_map(
        local,
        mesh=mesh,
        in_specs=(data, data, data, P("fsdp", None), flat) + weights,
        out_specs=(data, flat, flat, data, data) + weights,
        check_vma=False,
    )
```

time: 1040 us -> 866 us (0.83)
  Pallas kernels: 59.4 us -> 469 us
  waiting for transfers between devices: 309 us -> 102 us
  starting transfers between devices: 173 us -> 15.1 us
  matrix products: 215 us -> 89.2 us
  local copies, waits for them, and re-layouts: 162 us -> 106 us
  other arithmetic: 101 us -> 58.9 us
  between operations: 4.33 us -> 15.4 us
    pallas_call x0 -> x10, Pallas kernels: none -> 410 us  [the longest x2 193 us: line_sum(): pl.pallas_call(functools.partial(line_sum_kernel, count, chunks, window,...]
    ppermute x39 -> x3, waiting for transfers between devices: 109 us -> 7.2 us  [tp_list(): lax.ppermute(value, 'tp', [(i, (i + k) % count) for i in range(count)])]
    ppermute x49 -> x8, waiting for transfers between devices: 132 us -> 31.1 us  [swap(): return lax.ppermute(value, axis, [(i, i ^ bit) for i in range(count)])]
    ppermute x39 -> x3, starting transfers between devices: 82.9 us -> 6.96 us  [tp_list(): lax.ppermute(value, 'tp', [(i, (i + k) % count) for i in range(count)])]
    ppermute x32 -> x0, waiting for transfers between devices: 67.3 us -> none  [the longest x18 63 us: tp_sum(): lax.ppermute(block(k), 'tp', [(i, (i + k) % count) for i in range(count)])]
    all_gather x0 -> x2, waiting for transfers between devices: none -> 63.1 us  [the longest x1 63.1 us: local(): whole = lax.all_gather(packed, PLANE, axis=0, tiled=True)]
    ppermute x32 -> x0, starting transfers between devices: 50.8 us -> none  [the longest x18 35.3 us: tp_sum(): lax.ppermute(block(k), 'tp', [(i, (i + k) % count) for i in range(count)])]
    dot_general x20 -> x7, matrix products: 79.7 us -> 28.9 us  [mat_nt(): lax.dot_general(left, right, (((1,), (1,)), ((), ())), preferred_element_...]
  transfers between devices with their start and end apart: 120 -> 15, of which waited for: 44 -> 6; matrix products, arithmetic and copies ran while one was open for 39% -> 17% of each run, Pallas kernels for 6% -> 35%
where the time goes in v2:
time: 866 us; the launch traced here: 855 us
  Pallas kernels  469 us (54%)
  local copies, waits for them, and re-layouts  106 us (12%)
  waiting for transfers between devices  102 us (12%)
  matrix products  89.2 us (10%)
  other arithmetic  58.9 us (7%)
  between operations  15.4 us (2%)
  starting transfers between devices  15.1 us (2%)
    pallas_call x2, Pallas kernels, line_sum(): pl.pallas_call(functools.partial(line_sum_kernel, count, chunks, window,...  193 us
    pallas_call x3, Pallas kernels, line_project(): pl.pallas_call(functools.partial(line_project_kernel, count, chunks), in_...  118 us
    all_gather x1, waiting for transfers between devices, local(): whole = lax.all_gather(packed, PLANE, axis=0, tiled=True)  63.1 us
    unnamed x207, local copies, waits for them, and re-layouts  53.7 us
    dot_general x8, matrix products, mat(): return jnp.dot(left, right, preferred_element_type=F32)  41.1 us
    pallas_call x1, Pallas kernels, exit_backward(): pl.pallas_call(functools.partial(exit_backward_kernel, valid), grid=(padd...  35.4 us
    pallas_call x4, Pallas kernels, attend_back(): pl.pallas_call(body, grid=(rows // tile,), in_specs=specs, out_specs=[pl....  33.3 us
    ppermute x8, waiting for transfers between devices, swap(): return lax.ppermute(value, axis, [(i, i ^ bit) for i in range(count)])  31.1 us
  transfers between devices with their start and end apart: 15, of which 6 were waited for; matrix products, arithmetic and copies ran while one was open for 17% of the time, Pallas kernels for 35%

profile of v2, /device:TPU:0, one launch (start us, length us, event | category | flops | bytes accessed | tf_op | source)
XLA Modules:
  0.0 855.4 jit_solution(2369375138283122678)
XLA Ops:
  11.2 3.0 collective-permute-start.2
  20.1 15.7 %plane_gather.1 = bf16[8,96,1280]{2,1,0:T(8,128)(2,1)S(1)} custom-call(bf16[96,1280]{1,0:T(8,128)(2,1)S(1)} %concatenate.82.x_ref), custom_call_target="tpu_custom_call" | custom-call | tf_op jit(solution)/shard_map/plane_gather/pallas_call | solution.py:120
  37.1 7.2 collective-permute-done.3
  53.9 3.6 concatenate.88
  63.4 3.1 convolution_convert_fusion.3
  69.9 3.0 fusion.33
  82.7 3.3 convert_element_type.133.base_ref
  90.7 9.4 %collective-permute-done = bf16[512,384]{1,0:T(8,128)(2,1)} collective-permute-done((bf16[512,384]{1,0:T(8,128)(2,1)}, bf16[512,384]{1,0:T(8,128)(2,1)}, u32[]{:S(2)}, u32[]{:S(2)}) %collective-permute-start) | collective-permute-done | bytes 393248 | tf_op jit(solution)/shard_map/ppermute | solution.py:43
  101.4 5.1 attend_masked.2
  106.5 4.6 attend_masked.3
  111.9 63.1 %all-gather.3.cloned.1.call-done = bf16[768,8448]{1,0:T(8,128)(2,1)} async-done(((bf16[96,8448]{1,0:T(8,128)(2,1)}), bf16[768,8448]{1,0:T(8,128)(2,1)}) %all-gather.3.cloned.1.call-update) | async-done | bytes 12976144 | tf_op jit(solution)/shard_map/all_gather | solution.py:908
  175.0 4.0 slice_bitcast_fusion.3
  180.1 47.5 %line_project.3.base_ref = f32[1024,768]{1,0:T(8,128)S(1)} custom-call(bf16[1024,192]{1,0:T(8,128)(2,1)S(1)} %copy-done.19, bf16[4,768,192]{2,1,0:T(8,128)(2,1)S(1)} %pad_maximum_fusion.2.w_ref, f32[1024,768]{1,0:T(8,128)} %convert_element_type.133.base_ref), custom_call_target="tpu_custom_call" | custom-call | tf_op jit(solution)/shard_map/line_project/pallas_call | solution.py:277
  233.7 7.9 attend.2
  244.1 7.8 attend.3
  253.6 39.8 %line_project.4 = f32[1024,768]{1,0:T(8,128)S(1)} custom-call(bf16[1024,192]{1,0:T(8,128)(2,1)S(1)} %constant_dynamic-update-slice_fusion.6.x_ref, bf16[4,768,192]{2,1,0:T(8,128)(2,1)S(1)} %get-tuple-element.266.w_ref, f32[1024,768]{1,0:T(8,128)} %copy-done.1), custom_call_target="tpu_custom_call" | custom-call | tf_op jit(solution)/shard_map/line_project/pallas_call | solution.py:277
  294.0 6.3 fusion.31
  300.4 9.8 %multiply_convert_fusion.1 = (bf16[1024,2048]{1,0:T(8,128)(2,1)S(1)}, f32[1024,2048]{1,0:T(8,128)}) fusion(f32[1024,2048]{1,0:T(8,128)S(1)} %fusion.31, bf16[1024,768]{1,0:T(8,128)(2,1)S(1)} %multiply_convert_fusion.3, bf16[768,8448]{1,0:T(8,128)(2,1)} %all-gather.3.cloned.1.call-done), kind=kOutput, calls=%fused_computation.11 | convolution fusion | flops 3242196992 | bytes 25690112 | tf_op jit(solution)/shard_map/dot_general | solution.py:26
  310.2 7.1 multiply_reduce_fusion.4
  323.6 24.4 %exit_forward.1 = (f32[1024,8192]{1,0:T(8,128)}, f32[1024,1]{1,0:T(8,128)S(1)}, f32[1024,1]{1,0:T(8,128)S(1)}, f32[1024,1]{1,0:T(8,128)S(1)}) custom-call(bf16[1024,768]{1,0:T(8,128)(2,1)S(1)} %copy-done.27, bf16[768,8192]{1,0:T(8,128)(2,1)} %all-gather.5.cloned.1.call-done.e_ref, s32[1024,1]{1,0:T(8,128)S(1)} %copy-done.37), custom_call_target="tpu_custom_call" | custom-call | flops 12884901888 | bytes 46137344 | tf_op jit(solution)/shard_map/exit_forward/pallas_call | solution.py:604
  354.8 6.9 share_stats.1
  369.5 35.4 %exit_backward.1 = (bf16[768,8192]{1,0:T(8,128)(2,1)}, bf16[1024,768]{1,0:T(8,128)(2,1)S(1)}) custom-call(f32[1024,8192]{1,0:T(8,128)} %get-tuple-element.75.logits_ref, bf16[768,8192]{1,0:T(8,128)(2,1)} %all-gather.5.cloned.1.call-done.e_ref, bf16[768,1024]{1,0:T(8,128)(2,1)S(1)} %copy-done.20, s32[1024,1]{1,0:T(8,128)S(1)} %copy-done.38, ...), custom_call_target="tpu_custom_call" | custom-call | flops 25769803776 | bytes 58720256 | tf_op jit(solution)/shard_map/exit_backward/pallas_call | solution.py:652
  404.9 54.2 %line_sum.2 = bf16[1024,768]{1,0:T(8,128)(2,1)S(1)} custom-call(bf16[1024,768]{1,0:T(8,128)(2,1)S(1)} %get-tuple-element.76.x_ref), custom_call_target="tpu_custom_call" | custom-call | tf_op jit(solution)/shard_map/line_sum/pallas_call | solution.py:463
  462.6 3.2 convolution_convert_fusion.5
  465.8 13.6 %fusion.7 = (bf16[1024,2048]{1,0:T(8,128)(2,1)S(1)}, bf16[1024,2048]{1,0:T(8,128)(2,1)}) fusion(f32[1024,2048]{1,0:T(8,128)} %get-tuple-element.260, f32[1024,2048]{1,0:T(8,128)} %copy-done.90, bf16[768,8448]{1,0:T(8,128)(2,1)} %all-gather.3.cloned.1.call-done, f32[1024,768]{1,0:T(8,128)S(1)} %get-tuple-element.229), kind=kOutput, calls=%fused_computation.9 | convolution fusion | flops 3270246400 | bytes 31457280 | tf_op jit(solution)/shard_map/dot_general | solution.py:26
  483.8 5.5 fusion.25
  489.3 5.8 multiply_reduce_fusion
  499.7 10.8 %attend_back.2 = (bf16[512,192]{1,0:T(8,128)(2,1)S(1)}, bf16[2048,384]{1,0:T(8,128)(2,1)S(1)}) custom-call(bf16[512,192]{1,0:T(8,128)(2,1)S(1)} %copy-done.49, bf16[2048,384]{1,0:T(8,128)(2,1)S(1)} %copy-done.41, f32[3,512]{1,0:T(4,128)S(1)} %get-tuple-element.77.rest_0_, bf16[512,192]{1,0:T(8,128)(2,1)S(1)} %get-tuple-element.247.rest_1_), custom_call_target="tpu_custom_call" | custom-call | flops 8053063680 | bytes 4128768 | tf_op jit(solution)/shard_map/attend_back/pallas_call | solution.py:784
  511.7 10.7 %attend_back.3 = (bf16[512,192]{1,0:T(8,128)(2,1)S(1)}, bf16[2048,384]{1,0:T(8,128)(2,1)S(1)}) custom-call(bf16[512,192]{1,0:T(8,128)(2,1)S(1)} %copy-done.47, bf16[2048,384]{1,0:T(8,128)(2,1)S(1)} %copy-done.43, f32[3,512]{1,0:T(4,128)S(1)} %get-tuple-element.79.rest_0_, bf16[512,192]{1,0:T(8,128)(2,1)S(1)} %get-tuple-element.246.rest_1_), custom_call_target="tpu_custom_call" | custom-call | flops 8053063680 | bytes 4128768 | tf_op jit(solution)/shard_map/attend_back/pallas_call | solution.py:784
  526.1 30.5 %line_project.5 = f32[1024,768]{1,0:T(8,128)S(1)} custom-call(bf16[1024,192]{1,0:T(8,128)(2,1)S(1)} %constant_dynamic-update-slice_fusion.8.x_ref, bf16[4,768,192]{2,1,0:T(8,128)(2,1)S(1)} %copy-done.11, f32[1024,768]{1,0:T(8,128)} %broadcast_in_dim.93.base_ref), custom_call_target="tpu_custom_call" | custom-call | tf_op jit(solution)/shard_map/line_project/pallas_call | solution.py:277
  559.9 4.5 copy.141
  565.1 3.8 multiply_reduce_fusion.1
  576.8 5.8 attend_back_masked.2
  586.3 5.9 attend_back_masked.3
  600.7 3.2 convolution_convert_fusion.13
  607.7 4.9 collective-permute-done.8
  614.5 4.0 convolution_convert_fusion.4
  621.0 3.1 convolution_convert_fusion.2
  624.1 8.0 collective-permute-done.9
  633.6 8.7 %collective-permute-done.10 = bf16[1024,384]{1,0:T(8,128)(2,1)} collective-permute-done((bf16[1024,384]{1,0:T(8,128)(2,1)}, bf16[1024,384]{1,0:T(8,128)(2,1)}, u32[]{:S(2)}, u32[]{:S(2)}) %collective-permute-start.10) | collective-permute-done | bytes 786464 | tf_op jit(solution)/shard_map/ppermute | solution.py:43
  644.7 3.0 convolution_convert_fusion
  650.2 138.5 %line_sum.3 = bf16[3072,768]{1,0:T(8,128)(2,1)S(1)} custom-call(bf16[3072,768]{1,0:T(8,128)(2,1)} %pad_maximum_fusion.x_ref), custom_call_target="tpu_custom_call" | custom-call | tf_op jit(solution)/shard_map/line_sum/pallas_call | solution.py:463
  793.0 3.7 fusion.40
  798.8 5.0 concatenate.103.x_ref
  805.4 17.4 %plane_scatter.1 = f32[96,1408]{1,0:T(8,128)S(1)} custom-call(bf16[8,96,1408]{2,1,0:T(8,128)(2,1)S(1)} %copy-done.8), custom_call_target="tpu_custom_call" | custom-call | tf_op jit(solution)/shard_map/plane_scatter/pallas_call | solution.py:178
  827.0 5.3 fusion.14
  832.3 5.1 slice_convert_fusion
  845.4 3.2 convert_bitcast_fusion
  (342 shorter events, 154.5 us)
Async XLA Ops:
  7.2 62.7 %copy-start = (bf16[2048,768]{1,0:T(8,128)(2,1)S(1)}, bf16[2048,768]{1,0:T(8,128)(2,1)}, u32[]{:S(2)}) copy-start(bf16[2048,768]{1,0:T(8,128)(2,1)} %param.22) | copy-start | bytes 9437188
  7.2 167.8 %all-gather.3.cloned.1.call-start = ((), (), s32[]{:S(2)}) async-start(), calls=%async_computation.2 | async-start | bytes 14598144 | tf_op jit(solution)/shard_map/all_gather | solution.py:908
  11.2 25.8 %collective-permute-start.2 = (bf16[96,2112]{1,0:T(8,128)(2,1)}, bf16[96,2112]{1,0:T(8,128)(2,1)}, u32[]{:S(2)}, u32[]{:S(2)}) collective-permute-start(bf16[96,2112]{1,0:T(8,128)(2,1)} %concatenate.87), channel_id=1, source_target_pairs={{0,1},{1,2},{2,3},{3,0},{4,5},{5,6},{6,7},{7,4},{8,9},{9,10},{10,1... | collective-permute-start | bytes 1216520 | tf_op jit(solution)/shard_map/ppermute | solution.py:521
  14.3 30.0 %collective-permute-start.3 = (bf16[96,2112]{1,0:T(8,128)(2,1)}, bf16[96,2112]{1,0:T(8,128)(2,1)}, u32[]{:S(2)}, u32[]{:S(2)}) collective-permute-start(bf16[96,2112]{1,0:T(8,128)(2,1)} %concatenate.87), channel_id=1, source_target_pairs={{0,2},{1,3},{2,0},{3,1},{4,6},{5,7},{6,4},{7,5},{8,10},{9,11},{10,... | collective-permute-start | bytes 1216520 | tf_op jit(solution)/shard_map/ppermute | solution.py:521
  16.9 27.4 %collective-permute-start.4 = (bf16[96,2112]{1,0:T(8,128)(2,1)}, bf16[96,2112]{1,0:T(8,128)(2,1)}, u32[]{:S(2)}, u32[]{:S(2)}) collective-permute-start(bf16[96,2112]{1,0:T(8,128)(2,1)} %concatenate.87), channel_id=1, source_target_pairs={{0,3},{1,0},{2,1},{3,2},{4,7},{5,4},{6,5},{7,6},{8,11},{9,8},{10,9... | collective-permute-start | bytes 1216520 | tf_op jit(solution)/shard_map/ppermute | solution.py:521
  37.1 14.5 %copy-start.62 = (bf16[96,2112]{1,0:T(8,128)(2,1)S(1)}, bf16[96,2112]{1,0:T(8,128)(2,1)}, u32[]{:S(2)}) copy-start(bf16[96,2112]{1,0:T(8,128)(2,1)} %concatenate.87) | copy-start | bytes 1216516
  57.6 263.6 %all-gather.5.cloned.1.call-start = ((), (), s32[]{:S(2)}) async-start(), calls=%async_computation.3 | async-start | bytes 14155776 | tf_op jit(solution)/shard_map/all_gather | solution.py:925
  60.4 777.1 %reduce-scatter.7.cloned.1.call-start = ((), (), s32[]{:S(2)}) async-start(), calls=%async_computation.5 | async-start | bytes 3096576
  61.6 169.5 %copy-start.75 = (f32[768]{0:T(1024)}, f32[768]{0:T(1024)S(1)}, u32[]{:S(2)}) copy-start(f32[768]{0:T(1024)S(1)} %get-tuple-element.189) | copy-start | bytes 9220
  67.9 21.5 %collective-permute-start.1 = (bf16[512,384]{1,0:T(8,128)(2,1)}, bf16[512,384]{1,0:T(8,128)(2,1)}, u32[]{:S(2)}, u32[]{:S(2)}) collective-permute-start(bf16[512,384]{1,0:T(8,128)(2,1)} %get-tuple-element.233), channel_id=1, source_target_pairs={{0,4},{4,0},{1,5},{5,1},{2,6},{6,2},{3,7},{7,3},{8,12},{12,8},{9,1... | collective-permute-start | bytes 1179656 | tf_op jit(solution)/shard_map/ppermute | solution.py:43
  69.4 30.8 %collective-permute-start = (bf16[512,384]{1,0:T(8,128)(2,1)}, bf16[512,384]{1,0:T(8,128)(2,1)}, u32[]{:S(2)}, u32[]{:S(2)}) collective-permute-start(bf16[512,384]{1,0:T(8,128)(2,1)} %get-tuple-element.234), channel_id=1, source_target_pairs={{0,4},{4,0},{1,5},{5,1},{2,6},{6,2},{3,7},{7,3},{8,12},{12,8},{9,1... | collective-permute-start | bytes 1179656 | tf_op jit(solution)/shard_map/ppermute | solution.py:43
  74.3 153.4 %collective-permute-start.6 = (bf16[1024,384]{1,0:T(8,128)(2,1)}, bf16[1024,384]{1,0:T(8,128)(2,1)}, u32[]{:S(2)}, u32[]{:S(2)}) collective-permute-start(bf16[1024,384]{1,0:T(8,128)(2,1)} %get-tuple-element.65), channel_id=1, source_target_pairs={{0,4},{4,0},{1,5},{5,1},{2,6},{6,2},{3,7},{7,3},{8,12},{12,8},{9,1... | collective-permute-start | bytes 2359304 | tf_op jit(solution)/shard_map/ppermute | solution.py:43
  75.8 151.9 %collective-permute-start.5 = (bf16[1024,384]{1,0:T(8,128)(2,1)}, bf16[1024,384]{1,0:T(8,128)(2,1)}, u32[]{:S(2)}, u32[]{:S(2)}) collective-permute-start(bf16[1024,384]{1,0:T(8,128)(2,1)} %get-tuple-element.62), channel_id=1, source_target_pairs={{0,4},{4,0},{1,5},{5,1},{2,6},{6,2},{3,7},{7,3},{8,12},{12,8},{9,1... | collective-permute-start | bytes 2359304 | tf_op jit(solution)/shard_map/ppermute | solution.py:43
  89.3 12.0 %copy-start.44 = (bf16[512,192]{1,0:T(8,128)(2,1)S(1)}, bf16[512,192]{1,0:T(8,128)(2,1)}, u32[]{:S(2)}) copy-start(bf16[512,192]{1,0:T(8,128)(2,1)} %get-tuple-element.236.q_ref) | copy-start | bytes 589828
  89.3 12.0 %copy-start.52 = (f32[1024,512]{1,0:T(8,128)S(1)}, f32[1024,512]{1,0:T(8,128)}, u32[]{:S(2)}) copy-start(f32[1024,512]{1,0:T(8,128)} %and_select_fusion.1.bias_ref) | copy-start | bytes 6291460
  90.7 15.8 %copy-start.28 = (bf16[1024,384]{1,0:T(8,128)(2,1)}, bf16[1024,384]{1,0:T(8,128)(2,1)S(1)}, u32[]{:S(2)}) copy-start(bf16[1024,384]{1,0:T(8,128)(2,1)S(1)} %pad_maximum_fusion.9.kv_ref) | copy-start | bytes 2359300
  180.1 47.5 %copy-start.9 = (bf16[4,768,192]{2,1,0:T(8,128)(2,1)}, bf16[4,768,192]{2,1,0:T(8,128)(2,1)S(1)}, u32[]{:S(2)}) copy-start(bf16[4,768,192]{2,1,0:T(8,128)(2,1)S(1)} %pad_maximum_fusion.2.w_ref) | copy-start | bytes 3538948
  233.7 7.9 copy-start.48
  233.7 10.5 %copy-start.46 = (bf16[512,192]{1,0:T(8,128)(2,1)}, bf16[512,192]{1,0:T(8,128)(2,1)S(1)}, u32[]{:S(2)}) copy-start(bf16[512,192]{1,0:T(8,128)(2,1)S(1)} %get-tuple-element.248.q) | copy-start | bytes 589828
  244.1 7.8 copy-start.42
  253.6 39.8 %copy-start.10 = (bf16[4,768,192]{2,1,0:T(8,128)(2,1)}, bf16[4,768,192]{2,1,0:T(8,128)(2,1)S(1)}, u32[]{:S(2)}) copy-start(bf16[4,768,192]{2,1,0:T(8,128)(2,1)S(1)} %get-tuple-element.266.w_ref) | copy-start | bytes 3538948
  293.4 16.8 %copy-start.3 = (f32[1024,768]{1,0:T(8,128)}, f32[1024,768]{1,0:T(8,128)S(1)}, u32[]{:S(2)}) copy-start(f32[1024,768]{1,0:T(8,128)S(1)} %line_project.4) | copy-start | bytes 9437188
  300.4 9.8 %copy-start.90 = (f32[1024,2048]{1,0:T(8,128)}, f32[1024,2048]{1,0:T(8,128)S(1)}, u32[]{:S(2)}) copy-start(f32[1024,2048]{1,0:T(8,128)S(1)} %fusion.31) | copy-start | bytes 25165828
  310.2 7.1 copy-start.88
  404.9 54.2 %copy-start.58 = (f32[1024,768]{1,0:T(8,128)S(1)}, f32[1024,768]{1,0:T(8,128)}, u32[]{:S(2)}) copy-start(f32[1024,768]{1,0:T(8,128)} %copy-done.57) | copy-start | bytes 9437188
  465.8 13.6 %copy-start.65 = (bf16[1024,768]{1,0:T(8,128)(2,1)S(1)}, bf16[1024,768]{1,0:T(8,128)(2,1)}, u32[]{:S(2)}) copy-start(bf16[1024,768]{1,0:T(8,128)(2,1)} %copy-done.64) | copy-start | bytes 4718596
  499.7 12.1 %copy-start.43 = (bf16[2048,384]{1,0:T(8,128)(2,1)S(1)}, bf16[2048,384]{1,0:T(8,128)(2,1)}, u32[]{:S(2)}) copy-start(bf16[2048,384]{1,0:T(8,128)(2,1)} %copy-done.42) | copy-start | bytes 4718596
  499.7 12.1 %copy-start.47 = (bf16[512,192]{1,0:T(8,128)(2,1)S(1)}, bf16[512,192]{1,0:T(8,128)(2,1)}, u32[]{:S(2)}) copy-start(bf16[512,192]{1,0:T(8,128)(2,1)} %copy-done.46) | copy-start | bytes 589828
  523.6 33.0 %copy-start.16 = (bf16[1024,192]{1,0:T(8,128)(2,1)}, bf16[1024,192]{1,0:T(8,128)(2,1)S(1)}, u32[]{:S(2)}) copy-start(bf16[1024,192]{1,0:T(8,128)(2,1)S(1)} %constant_dynamic-update-slice_fusion.8.x_ref) | copy-start | bytes 1179652
  526.0 32.1 %copy-start.70 = (bf16[768,512]{0,1:T(8,128)(2,1)S(1)}, bf16[768,512]{0,1:T(8,128)(2,1)}, u32[]{:S(2)}) copy-start(bf16[768,512]{0,1:T(8,128)(2,1)} %convolution_convert_fusion.5) | copy-start | bytes 2359300
  526.1 32.1 %copy-start.71 = (bf16[768,512]{0,1:T(8,128)(2,1)S(1)}, bf16[768,512]{0,1:T(8,128)(2,1)}, u32[]{:S(2)}) copy-start(bf16[768,512]{0,1:T(8,128)(2,1)} %convolution_convert_fusion.7) | copy-start | bytes 2359300
  526.1 32.1 %copy-start.72 = (bf16[768,512]{0,1:T(8,128)(2,1)S(1)}, bf16[768,512]{0,1:T(8,128)(2,1)}, u32[]{:S(2)}) copy-start(bf16[768,512]{0,1:T(8,128)(2,1)} %convolution_convert_fusion.6) | copy-start | bytes 2359300
  564.4 281.0 %reduce-scatter.5.cloned.1.call-start = ((), (), s32[]{:S(2)}) async-start(), calls=%async_computation.4 | async-start | bytes 14155776 | tf_op jit(solution)/shard_map/reduce_scatter | solution.py:980
  576.8 7.6 copy-start.29
  584.3 22.2 %collective-permute-start.7 = (bf16[512,384]{1,0:T(8,128)(2,1)}, bf16[512,384]{1,0:T(8,128)(2,1)}, u32[]{:S(2)}, u32[]{:S(2)}) collective-permute-start(bf16[512,384]{1,0:T(8,128)(2,1)} %slice.333), channel_id=1, source_target_pairs={{0,4},{4,0},{1,5},{5,1},{2,6},{6,2},{3,7},{7,3},{8,12},{12,8},{9,1... | collective-permute-start | bytes 1179656 | tf_op jit(solution)/shard_map/ppermute | solution.py:43
  586.3 8.6 %copy-start.22 = (bf16[2048,384]{1,0:T(8,128)(2,1)S(1)}, bf16[2048,384]{1,0:T(8,128)(2,1)}, u32[]{:S(2)}) copy-start(bf16[2048,384]{1,0:T(8,128)(2,1)} %copy-done.21) | copy-start | bytes 4718596
  586.3 9.8 %copy-start.25 = (bf16[2048,384]{1,0:T(8,128)(2,1)S(1)}, bf16[2048,384]{1,0:T(8,128)(2,1)}, u32[]{:S(2)}) copy-start(bf16[2048,384]{1,0:T(8,128)(2,1)} %copy-done.24) | copy-start | bytes 4718596
  592.2 6.7 copy-start.17
  593.0 19.5 %collective-permute-start.8 = (bf16[512,384]{1,0:T(8,128)(2,1)}, bf16[512,384]{1,0:T(8,128)(2,1)}, u32[]{:S(2)}, u32[]{:S(2)}) collective-permute-start(bf16[512,384]{1,0:T(8,128)(2,1)} %slice.335), channel_id=1, source_target_pairs={{0,4},{4,0},{1,5},{5,1},{2,6},{6,2},{3,7},{7,3},{8,12},{12,8},{9,1... | collective-permute-start | bytes 1179656 | tf_op jit(solution)/shard_map/ppermute | solution.py:43
  595.9 36.2 %collective-permute-start.9 = (bf16[1024,384]{1,0:T(8,128)(2,1)}, bf16[1024,384]{1,0:T(8,128)(2,1)}, u32[]{:S(2)}, u32[]{:S(2)}) collective-permute-start(bf16[1024,384]{1,0:T(8,128)(2,1)} %slice.337), channel_id=1, source_target_pairs={{0,4},{4,0},{1,5},{5,1},{2,6},{6,2},{3,7},{7,3},{8,12},{12,8},{9,1... | collective-permute-start | bytes 2359304 | tf_op jit(solution)/shard_map/ppermute | solution.py:43
  597.1 45.3 %collective-permute-start.10 = (bf16[1024,384]{1,0:T(8,128)(2,1)}, bf16[1024,384]{1,0:T(8,128)(2,1)}, u32[]{:S(2)}, u32[]{:S(2)}) collective-permute-start(bf16[1024,384]{1,0:T(8,128)(2,1)} %slice.339), channel_id=1, source_target_pairs={{0,4},{4,0},{1,5},{5,1},{2,6},{6,2},{3,7},{7,3},{8,12},{12,8},{9,1... | collective-permute-start | bytes 2359304 | tf_op jit(solution)/shard_map/ppermute | solution.py:43
  600.7 13.9 %copy-start.55 = (bf16[512,192]{1,0:T(8,128)(2,1)S(1)}, bf16[512,192]{1,0:T(8,128)(2,1)}, u32[]{:S(2)}) copy-start(bf16[512,192]{1,0:T(8,128)(2,1)} %copy-done.54) | copy-start | bytes 589828
  600.7 13.9 %copy-start.80 = (f32[768]{0:T(1024)S(1)}, f32[768]{0:T(1024)}, u32[]{:S(2)}) copy-start(f32[768]{0:T(1024)} %copy-done.79) | copy-start | bytes 9220
  600.7 13.9 %copy-start.82 = (f32[1024]{0:T(1024)S(1)}, f32[1024]{0:T(1024)}, u32[]{:S(2)}) copy-start(f32[1024]{0:T(1024)} %copy-done.81) | copy-start | bytes 12292
  621.0 11.1 %copy-start.23 = (bf16[2048,384]{1,0:T(8,128)(2,1)S(1)}, bf16[2048,384]{1,0:T(8,128)(2,1)}, u32[]{:S(2)}) copy-start(bf16[2048,384]{1,0:T(8,128)(2,1)} %copy-done.21) | copy-start | bytes 4718596
  621.0 21.4 %copy-start.26 = (bf16[2048,384]{1,0:T(8,128)(2,1)S(1)}, bf16[2048,384]{1,0:T(8,128)(2,1)}, u32[]{:S(2)}) copy-start(bf16[2048,384]{1,0:T(8,128)(2,1)} %copy-done.24) | copy-start | bytes 4718596
  633.6 10.2 %copy-start.68 = (bf16[1024,384]{1,0:T(8,128)(2,1)}, bf16[1024,384]{1,0:T(8,128)(2,1)S(1)}, u32[]{:S(2)}) copy-start(bf16[1024,384]{1,0:T(8,128)(2,1)S(1)} %add_convert_fusion.1) | copy-start | bytes 2359300
  650.2 140.7 %copy-start.61 = (bf16[1024,768]{1,0:T(8,128)(2,1)S(1)}, bf16[1024,768]{1,0:T(8,128)(2,1)}, u32[]{:S(2)}) copy-start(bf16[1024,768]{1,0:T(8,128)(2,1)} %param.21) | copy-start | bytes 4718596
  (58 other events, 150.3 us)
Sparse Core Ops, SparseCore 0:
  57.7 117.2 all-gather.2
  176.9 78.5 all-gather.4
  564.5 54.4 reduce-scatter.6
  622.7 92.4 reduce-scatter.4

commit v3 on v2

--- a/solution.py
+++ b/solution.py
@@ -20,6 +20,8 @@
 MESH = pl.DeviceIdType.MESH
 TILE = 1024
 LOWEST = -3.0e38
+VMEM_MOST = 58 * 1024 * 1024
+Q2 = 1024
 
 
 def mat(left, right):
@@ -843,6 +845,726 @@
     return value, slope
 
 
+class Line:
+    def __init__(self, t, count, left, right, own, place, sems):
+        self.t, self.count, self.left, self.right = t, count, left, right
+        self.own, self.place = own, place
+        self.to_right, self.to_left, self.recv = sems
+
+    def copy(self, d, way):
+        origin = self.t - d if way == 0 else self.t + d
+        sems, peer = (self.to_right, self.right) if way == 0 else (self.to_left, self.left)
+        src = self.own if d == 0 else self.place(origin)
+        return remote(src, self.place(origin), sems.at[d], self.recv.at[origin], peer)
+
+    def landed(self, origin):
+        return remote(
+            self.place(origin),
+            self.place(origin),
+            self.to_right.at[0],
+            self.recv.at[origin],
+            self.right,
+        )
+
+    def start(self):
+        @pl.when(self.t < self.count - 1)
+        def _():
+            self.copy(0, 0).start()
+
+        @pl.when(self.t > 0)
+        def _():
+            self.copy(0, 1).start()
+
+    def hop(self, d):
+        t, last = self.t, self.count - 1
+
+        @pl.when(t - d >= 0)
+        def _():
+            self.landed(t - d).wait_recv()
+            if d < last:
+
+                @pl.when(t < last)
+                def _():
+                    self.copy(d, 0).start()
+
+        @pl.when(t + d <= last)
+        def _():
+            self.landed(t + d).wait_recv()
+            if d < last:
+
+                @pl.when(t > 0)
+                def _():
+                    self.copy(d, 1).start()
+
+    def finish(self):
+        t, last = self.t, self.count - 1
+        for d in range(last):
+
+            @pl.when((t - d >= 0) & (t < last))
+            def _():
+                self.copy(d, 0).wait_send()
+
+            @pl.when((t + d <= last) & (t > 0))
+            def _():
+                self.copy(d, 1).wait_send()
+
+
+class Spread:
+    def __init__(self, x_peer, y_peer, core_peer, own, place, send, recv):
+        self.send, self.recv = send, recv
+        home, across, aside, diagonal = place(0, 0), place(0, 1), place(2, 0), place(2, 1)
+        moves = [
+            (own, home, x_peer),
+            (own, home, y_peer),
+            (across, across, y_peer),
+            (own, home, core_peer),
+            (across, across, core_peer),
+            (aside, aside, core_peer),
+            (diagonal, diagonal, core_peer),
+        ]
+        self.copies = [
+            remote(src, dst, send.at[j], recv.at[j], peer)
+            for j, (src, dst, peer) in enumerate(moves)
+        ]
+
+    def step(self, k):
+        copies = self.copies
+        if k == 0:
+            for j in (0, 1, 3):
+                copies[j].start()
+        elif k == 1:
+            copies[0].wait_recv()
+            copies[2].start()
+            copies[4].start()
+        elif k == 2:
+            copies[1].wait_recv()
+            copies[5].start()
+        elif k == 3:
+            copies[2].wait_recv()
+            copies[6].start()
+        elif k == 4:
+            for j in (3, 4, 5, 6):
+                copies[j].wait_recv()
+        else:
+            for copy in copies:
+                copy.wait_send()
+
+
+def attend_head(h, i, tile, q_ref, kv_ref, bias_ref, out_ref, total_ref):
+    rows, width = q_ref.shape[0] // MB, q_ref.shape[1]
+    cols = slice(h * HD, (h + 1) * HD)
+    vcols = slice(width + h * HD, width + (h + 1) * HD)
+
+    @pl.loop(0, rows // tile)
+    def _(n):
+        at = pl.ds(pl.multiple_of(i * rows + n * tile, tile), tile)
+        here_at = pl.ds(pl.multiple_of(n * tile, tile), tile)
+        scores = mat_nt(kv_ref[i, :, cols], q_ref[at, cols])
+        if bias_ref is not None:
+            scores = scores + bias_ref[i, :, here_at]
+        highest = jnp.max(scores, axis=0, keepdims=True)
+        exponent = jnp.exp(scores - highest)
+        denominator = jnp.sum(exponent, axis=0, keepdims=True)
+        outcome = mat_tn(kv_ref[i, :, vcols], exponent.astype(BF16)) / denominator
+        out_ref[at, cols] = outcome.T.astype(BF16)
+        total_ref[i, h : h + 1, here_at] = highest + jnp.log(denominator)
+
+
+def build_bias(parents_ref, bias_ref, c):
+    trees, keys, rows = bias_ref.shape
+    mine = rows // BLK
+    block_count = keys // BLK
+    key_iota = lax.broadcasted_iota(jnp.int32, (BLK, BLK), 0)
+    query_iota = lax.broadcasted_iota(jnp.int32, (BLK, BLK), 1)
+    causal = jnp.where(key_iota <= query_iota, 0.0, MASKED)
+    for i in range(trees):
+        lines = [jnp.int32(1)]
+        for b in range(1, block_count):
+            parent = parents_ref[i, b]
+            line = jnp.int32(1 << b)
+            for j in range(b):
+                line = line + jnp.where(parent == j, lines[j], 0)
+            lines.append(line)
+        for q in range(mine):
+            line = jnp.int32(0)
+            for b in range(block_count):
+                line = line + jnp.where(c * mine + q == b, lines[b], 0)
+            for k in range(block_count):
+                at = (slice(k * BLK, (k + 1) * BLK), slice(q * BLK, (q + 1) * BLK))
+                if k == q:
+                    bias_ref[(i,) + at] = causal
+                    continue
+                block = c * mine + k if k < mine else (1 - c) * mine + k - mine
+                seen = lax.shift_right_logical(line, block) & 1
+                value = jnp.where(seen == 1, 0.0, MASKED)
+                bias_ref[(i,) + at] = jnp.full((BLK, BLK), value, F32)
+
+
+def layer_forward_kernel(
+    count,
+    parents_ref,
+    tok_ref,
+    enc_ref,
+    heads_in,
+    op_in,
+    ff_in,
+    heads_all,
+    op_all,
+    ff_all,
+    gains_out,
+    bias,
+    q_out,
+    kvs,
+    kvc,
+    att,
+    tots,
+    cq,
+    crs,
+    totc,
+    as_out,
+    ac_out,
+    zop,
+    zff,
+    held_s,
+    held_c,
+    spread_send,
+    spread_recv,
+    line_right,
+    line_left,
+    line_recv,
+    ctx_send,
+    ctx_recv,
+    local_sem,
+):
+    f, c, t = here()
+    right, left = (f, c, t + 1), (f, c, t - 1)
+    x_peer, y_peer, core_peer = (f, 1 - c, t), (f ^ 2, c, t), (f ^ 1, c, t)
+    rows, enc_rows = tok_ref.shape[0] // MB, enc_ref.shape[0] // MB
+    width = q_out.shape[1]
+    shard, ff_cols = ff_in.shape
+    tile = 256
+
+    barrier = pltpu.get_barrier_semaphore()
+    for peer in (x_peer, y_peer, core_peer):
+        pl.semaphore_signal(barrier, inc=1, device_id=peer, device_id_type=MESH)
+
+    @pl.when(t > 0)
+    def _():
+        pl.semaphore_signal(barrier, inc=1, device_id=left, device_id_type=MESH)
+
+    @pl.when(t < count - 1)
+    def _():
+        pl.semaphore_signal(barrier, inc=1, device_id=right, device_id_type=MESH)
+
+    at_end = (t == 0) | (t == count - 1)
+    pl.semaphore_wait(barrier, jnp.where(at_end, 4, 5).astype(jnp.int32))
+
+    def block(df, dc):
+        slot = (f ^ df) * 2 + (c ^ dc)
+        return pl.ds(pl.multiple_of(slot * shard, shard), shard)
+
+    def spread(j, own, place):
+        return Spread(
+            x_peer, y_peer, core_peer, own, place, spread_send.at[j], spread_recv.at[j]
+        )
+
+    def line(j, own, place):
+        sems = (line_right.at[j], line_left.at[j], line_recv.at[j])
+        return Line(t, count, left, right, own, place, sems)
+
+    def part(i):
+        return pl.ds(i * rows, rows)
+
+    heads = spread(0, heads_in, lambda df, dc: heads_all.at[block(df, dc)])
+    op_line = line(0, op_in, lambda origin: zop.at[:, origin])
+    op = spread(1, zop, lambda df, dc: op_all.at[:, :, block(df, dc)])
+
+    def ff_place(origin):
+        return zff.at[:, pl.ds(pl.multiple_of(origin * ff_cols, 128), ff_cols)]
+
+    ff_line = line(1, ff_in, ff_place)
+    ff = spread(2, zff, lambda df, dc: ff_all.at[block(df, dc)])
+    ff_own = pltpu.make_async_copy(zff, ff_all.at[block(0, 0)], local_sem)
+    self_lines = [
+        line(2 + i, att.at[part(i)], lambda origin, i=i: held_s.at[origin, part(i)])
+        for i in range(MB)
+    ]
+    cross_lines = [
+        line(4 + i, crs.at[part(i)], lambda origin, i=i: held_c.at[origin, part(i)])
+        for i in range(MB)
+    ]
+
+    def ctx_copy(j, ref, i, size):
+        return remote(
+            ref.at[i, pl.ds(0, size)],
+            ref.at[i, pl.ds(size, size)],
+            ctx_send.at[j],
+            ctx_recv.at[j],
+            x_peer,
+        )
+
+    ctx_self = [ctx_copy(i, kvs, i, rows) for i in range(MB)]
+    ctx_cross = [ctx_copy(2 + i, kvc, i, enc_rows) for i in range(MB)]
+
+    def project_tokens(i):
+        @pl.loop(0, rows // tile)
+        def _(n):
+            at = pl.ds(pl.multiple_of(i * rows + n * tile, tile), tile)
+            value = tok_ref[at].astype(F32)
+            hidden = (value * rms_scale(value) * gains_out[0:1]).astype(BF16)
+            q_out[at] = mat(hidden, heads_all[:, 4 * width : 5 * width]).astype(BF16)
+            inner = pl.ds(pl.multiple_of(n * tile, tile), tile)
+            kvs[i, inner] = mat(hidden, heads_all[:, : 2 * width]).astype(BF16)
+
+    def project_encoder(i):
+        @pl.loop(0, enc_rows // tile)
+        def _(n):
+            at = pl.ds(pl.multiple_of(i * enc_rows + n * tile, tile), tile)
+            inner = pl.ds(pl.multiple_of(n * tile, tile), tile)
+            kvc[i, inner] = mat(enc_ref[at], heads_all[:, 2 * width : 4 * width]).astype(BF16)
+
+    def self_head(i, h):
+        attend_head(h, i, tile, q_out, kvs, bias, att, tots)
+
+    def cross_head(i, h):
+        attend_head(h, i, tile, cq, kvc, None, crs, totc)
+
+    def out_self(i):
+        @pl.loop(0, rows // tile)
+        def _(n):
+            at = pl.ds(pl.multiple_of(i * rows + n * tile, tile), tile)
+            total = tok_ref[at].astype(F32)
+            for origin in range(count):
+                total = total + mat_nt(held_s[origin, at], op_all[0, origin])
+            as_out[at] = total
+            hidden = (total * rms_scale(total) * gains_out[1:2]).astype(BF16)
+            cq[at] = mat(hidden, heads_all[:, Q2 : Q2 + width]).astype(BF16)
+
+    def out_cross(i):
+        @pl.loop(0, rows // tile)
+        def _(n):
+            at = pl.ds(pl.multiple_of(i * rows + n * tile, tile), tile)
+            total = as_out[at]
+            for origin in range(count):
+                total = total + mat_nt(held_c[origin, at], op_all[1, origin])
+            ac_out[at] = total
+
+    heads.step(0)
+    op_line.start()
+    heads_all[block(0, 0)] = heads_in[...]
+    zop[:, t] = op_in[...]
+    zff[:, pl.ds(pl.multiple_of(t * ff_cols, 128), ff_cols)] = ff_in[...]
+    build_bias(parents_ref, bias, c)
+    op_line.hop(1)
+    heads.step(1)
+    op_line.hop(2)
+    ff_line.start()
+    heads.step(2)
+    op_line.hop(3)
+    op.step(0)
+    op_all[:, :, block(0, 0)] = zop[...]
+    heads.step(3)
+    heads.step(4)
+    gains_out[...] = heads_all[:, Q2 - 128 : Q2].astype(F32).T[64:72]
+    project_tokens(0)
+    ctx_self[0].start()
+    project_tokens(1)
+    ctx_self[1].start()
+    op.step(1)
+    ff_line.hop(1)
+    project_encoder(0)
+    ctx_cross[0].start()
+    project_encoder(1)
+    ctx_cross[1].start()
+    op.step(2)
+    ctx_self[0].wait_recv()
+    self_head(0, 0)
+    ff_line.hop(2)
+    self_head(0, 1)
+    op.step(3)
+    self_head(0, 2)
+    held_s[t, part(0)] = att[part(0)]
+    self_lines[0].start()
+    ff_line.hop(3)
+    ff_own.start()
+    ctx_self[1].wait_recv()
+    self_head(1, 0)
+    self_lines[0].hop(1)
+    self_head(1, 1)
+    op.step(4)
+    self_head(1, 2)
+    held_s[t, part(1)] = att[part(1)]
+    self_lines[1].start()
+    self_lines[0].hop(2)
+    ff.step(0)
+    self_lines[0].hop(3)
+    out_self(0)
+    self_lines[1].hop(1)
+    ctx_cross[0].wait_recv()
+    cross_head(0, 0)
+    self_lines[1].hop(2)
+    ff.step(1)
+    cross_head(0, 1)
+    self_lines[1].hop(3)
+    cross_head(0, 2)
+    held_c[t, part(0)] = crs[part(0)]
+    cross_lines[0].start()
+    out_self(1)
+    ctx_cross[1].wait_recv()
+    ff.step(2)
+    cross_head(1, 0)
+    cross_lines[0].hop(1)
+    cross_head(1, 1)
+    cross_lines[0].hop(2)
+    cross_head(1, 2)
+    held_c[t, part(1)] = crs[part(1)]
+    cross_lines[1].start()
+    cross_lines[0].hop(3)
+    out_cross(0)
+    cross_lines[1].hop(1)
+    ff.step(3)
+    cross_lines[1].hop(2)
+    cross_lines[1].hop(3)
+    out_cross(1)
+    ff.step(4)
+    heads.step(5)
+    op.step(5)
+    ff.step(5)
+    for one in [op_line, ff_line] + self_lines + cross_lines:
+        one.finish()
+    for copy in ctx_self + ctx_cross:
+        copy.wait_send()
+    ff_own.wait()
+
+
+def layer_forward(parents, tokens, encoder, heads_in, op_in, ff_in, collective_id):
+    count = lax.axis_size("tp")
+    tok_rows, features = tokens.shape
+    enc_rows = encoder.shape[0]
+    shard, ff_cols = ff_in.shape
+    width = op_in.shape[2]
+    nh = width // HD
+    rows = tok_rows // MB
+    vmem = pl.BlockSpec(memory_space=pltpu.VMEM)
+
+    def low(*shape):
+        return jax.ShapeDtypeStruct(shape, BF16)
+
+    def full(*shape):
+        return jax.ShapeDtypeStruct(shape, F32)
+
+    return pl.pallas_call(
+        functools.partial(layer_forward_kernel, count),
+        in_specs=[pl.BlockSpec(memory_space=pltpu.SMEM)] + [vmem] * 5,
+        out_specs=[vmem, vmem, pl.BlockSpec(memory_space=pl.ANY)] + [vmem] * 12,
+        out_shape=[
+            low(features, heads_in.shape[1]),
+            low(3, count, features, width),
+            low(features, count * ff_cols),
+            full(8, features),
+            full(MB, 2 * rows, rows),
+            low(tok_rows, width),
+            low(MB, 2 * rows, 2 * width),
+            low(MB, enc_rows, 2 * width),
+            low(tok_rows, width),
+            full(MB, nh, rows),
+            low(tok_rows, width),
+            low(tok_rows, width),
+            full(MB, nh, rows),
+            full(tok_rows, features),
+            full(tok_rows, features),
+        ],
+        scratch_shapes=[
+            pltpu.VMEM((3, count, shard, width), BF16),
+            pltpu.VMEM((shard, count * ff_cols), BF16),
+            pltpu.VMEM((count, tok_rows, width), BF16),
+            pltpu.VMEM((count, tok_rows, width), BF16),
+            pltpu.SemaphoreType.DMA((3, 7)),
+            pltpu.SemaphoreType.DMA((3, 7)),
+            pltpu.SemaphoreType.DMA((6, count)),
+            pltpu.SemaphoreType.DMA((6, count)),
+            pltpu.SemaphoreType.DMA((6, count)),
+            pltpu.SemaphoreType.DMA((4,)),
+            pltpu.SemaphoreType.DMA((4,)),
+            pltpu.SemaphoreType.DMA,
+        ],
+        compiler_params=pltpu.CompilerParams(
+            collective_id=collective_id, has_side_effects=True, vmem_limit_bytes=VMEM_MOST
+        ),
+        name="layer_forward",
+    )(parents, tokens, encoder, heads_in, op_in, ff_in)
+
+
+def ff_forward_kernel(
+    shrink, ac_ref, gains_ref, w_ref, gate_ref, up_ref, mixed_ref, low_ref, exit_ref, exit_t_ref, h_acc
+):
+    step = pl.program_id(0)
+    rows = ac_ref.shape[0]
+    units = gate_ref.shape[1]
+    tile = min(rows, 256)
+
+    @pl.loop(0, rows // tile)
+    def _(n):
+        at = pl.ds(pl.multiple_of(n * tile, tile), tile)
+
+        @pl.when(step == 0)
+        def _():
+            value = ac_ref[at]
+            h_acc[at] = (value * rms_scale(value) * gains_ref[2:3]).astype(BF16)
+            mixed_ref[at] = value
+
+        hidden = h_acc[at]
+        gate = mat(hidden, w_ref[:, :units])
+        up = mat(hidden, w_ref[:, units : 2 * units])
+        gate_ref[at] = gate
+        up_ref[at] = up
+        activated = (gelu_parts(gate)[0] * up).astype(BF16)
+        mixed_ref[at] += mat_nt(activated, w_ref[:, 2 * units :])
+
+        @pl.when(step == pl.num_programs(0) - 1)
+        def _():
+            value = mixed_ref[at]
+            low_ref[at] = value.astype(BF16)
+            exit_in = value * rms_scale(value) * gains_ref[3:4] * shrink
+            exit_ref[at] = exit_in.astype(BF16)
+
+    @pl.when(step == pl.num_programs(0) - 1)
+    def _():
+        exit_t_ref[...] = exit_ref[...].T
+
+
+def ff_forward(after_cross, gains, ff_all, count, shrink):
+    rows, features = after_cross.shape
+    cols = ff_all.shape[1] // count
+    units = cols // 3
+
+    def fixed(*shape):
+        return pl.BlockSpec(shape, lambda i: (0,) * len(shape))
+
+    moving = pl.BlockSpec((rows, units), lambda i: (0, i))
+    return pl.pallas_call(
+        functools.partial(ff_forward_kernel, shrink),
+        grid=(count,),
+        in_specs=[
+            fixed(rows, features),
+            fixed(8, features),
+            pl.BlockSpec((features, cols), lambda i: (0, i)),
+        ],
+        out_specs=[moving, moving] + [fixed(rows, features)] * 3 + [fixed(features, rows)],
+        out_shape=[
+            jax.ShapeDtypeStruct((rows, count * units), F32),
+            jax.ShapeDtypeStruct((rows, count * units), F32),
+            jax.ShapeDtypeStruct((rows, features), F32),
+            jax.ShapeDtypeStruct((rows, features), BF16),
+            jax.ShapeDtypeStruct((rows, features), BF16),
+            jax.ShapeDtypeStruct((features, rows), BF16),
+        ],
+        scratch_shapes=[pltpu.VMEM((rows, features), BF16)],
+        compiler_params=pltpu.CompilerParams(vmem_limit_bytes=VMEM_MOST),
+        cost_estimate=pl.CostEstimate(
+            flops=2 * rows * features * count * cols,
+            bytes_accessed=2 * features * count * cols + 8 * rows * count * units,
+            transcendentals=rows * count * units,
+        ),
+        name="ff_forward",
+    )(after_cross, gains, ff_all)
+
+
+def ff_backward_kernel(
+    shrink,
+    ge_ref,
+    mixed_ref,
+    cot_ref,
+    ac_ref,
+    gains_ref,
+    co_ref,
+    w_ref,
+    gate_ref,
+    up_ref,
+    gac_ref,
+    low_ref,
+    gcl_ref,
+    gcr_ref,
+    hid_ref,
+    act_ref,
+    gg_ref,
+    gu_ref,
+    norms_ref,
+    acc,
+):
+    step = pl.program_id(0)
+    t = lax.axis_index("tp")
+    last = pl.num_programs(0) - 1
+    rows = ac_ref.shape[0]
+    units = gate_ref.shape[1]
+    tile = min(rows, 256)
+
+    @pl.when(step == 0)
+    def _():
+        norms_ref[...] = jnp.zeros_like(norms_ref)
+
+    @pl.loop(0, rows // tile)
+    def _(n):
+        at = pl.ds(pl.multiple_of(n * tile, tile), tile)
+
+        @pl.when(step == 0)
+        def _():
+            grad_exit = ge_ref[at].astype(F32) * shrink
+            mixed = mixed_ref[at]
+            scale = rms_scale(mixed)
+            normed = mixed * scale
+            norms_ref[0:1] += jnp.sum(grad_exit * normed, axis=0, keepdims=True)
+            grad_mixed = cot_ref[at].astype(F32) + rms_back(
+                grad_exit * gains_ref[3:4], normed, scale
+            )
+            gac_ref[at] = grad_mixed
+            low_ref[at] = grad_mixed.astype(BF16)
+            value = ac_ref[at]
+            hid_ref[at] = (value * rms_scale(value) * gains_ref[2:3]).astype(BF16)
+            acc[at] = jnp.zeros_like(acc[at])
+
+        gate = gate_ref[at]
+        up = up_ref[at]
+        grad_act = mat(low_ref[at], w_ref[:, 2 * units :])
+        value, slope = gelu_parts(gate)
+        grad_gate = (grad_act * slope * up).astype(BF16)
+        grad_up = (grad_act * value).astype(BF16)
+        acc[at] += mat_nt(grad_gate, w_ref[:, :units]) + mat_nt(
+            grad_up, w_ref[:, units : 2 * units]
+        )
+
+        @pl.when(step == t)
+        def _():
+            act_ref[at] = (value * up).astype(BF16)
+            gg_ref[at] = grad_gate
+            gu_ref[at] = grad_up
+
+        @pl.when(step == last)
+        def _():
+            value = ac_ref[at]
+            scale = rms_scale(value)
+            normed = value * scale
+            grad = acc[at]
+            norms_ref[1:2] += jnp.sum(grad * normed, axis=0, keepdims=True)
+            total = gac_ref[at] + rms_back(grad * gains_ref[2:3], normed, scale)
+            gac_ref[at] = total
+            gcl_ref[at] = total.astype(BF16)
+            gcr_ref[at] = mat(total.astype(BF16), co_ref[...]).astype(BF16)
+
+
+def ff_backward(
+    grad_exit, mixed, cotangent, after_cross, gains, c_out_own, ff_all, gate, up, count, shrink
+):
+    rows, features = after_cross.shape
+    cols = ff_all.shape[1] // count
+    units = cols // 3
+    width = c_out_own.shape[1]
+
+    def fixed(*shape):
+        return pl.BlockSpec(shape, lambda i: (0,) * len(shape))
+
+    def low(*shape):
+        return jax.ShapeDtypeStruct(shape, BF16)
+
+    moving = pl.BlockSpec((rows, units), lambda i: (0, i))
+    return pl.pallas_call(
+        functools.partial(ff_backward_kernel, shrink),
+        grid=(count,),
+        in_specs=[fixed(rows, features)] * 4
+        + [
+            fixed(8, features),
+            fixed(features, width),
+            pl.BlockSpec((features, cols), lambda i: (0, i)),
+            moving,
+            moving,
+        ],
+        out_specs=[fixed(rows, features)] * 3
+        + [fixed(rows, width), fixed(rows, features)]
+        + [fixed(rows, units)] * 3
+        + [fixed(8, features)],
+        out_shape=[
+            jax.ShapeDtypeStruct((rows, features), F32),
+            low(rows, features),
+            low(rows, features),
+            low(rows, width),
+            low(rows, features),
+            low(rows, units),
+            low(rows, units),
+            low(rows, units),
+            jax.ShapeDtypeStruct((8, features), F32),
+        ],
+        scratch_shapes=[pltpu.VMEM((rows, features), F32)],
+        compiler_params=pltpu.CompilerParams(vmem_limit_bytes=VMEM_MOST),
+        cost_estimate=pl.CostEstimate(
+            flops=2 * rows * features * count * cols,
+            bytes_accessed=2 * features * count * cols + 8 * rows * count * units,
+            transcendentals=rows * count * units,
+        ),
+        name="ff_backward",
+    )(grad_exit, mixed, cotangent, after_cross, gains, c_out_own, ff_all, gate, up)
+
+
+def layer_forward_plain(parents, tokens, encoder, heads_in, op_in, ff_in, collective_id):
+    rows = tokens.shape[0] // MB
+    enc_rows = encoder.shape[0] // MB
+    width = op_in.shape[2]
+    heads_all = lax.all_gather(heads_in, PLANE, axis=0, tiled=True)
+    op_all = lax.all_gather(
+        lax.all_gather(op_in, "tp", axis=1, tiled=False), PLANE, axis=2, tiled=True
+    )
+    ff_all = lax.all_gather(
+        lax.all_gather(ff_in, "tp", axis=1, tiled=True), PLANE, axis=0, tiled=True
+    )
+    gains = heads_all[:, Q2 - 64 : Q2 - 56].astype(F32).T
+    tok = tokens.astype(F32)
+    hidden_one = (tok * rms_scale(tok) * gains[0:1]).astype(BF16)
+    queries = mat(hidden_one, heads_all[:, 4 * width : 5 * width]).astype(BF16)
+    kv = mat(hidden_one, heads_all[:, : 2 * width]).astype(BF16)
+    enc_kv = mat(encoder, heads_all[:, 2 * width : 4 * width]).astype(BF16)
+
+    def both_sides(value, i, count):
+        return ctx_gather(value[i * count : (i + 1) * count])
+
+    kv_self = jnp.stack([both_sides(kv, i, rows) for i in range(MB)])
+    kv_cross = jnp.stack([both_sides(enc_kv, i, enc_rows) for i in range(MB)])
+    bias = jnp.stack([mask_bias(parents[i], rows) for i in range(MB)])
+
+    def attention(values, keys_values, masks):
+        outcome = [
+            attend(
+                values[i * rows : (i + 1) * rows],
+                keys_values[i],
+                None if masks is None else masks[i],
+            )
+            for i in range(MB)
+        ]
+        return jnp.concatenate([o[0] for o in outcome]), jnp.stack([o[1] for o in outcome])
+
+    attended, totals_self = attention(queries, kv_self, bias)
+    after_self = line_project(attended, op_all[0], tok, 2)
+    hidden_two = (after_self * rms_scale(after_self) * gains[1:2]).astype(BF16)
+    cross_q = mat(hidden_two, heads_all[:, Q2 : Q2 + width]).astype(BF16)
+    crossed, totals_cross = attention(cross_q, kv_cross, None)
+    after_cross = line_project(crossed, op_all[1], after_self, 3)
+    return (
+        heads_all,
+        op_all,
+        ff_all,
+        gains,
+        bias,
+        queries,
+        kv_self,
+        kv_cross,
+        attended,
+        totals_self,
+        cross_q,
+        crossed,
+        totals_cross,
+        after_self,
+        after_cross,
+    )
+
+
 def local(
     tokens,
     encoder,
@@ -867,103 +1589,56 @@
     norm_exit,
 ):
     t = lax.axis_index("tp")
+    tp_count = lax.axis_size("tp")
     rows = tokens.shape[0] // MB
     features = tokens.shape[1]
     width = w_query.shape[1]
     hidden_units = w_gate.shape[1]
     vocab = embedding.shape[0]
-    tp_count = lax.axis_size("tp")
     trees = range(MB)
+    shrink = 1.0 / math.sqrt(features)
 
     def tree_rows(value, i):
         count = value.shape[0] // MB
         return value[i * count : (i + 1) * count]
 
-    gains_in = jnp.pad(
-        jnp.stack([norm_self, norm_cross, norm_ff, norm_exit], axis=1), ((0, 0), (0, 124))
-    )
-    w_heads = plane_gather(
-        jnp.concatenate([w_query, w_key, w_value, c_key, c_value, c_query, gains_in], axis=1), 1
-    )
-    w_qkv = w_heads[:, : 3 * width]
-    c_kv = w_heads[:, 3 * width : 5 * width]
-    c_q = w_heads[:, 5 * width : 6 * width]
-    gains = w_heads[:, 6 * width : 6 * width + 4].astype(F32).T
-    gain_self, gain_cross, gain_ff, gain_exit = (gains[j][None, :] for j in range(4))
-
-    pieces = tp_list(
-        jnp.concatenate([w_out.T, c_out.T, c_query, w_gate, w_up, w_down.T], axis=1)
-    )
-    pieces = after(pieces, w_heads)
-    pieces = lax.dynamic_slice_in_dim(jnp.stack(pieces[::-1] * 2), tp_count - 1 - t, tp_count, 0)
-    spans = [0, width, 2 * width, 3 * width]
-    spans += [spans[-1] + hidden_units * j for j in (1, 2, 3)]
-    packed = jnp.concatenate(
-        [
-            jnp.concatenate([pieces[k, :, spans[j] : spans[j + 1]] for k in range(tp_count)], axis=1)
-            for j in range(6)
-        ],
+    gains_in = jnp.stack([norm_self, norm_cross, norm_ff, norm_exit], axis=1)
+    heads_in = jnp.concatenate(
+        [w_key, w_value, c_key, c_value, w_query]
+        + [jnp.pad(gains_in, ((0, 0), (0, 60))), c_query, jnp.zeros_like(c_query[:, :64])],
         axis=1,
     )
-    whole = lax.all_gather(packed, PLANE, axis=0, tiled=True)
-    cuts = [tp_count * s for s in spans]
-    gate_all, up_all, down_t = (whole[:, cuts[j] : cuts[j + 1]] for j in range(3, 6))
-
-    def own_units(value):
-        return lax.dynamic_slice_in_dim(value, t * hidden_units, hidden_units, 1)
-
-    def own_heads(value):
-        return lax.dynamic_index_in_dim(value, t, 0, False)
-
-    def stacked(j):
-        return jnp.stack(
-            [whole[:, cuts[j] + k * width : cuts[j] + (k + 1) * width] for k in range(tp_count)]
-        )
-
-    w_out_4, c_out_4, c_query_4 = stacked(0), stacked(1), stacked(2)
+    op_in = jnp.stack([w_out.T, c_out.T, c_query])
+    ff_in = jnp.concatenate([w_gate, w_up, w_down.T], axis=1)
     padded = -(-vocab // TILE) * TILE
-    embed_t = lax.all_gather(
-        jnp.pad(after(embedding, packed).T, ((0, 0), (0, padded - vocab))),
-        PLANE,
-        axis=0,
-        tiled=True,
+    embed_in = jnp.pad(embedding.T, ((0, 0), (0, padded - vocab)))
+    embed_t = lax.all_gather(embed_in, PLANE, axis=0, tiled=True)
+    forward = layer_forward if small_plane() else layer_forward_plain
+    (
+        heads_all,
+        op_all,
+        ff_all,
+        gains,
+        bias,
+        queries,
+        kv_self,
+        kv_cross,
+        attended,
+        totals_self,
+        cross_q,
+        crossed,
+        totals_cross,
+        after_self,
+        after_cross,
+    ) = forward(parents, after(tokens, embed_in), encoder, heads_in, op_in, ff_in, 1)
+    gain_self, gain_cross = gains[0:1], gains[1:2]
+    w_kv, w_q = heads_all[:, : 2 * width], heads_all[:, 4 * width : 5 * width]
+    c_kv = heads_all[:, 2 * width : 4 * width]
+    own_out = lax.dynamic_index_in_dim(op_all[:2], t, 1, False)
+    w_out_own, c_out_own = own_out[0], own_out[1]
+    gate_pre, up_pre, mixed, mixed_low, exit_in, exit_in_t = ff_forward(
+        after_cross, gains, ff_all, tp_count, shrink
     )
-
-    tok = tokens.astype(F32)
-    scale_one = rms_scale(tok)
-    normed_one = tok * scale_one
-    hidden_one = (normed_one * gain_self).astype(BF16)
-    qkv = mat(hidden_one, w_qkv).astype(BF16)
-    enc_kv = mat(encoder, c_kv).astype(BF16)
-    queries = [tree_rows(qkv, i)[:, :width] for i in trees]
-    kv_self = [ctx_gather(tree_rows(qkv, i)[:, width:]) for i in trees]
-    kv_cross = [ctx_pair(tree_rows(enc_kv, i)) for i in trees]
-    biases = [mask_bias(parents[i], rows) for i in trees]
-    shrink = 1.0 / math.sqrt(features)
-
-    outcome = [attend(queries[i], kv_self[i], biases[i]) for i in trees]
-    attended = jnp.concatenate([o[0] for o in outcome], axis=0)
-    totals_self = [o[1] for o in outcome]
-    after_self = line_project(attended, w_out_4, tok, 2)
-    scale_two = rms_scale(after_self)
-    normed_two = after_self * scale_two
-    hidden_two = (normed_two * gain_cross).astype(BF16)
-    cross_q = mat(hidden_two, c_q).astype(BF16)
-    kv_cross = [ctx_join(after(kv_cross[i], after_self)) for i in trees]
-    outcome = [attend(tree_rows(cross_q, i), kv_cross[i], None) for i in trees]
-    crossed = jnp.concatenate([o[0] for o in outcome], axis=0)
-    totals_cross = [o[1] for o in outcome]
-    after_cross = line_project(crossed, c_out_4, after_self, 3)
-    scale_three = rms_scale(after_cross)
-    normed_three = after_cross * scale_three
-    hidden_three = (normed_three * gain_ff).astype(BF16)
-    gate_pre = mat(hidden_three, gate_all)
-    up_pre = mat(hidden_three, up_all)
-    activated = (gelu_parts(gate_pre)[0] * up_pre).astype(BF16)
-    mixed = after_cross + mat_nt(activated, down_t)
-    scale_four = rms_scale(mixed)
-    normed_four = mixed * scale_four
-    exit_in = (normed_four * gain_exit * shrink).astype(BF16)
 
     targets_local = targets - t * vocab
     inside = (targets_local >= 0) & (targets_local < vocab)
@@ -974,33 +1649,36 @@
     losses = (log_total - picked).reshape(-1)
     scores = (top - log_total).reshape(-1)
     grad_embed, grad_exit_part = exit_backward(
-        logits, embed_t, exit_in.T, targets_local, log_total.reshape(-1, 1), vocab
+        logits, embed_t, exit_in_t, targets_local, log_total.reshape(-1, 1), vocab
     )
     grad_embed_own = lax.optimization_barrier(
         lax.psum_scatter(grad_embed, PLANE, scatter_dimension=0, tiled=True)
     )
-    grad_exit = line_sum(grad_exit_part, 5).astype(F32) * shrink
-
-    def norm_grad(grad, normed):
-        return jnp.sum(grad * normed, axis=0)
-
-    norm_exit_grad = norm_grad(grad_exit, normed_four)
-    grad_mixed = cotangent.astype(F32) + rms_back(grad_exit * gain_exit, normed_four, scale_four)
-    grad_mixed_low = grad_mixed.astype(BF16)
-    grad_down = mat_tn(grad_mixed_low, own_units(activated))
-    grad_act = mat(grad_mixed_low, down_t)
-    value, slope = gelu_parts(gate_pre)
-    grad_gate = (grad_act * slope * up_pre).astype(BF16)
-    grad_up = (grad_act * value).astype(BF16)
-    grad_gate_w = mat_tn(hidden_three, own_units(grad_gate))
-    grad_up_w = mat_tn(hidden_three, own_units(grad_up))
-    grad_three = mat_nt(grad_gate, gate_all) + mat_nt(grad_up, up_all)
-    norm_ff_grad = norm_grad(grad_three, normed_three)
-    grad_after_cross = grad_mixed + rms_back(grad_three * gain_ff, normed_three, scale_three)
-    grad_cross_low = grad_after_cross.astype(BF16)
-    grad_c_out = mat_tn(grad_cross_low, crossed)
-    ff_grads = jnp.concatenate([grad_c_out, grad_gate_w, grad_up_w, grad_down], axis=1).astype(BF16)
-    grad_crossed = mat(grad_cross_low, own_heads(c_out_4)).astype(BF16)
+    grad_exit = line_sum(grad_exit_part, 5)
+
+    (
+        grad_after_cross,
+        grad_mixed_low,
+        grad_cross_low,
+        grad_crossed,
+        hidden_three,
+        activated_own,
+        grad_gate_own,
+        grad_up_own,
+        norms,
+    ) = ff_backward(
+        grad_exit,
+        mixed,
+        cotangent,
+        after_cross,
+        gains,
+        c_out_own,
+        ff_all,
+        gate_pre,
+        up_pre,
+        tp_count,
+        shrink,
+    )
     outcome = [
         attend_back(
             tree_rows(cross_q, i), kv_cross[i], None, totals_cross[i], tree_rows(grad_crossed, i)
@@ -1009,43 +1687,59 @@
     ]
     grad_cq = jnp.concatenate([o[0] for o in outcome], axis=0)
     grad_kv_cross = jnp.concatenate([ctx_scatter(o[1]) for o in outcome], axis=0)
-    grad_c_kv = mat_tn(encoder, grad_kv_cross)
-    grad_c_query = mat_tn(hidden_two, grad_cq)
     encoder_part = mat_nt(grad_kv_cross, c_kv).astype(BF16)
-    grad_two = line_project(grad_cq, c_query_4, jnp.zeros_like(tok), 6)
-    ff_own = lax.psum_scatter(after(ff_grads, grad_two), PLANE, scatter_dimension=0, tiled=True)
-    norm_cross_grad = norm_grad(grad_two, normed_two)
+    grad_two = line_project(grad_cq, op_all[2], jnp.zeros_like(after_self), 6)
+    scale_two = rms_scale(after_self)
+    normed_two = after_self * scale_two
+    hidden_two = (normed_two * gain_cross).astype(BF16)
+    norm_cross_grad = jnp.sum(grad_two * normed_two, axis=0)
     grad_after_self = grad_after_cross + rms_back(grad_two * gain_cross, normed_two, scale_two)
     grad_self_low = grad_after_self.astype(BF16)
-    grad_w_out = mat_tn(grad_self_low, attended)
-    grad_attended = mat(grad_self_low, own_heads(w_out_4)).astype(BF16)
+    grad_attended = mat(grad_self_low, w_out_own).astype(BF16)
     outcome = [
         attend_back(
-            queries[i], kv_self[i], biases[i], totals_self[i], tree_rows(grad_attended, i)
+            tree_rows(queries, i), kv_self[i], bias[i], totals_self[i], tree_rows(grad_attended, i)
         )
         for i in trees
     ]
-    grad_qkv = jnp.concatenate(
+    grad_q = jnp.concatenate([o[0] for o in outcome], axis=0)
+    grad_kv_self = jnp.concatenate([ctx_scatter(o[1]) for o in outcome], axis=0)
+    one_part = (mat_nt(grad_q, w_q) + mat_nt(grad_kv_self, w_kv)).astype(BF16)
+    both = line_sum(jnp.concatenate([one_part, encoder_part], axis=0), 7, 12)
+    grad_one = both[: MB * rows].astype(F32)
+    grad_encoder = both[MB * rows :].astype(F32)
+    tok = tokens.astype(F32)
+    scale_one = rms_scale(tok)
+    normed_one = tok * scale_one
+    hidden_one = (normed_one * gain_self).astype(BF16)
+    norm_self_grad = jnp.sum(grad_one * normed_one, axis=0)
+    grad_tokens = grad_after_self + rms_back(grad_one * gain_self, normed_one, scale_one)
+
+    ff_grads = jnp.concatenate(
         [
-            jnp.concatenate([o[0] for o in outcome], axis=0),
-            jnp.concatenate([ctx_scatter(o[1]) for o in outcome], axis=0),
+            mat_tn(hidden_three, grad_gate_own),
+            mat_tn(hidden_three, grad_up_own),
+            mat_tn(grad_mixed_low, activated_own),
+            mat_tn(grad_cross_low, crossed),
         ],
         axis=1,
-    )
-    both = jnp.concatenate([mat_nt(grad_qkv, w_qkv).astype(BF16), encoder_part], axis=0)
-    both = line_sum(both, 7, 12)
-    grad_encoder = both[MB * rows :].astype(F32)
-    grad_w_qkv = mat_tn(hidden_one, grad_qkv)
-    grad_one = both[: MB * rows].astype(F32)
-    norm_self_grad = norm_grad(grad_one, normed_one)
-    grad_tokens = grad_after_self + rms_back(grad_one * gain_self, normed_one, scale_one)
+    ).astype(BF16)
+    ff_own = lax.psum_scatter(after(ff_grads, grad_two), PLANE, scatter_dimension=0, tiled=True)
     norm_block = jnp.pad(
-        jnp.stack([norm_self_grad, norm_cross_grad, norm_ff_grad, norm_exit_grad], axis=1),
+        jnp.stack([norm_self_grad, norm_cross_grad, norms[1], norms[0]], axis=1),
         ((0, 0), (0, 60)),
     )
     own = plane_scatter(
         jnp.concatenate(
-            [grad_w_qkv, grad_c_kv, grad_c_query, grad_w_out, norm_block], axis=1
+            [
+                mat_tn(hidden_one, grad_kv_self),
+                mat_tn(encoder, grad_kv_cross),
+                mat_tn(hidden_one, grad_q),
+                norm_block,
+                mat_tn(hidden_two, grad_cq),
+                mat_tn(grad_self_low, attended),
+            ],
+            axis=1,
         ).astype(BF16),
         9,
     )
@@ -1053,24 +1747,24 @@
     def part(value, start, size):
         return value[:, start : start + size].astype(F32)
 
-    base = 7 * width
+    base = Q2 - 64
     return (
-        mixed.astype(BF16),
+        mixed_low,
         losses,
         scores,
         grad_tokens,
         grad_encoder,
+        part(own, 4 * width, width),
         part(own, 0, width),
         part(own, width, width),
+        part(own, Q2 + width, width).T,
+        part(own, Q2, width),
         part(own, 2 * width, width),
-        part(own, 6 * width, width).T,
-        part(own, 5 * width, width),
         part(own, 3 * width, width),
-        part(own, 4 * width, width),
-        part(ff_own, 0, width).T,
-        part(ff_own, width, hidden_units),
-        part(ff_own, width + hidden_units, hidden_units),
-        part(ff_own, width + 2 * hidden_units, hidden_units).T,
+        part(ff_own, 3 * hidden_units, width).T,
+        part(ff_own, 0, hidden_units),
+        part(ff_own, hidden_units, hidden_units),
+        part(ff_own, 2 * hidden_units, hidden_units).T,
         grad_embed_own[:, :vocab].astype(F32).T,
         own[:, base],
         own[:, base + 1],

time: 866 us -> 759 us (0.88)
  Pallas kernels: 469 us -> 599 us
  waiting for transfers between devices: 102 us -> 18.5 us
  matrix products: 89.2 us -> 19.4 us
  local copies, waits for them, and re-layouts: 106 us -> 61.5 us
  other arithmetic: 58.9 us -> 38.2 us
  starting transfers between devices: 15.1 us -> 4.44 us
    pallas_call x5 -> x3, Pallas kernels: 40.9 us -> 262 us  [the longest x1 204 us: layer_forward(): pl.pallas_call(functools.partial(layer_forward_kernel, count), in_specs=[...]
    pallas_call x3 -> x1, Pallas kernels: 118 us -> 31.5 us  [line_project(): pl.pallas_call(functools.partial(line_project_kernel, count, chunks), in_...]
    all_gather x2 -> x1, waiting for transfers between devices: 63.1 us -> 0.02 us  [local(): embed_t = lax.all_gather(embed_in, PLANE, axis=0, tiled=True)]
    dot_general x8 -> x1, matrix products: 41.1 us -> 1.97 us  [mat(): return jnp.dot(left, right, preferred_element_type=F32)]
    unnamed x207 -> x154, local copies, waits for them, and re-layouts: 53.7 us -> 27 us
    dot_general x7 -> x3, matrix products: 28.9 us -> 4.73 us  [mat_nt(): lax.dot_general(left, right, (((1,), (1,)), ((), ())), preferred_element_...]
    ppermute x8 -> x4, waiting for transfers between devices: 31.1 us -> 18 us  [swap(): return lax.ppermute(value, axis, [(i, i ^ bit) for i in range(count)])]
    concatenate x8 -> x3, local copies, waits for them, and re-layouts: 14.3 us -> 4.96 us  [the longest x1 4.11 us: local(): jnp.concatenate([mat_tn(hidden_one, grad_kv_self), mat_tn(encoder, grad_k...]
  transfers between devices with their start and end apart: 15 -> 7, of which waited for: 6 -> 2; matrix products, arithmetic and copies ran while one was open for 17% -> 10% of each run, Pallas kernels for 35% -> 52%
where the time goes in v3:
time: 759 us; the launch traced here: 756 us
  Pallas kernels  599 us (79%)
  local copies, waits for them, and re-layouts  61.5 us (8%)
  other arithmetic  38.2 us (5%)
  matrix products  19.4 us (3%)
  waiting for transfers between devices  18.5 us (2%)
  between operations  15.1 us (2%)
    pallas_call x1, Pallas kernels, layer_forward(): pl.pallas_call(functools.partial(layer_forward_kernel, count), in_specs=[...  204 us
    pallas_call x2, Pallas kernels, line_sum(): pl.pallas_call(functools.partial(line_sum_kernel, count, chunks, window,...  184 us
    pallas_call x1, Pallas kernels, exit_backward(): pl.pallas_call(functools.partial(exit_backward_kernel, valid), grid=(padd...  35 us
    pallas_call x1, Pallas kernels, ff_backward(): pl.pallas_call(functools.partial(ff_backward_kernel, shrink), grid=(count...  34.3 us
    pallas_call x4, Pallas kernels, attend_back(): pl.pallas_call(body, grid=(rows // tile,), in_specs=specs, out_specs=[pl....  33.5 us
    pallas_call x1, Pallas kernels, line_project(): pl.pallas_call(functools.partial(line_project_kernel, count, chunks), in_...  31.5 us
    unnamed x154, local copies, waits for them, and re-layouts  27 us
    pallas_call x1, Pallas kernels, exit_forward(): pl.pallas_call(functools.partial(exit_forward_kernel, valid), grid=(padde...  24.4 us
  transfers between devices with their start and end apart: 7, of which 2 were waited for; matrix products, arithmetic and copies ran while one was open for 10% of the time, Pallas kernels for 52%

profile of v3, /device:TPU:0, one launch (start us, length us, event | category | flops | bytes accessed | tf_op | source)
XLA Modules:
  0.0 755.9 jit_solution(4764499125954347662)
XLA Ops:
  7.4 2.9 pad.13
  14.1 203.9 %layer_forward.1 = (bf16[768,1280]{1,0:T(8,128)(2,1)}, bf16[3,4,768,192]{3,2,1,0:T(8,128)(2,1)}, bf16[768,6144]{1,0:T(8,128)(2,1)}, f32[8,768]{1,0:T(8,128)}, f3...) custom-call(s32[2,8]{1,0:T(2,128)} %parents_ref.1, ...), custom_call_target="tpu_custom_call" | custom-call | tf_op jit(solution)/shard_map/layer_forward/pallas_call | solution.py:1256
  218.1 2.1 slice.169
  221.0 3.5 fusion.30
  224.6 2.6 slice_bitcast_fusion.2.w_ref
  227.5 23.8 %ff_forward.1 = (f32[1024,2048]{1,0:T(8,128)}, f32[1024,2048]{1,0:T(8,128)}, f32[1024,768]{1,0:T(8,128)}, bf16[1024,768]{1,0:T(8,128)(2,1)}, bf16[1024,768]{1,0:T(8,128)(2,1)}, /*index=5*/bf16[768,1024]{1,0:T(8,128)(2,1)}) custom-call(f32[1024,768]{1,0:T(8,128)} %get-tuple-element.71.ac_ref, f32[8,768]{1,0:T(8,128)} %get-tuple-element.72.gains_ref, ...), custom_call_target="tpu_custom_call" | custom-call | flops 9663676416 | bytes 26214400 | tf_op jit(solution)/shard_map/ff_forward/pallas_call | solution.py:1345
  252.4 1.4 copy-done.21
  253.8 24.4 %exit_forward.1 = (f32[1024,8192]{1,0:T(8,128)}, f32[1024,1]{1,0:T(8,128)S(1)}, f32[1024,1]{1,0:T(8,128)S(1)}, f32[1024,1]{1,0:T(8,128)S(1)}) custom-call(bf16[1024,768]{1,0:T(8,128)(2,1)S(1)} %copy-done.21, bf16[768,8192]{1,0:T(8,128)(2,1)} %all-gather.2.cloned.1.call-done.e_ref, s32[1024,1]{1,0:T(8,128)S(1)} %copy-done.14), custom_call_target="tpu_custom_call" | custom-call | flops 12884901888 | bytes 46137344 | tf_op jit(solution)/shard_map/exit_forward/pallas_call | solution.py:606
  285.0 6.9 share_stats.1
  291.9 1.7 copy.81.log_ref
  295.7 1.4 copy-done.20
  297.1 35.0 %exit_backward.1 = (bf16[768,8192]{1,0:T(8,128)(2,1)}, bf16[1024,768]{1,0:T(8,128)(2,1)S(1)}) custom-call(f32[1024,8192]{1,0:T(8,128)} %get-tuple-element.82.logits_ref, bf16[768,8192]{1,0:T(8,128)(2,1)} %all-gather.2.cloned.1.call-done.e_ref, bf16[768,1024]{1,0:T(8,128)(2,1)S(1)} %copy-done.20, s32[1024,1]{1,0:T(8,128)S(1)} %copy-done.15, ...), custom_call_target="tpu_custom_call" | custom-call | flops 25769803776 | bytes 58720256 | tf_op jit(solution)/shard_map/exit_backward/pallas_call | solution.py:654
  332.1 51.9 %line_sum.2.ge_ref = bf16[1024,768]{1,0:T(8,128)(2,1)S(1)} custom-call(bf16[1024,768]{1,0:T(8,128)(2,1)S(1)} %get-tuple-element.84.x_ref), custom_call_target="tpu_custom_call" | custom-call | tf_op jit(solution)/shard_map/line_sum/pallas_call | solution.py:465
  385.1 34.3 %ff_backward.1 = (f32[1024,768]{1,0:T(8,128)}, bf16[1024,768]{1,0:T(8,128)(2,1)}, bf16[1024,768]{1,0:T(8,128)(2,1)}, bf16[1024,192]{1,0:T(8,128)(2,1)}, bf16[102...) custom-call(bf16[1024,768]{1,0:T(8,128)(2,1)} %copy-done.1, ...), custom_call_target="tpu_custom_call" | custom-call | flops 9663676416 | bytes 26214400 | tf_op jit(solution)/shard_map/ff_backward/pallas_call | solution.py:1470
  420.5 10.6 %attend_back.2 = (bf16[512,192]{1,0:T(8,128)(2,1)S(1)}, bf16[2048,384]{1,0:T(8,128)(2,1)S(1)}) custom-call(bf16[512,192]{1,0:T(8,128)(2,1)S(1)} %copy-done.19, bf16[2048,384]{1,0:T(8,128)(2,1)S(1)} %get-tuple-element.195.k, f32[3,512]{1,0:T(4,128)S(1)} %get-tuple-element.224.rest_0_, bf16[512,192]{1,0:T(8,128)(2,1)S(1)} %get-tuple-element.210.rest_1_), custom_call_target="tpu_custom_call" | custom-call | flops 8053063680 | bytes 4128768 | tf_op jit(solution)/shard_map/attend_back/pallas_call | solution.py:786
  434.0 10.8 %attend_back.3 = (bf16[512,192]{1,0:T(8,128)(2,1)S(1)}, bf16[2048,384]{1,0:T(8,128)(2,1)S(1)}) custom-call(bf16[512,192]{1,0:T(8,128)(2,1)S(1)} %copy-done.18, bf16[2048,384]{1,0:T(8,128)(2,1)S(1)} %get-tuple-element.194.k, f32[3,512]{1,0:T(4,128)S(1)} %get-tuple-element.225.rest_0_, bf16[512,192]{1,0:T(8,128)(2,1)S(1)} %get-tuple-element.209.rest_1_), custom_call_target="tpu_custom_call" | custom-call | flops 8053063680 | bytes 4128768 | tf_op jit(solution)/shard_map/attend_back/pallas_call | solution.py:786
  445.5 1.6 copy-done.61
  448.4 1.9 broadcast_in_dim.20.base_ref
  450.4 31.5 %line_project.1 = f32[1024,768]{1,0:T(8,128)S(1)} custom-call(bf16[1024,192]{1,0:T(8,128)(2,1)S(1)} %constant_dynamic-update-slice_fusion.x_ref, bf16[4,768,192]{2,1,0:T(8,128)(2,1)S(1)} %copy-done.2, f32[1024,768]{1,0:T(8,128)} %broadcast_in_dim.20.base_ref), custom_call_target="tpu_custom_call" | custom-call | tf_op jit(solution)/shard_map/line_project/pallas_call | solution.py:279
  481.9 1.7 pad_maximum_fusion.1
  483.5 4.5 copy.93
  489.7 1.8 fusion.8
  491.5 2.5 multiply_reduce_fusion.2
  498.7 1.8 collective-permute-start.2
  500.5 1.3 multiply_reduce_fusion
  503.1 2.0 convolution_convert_fusion.6
  505.1 5.9 attend_back_masked.3
  512.2 6.3 attend_back_masked.2
  518.5 1.7 collective-permute-start
  523.9 2.6 fusion.14
  527.5 2.4 convolution_convert_fusion.8
  530.8 1.9 fusion.21
  533.4 14.9 %collective-permute-done.1 = bf16[512,384]{1,0:T(8,128)(2,1)} collective-permute-done((bf16[512,384]{1,0:T(8,128)(2,1)}, bf16[512,384]{1,0:T(8,128)(2,1)}, u32[]{:S(2)}, u32[]{:S(2)}) %collective-permute-start.1) | collective-permute-done | bytes 393248 | tf_op jit(solution)/shard_map/ppermute | solution.py:45
  549.4 3.1 collective-permute-done
  553.6 2.0 convolution_convert_fusion.5
  557.4 1.5 add_convert_fusion.1
  559.0 1.4 add_convert_fusion.2
  560.4 1.8 convolution_convert_fusion
  562.2 2.8 pad_maximum_fusion.x_ref
  565.0 132.4 %line_sum.3 = bf16[3072,768]{1,0:T(8,128)(2,1)S(1)} custom-call(bf16[3072,768]{1,0:T(8,128)(2,1)} %pad_maximum_fusion.x_ref), custom_call_target="tpu_custom_call" | custom-call | tf_op jit(solution)/shard_map/line_sum/pallas_call | solution.py:465
  697.4 2.2 copy-done
  699.6 1.4 fusion.13
  701.4 2.6 fusion.9
  704.3 4.1 concatenate.56.x_ref
  708.4 21.1 %plane_scatter.1 = f32[96,1408]{1,0:T(8,128)S(1)} custom-call(bf16[8,96,1408]{2,1,0:T(8,128)(2,1)S(1)} %concatenate.56.x_ref), custom_call_target="tpu_custom_call" | custom-call | tf_op jit(solution)/shard_map/plane_scatter/pallas_call | solution.py:180
  731.8 5.5 fusion.5
  737.3 3.2 slice_convert_fusion
  745.9 3.2 convert_bitcast_fusion
  (220 shorter events, 49.1 us)
Async XLA Ops:
  7.2 3.1 copy-start.57
  7.2 3.1 copy-start.58
  7.2 3.1 copy-start.59
  7.2 3.1 copy-start.60
  7.2 3.3 copy-start.45
  7.2 3.4 copy-start.46
  7.3 3.5 copy-start.56
  7.3 4.5 copy-start.40
  7.3 4.5 copy-start.41
  7.3 4.5 copy-start.42
  7.3 4.5 copy-start.43
  7.3 4.5 copy-start.44
  7.3 4.5 copy-start.36
  7.3 244.0 %all-gather.2.cloned.1.call-start = ((), (), s32[]{:S(2)}) async-start(), calls=%async_computation.2 | async-start | bytes 14155776 | tf_op jit(solution)/shard_map/all_gather | solution.py:1615
  7.4 6.0 copy-start.37
  7.4 6.0 copy-start.38
  7.4 6.0 copy-start.39
  10.3 730.2 %reduce-scatter.7.cloned.1.call-start = ((), (), s32[]{:S(2)}) async-start(), calls=%async_computation.4 | async-start | bytes 3096576
  218.1 3.0 copy-start.50
  218.1 2.9 copy-start.51
  220.2 7.0 copy-start.26
  220.2 7.0 copy-start.29
  385.1 35.4 %copy-start.19 = (bf16[512,192]{1,0:T(8,128)(2,1)S(1)}, bf16[512,192]{1,0:T(8,128)(2,1)}, u32[]{:S(2)}) copy-start(bf16[512,192]{1,0:T(8,128)(2,1)} %get-tuple-element.226.q) | copy-start | bytes 589828
  420.5 10.7 %copy-start.63 = (bf16[1024,768]{1,0:T(8,128)(2,1)S(1)}, bf16[1024,768]{1,0:T(8,128)(2,1)}, u32[]{:S(2)}) copy-start(bf16[1024,768]{1,0:T(8,128)(2,1)} %get-tuple-element.110) | copy-start | bytes 4718596
  420.5 10.7 %copy-start.66 = (bf16[1024,512]{1,0:T(8,128)(2,1)S(1)}, bf16[1024,512]{1,0:T(8,128)(2,1)}, u32[]{:S(2)}) copy-start(bf16[1024,512]{1,0:T(8,128)(2,1)} %get-tuple-element.112) | copy-start | bytes 3145732
  434.0 10.9 %copy-start.62 = (bf16[1024,768]{1,0:T(8,128)(2,1)S(1)}, bf16[1024,768]{1,0:T(8,128)(2,1)}, u32[]{:S(2)}) copy-start(bf16[1024,768]{1,0:T(8,128)(2,1)} %get-tuple-element.115) | copy-start | bytes 4718596
  434.0 10.9 %copy-start.67 = (bf16[1024,192]{1,0:T(8,128)(2,1)S(1)}, bf16[1024,192]{1,0:T(8,128)(2,1)}, u32[]{:S(2)}) copy-start(bf16[1024,192]{1,0:T(8,128)(2,1)} %get-tuple-element.116) | copy-start | bytes 1179652
  444.8 3.5 copy-start.8
  444.9 5.3 copy-start.3
  488.0 257.9 %reduce-scatter.5.cloned.1.call-start = ((), (), s32[]{:S(2)}) async-start(), calls=%async_computation.3 | async-start | bytes 14155776 | tf_op jit(solution)/shard_map/reduce_scatter | solution.py:1655
  488.8 5.3 copy-start.31
  491.5 3.5 copy-start.27
  495.4 5.1 copy-start.22
  497.5 59.2 %collective-permute-start.3 = (bf16[1024,384]{1,0:T(8,128)(2,1)}, bf16[1024,384]{1,0:T(8,128)(2,1)}, u32[]{:S(2)}, u32[]{:S(2)}) collective-permute-start(bf16[1024,384]{1,0:T(8,128)(2,1)} %slice.201), channel_id=1, source_target_pairs={{0,4},{4,0},{1,5},{5,1},{2,6},{6,2},{3,7},{7,3},{8,12},{12,8},{9,1... | collective-permute-start | bytes 2359304 | tf_op jit(solution)/shard_map/ppermute | solution.py:45
  498.7 60.3 %collective-permute-start.2 = (bf16[1024,384]{1,0:T(8,128)(2,1)}, bf16[1024,384]{1,0:T(8,128)(2,1)}, u32[]{:S(2)}, u32[]{:S(2)}) collective-permute-start(bf16[1024,384]{1,0:T(8,128)(2,1)} %slice.199), channel_id=1, source_target_pairs={{0,4},{4,0},{1,5},{5,1},{2,6},{6,2},{3,7},{7,3},{8,12},{12,8},{9,1... | collective-permute-start | bytes 2359304 | tf_op jit(solution)/shard_map/ppermute | solution.py:45
  511.8 36.4 %collective-permute-start.1 = (bf16[512,384]{1,0:T(8,128)(2,1)}, bf16[512,384]{1,0:T(8,128)(2,1)}, u32[]{:S(2)}, u32[]{:S(2)}) collective-permute-start(bf16[512,384]{1,0:T(8,128)(2,1)} %slice.196), channel_id=1, source_target_pairs={{0,4},{4,0},{1,5},{5,1},{2,6},{6,2},{3,7},{7,3},{8,12},{12,8},{9,1... | collective-permute-start | bytes 1179656 | tf_op jit(solution)/shard_map/ppermute | solution.py:45
  512.2 8.9 %copy-start.24 = (bf16[1024,768]{1,0:T(8,128)(2,1)S(1)}, bf16[1024,768]{1,0:T(8,128)(2,1)}, u32[]{:S(2)}) copy-start(bf16[1024,768]{1,0:T(8,128)(2,1)} %tok_ref) | copy-start | bytes 4718596
  518.4 4.3 copy-start.48
  518.4 4.9 copy-start.53
  518.4 5.5 copy-start.4
  518.5 34.0 %collective-permute-start = (bf16[512,384]{1,0:T(8,128)(2,1)S(1)}, bf16[512,384]{1,0:T(8,128)(2,1)}, u32[]{:S(2)}, u32[]{:S(2)}) collective-permute-start(bf16[512,384]{1,0:T(8,128)(2,1)S(1)} %slice.194), channel_id=1, source_target_pairs={{0,4},{4,0},{1,5},{5,1},{2,6},{6,2},{3,7},{7,3},{8,12},{12,8},{9,1... | collective-permute-start | bytes 1179656 | tf_op jit(solution)/shard_map/ppermute | solution.py:45
  521.8 5.6 copy-start.34
  530.8 22.8 %copy-start.25 = (bf16[1024,768]{1,0:T(8,128)(2,1)S(1)}, bf16[1024,768]{1,0:T(8,128)(2,1)}, u32[]{:S(2)}) copy-start(bf16[1024,768]{1,0:T(8,128)(2,1)} %tok_ref) | copy-start | bytes 4718596
  555.6 3.3 copy-start.7
  565.0 134.6 %copy-start.28 = (bf16[2048,768]{1,0:T(8,128)(2,1)S(1)}, bf16[2048,768]{1,0:T(8,128)(2,1)}, u32[]{:S(2)}) copy-start(bf16[2048,768]{1,0:T(8,128)(2,1)} %enc_ref.1) | copy-start | bytes 9437188
  701.1 3.2 copy-start.32
  730.3 7.0 slice-start
  731.8 5.5 slice-start.1
  (29 other events, 50.4 us)
Sparse Core Ops, SparseCore 0:
  10.4 123.6 all-gather.1
  488.2 54.6 reduce-scatter.6
  546.8 92.1 reduce-scatter.4

commit v4 on v3

--- a/solution.py
+++ b/solution.py
@@ -992,12 +992,12 @@
             for k in range(block_count):
                 at = (slice(k * BLK, (k + 1) * BLK), slice(q * BLK, (q + 1) * BLK))
                 if k == q:
-                    bias_ref[(i,) + at] = causal
+                    bias_ref[(i,) + at] = causal.astype(BF16)
                     continue
                 block = c * mine + k if k < mine else (1 - c) * mine + k - mine
                 seen = lax.shift_right_logical(line, block) & 1
                 value = jnp.where(seen == 1, 0.0, MASKED)
-                bias_ref[(i,) + at] = jnp.full((BLK, BLK), value, F32)
+                bias_ref[(i,) + at] = jnp.full((BLK, BLK), value, F32).astype(BF16)
 
 
 def layer_forward_kernel(
@@ -1262,7 +1262,7 @@
             low(3, count, features, width),
             low(features, count * ff_cols),
             full(8, features),
-            full(MB, 2 * rows, rows),
+            low(MB, 2 * rows, rows),
             low(tok_rows, width),
             low(MB, 2 * rows, 2 * width),
             low(MB, enc_rows, 2 * width),
@@ -1527,7 +1527,7 @@
 
     kv_self = jnp.stack([both_sides(kv, i, rows) for i in range(MB)])
     kv_cross = jnp.stack([both_sides(enc_kv, i, enc_rows) for i in range(MB)])
-    bias = jnp.stack([mask_bias(parents[i], rows) for i in range(MB)])
+    bias = jnp.stack([mask_bias(parents[i], rows) for i in range(MB)]).astype(BF16)
 
     def attention(values, keys_values, masks):
         outcome = [
@@ -1562,6 +1562,533 @@
         totals_cross,
         after_self,
         after_cross,
+    )
+
+
+class LineSum:
+    def __init__(self, t, count, left, right, x, out, buffers, sems, chunks):
+        self.t, self.count, self.left, self.right = t, count, left, right
+        self.x, self.out, self.chunks = x, out, chunks
+        self.low_in, self.high_in = buffers.at[0], buffers.at[1]
+        self.sems = sems
+        self.half = x.shape[0] // 2
+        self.rows = self.half // chunks
+
+    def low(self, j):
+        return pl.ds(j * self.rows, self.rows)
+
+    def high(self, j):
+        return pl.ds(self.half + j * self.rows, self.rows)
+
+    def down(self, j, own):
+        src = self.x.at[self.low(j)] if own else self.low_in.at[self.low(j)]
+        dst = self.low_in.at[self.low(j)]
+        return remote(src, dst, self.sems.at[0, j], self.sems.at[1, j], self.left)
+
+    def up(self, j, own):
+        src = self.x.at[self.high(j)] if own else self.high_in.at[self.low(j)]
+        dst = self.high_in.at[self.low(j)]
+        return remote(src, dst, self.sems.at[2, j], self.sems.at[3, j], self.right)
+
+    def low_back(self, j):
+        ref = self.out.at[self.low(j)]
+        return remote(ref, ref, self.sems.at[4, j], self.sems.at[5, j], self.right)
+
+    def high_back(self, j):
+        ref = self.out.at[self.high(j)]
+        return remote(ref, ref, self.sems.at[6, j], self.sems.at[7, j], self.left)
+
+    def start(self):
+        @pl.when(self.t == self.count - 1)
+        def _():
+            for j in range(self.chunks):
+                self.down(j, True).start()
+
+        @pl.when(self.t == 0)
+        def _():
+            for j in range(self.chunks):
+                self.up(j, True).start()
+
+    def low_step(self, j):
+        if not 0 <= j < self.chunks:
+            return
+
+        @pl.when(self.t < self.count - 1)
+        def _():
+            self.down(j, False).wait_recv()
+            at = self.low(j)
+            total = (self.low_in[at].astype(F32) + self.x[at].astype(F32)).astype(BF16)
+
+            @pl.when(self.t > 0)
+            def _():
+                self.low_in[at] = total
+                self.down(j, False).start()
+
+            @pl.when(self.t == 0)
+            def _():
+                self.out[at] = total
+                self.low_back(j).start()
+
+    def high_step(self, j):
+        if not 0 <= j < self.chunks:
+            return
+
+        @pl.when(self.t > 0)
+        def _():
+            self.up(j, False).wait_recv()
+            at = self.high(j)
+            total = (self.high_in[self.low(j)].astype(F32) + self.x[at].astype(F32)).astype(BF16)
+
+            @pl.when(self.t < self.count - 1)
+            def _():
+                self.high_in[self.low(j)] = total
+                self.up(j, False).start()
+
+            @pl.when(self.t == self.count - 1)
+            def _():
+                self.out[at] = total
+                self.high_back(j).start()
+
+    def low_forward(self, j):
+        @pl.when(self.t > 0)
+        def _():
+            self.low_back(j).wait_recv()
+
+            @pl.when(self.t < self.count - 1)
+            def _():
+                self.low_back(j).start()
+
+    def high_forward(self, j):
+        @pl.when(self.t < self.count - 1)
+        def _():
+            self.high_back(j).wait_recv()
+
+            @pl.when(self.t > 0)
+            def _():
+                self.high_back(j).start()
+
+    def reduce(self, j):
+        @pl.when(self.t < self.count // 2)
+        def _():
+            self.high_step(j)
+            self.low_step(j - 1)
+
+        @pl.when(self.t >= self.count // 2)
+        def _():
+            self.low_step(j)
+            self.high_step(j - 1)
+
+    def back(self, j):
+        @pl.when(self.t < self.count // 2)
+        def _():
+            self.low_forward(j)
+            self.high_forward(j)
+
+        @pl.when(self.t >= self.count // 2)
+        def _():
+            self.high_forward(j)
+            self.low_forward(j)
+
+    def finish(self):
+        last = self.count - 1
+        for j in range(self.chunks):
+
+            @pl.when(self.t > 0)
+            def _():
+                self.down(j, False).wait_send()
+                self.high_back(j).wait_send()
+
+            @pl.when(self.t < last)
+            def _():
+                self.up(j, False).wait_send()
+                self.low_back(j).wait_send()
+
+
+def attend_back_head(
+    h, i, tile, q_ref, kv_ref, bias_ref, total_ref, go_ref, dq_ref, dkv_ref, acc_ref
+):
+    rows, width = q_ref.shape[0] // MB, q_ref.shape[1]
+    keys_count = kv_ref.shape[1]
+    cols = slice(h * HD, (h + 1) * HD)
+    vcols = slice(width + h * HD, width + (h + 1) * HD)
+    acc_ref[:keys_count] = jnp.zeros((keys_count, 2 * HD), F32)
+
+    @pl.loop(0, rows // tile)
+    def _(n):
+        at = pl.ds(pl.multiple_of(i * rows + n * tile, tile), tile)
+        here_at = pl.ds(pl.multiple_of(n * tile, tile), tile)
+        keys, values = kv_ref[i, :, cols], kv_ref[i, :, vcols]
+        queries, go = q_ref[at, cols], go_ref[at, cols]
+        scores = mat_nt(keys, queries)
+        if bias_ref is not None:
+            scores = scores + bias_ref[i, :, here_at]
+        probs = jnp.exp(scores - total_ref[i, h : h + 1, here_at])
+        grad_probs = mat_nt(values, go)
+        inner = jnp.sum(probs * grad_probs, axis=0, keepdims=True)
+        grad_scores = (probs * (grad_probs - inner)).astype(BF16)
+        acc_ref[:keys_count, :HD] += mat(grad_scores, queries)
+        acc_ref[:keys_count, HD:] += mat(probs.astype(BF16), go)
+        dq_ref[at, cols] = mat_tn(keys, grad_scores).T.astype(BF16)
+
+    dkv_ref[i, :, cols] = acc_ref[:keys_count, :HD].astype(BF16)
+    dkv_ref[i, :, vcols] = acc_ref[:keys_count, HD:].astype(BF16)
+
+
+def layer_backward_kernel(
+    count,
+    gcr_ref,
+    cq_ref,
+    kvc_ref,
+    totc_ref,
+    q_ref,
+    kvs_ref,
+    bias_ref,
+    tots_ref,
+    gac_ref,
+    as_ref,
+    tok_ref,
+    wo_ref,
+    cq4_ref,
+    heads_ref,
+    gains_ref,
+    gt_out,
+    enc_sum,
+    gcq,
+    gkvc,
+    gq,
+    gkvs,
+    gsl,
+    norms,
+    dkvc,
+    dkvc_in,
+    dkvs,
+    dkvs_in,
+    acc,
+    held,
+    gatt,
+    enc_part,
+    one_part,
+    one_sum,
+    enc_buffers,
+    one_buffers,
+    line_right,
+    line_left,
+    line_recv,
+    ctx_send,
+    ctx_recv,
+    sum_sems,
+):
+    f, c, t = here()
+    right, left = (f, c, t + 1), (f, c, t - 1)
+    x_peer = (f, 1 - c, t)
+    rows, enc_rows = tok_ref.shape[0] // MB, gkvc.shape[0] // MB
+    width = q_ref.shape[1]
+    tile = 256
+
+    barrier = pltpu.get_barrier_semaphore()
+    pl.semaphore_signal(barrier, inc=1, device_id=x_peer, device_id_type=MESH)
+
+    @pl.when(t > 0)
+    def _():
+        pl.semaphore_signal(barrier, inc=1, device_id=left, device_id_type=MESH)
+
+    @pl.when(t < count - 1)
+    def _():
+        pl.semaphore_signal(barrier, inc=1, device_id=right, device_id_type=MESH)
+
+    at_end = (t == 0) | (t == count - 1)
+    pl.semaphore_wait(barrier, jnp.where(at_end, 2, 3).astype(jnp.int32))
+
+    def part(i):
+        return pl.ds(i * rows, rows)
+
+    def enc_at(i):
+        return pl.ds(i * enc_rows, enc_rows)
+
+    def line(j, own, place):
+        sems = (line_right.at[j], line_left.at[j], line_recv.at[j])
+        return Line(t, count, left, right, own, place, sems)
+
+    query_lines = [
+        line(i, gcq.at[part(i)], lambda origin, i=i: held.at[origin, part(i)]) for i in range(MB)
+    ]
+
+    def ctx_copy(j, ref, landing, i, size):
+        return remote(
+            ref.at[i, pl.ds(size, size)], landing.at[i], ctx_send.at[j], ctx_recv.at[j], x_peer
+        )
+
+    ctx_cross = [ctx_copy(i, dkvc, dkvc_in, i, enc_rows) for i in range(MB)]
+    ctx_self = [ctx_copy(MB + i, dkvs, dkvs_in, i, rows) for i in range(MB)]
+
+    def summed(j, x, out, buffers, chunks):
+        return LineSum(t, count, left, right, x, out, buffers, sum_sems.at[j], chunks)
+
+    enc_chunks = enc_rows // 256
+    one_chunks = rows // 256
+    enc_sums = [
+        summed(i, enc_part.at[enc_at(i)], enc_sum.at[enc_at(i)], enc_buffers.at[i], enc_chunks)
+        for i in range(MB)
+    ]
+    one_sums = [
+        summed(MB + i, one_part.at[part(i)], one_sum.at[part(i)], one_buffers.at[i], one_chunks)
+        for i in range(MB)
+    ]
+
+    def tiles(i, count_rows, body):
+        @pl.loop(0, count_rows // tile)
+        def _(n):
+            at = pl.ds(pl.multiple_of(i * count_rows + n * tile, tile), tile)
+            body(at, pl.ds(pl.multiple_of(n * tile, tile), tile))
+
+    def cross_head(i, h):
+        attend_back_head(h, i, tile, cq_ref, kvc_ref, None, totc_ref, gcr_ref, gcq, dkvc, acc)
+
+    def self_head(i, h):
+        attend_back_head(h, i, tile, q_ref, kvs_ref, bias_ref, tots_ref, gatt, gq, dkvs, acc)
+
+    def send_queries(i):
+        held[t, part(i)] = gcq[part(i)]
+        query_lines[i].start()
+
+    def encoder_part(i):
+        ctx_cross[i].wait_recv()
+
+        def body(at, inner):
+            total = dkvc[i, inner].astype(F32) + dkvc_in[i, inner].astype(F32)
+            gkvc[at] = total.astype(BF16)
+            enc_part[at] = mat_nt(
+                total.astype(BF16), heads_ref[:, 2 * width : 4 * width]
+            ).astype(BF16)
+
+        tiles(i, enc_rows, body)
+        enc_sums[i].start()
+
+    def after_queries(i):
+        def body(at, inner):
+            grad = mat_nt(held[0, at], cq4_ref[0])
+            for origin in range(1, count):
+                grad = grad + mat_nt(held[origin, at], cq4_ref[origin])
+            value = as_ref[at]
+            scale = rms_scale(value)
+            normed = value * scale
+            norms[1:2] += jnp.sum(grad * normed, axis=0, keepdims=True)
+            total = gac_ref[at] + rms_back(grad * gains_ref[1:2], normed, scale)
+            gt_out[at] = total
+            gsl[at] = total.astype(BF16)
+            gatt[at] = mat(total.astype(BF16), wo_ref[...]).astype(BF16)
+
+        tiles(i, rows, body)
+
+    def token_part(i):
+        ctx_self[i].wait_recv()
+
+        def body(at, inner):
+            total = (dkvs[i, inner].astype(F32) + dkvs_in[i, inner].astype(F32)).astype(BF16)
+            gkvs[at] = total
+            product = mat_nt(total, heads_ref[:, : 2 * width])
+            product = product + mat_nt(gq[at], heads_ref[:, 4 * width : 5 * width])
+            one_part[at] = product.astype(BF16)
+
+        tiles(i, rows, body)
+        one_sums[i].start()
+
+    def finish_tokens(i):
+        def body(at, inner):
+            grad = one_sum[at].astype(F32)
+            value = tok_ref[at].astype(F32)
+            scale = rms_scale(value)
+            normed = value * scale
+            norms[0:1] += jnp.sum(grad * normed, axis=0, keepdims=True)
+            gt_out[at] = gt_out[at] + rms_back(grad * gains_ref[0:1], normed, scale)
+
+        tiles(i, rows, body)
+
+    norms[...] = jnp.zeros_like(norms)
+    for h in range(width // HD):
+        cross_head(0, h)
+    send_queries(0)
+    ctx_cross[0].start()
+    cross_head(1, 0)
+    query_lines[0].hop(1)
+    cross_head(1, 1)
+    query_lines[0].hop(2)
+    cross_head(1, 2)
+    send_queries(1)
+    ctx_cross[1].start()
+    query_lines[0].hop(3)
+    after_queries(0)
+    self_head(0, 0)
+    query_lines[1].hop(1)
+    self_head(0, 1)
+    encoder_part(0)
+    query_lines[1].hop(2)
+    self_head(0, 2)
+    ctx_self[0].start()
+    enc_sums[0].reduce(0)
+    query_lines[1].hop(3)
+    after_queries(1)
+    enc_sums[0].reduce(1)
+    self_head(1, 0)
+    enc_sums[0].reduce(2)
+    self_head(1, 1)
+    enc_sums[0].reduce(3)
+    self_head(1, 2)
+    ctx_self[1].start()
+    token_part(0)
+    encoder_part(1)
+    enc_sums[0].reduce(4)
+    one_sums[0].reduce(0)
+    enc_sums[0].back(0)
+    one_sums[0].reduce(1)
+    enc_sums[1].reduce(0)
+    token_part(1)
+    one_sums[0].reduce(2)
+    enc_sums[1].reduce(1)
+    enc_sums[0].back(1)
+    one_sums[1].reduce(0)
+    enc_sums[1].reduce(2)
+    one_sums[0].back(0)
+    one_sums[1].reduce(1)
+    enc_sums[0].back(2)
+    enc_sums[1].reduce(3)
+    one_sums[1].reduce(2)
+    one_sums[0].back(1)
+    enc_sums[1].reduce(4)
+    enc_sums[0].back(3)
+    finish_tokens(0)
+    one_sums[1].back(0)
+    enc_sums[1].back(0)
+    one_sums[1].back(1)
+    enc_sums[1].back(1)
+    finish_tokens(1)
+    enc_sums[1].back(2)
+    enc_sums[1].back(3)
+    for one in query_lines + enc_sums + one_sums:
+        one.finish()
+    for copy in ctx_self + ctx_cross:
+        copy.wait_send()
+
+
+def layer_backward(operands, tokens, enc_rows, collective_id):
+    count = lax.axis_size("tp")
+    tok_rows, features = tokens.shape
+    rows = tok_rows // MB
+    enc_tree = enc_rows // MB
+    width = operands[0].shape[1]
+    vmem = pl.BlockSpec(memory_space=pltpu.VMEM)
+    outs = [
+        ((tok_rows, features), F32),
+        ((enc_rows, features), BF16),
+        ((tok_rows, width), BF16),
+        ((enc_rows, 2 * width), BF16),
+        ((tok_rows, width), BF16),
+        ((tok_rows, 2 * width), BF16),
+        ((tok_rows, features), BF16),
+        ((8, features), F32),
+    ]
+    scratch = [
+        ((MB, 2 * enc_tree, 2 * width), BF16),
+        ((MB, enc_tree, 2 * width), BF16),
+        ((MB, 2 * rows, 2 * width), BF16),
+        ((MB, rows, 2 * width), BF16),
+        ((2 * enc_tree, 2 * HD), F32),
+        ((count, tok_rows, width), BF16),
+        ((tok_rows, width), BF16),
+        ((enc_rows, features), BF16),
+        ((tok_rows, features), BF16),
+        ((tok_rows, features), BF16),
+        ((MB, 2, enc_tree // 2, features), BF16),
+        ((MB, 2, rows // 2, features), BF16),
+    ]
+    return pl.pallas_call(
+        functools.partial(layer_backward_kernel, count),
+        in_specs=[vmem] * 15,
+        out_specs=[vmem] * len(outs),
+        out_shape=[jax.ShapeDtypeStruct(shape, kind) for shape, kind in outs],
+        scratch_shapes=[pltpu.VMEM(shape, kind) for shape, kind in scratch]
+        + [
+            pltpu.SemaphoreType.DMA((MB, count)),
+            pltpu.SemaphoreType.DMA((MB, count)),
+            pltpu.SemaphoreType.DMA((MB, count)),
+            pltpu.SemaphoreType.DMA((2 * MB,)),
+            pltpu.SemaphoreType.DMA((2 * MB,)),
+            pltpu.SemaphoreType.DMA((2 * MB, 8, 4)),
+        ],
+        compiler_params=pltpu.CompilerParams(
+            collective_id=collective_id, has_side_effects=True, vmem_limit_bytes=VMEM_MOST
+        ),
+        name="layer_backward",
+    )(*operands)
+
+
+def layer_backward_plain(operands, tokens, enc_rows, collective_id):
+    (
+        grad_crossed,
+        cross_q,
+        kv_cross,
+        totals_cross,
+        queries,
+        kv_self,
+        bias,
+        totals_self,
+        grad_after_cross,
+        after_self,
+        tokens,
+        w_out_own,
+        c_query_all,
+        heads_all,
+        gains,
+    ) = operands
+    rows, width = queries.shape[0] // MB, queries.shape[1]
+    trees = range(MB)
+
+    def tree_rows(value, i):
+        return value[i * rows : (i + 1) * rows]
+
+    outcome = [
+        attend_back(
+            tree_rows(cross_q, i), kv_cross[i], None, totals_cross[i], tree_rows(grad_crossed, i)
+        )
+        for i in trees
+    ]
+    grad_cq = jnp.concatenate([o[0] for o in outcome], axis=0)
+    grad_kv_cross = jnp.concatenate([ctx_scatter(o[1]) for o in outcome], axis=0)
+    encoder_part = mat_nt(grad_kv_cross, heads_all[:, 2 * width : 4 * width]).astype(BF16)
+    grad_two = line_project(grad_cq, c_query_all, jnp.zeros_like(after_self), 6)
+    scale_two = rms_scale(after_self)
+    normed_two = after_self * scale_two
+    norm_cross = jnp.sum(grad_two * normed_two, axis=0)
+    grad_after_self = grad_after_cross + rms_back(grad_two * gains[1:2], normed_two, scale_two)
+    grad_self_low = grad_after_self.astype(BF16)
+    grad_attended = mat(grad_self_low, w_out_own).astype(BF16)
+    outcome = [
+        attend_back(
+            tree_rows(queries, i), kv_self[i], bias[i], totals_self[i], tree_rows(grad_attended, i)
+        )
+        for i in trees
+    ]
+    grad_q = jnp.concatenate([o[0] for o in outcome], axis=0)
+    grad_kv_self = jnp.concatenate([ctx_scatter(o[1]) for o in outcome], axis=0)
+    part = mat_nt(grad_q, heads_all[:, 4 * width : 5 * width])
+    part = (part + mat_nt(grad_kv_self, heads_all[:, : 2 * width])).astype(BF16)
+    both = line_sum(jnp.concatenate([part, encoder_part], axis=0), 7, 12)
+    grad_one = both[: MB * rows].astype(F32)
+    tok = tokens.astype(F32)
+    scale_one = rms_scale(tok)
+    normed_one = tok * scale_one
+    norm_self = jnp.sum(grad_one * normed_one, axis=0)
+    grad_tokens = grad_after_self + rms_back(grad_one * gains[0:1], normed_one, scale_one)
+    norms = jnp.stack([norm_self, norm_cross] + [jnp.zeros_like(norm_self)] * 6)
+    return (
+        grad_tokens,
+        both[MB * rows :],
+        grad_cq,
+        grad_kv_cross,
+        grad_q,
+        grad_kv_self,
+        grad_self_low,
+        norms,
     )
 
 
@@ -1632,8 +2159,6 @@
         after_cross,
     ) = forward(parents, after(tokens, embed_in), encoder, heads_in, op_in, ff_in, 1)
     gain_self, gain_cross = gains[0:1], gains[1:2]
-    w_kv, w_q = heads_all[:, : 2 * width], heads_all[:, 4 * width : 5 * width]
-    c_kv = heads_all[:, 2 * width : 4 * width]
     own_out = lax.dynamic_index_in_dim(op_all[:2], t, 1, False)
     w_out_own, c_out_own = own_out[0], own_out[1]
     gate_pre, up_pre, mixed, mixed_low, exit_in, exit_in_t = ff_forward(
@@ -1679,41 +2204,41 @@
         tp_count,
         shrink,
     )
-    outcome = [
-        attend_back(
-            tree_rows(cross_q, i), kv_cross[i], None, totals_cross[i], tree_rows(grad_crossed, i)
-        )
-        for i in trees
-    ]
-    grad_cq = jnp.concatenate([o[0] for o in outcome], axis=0)
-    grad_kv_cross = jnp.concatenate([ctx_scatter(o[1]) for o in outcome], axis=0)
-    encoder_part = mat_nt(grad_kv_cross, c_kv).astype(BF16)
-    grad_two = line_project(grad_cq, op_all[2], jnp.zeros_like(after_self), 6)
-    scale_two = rms_scale(after_self)
-    normed_two = after_self * scale_two
-    hidden_two = (normed_two * gain_cross).astype(BF16)
-    norm_cross_grad = jnp.sum(grad_two * normed_two, axis=0)
-    grad_after_self = grad_after_cross + rms_back(grad_two * gain_cross, normed_two, scale_two)
-    grad_self_low = grad_after_self.astype(BF16)
-    grad_attended = mat(grad_self_low, w_out_own).astype(BF16)
-    outcome = [
-        attend_back(
-            tree_rows(queries, i), kv_self[i], bias[i], totals_self[i], tree_rows(grad_attended, i)
-        )
-        for i in trees
-    ]
-    grad_q = jnp.concatenate([o[0] for o in outcome], axis=0)
-    grad_kv_self = jnp.concatenate([ctx_scatter(o[1]) for o in outcome], axis=0)
-    one_part = (mat_nt(grad_q, w_q) + mat_nt(grad_kv_self, w_kv)).astype(BF16)
-    both = line_sum(jnp.concatenate([one_part, encoder_part], axis=0), 7, 12)
-    grad_one = both[: MB * rows].astype(F32)
-    grad_encoder = both[MB * rows :].astype(F32)
+    backward = layer_backward if small_plane() else layer_backward_plain
+    (
+        grad_tokens,
+        grad_encoder,
+        grad_cq,
+        grad_kv_cross,
+        grad_q,
+        grad_kv_self,
+        grad_self_low,
+        norms_low,
+    ) = backward(
+        (
+            grad_crossed,
+            cross_q,
+            kv_cross,
+            totals_cross,
+            queries,
+            kv_self,
+            bias,
+            totals_self,
+            grad_after_cross,
+            after_self,
+            tokens,
+            w_out_own,
+            op_all[2],
+            heads_all,
+            gains,
+        ),
+        tokens,
+        encoder.shape[0],
+        6,
+    )
     tok = tokens.astype(F32)
-    scale_one = rms_scale(tok)
-    normed_one = tok * scale_one
-    hidden_one = (normed_one * gain_self).astype(BF16)
-    norm_self_grad = jnp.sum(grad_one * normed_one, axis=0)
-    grad_tokens = grad_after_self + rms_back(grad_one * gain_self, normed_one, scale_one)
+    hidden_one = (tok * rms_scale(tok) * gain_self).astype(BF16)
+    hidden_two = (after_self * rms_scale(after_self) * gain_cross).astype(BF16)
 
     ff_grads = jnp.concatenate(
         [
@@ -1724,9 +2249,9 @@
         ],
         axis=1,
     ).astype(BF16)
-    ff_own = lax.psum_scatter(after(ff_grads, grad_two), PLANE, scatter_dimension=0, tiled=True)
+    ff_own = lax.psum_scatter(ff_grads, PLANE, scatter_dimension=0, tiled=True)
     norm_block = jnp.pad(
-        jnp.stack([norm_self_grad, norm_cross_grad, norms[1], norms[0]], axis=1),
+        jnp.stack([norms_low[0], norms_low[1], norms[1], norms[0]], axis=1),
         ((0, 0), (0, 60)),
     )
     own = plane_scatter(
@@ -1753,7 +2278,7 @@
         losses,
         scores,
         grad_tokens,
-        grad_encoder,
+        grad_encoder.astype(F32),
         part(own, 4 * width, width),
         part(own, 0, width),
         part(own, width, width),

time: 759 us -> 696 us (0.917)
  other arithmetic: 38.2 us -> 15.5 us
  local copies, waits for them, and re-layouts: 61.5 us -> 40.1 us
  waiting for transfers between devices: 18.5 us -> 0.73 us
    pallas_call x5 -> x1, Pallas kernels: 65.1 us -> 207 us  [layer_backward(): pl.pallas_call(functools.partial(layer_backward_kernel, count), in_specs=...]
    pallas_call x2 -> x1, Pallas kernels: 184 us -> 52.5 us  [line_sum(): pl.pallas_call(functools.partial(line_sum_kernel, count, chunks, window,...]
    ppermute x4 -> x0, waiting for transfers between devices: 18 us -> none  [swap(): return lax.ppermute(value, axis, [(i, i ^ bit) for i in range(count)])]
    unnamed x154 -> x83, local copies, waits for them, and re-layouts: 27 us -> 15.1 us
  transfers between devices with their start and end apart: 7 -> 3, of which waited for: 2 -> 0; matrix products, arithmetic and copies ran while one was open for 10% -> 7% of each run, Pallas kernels for 52% -> 65%
where the time goes in v4:
time: 696 us; the launch traced here: 691 us
  Pallas kernels  603 us (87%)
  local copies, waits for them, and re-layouts  40.1 us (6%)
  matrix products  16.9 us (2%)
  other arithmetic  15.5 us (2%)
  between operations  14.6 us (2%)
    pallas_call x1, Pallas kernels, layer_backward(): pl.pallas_call(functools.partial(layer_backward_kernel, count), in_specs=...  207 us
    pallas_call x1, Pallas kernels, layer_forward(): pl.pallas_call(functools.partial(layer_forward_kernel, count), in_specs=[...  203 us
    pallas_call x1, Pallas kernels, line_sum(): pl.pallas_call(functools.partial(line_sum_kernel, count, chunks, window,...  52.5 us
    pallas_call x1, Pallas kernels, exit_backward(): pl.pallas_call(functools.partial(exit_backward_kernel, valid), grid=(padd...  35 us
    pallas_call x1, Pallas kernels, ff_backward(): pl.pallas_call(functools.partial(ff_backward_kernel, shrink), grid=(count...  34.3 us
    pallas_call x1, Pallas kernels, exit_forward(): pl.pallas_call(functools.partial(exit_forward_kernel, valid), grid=(padde...  24.4 us
    pallas_call x1, Pallas kernels, ff_forward(): pl.pallas_call(functools.partial(ff_forward_kernel, shrink), grid=(count,...  23.8 us
    dot_general x9, matrix products, mat_tn(): lax.dot_general(left, right, (((0,), (0,)), ((), ())), preferred_element_...  16.9 us
  transfers between devices with their start and end apart: 3, of which 0 were waited for; matrix products, arithmetic and copies ran while one was open for 7% of the time, Pallas kernels for 65%

profile of v4, /device:TPU:0, one launch (start us, length us, event | category | flops | bytes accessed | tf_op | source)
XLA Modules:
  0.0 691.5 jit_solution(5829751244667704674)
XLA Ops:
  7.4 2.9 pad.13
  11.1 0.8 concatenate.28.heads_in
  11.9 0.7 pad_maximum_fusion.2.op_in
  12.6 0.7 pad_maximum_fusion.1.ff_in
  13.4 203.3 %layer_forward.1 = (bf16[768,1280]{1,0:T(8,128)(2,1)}, bf16[3,4,768,192]{3,2,1,0:T(8,128)(2,1)}, bf16[768,6144]{1,0:T(8,128)(2,1)}, f32[8,768]{1,0:T(8,128)}, bf...) custom-call(s32[2,8]{1,0:T(2,128)} %parents_ref.1, ...), custom_call_target="tpu_custom_call" | custom-call | tf_op jit(solution)/shard_map/layer_forward/pallas_call | solution.py:1256
  216.6 3.8 slice.84
  220.4 2.1 dynamic-slice_bitcast_fusion
  222.4 23.8 %ff_forward.1 = (f32[1024,2048]{1,0:T(8,128)}, f32[1024,2048]{1,0:T(8,128)}, f32[1024,768]{1,0:T(8,128)}, bf16[1024,768]{1,0:T(8,128)(2,1)}, bf16[1024,768]{1,0:T(8,128)(2,1)}, /*index=5*/bf16[768,1024]{1,0:T(8,128)(2,1)}) custom-call(f32[1024,768]{1,0:T(8,128)} %get-tuple-element.70.ac_ref, f32[8,768]{1,0:T(8,128)} %get-tuple-element.71.gains_ref, ...), custom_call_target="tpu_custom_call" | custom-call | flops 9663676416 | bytes 26214400 | tf_op jit(solution)/shard_map/ff_forward/pallas_call | solution.py:1345
  246.3 1.4 copy-done.2
  247.7 24.4 %exit_forward.1 = (f32[1024,8192]{1,0:T(8,128)}, f32[1024,1]{1,0:T(8,128)S(1)}, f32[1024,1]{1,0:T(8,128)S(1)}, f32[1024,1]{1,0:T(8,128)S(1)}) custom-call(bf16[1024,768]{1,0:T(8,128)(2,1)S(1)} %copy-done.2, bf16[768,8192]{1,0:T(8,128)(2,1)} %all-gather.2.cloned.1.call-done.e_ref, s32[1024,1]{1,0:T(8,128)S(1)} %copy.77.target_ref), custom_call_target="tpu_custom_call" | custom-call | flops 12884901888 | bytes 46137344 | tf_op jit(solution)/shard_map/exit_forward/pallas_call | solution.py:606
  273.3 6.9 share_stats.1
  280.2 0.9 copy.79.log_ref
  281.1 1.4 copy-done.1
  282.5 35.0 %exit_backward.1 = (bf16[768,8192]{1,0:T(8,128)(2,1)}, bf16[1024,768]{1,0:T(8,128)(2,1)S(1)}) custom-call(f32[1024,8192]{1,0:T(8,128)} %get-tuple-element.81.logits_ref, bf16[768,8192]{1,0:T(8,128)(2,1)} %all-gather.2.cloned.1.call-done.e_ref, bf16[768,1024]{1,0:T(8,128)(2,1)S(1)} %copy-done.1, s32[1024,1]{1,0:T(8,128)S(1)} %copy.77.target_ref, ...), custom_call_target="tpu_custom_call" | custom-call | flops 25769803776 | bytes 58720256 | tf_op jit(solution)/shard_map/exit_backward/pallas_call | solution.py:654
  317.5 52.5 %line_sum.1.ge_ref = bf16[1024,768]{1,0:T(8,128)(2,1)S(1)} custom-call(bf16[1024,768]{1,0:T(8,128)(2,1)S(1)} %get-tuple-element.83.x_ref), custom_call_target="tpu_custom_call" | custom-call | tf_op jit(solution)/shard_map/line_sum/pallas_call | solution.py:465
  370.0 1.1 copy-done
  371.2 34.3 %ff_backward.1 = (f32[1024,768]{1,0:T(8,128)}, bf16[1024,768]{1,0:T(8,128)(2,1)}, bf16[1024,768]{1,0:T(8,128)(2,1)}, bf16[1024,192]{1,0:T(8,128)(2,1)}, bf16[102...) custom-call(bf16[1024,768]{1,0:T(8,128)(2,1)} %copy-done, ...), custom_call_target="tpu_custom_call" | custom-call | flops 9663676416 | bytes 26214400 | tf_op jit(solution)/shard_map/ff_backward/pallas_call | solution.py:1470
  405.4 2.9 convolution_convert_fusion.2
  408.4 1.1 convolution_convert_fusion.1
  411.2 1.1 convolution_convert_fusion
  412.6 4.2 copy.89
  416.9 0.7 reduce-scatter.5.cloned.1.call-update
  417.6 1.0 slice_reduce_fusion.4
  418.6 1.8 fusion
  420.7 2.7 slice_bitcast_fusion.cq4_ref
  423.3 206.8 %layer_backward.1 = (f32[1024,768]{1,0:T(8,128)}, bf16[2048,768]{1,0:T(8,128)(2,1)}, bf16[1024,192]{1,0:T(8,128)(2,1)}, bf16[2048,384]{1,0:T(8,128)(2,1)}, bf16[...) custom-call(bf16[1024,192]{1,0:T(8,128)(2,1)} %get-tuple-element.88.gcr_ref, ...), custom_call_target="tpu_custom_call" | custom-call | tf_op jit(solution)/shard_map/layer_backward/pallas_call | solution.py:2004
  630.2 0.8 convert.59
  631.0 1.7 fusion.7
  632.7 0.9 copy.83
  633.7 2.1 convolution_convert_fusion.6
  635.7 0.9 copy.84
  637.0 0.7 convolution_convert_fusion.7
  637.7 0.9 copy.81
  638.6 3.8 fusion.6
  642.7 3.1 convolution_convert_fusion.4
  645.8 4.0 concatenate.36.x_ref
  649.8 16.6 %plane_scatter.1 = f32[96,1408]{1,0:T(8,128)S(1)} custom-call(bf16[8,96,1408]{2,1,0:T(8,128)(2,1)S(1)} %concatenate.36.x_ref), custom_call_target="tpu_custom_call" | custom-call | tf_op jit(solution)/shard_map/plane_scatter/pallas_call | solution.py:180
  666.4 0.8 fusion.10
  667.3 0.7 copy.85
  668.0 5.1 convert_element_type.30
  673.1 0.8 slice_reduce_fusion
  674.5 0.8 slice.114
  675.4 1.0 fusion.11
  676.6 0.8 copy.88
  677.5 0.8 copy.87
  678.4 0.8 copy.86
  679.8 3.2 convert_bitcast_fusion
  683.1 1.7 copy.97
  (105 shorter events, 6.8 us)
Async XLA Ops:
  7.2 3.1 copy-start.23
  7.2 3.1 copy-start.24
  7.2 3.1 copy-start.25
  7.2 3.1 copy-start.26
  7.2 3.3 copy-start.16
  7.2 3.4 copy-start.17
  7.3 3.5 copy-start.22
  7.3 239.0 %all-gather.2.cloned.1.call-start = ((), (), s32[]{:S(2)}) async-start(), calls=%async_computation.2 | async-start | bytes 14155776 | tf_op jit(solution)/shard_map/all_gather | solution.py:2142
  7.3 3.7 copy-start.7
  7.3 3.7 copy-start.11
  7.3 3.7 copy-start.12
  7.3 3.7 copy-start.13
  7.4 3.7 copy-start.14
  7.4 3.7 copy-start.15
  7.4 5.2 copy-start.8
  7.4 5.2 copy-start.9
  7.4 5.2 copy-start.10
  10.3 664.2 %reduce-scatter.7.cloned.1.call-start = ((), (), s32[]{:S(2)}) async-start(), calls=%async_computation.4 | async-start | bytes 3096576
  246.2 1.4 copy-start.2
  281.1 1.4 copy-start.1
  370.0 1.1 copy-start
  405.4 2.9 copy-start.29
  405.4 2.9 copy-start.31
  408.3 1.4 copy-start.28
  408.3 1.5 copy-start.33
  409.4 1.5 copy-start.27
  409.4 1.8 copy-start.30
  416.8 263.0 %reduce-scatter.5.cloned.1.call-start = ((), (), s32[]{:S(2)}) async-start(), calls=%async_computation.3 | async-start | bytes 14155776 | tf_op jit(solution)/shard_map/reduce_scatter | solution.py:2180
  416.9 3.5 copy-start.3
  423.3 207.6 %copy-start.18 = (f32[8,768]{1,0:T(8,128)S(1)}, f32[8,768]{1,0:T(8,128)}, u32[]{:S(2)}) copy-start(f32[8,768]{1,0:T(8,128)} %get-tuple-element.105) | copy-start | bytes 73732
  423.3 207.6 %copy-start.4 = (f32[1024,768]{1,0:T(8,128)S(1)}, f32[1024,768]{1,0:T(8,128)}, u32[]{:S(2)}) copy-start(f32[1024,768]{1,0:T(8,128)} %get-tuple-element.97.as_ref) | copy-start | bytes 9437188
  630.2 3.5 copy-start.32
  633.7 3.3 copy-start.5
  633.7 3.3 copy-start.34
  668.0 5.8 copy-start.19
  668.0 5.8 copy-start.20
  668.0 5.8 copy-start.21
  678.3 4.8 copy-start.6
Sparse Core Ops, SparseCore 0:
  10.4 123.6 all-gather.1
  416.9 52.1 reduce-scatter.6
  473.1 96.4 reduce-scatter.4

commit v5 on v4

--- a/solution.py
+++ b/solution.py
@@ -22,6 +22,9 @@
 LOWEST = -3.0e38
 VMEM_MOST = 58 * 1024 * 1024
 Q2 = 1024
+EXIT_PIECES = 2
+EXIT_CHUNKS = 4
+EXIT_STEPS = 24
 
 
 def mat(left, right):
@@ -622,62 +625,6 @@
         ),
         name="exit_forward",
     )(exit_in, embed_t, targets_local)
-
-
-def exit_backward_kernel(
-    valid, logits_ref, e_ref, x_t_ref, target_ref, log_ref, embed_ref, exit_ref, acc
-):
-    step = pl.program_id(0)
-    rows, tile = logits_ref.shape
-
-    @pl.when(step == 0)
-    def _():
-        acc[...] = jnp.zeros_like(acc)
-
-    lanes = lax.broadcasted_iota(jnp.int32, (rows, tile), 1)
-    relative = target_ref[...] - step * tile
-    probs = jnp.exp(logits_ref[...] - log_ref[...])
-    probs = jnp.where(lanes < valid - step * tile, probs, 0.0)
-    grad = (probs - jnp.where(lanes == relative, 1.0, 0.0)).astype(BF16)
-    acc[...] += mat_nt(grad, e_ref[...])
-    embed_ref[...] = mat(x_t_ref[...], grad).astype(BF16)
-
-    @pl.when(step == pl.num_programs(0) - 1)
-    def _():
-        exit_ref[...] = acc[...].astype(BF16)
-
-
-def exit_backward(logits, embed_t, exit_in_t, targets_local, log_total, valid):
-    rows, padded = logits.shape
-    features = embed_t.shape[0]
-    column = pl.BlockSpec((rows, 1), lambda i: (0, 0))
-    return pl.pallas_call(
-        functools.partial(exit_backward_kernel, valid),
-        grid=(padded // TILE,),
-        in_specs=[
-            pl.BlockSpec((rows, TILE), lambda i: (0, i)),
-            pl.BlockSpec((features, TILE), lambda i: (0, i)),
-            pl.BlockSpec((features, rows), lambda i: (0, 0)),
-            column,
-            column,
-        ],
-        out_specs=[
-            pl.BlockSpec((features, TILE), lambda i: (0, i)),
-            pl.BlockSpec((rows, features), lambda i: (0, 0)),
-        ],
-        out_shape=[
-            jax.ShapeDtypeStruct((features, padded), BF16),
-            jax.ShapeDtypeStruct((rows, features), BF16),
-        ],
-        scratch_shapes=[pltpu.VMEM((rows, features), F32)],
-        compiler_params=pltpu.CompilerParams(vmem_limit_bytes=VMEM_LIMIT),
-        cost_estimate=pl.CostEstimate(
-            flops=4 * rows * features * padded,
-            bytes_accessed=4 * rows * padded + 4 * features * padded,
-            transcendentals=rows * padded,
-        ),
-        name="exit_backward",
-    )(logits, embed_t, exit_in_t, targets_local, log_total)
 
 
 def forward_kernel(heads, q_ref, kv_ref, bias_ref, out_ref, total_ref):
@@ -845,6 +792,25 @@
     return value, slope
 
 
+FORWARD_ORDER = (
+    ("GX", "h"), ("CP",), ("FL", 0), ("GY", "h"), ("OL", 0), ("GX", "e0"), ("GA", "h"),
+    ("GY", "e2"), ("GF", "h"), ("GX", "e2"), ("OL", 1), ("FL", 1), ("GD", "h"), ("GY", "e0"),
+    ("GE", "h"), ("GF", "e0"), ("GF", "e2"), ("OL", 2), ("PT", 1), ("CS", 1), ("FL", 2),
+    ("PT", 0), ("BI",), ("OL", 3), ("CS", 0), ("GX", "e1"), ("GA", "e2"), ("PE", 1), ("FL", 3),
+    ("WS", 1), ("GY", "o"), ("PE", 0), ("GX", "o"), ("S", 1, 0), ("S", 1, 1), ("S", 1, 2),
+    ("WS", 0), ("GY", "e1"), ("GA", "o"), ("S", 0, 0), ("AL", 1), ("CC", 0), ("AH", 1, 1),
+    ("GA", "e0"), ("S", 0, 1), ("GF", "o"), ("S", 0, 2), ("AH", 1, 2), ("AL", 0), ("GD", "o"),
+    ("CC", 1), ("GY", "f0"), ("GX", "f0"), ("AH", 0, 1), ("AH", 0, 2), ("AH", 0, 3), ("GE", "o"),
+    ("GX", "f1"), ("OS", 0), ("WC", 0), ("AH", 1, 3), ("GD", "e0"), ("GA", "f0"), ("X", 0, 0),
+    ("X", 0, 1), ("GF", "e1"), ("X", 0, 2), ("BL", 0), ("OS", 1), ("WC", 1), ("GY", "f1"),
+    ("X", 1, 0), ("BH", 0, 1), ("GF", "f0"), ("GF", "f1"), ("GE", "e0"), ("GA", "e1"),
+    ("X", 1, 1), ("GD", "e2"), ("X", 1, 2), ("BL", 1), ("GD", "e1"), ("BH", 0, 2), ("BH", 0, 3),
+    ("GE", "e2"), ("OC", 0), ("BH", 1, 1), ("GD", "f0"), ("BH", 1, 2), ("GA", "f1"), ("GD", "f1"),
+    ("BH", 1, 3), ("GE", "e1"), ("GE", "f0"), ("OC", 1), ("GE", "f1"),
+)
+EMBED_PIECES = ((2816, "xy"), (2816, "xy"), (2560, "yx"))
+
+
 class Line:
     def __init__(self, t, count, left, right, own, place, sems):
         self.t, self.count, self.left, self.right = t, count, left, right
@@ -910,13 +876,13 @@
 
 
 class Spread:
-    def __init__(self, x_peer, y_peer, core_peer, own, place, send, recv):
-        self.send, self.recv = send, recv
-        home, across, aside, diagonal = place(0, 0), place(0, 1), place(2, 0), place(2, 1)
+    def __init__(self, peers, own, blocks, send, recv):
+        first_peer, second_peer, core_peer = peers
+        home, across, aside, diagonal = blocks
         moves = [
-            (own, home, x_peer),
-            (own, home, y_peer),
-            (across, across, y_peer),
+            (own, home, first_peer),
+            (own, home, second_peer),
+            (across, across, second_peer),
             (own, home, core_peer),
             (across, across, core_peer),
             (aside, aside, core_peer),
@@ -927,27 +893,33 @@
             for j, (src, dst, peer) in enumerate(moves)
         ]
 
-    def step(self, k):
-        copies = self.copies
-        if k == 0:
-            for j in (0, 1, 3):
-                copies[j].start()
-        elif k == 1:
-            copies[0].wait_recv()
-            copies[2].start()
-            copies[4].start()
-        elif k == 2:
-            copies[1].wait_recv()
-            copies[5].start()
-        elif k == 3:
-            copies[2].wait_recv()
-            copies[6].start()
-        elif k == 4:
-            for j in (3, 4, 5, 6):
-                copies[j].wait_recv()
-        else:
-            for copy in copies:
-                copy.wait_send()
+    def start_first(self):
+        self.copies[0].start()
+
+    def start_second(self):
+        self.copies[1].start()
+        self.copies[3].start()
+
+    def pass_across(self):
+        self.copies[0].wait_recv()
+        self.copies[2].start()
+        self.copies[4].start()
+
+    def pass_aside(self):
+        self.copies[1].wait_recv()
+        self.copies[5].start()
+
+    def pass_diagonal(self):
+        self.copies[2].wait_recv()
+        self.copies[6].start()
+
+    def arrive(self):
+        for j in (3, 4, 5, 6):
+            self.copies[j].wait_recv()
+
+    def finish(self):
+        for copy in self.copies:
+            copy.wait_send()
 
 
 def attend_head(h, i, tile, q_ref, kv_ref, bias_ref, out_ref, total_ref):
@@ -1008,9 +980,11 @@
     heads_in,
     op_in,
     ff_in,
+    embed_in,
     heads_all,
     op_all,
     ff_all,
+    embed_all,
     gains_out,
     bias,
     q_out,
@@ -1063,10 +1037,13 @@
         slot = (f ^ df) * 2 + (c ^ dc)
         return pl.ds(pl.multiple_of(slot * shard, shard), shard)
 
-    def spread(j, own, place):
-        return Spread(
-            x_peer, y_peer, core_peer, own, place, spread_send.at[j], spread_recv.at[j]
-        )
+    def spread(j, way, own, place):
+        blocks = [place(block(df, dc)) for df, dc in ((0, 0), (0, 1), (2, 0), (2, 1))]
+        peers = (x_peer, y_peer, core_peer)
+        if way == "yx":
+            blocks = [blocks[0], blocks[2], blocks[1], blocks[3]]
+            peers = (y_peer, x_peer, core_peer)
+        return Spread(peers, own, blocks, spread_send.at[j], spread_recv.at[j])
 
     def line(j, own, place):
         sems = (line_right.at[j], line_left.at[j], line_recv.at[j])
@@ -1075,16 +1052,28 @@
     def part(i):
         return pl.ds(i * rows, rows)
 
-    heads = spread(0, heads_in, lambda df, dc: heads_all.at[block(df, dc)])
-    op_line = line(0, op_in, lambda origin: zop.at[:, origin])
-    op = spread(1, zop, lambda df, dc: op_all.at[:, :, block(df, dc)])
-
     def ff_place(origin):
         return zff.at[:, pl.ds(pl.multiple_of(origin * ff_cols, 128), ff_cols)]
 
+    op_line = line(0, op_in, lambda origin: zop.at[:, origin])
     ff_line = line(1, ff_in, ff_place)
-    ff = spread(2, zff, lambda df, dc: ff_all.at[block(df, dc)])
-    ff_own = pltpu.make_async_copy(zff, ff_all.at[block(0, 0)], local_sem)
+    spreads = {
+        "h": spread(0, "xy", heads_in, lambda at: heads_all.at[at]),
+        "o": spread(1, "xy", zop, lambda at: op_all.at[:, :, at]),
+    }
+    ff_half = zff.shape[1] // 2
+    pieces = [("f0", "xy", zff, ff_all, 0, ff_half), ("f1", "yx", zff, ff_all, ff_half, ff_half)]
+    start = 0
+    for j, (size, way) in enumerate(EMBED_PIECES):
+        pieces.append(("e%d" % j, way, embed_in, embed_all, start, size))
+        start += size
+    for name, way, own, target, first, size in pieces:
+        cols = pl.ds(first, size)
+        spreads[name] = spread(
+            len(spreads), way, own.at[:, cols], lambda at, ref=target, cols=cols: ref.at[at, cols]
+        )
+    ff_own = pltpu.make_async_copy(zff, ff_all.at[block(0, 0)], local_sem.at[0])
+    embed_own = pltpu.make_async_copy(embed_in, embed_all.at[block(0, 0)], local_sem.at[1])
     self_lines = [
         line(2 + i, att.at[part(i)], lambda origin, i=i: held_s.at[origin, part(i)])
         for i in range(MB)
@@ -1149,95 +1138,75 @@
                 total = total + mat_nt(held_c[origin, at], op_all[1, origin])
             ac_out[at] = total
 
-    heads.step(0)
-    op_line.start()
-    heads_all[block(0, 0)] = heads_in[...]
-    zop[:, t] = op_in[...]
-    zff[:, pl.ds(pl.multiple_of(t * ff_cols, 128), ff_cols)] = ff_in[...]
-    build_bias(parents_ref, bias, c)
-    op_line.hop(1)
-    heads.step(1)
-    op_line.hop(2)
-    ff_line.start()
-    heads.step(2)
-    op_line.hop(3)
-    op.step(0)
-    op_all[:, :, block(0, 0)] = zop[...]
-    heads.step(3)
-    heads.step(4)
-    gains_out[...] = heads_all[:, Q2 - 128 : Q2].astype(F32).T[64:72]
-    project_tokens(0)
-    ctx_self[0].start()
-    project_tokens(1)
-    ctx_self[1].start()
-    op.step(1)
-    ff_line.hop(1)
-    project_encoder(0)
-    ctx_cross[0].start()
-    project_encoder(1)
-    ctx_cross[1].start()
-    op.step(2)
-    ctx_self[0].wait_recv()
-    self_head(0, 0)
-    ff_line.hop(2)
-    self_head(0, 1)
-    op.step(3)
-    self_head(0, 2)
-    held_s[t, part(0)] = att[part(0)]
-    self_lines[0].start()
-    ff_line.hop(3)
-    ff_own.start()
-    ctx_self[1].wait_recv()
-    self_head(1, 0)
-    self_lines[0].hop(1)
-    self_head(1, 1)
-    op.step(4)
-    self_head(1, 2)
-    held_s[t, part(1)] = att[part(1)]
-    self_lines[1].start()
-    self_lines[0].hop(2)
-    ff.step(0)
-    self_lines[0].hop(3)
-    out_self(0)
-    self_lines[1].hop(1)
-    ctx_cross[0].wait_recv()
-    cross_head(0, 0)
-    self_lines[1].hop(2)
-    ff.step(1)
-    cross_head(0, 1)
-    self_lines[1].hop(3)
-    cross_head(0, 2)
-    held_c[t, part(0)] = crs[part(0)]
-    cross_lines[0].start()
-    out_self(1)
-    ctx_cross[1].wait_recv()
-    ff.step(2)
-    cross_head(1, 0)
-    cross_lines[0].hop(1)
-    cross_head(1, 1)
-    cross_lines[0].hop(2)
-    cross_head(1, 2)
-    held_c[t, part(1)] = crs[part(1)]
-    cross_lines[1].start()
-    cross_lines[0].hop(3)
-    out_cross(0)
-    cross_lines[1].hop(1)
-    ff.step(3)
-    cross_lines[1].hop(2)
-    cross_lines[1].hop(3)
-    out_cross(1)
-    ff.step(4)
-    heads.step(5)
-    op.step(5)
-    ff.step(5)
-    for one in [op_line, ff_line] + self_lines + cross_lines:
+    def own_parts():
+        heads_all[block(0, 0)] = heads_in[...]
+        zop[:, t] = op_in[...]
+        zff[:, pl.ds(pl.multiple_of(t * ff_cols, 128), ff_cols)] = ff_in[...]
+        embed_own.start()
+
+    def gather_done(name):
+        spreads[name].arrive()
+        if name == "h":
+            gains_out[...] = heads_all[:, Q2 - 128 : Q2].astype(F32).T[64:72]
+
+    def gather_first(name):
+        spreads[name].start_first()
+        if name == "o":
+            op_all[:, :, block(0, 0)] = zop[...]
+        if name == "f0":
+            ff_own.start()
+
+    def along(one, d):
+        if d == 0:
+            one.start()
+        else:
+            one.hop(d)
+
+    def send_self(i):
+        held_s[t, part(i)] = att[part(i)]
+        self_lines[i].start()
+
+    def send_cross(i):
+        held_c[t, part(i)] = crs[part(i)]
+        cross_lines[i].start()
+
+    steps = {
+        "GX": gather_first,
+        "GY": lambda name: spreads[name].start_second(),
+        "GF": lambda name: spreads[name].pass_across(),
+        "GA": lambda name: spreads[name].pass_aside(),
+        "GD": lambda name: spreads[name].pass_diagonal(),
+        "GE": gather_done,
+        "OL": lambda d: along(op_line, d),
+        "FL": lambda d: along(ff_line, d),
+        "CP": own_parts,
+        "BI": lambda: build_bias(parents_ref, bias, c),
+        "PT": project_tokens,
+        "PE": project_encoder,
+        "CS": lambda i: ctx_self[i].start(),
+        "CC": lambda i: ctx_cross[i].start(),
+        "WS": lambda i: ctx_self[i].wait_recv(),
+        "WC": lambda i: ctx_cross[i].wait_recv(),
+        "S": self_head,
+        "X": cross_head,
+        "AL": send_self,
+        "AH": lambda i, d: self_lines[i].hop(d),
+        "BL": send_cross,
+        "BH": lambda i, d: cross_lines[i].hop(d),
+        "OS": out_self,
+        "OC": out_cross,
+    }
+    for name, *rest in FORWARD_ORDER:
+        steps[name](*rest)
+    for one in list(spreads.values()) + [op_line, ff_line] + self_lines + cross_lines:
         one.finish()
     for copy in ctx_self + ctx_cross:
         copy.wait_send()
     ff_own.wait()
-
-
-def layer_forward(parents, tokens, encoder, heads_in, op_in, ff_in, collective_id):
+    embed_own.wait()
+
+
+def layer_forward(parents, tokens, encoder, heads_in, op_in, ff_in, embed_in, collective_id):
     count = lax.axis_size("tp")
     tok_rows, features = tokens.shape
     enc_rows = encoder.shape[0]
@@ -1246,6 +1215,7 @@
     nh = width // HD
     rows = tok_rows // MB
     vmem = pl.BlockSpec(memory_space=pltpu.VMEM)
+    anywhere = pl.BlockSpec(memory_space=pl.ANY)
 
     def low(*shape):
         return jax.ShapeDtypeStruct(shape, BF16)
@@ -1255,12 +1225,13 @@
 
     return pl.pallas_call(
         functools.partial(layer_forward_kernel, count),
-        in_specs=[pl.BlockSpec(memory_space=pltpu.SMEM)] + [vmem] * 5,
-        out_specs=[vmem, vmem, pl.BlockSpec(memory_space=pl.ANY)] + [vmem] * 12,
+        in_specs=[pl.BlockSpec(memory_space=pltpu.SMEM)] + [vmem] * 5 + [anywhere],
+        out_specs=[vmem, vmem, anywhere, anywhere] + [vmem] * 12,
         out_shape=[
             low(features, heads_in.shape[1]),
             low(3, count, features, width),
             low(features, count * ff_cols),
+            low(features, embed_in.shape[1]),
             full(8, features),
             low(MB, 2 * rows, rows),
             low(tok_rows, width),
@@ -1279,20 +1250,20 @@
             pltpu.VMEM((shard, count * ff_cols), BF16),
             pltpu.VMEM((count, tok_rows, width), BF16),
             pltpu.VMEM((count, tok_rows, width), BF16),
-            pltpu.SemaphoreType.DMA((3, 7)),
-            pltpu.SemaphoreType.DMA((3, 7)),
+            pltpu.SemaphoreType.DMA((4 + len(EMBED_PIECES), 7)),
+            pltpu.SemaphoreType.DMA((4 + len(EMBED_PIECES), 7)),
             pltpu.SemaphoreType.DMA((6, count)),
             pltpu.SemaphoreType.DMA((6, count)),
             pltpu.SemaphoreType.DMA((6, count)),
             pltpu.SemaphoreType.DMA((4,)),
             pltpu.SemaphoreType.DMA((4,)),
-            pltpu.SemaphoreType.DMA,
+            pltpu.SemaphoreType.DMA((2,)),
         ],
         compiler_params=pltpu.CompilerParams(
             collective_id=collective_id, has_side_effects=True, vmem_limit_bytes=VMEM_MOST
         ),
         name="layer_forward",
-    )(parents, tokens, encoder, heads_in, op_in, ff_in)
+    )(parents, tokens, encoder, heads_in, op_in, ff_in, embed_in)
 
 
 def ff_forward_kernel(
@@ -1504,7 +1475,9 @@
     )(grad_exit, mixed, cotangent, after_cross, gains, c_out_own, ff_all, gate, up)
 
 
-def layer_forward_plain(parents, tokens, encoder, heads_in, op_in, ff_in, collective_id):
+def layer_forward_plain(
+    parents, tokens, encoder, heads_in, op_in, ff_in, embed_in, collective_id
+):
     rows = tokens.shape[0] // MB
     enc_rows = encoder.shape[0] // MB
     width = op_in.shape[2]
@@ -1515,6 +1488,7 @@
     ff_all = lax.all_gather(
         lax.all_gather(ff_in, "tp", axis=1, tiled=True), PLANE, axis=0, tiled=True
     )
+    embed_all = lax.all_gather(embed_in, PLANE, axis=0, tiled=True)
     gains = heads_all[:, Q2 - 64 : Q2 - 56].astype(F32).T
     tok = tokens.astype(F32)
     hidden_one = (tok * rms_scale(tok) * gains[0:1]).astype(BF16)
@@ -1550,6 +1524,7 @@
         heads_all,
         op_all,
         ff_all,
+        embed_all,
         gains,
         bias,
         queries,
@@ -1565,6 +1540,23 @@
     )
 
 
+BACKWARD_ORDER = (
+    ("X", 0, 0), ("X", 0, 1), ("X", 0, 2), ("XC", 0), ("SQ", 0), ("X", 1, 0), ("X", 1, 1),
+    ("X", 1, 2), ("XC", 1), ("QH", 0, 1), ("SQ", 1), ("EP", 0), ("QH", 0, 2), ("ERN", 0, 0),
+    ("QH", 1, 1), ("QH", 0, 3), ("AQ", 0), ("ERN", 0, 1), ("S", 0, 0), ("EP", 1), ("QH", 1, 2),
+    ("ERF", 0, 0), ("QH", 1, 3), ("ERN", 0, 2), ("AQ", 1), ("ERF", 0, 1), ("ERN", 1, 0),
+    ("S", 0, 1), ("S", 0, 2), ("ERN", 1, 1), ("XS", 0), ("ERF", 1, 0), ("ERN", 0, 3),
+    ("ERF", 1, 1), ("ERN", 1, 2), ("S", 1, 0), ("ERF", 0, 2), ("S", 1, 1), ("EBN", 0, 0),
+    ("ERF", 0, 3), ("S", 1, 2), ("EBN", 0, 1), ("TP", 0), ("ERF", 1, 2), ("EBN", 1, 0),
+    ("EBF", 0, 0), ("XS", 1), ("ERN", 1, 3), ("EBN", 1, 1), ("EBF", 0, 1), ("EBF", 1, 0),
+    ("EBN", 0, 2), ("TP", 1), ("EBF", 1, 1), ("ERF", 1, 3), ("ORN", 0, 0), ("ORN", 0, 1),
+    ("EBN", 1, 2), ("EBF", 0, 2), ("ORF", 0, 0), ("ORF", 0, 1), ("ORN", 1, 0), ("EBF", 1, 2),
+    ("ORN", 1, 1), ("EBN", 0, 3), ("ORF", 1, 0), ("ORF", 1, 1), ("OBN", 0, 0), ("OBN", 0, 1),
+    ("EBF", 0, 3), ("OBF", 0, 0), ("OBF", 0, 1), ("OBN", 1, 0), ("OBN", 1, 1), ("EBN", 1, 3),
+    ("FT", 0), ("OBF", 1, 0), ("OBF", 1, 1), ("FT", 1), ("EBF", 1, 3),
+)
+
+
 class LineSum:
     def __init__(self, t, count, left, right, x, out, buffers, sems, chunks):
         self.t, self.count, self.left, self.right = t, count, left, right
@@ -1667,27 +1659,26 @@
             def _():
                 self.high_back(j).start()
 
-    def reduce(self, j):
+    def by_side(self, first, second, j):
         @pl.when(self.t < self.count // 2)
         def _():
-            self.high_step(j)
-            self.low_step(j - 1)
+            first(j)
 
         @pl.when(self.t >= self.count // 2)
         def _():
-            self.low_step(j)
-            self.high_step(j - 1)
-
-    def back(self, j):
-        @pl.when(self.t < self.count // 2)
-        def _():
-            self.low_forward(j)
-            self.high_forward(j)
-
-        @pl.when(self.t >= self.count // 2)
-        def _():
-            self.high_forward(j)
-            self.low_forward(j)
+            second(j)
+
+    def reduce_near(self, j):
+        self.by_side(self.high_step, self.low_step, j)
+
+    def reduce_far(self, j):
+        self.by_side(self.low_step, self.high_step, j)
+
+    def back_near(self, j):
+        self.by_side(self.low_forward, self.high_forward, j)
+
+    def back_far(self, j):
+        self.by_side(self.high_forward, self.low_forward, j)
 
     def finish(self):
         last = self.count - 1
@@ -1905,65 +1896,28 @@
         tiles(i, rows, body)
 
     norms[...] = jnp.zeros_like(norms)
-    for h in range(width // HD):
-        cross_head(0, h)
-    send_queries(0)
-    ctx_cross[0].start()
-    cross_head(1, 0)
-    query_lines[0].hop(1)
-    cross_head(1, 1)
-    query_lines[0].hop(2)
-    cross_head(1, 2)
-    send_queries(1)
-    ctx_cross[1].start()
-    query_lines[0].hop(3)
-    after_queries(0)
-    self_head(0, 0)
-    query_lines[1].hop(1)
-    self_head(0, 1)
-    encoder_part(0)
-    query_lines[1].hop(2)
-    self_head(0, 2)
-    ctx_self[0].start()
-    enc_sums[0].reduce(0)
-    query_lines[1].hop(3)
-    after_queries(1)
-    enc_sums[0].reduce(1)
-    self_head(1, 0)
-    enc_sums[0].reduce(2)
-    self_head(1, 1)
-    enc_sums[0].reduce(3)
-    self_head(1, 2)
-    ctx_self[1].start()
-    token_part(0)
-    encoder_part(1)
-    enc_sums[0].reduce(4)
-    one_sums[0].reduce(0)
-    enc_sums[0].back(0)
-    one_sums[0].reduce(1)
-    enc_sums[1].reduce(0)
-    token_part(1)
-    one_sums[0].reduce(2)
-    enc_sums[1].reduce(1)
-    enc_sums[0].back(1)
-    one_sums[1].reduce(0)
-    enc_sums[1].reduce(2)
-    one_sums[0].back(0)
-    one_sums[1].reduce(1)
-    enc_sums[0].back(2)
-    enc_sums[1].reduce(3)
-    one_sums[1].reduce(2)
-    one_sums[0].back(1)
-    enc_sums[1].reduce(4)
-    enc_sums[0].back(3)
-    finish_tokens(0)
-    one_sums[1].back(0)
-    enc_sums[1].back(0)
-    one_sums[1].back(1)
-    enc_sums[1].back(1)
-    finish_tokens(1)
-    enc_sums[1].back(2)
-    enc_sums[1].back(3)
+    steps = {
+        "X": cross_head,
+        "SQ": send_queries,
+        "XC": lambda i: ctx_cross[i].start(),
+        "QH": lambda i, d: query_lines[i].hop(d),
+        "AQ": after_queries,
+        "S": self_head,
+        "EP": encoder_part,
+        "XS": lambda i: ctx_self[i].start(),
+        "TP": token_part,
+        "FT": finish_tokens,
+        "ERN": lambda i, j: enc_sums[i].reduce_near(j),
+        "ERF": lambda i, j: enc_sums[i].reduce_far(j),
+        "EBN": lambda i, j: enc_sums[i].back_near(j),
+        "EBF": lambda i, j: enc_sums[i].back_far(j),
+        "ORN": lambda i, j: one_sums[i].reduce_near(j),
+        "ORF": lambda i, j: one_sums[i].reduce_far(j),
+        "OBN": lambda i, j: one_sums[i].back_near(j),
+        "OBF": lambda i, j: one_sums[i].back_far(j),
+    }
+    for name, *rest in BACKWARD_ORDER:
+        steps[name](*rest)
     for one in query_lines + enc_sums + one_sums:
         one.finish()
     for copy in ctx_self + ctx_cross:
@@ -2022,6 +1976,164 @@
     )(*operands)
 
 
+EXIT_ORDER = (
+    (8, "ST", 0), (11, "RN", 0, 0), (13, "RN", 0, 1), (14, "RN", 0, 2), (15, "ST", 1),
+    (15, "RN", 0, 3), (15, "RF", 0, 0), (17, "RN", 1, 0), (17, "RF", 0, 1), (17, "RF", 0, 2),
+    (17, "RN", 1, 1), (17, "RN", 1, 2), (17, "RF", 1, 0), (18, "RF", 1, 1), (18, "BN", 0, 0),
+    (19, "RF", 0, 3), (19, "RN", 1, 3), (19, "BN", 0, 1), (19, "RF", 1, 2), (19, "BF", 0, 0),
+    (19, "RF", 1, 3), (19, "BN", 1, 0), (20, "BN", 1, 1), (20, "BN", 0, 2), (20, "BF", 0, 1),
+    (21, "BF", 1, 0), (21, "BN", 1, 2), (21, "BF", 1, 1), (22, "BN", 0, 3), (22, "BF", 0, 2),
+    (23, "BN", 1, 3), (23, "BF", 1, 2), (23, "BF", 0, 3), (23, "BF", 1, 3),
+)
+
+
+def exit_backward_kernel(
+    count,
+    valid,
+    logits_ref,
+    e_ref,
+    x_t_ref,
+    target_ref,
+    log_ref,
+    embed_ref,
+    sum_ref,
+    grads,
+    acc,
+    partial,
+    total,
+    buffers,
+    sems,
+):
+    f, c, t = here()
+    right, left = (f, c, t + 1), (f, c, t - 1)
+    step = pl.program_id(0)
+    size, tile = logits_ref.shape
+    tiles = grads.shape[1] // tile
+    sums = [
+        LineSum(
+            t,
+            count,
+            left,
+            right,
+            partial.at[pl.ds(p * size, size)],
+            total.at[pl.ds(p * size, size)],
+            buffers.at[p],
+            sems.at[p],
+            EXIT_CHUNKS,
+        )
+        for p in range(EXIT_PIECES)
+    ]
+
+    @pl.when(step == 0)
+    def _():
+        greet_line(t, count, left, right)
+
+    @pl.when(step < EXIT_PIECES * tiles)
+    def _():
+        piece, k = step // tiles, lax.rem(step, tiles)
+        lanes = lax.broadcasted_iota(jnp.int32, (size, tile), 1)
+        probs = jnp.exp(logits_ref[...] - log_ref[...])
+        probs = jnp.where(lanes < valid - k * tile, probs, 0.0)
+        hits = jnp.where(lanes == target_ref[...] - k * tile, 1.0, 0.0)
+        grad = (probs - hits).astype(BF16)
+        rows = pl.ds(pl.multiple_of(piece * size, size), size)
+        grads[rows, pl.ds(pl.multiple_of(k * tile, tile), tile)] = grad
+        product = mat_nt(grad, e_ref[...])
+
+        @pl.when(k == 0)
+        def _():
+            acc[...] = product
+
+        @pl.when(k > 0)
+        def _():
+            acc[...] += product
+
+        @pl.when(k == tiles - 1)
+        def _():
+            partial[rows] = acc[...].astype(BF16)
+
+    @pl.when(step >= EXIT_PIECES * tiles)
+    def _():
+        k = step - EXIT_PIECES * tiles
+        columns = pl.ds(pl.multiple_of(k * tile, tile), tile)
+        embed_ref[...] = mat(x_t_ref[...], grads[:, columns]).astype(BF16)
+
+    steps = {
+        "ST": lambda p: sums[p].start(),
+        "RN": lambda p, j: sums[p].reduce_near(j),
+        "RF": lambda p, j: sums[p].reduce_far(j),
+        "BN": lambda p, j: sums[p].back_near(j),
+        "BF": lambda p, j: sums[p].back_far(j),
+    }
+    for when in sorted({item[0] for item in EXIT_ORDER}):
+
+        @pl.when(step == when)
+        def _():
+            for at, name, *rest in EXIT_ORDER:
+                if at == when:
+                    steps[name](*rest)
+
+    @pl.when(step == pl.num_programs(0) - 1)
+    def _():
+        for one in sums:
+            one.finish()
+        sum_ref[...] = total[...]
+
+
+def exit_backward(logits, embed_t, exit_in_t, targets_local, log_total, valid, collective_id):
+    rows, padded = logits.shape
+    features = embed_t.shape[0]
+    count = lax.axis_size("tp")
+    size = rows // EXIT_PIECES
+    tiles = padded // TILE
+    if tiles * (EXIT_PIECES + 1) != EXIT_STEPS:
+        raise ValueError("steps")
+
+    def piece_of(i):
+        return jnp.minimum(i // tiles, EXIT_PIECES - 1)
+
+    def tile_of(i):
+        return jnp.where(i < EXIT_PIECES * tiles, lax.rem(i, tiles), tiles - 1)
+
+    column = pl.BlockSpec((size, 1), lambda i: (piece_of(i), 0))
+    return pl.pallas_call(
+        functools.partial(exit_backward_kernel, count, valid),
+        grid=(EXIT_STEPS,),
+        in_specs=[
+            pl.BlockSpec((size, TILE), lambda i: (piece_of(i), tile_of(i))),
+            pl.BlockSpec((features, TILE), lambda i: (0, tile_of(i))),
+            pl.BlockSpec((features, rows), lambda i: (0, 0)),
+            column,
+            column,
+        ],
+        out_specs=[
+            pl.BlockSpec((features, TILE), lambda i: (0, jnp.maximum(i - EXIT_PIECES * tiles, 0))),
+            pl.BlockSpec((rows, features), lambda i: (0, 0)),
+        ],
+        out_shape=[
+            jax.ShapeDtypeStruct((features, padded), BF16),
+            jax.ShapeDtypeStruct((rows, features), BF16),
+        ],
+        scratch_shapes=[
+            pltpu.VMEM((rows, padded), BF16),
+            pltpu.VMEM((size, features), F32),
+            pltpu.VMEM((rows, features), BF16),
+            pltpu.VMEM((rows, features), BF16),
+            pltpu.VMEM((EXIT_PIECES, 2, size // 2, features), BF16),
+            pltpu.SemaphoreType.DMA((EXIT_PIECES, 8, EXIT_CHUNKS)),
+        ],
+        compiler_params=pltpu.CompilerParams(
+            collective_id=collective_id, has_side_effects=True, vmem_limit_bytes=VMEM_MOST
+        ),
+        cost_estimate=pl.CostEstimate(
+            flops=4 * rows * features * padded,
+            bytes_accessed=4 * rows * padded + 4 * features * padded,
+            transcendentals=rows * padded,
+        ),
+        name="exit_backward",
+    )(logits, embed_t, exit_in_t, targets_local, log_total)
+
+
 def layer_backward_plain(operands, tokens, enc_rows, collective_id):
     (
         grad_crossed,
@@ -2139,12 +2251,12 @@
     ff_in = jnp.concatenate([w_gate, w_up, w_down.T], axis=1)
     padded = -(-vocab // TILE) * TILE
     embed_in = jnp.pad(embedding.T, ((0, 0), (0, padded - vocab)))
-    embed_t = lax.all_gather(embed_in, PLANE, axis=0, tiled=True)
     forward = layer_forward if small_plane() else layer_forward_plain
     (
         heads_all,
         op_all,
         ff_all,
+        embed_t,
         gains,
         bias,
         queries,
@@ -2157,7 +2269,7 @@
         totals_cross,
         after_self,
         after_cross,
-    ) = forward(parents, after(tokens, embed_in), encoder, heads_in, op_in, ff_in, 1)
+    ) = forward(parents, tokens, encoder, heads_in, op_in, ff_in, embed_in, 1)
     gain_self, gain_cross = gains[0:1], gains[1:2]
     own_out = lax.dynamic_index_in_dim(op_all[:2], t, 1, False)
     w_out_own, c_out_own = own_out[0], own_out[1]
@@ -2173,13 +2285,12 @@
     top, log_total, picked = share_stats(stats, 4)
     losses = (log_total - picked).reshape(-1)
     scores = (top - log_total).reshape(-1)
-    grad_embed, grad_exit_part = exit_backward(
-        logits, embed_t, exit_in_t, targets_local, log_total.reshape(-1, 1), vocab
+    grad_embed, grad_exit = exit_backward(
+        logits, embed_t, exit_in_t, targets_local, log_total.reshape(-1, 1), vocab, 5
     )
     grad_embed_own = lax.optimization_barrier(
         lax.psum_scatter(grad_embed, PLANE, scatter_dimension=0, tiled=True)
     )
-    grad_exit = line_sum(grad_exit_part, 5)
 
     (
         grad_after_cross,

time: 696 us -> 630 us (0.905)
  Pallas kernels: 603 us -> 533 us
    pallas_call x1, Pallas kernels: 203 us -> 173 us  [layer_forward(): pl.pallas_call(functools.partial(layer_forward_kernel, count), in_specs=[...]
    pallas_call x1, Pallas kernels: 207 us -> 179 us  [layer_backward(): pl.pallas_call(functools.partial(layer_backward_kernel, count), in_specs=...]
    pallas_call x2 -> x1, Pallas kernels: 87.5 us -> 73.7 us  [exit_backward(): pl.pallas_call(functools.partial(exit_backward_kernel, count, valid), gri...]
    unnamed x83 -> x67, local copies, waits for them, and re-layouts: 15.1 us -> 14.1 us
  transfers between devices with their start and end apart: 3 -> 2, of which waited for: 0 -> 0; matrix products, arithmetic and copies ran while one was open for 7% -> 6% of each run, Pallas kernels for 65% -> 32%
where the time goes in v5:
time: 630 us; the launch traced here: 619 us
  Pallas kernels  533 us (85%)
  local copies, waits for them, and re-layouts  39.8 us (6%)
  matrix products  15.9 us (3%)
  other arithmetic  15.6 us (2%)
  between operations  14.8 us (2%)
    pallas_call x1, Pallas kernels, layer_backward(): pl.pallas_call(functools.partial(layer_backward_kernel, count), in_specs=...  179 us
    pallas_call x1, Pallas kernels, layer_forward(): pl.pallas_call(functools.partial(layer_forward_kernel, count), in_specs=[...  173 us
    pallas_call x1, Pallas kernels, exit_backward(): pl.pallas_call(functools.partial(exit_backward_kernel, count, valid), gri...  73.7 us
    pallas_call x1, Pallas kernels, ff_backward(): pl.pallas_call(functools.partial(ff_backward_kernel, shrink), grid=(count...  34.3 us
    pallas_call x1, Pallas kernels, exit_forward(): pl.pallas_call(functools.partial(exit_forward_kernel, valid), grid=(padde...  24.4 us
    pallas_call x1, Pallas kernels, ff_forward(): pl.pallas_call(functools.partial(ff_forward_kernel, shrink), grid=(count,...  23.8 us
    pallas_call x1, Pallas kernels, plane_scatter(): pl.pallas_call(plane_scatter_kernel, in_specs=[pl.BlockSpec(memory_space=...  17 us
    dot_general x9, matrix products, mat_tn(): lax.dot_general(left, right, (((0,), (0,)), ((), ())), preferred_element_...  15.9 us
  transfers between devices with their start and end apart: 2, of which 0 were waited for; matrix products, arithmetic and copies ran while one was open for 6% of the time, Pallas kernels for 32%

profile of v5, /device:TPU:0, one launch (start us, length us, event | category | flops | bytes accessed | tf_op | source)
XLA Modules:
  0.0 619.4 jit_solution(3096564933921463209)
XLA Ops:
  7.3 0.8 pad_maximum_fusion.5
  8.3 0.9 copy.75
  9.2 0.9 copy.76
  10.1 0.7 and_select_fusion
  11.0 2.9 pad.14.embed_in
  13.9 0.7 pad_maximum_fusion.2.op_in
  14.6 0.7 pad_maximum_fusion.1.ff_in
  15.4 0.8 concatenate.28.heads_in
  16.2 173.0 %layer_forward.1 = (bf16[768,1280]{1,0:T(8,128)(2,1)}, bf16[3,4,768,192]{3,2,1,0:T(8,128)(2,1)}, bf16[768,6144]{1,0:T(8,128)(2,1)}, bf16[768,8192]{1,0:T(8,128)(...) custom-call(s32[2,8]{1,0:T(2,128)} %parents_ref.1, ...), custom_call_target="tpu_custom_call" | custom-call | tf_op jit(solution)/shard_map/layer_forward/pallas_call | solution.py:1226
  189.3 3.8 slice.84
  193.0 23.8 %ff_forward.1 = (f32[1024,2048]{1,0:T(8,128)}, f32[1024,2048]{1,0:T(8,128)}, f32[1024,768]{1,0:T(8,128)}, bf16[1024,768]{1,0:T(8,128)(2,1)}, bf16[1024,768]{1,0:T(8,128)(2,1)}, /*index=5*/bf16[768,1024]{1,0:T(8,128)(2,1)}) custom-call(f32[1024,768]{1,0:T(8,128)} %get-tuple-element.69.ac_ref, f32[8,768]{1,0:T(8,128)} %get-tuple-element.70.gains_ref, ...), custom_call_target="tpu_custom_call" | custom-call | flops 9663676416 | bytes 26214400 | tf_op jit(solution)/shard_map/ff_forward/pallas_call | solution.py:1316
  216.8 1.4 copy-done.1
  218.2 24.4 %exit_forward.1 = (f32[1024,8192]{1,0:T(8,128)}, f32[1024,1]{1,0:T(8,128)S(1)}, f32[1024,1]{1,0:T(8,128)S(1)}, f32[1024,1]{1,0:T(8,128)S(1)}) custom-call(bf16[1024,768]{1,0:T(8,128)(2,1)S(1)} %copy-done.1, bf16[768,8192]{1,0:T(8,128)(2,1)} %get-tuple-element.74.e_ref, s32[1024,1]{1,0:T(8,128)S(1)} %copy.77.target_ref), custom_call_target="tpu_custom_call" | custom-call | flops 12884901888 | bytes 46137344 | tf_op jit(solution)/shard_map/exit_forward/pallas_call | solution.py:609
  243.9 6.9 %share_stats.1 = (f32[8,128]{1,0:T(8,128)}, f32[8,128]{1,0:T(8,128)}, f32[8,128]{1,0:T(8,128)}) custom-call(f32[3,8,128]{2,1,0:T(8,128)} %pad_maximum_fusion.3.x_ref), custom_call_target="tpu_custom_call" | custom-call | tf_op jit(solution)/shard_map/share_stats/pallas_call | solution.py:504
  250.8 1.7 copy.79.log_ref
  252.5 2.1 dynamic-slice_bitcast_fusion
  254.5 73.7 %exit_backward.1 = (bf16[768,8192]{1,0:T(8,128)(2,1)}, bf16[1024,768]{1,0:T(8,128)(2,1)}) custom-call(f32[1024,8192]{1,0:T(8,128)} %get-tuple-element.81.logits_ref, bf16[768,8192]{1,0:T(8,128)(2,1)} %get-tuple-element.74.e_ref, bf16[768,1024]{1,0:T(8,128)(2,1)} %get-tuple-element.82.x_t_ref, s32[1024,1]{1,0:T(8,128)} %copy-done, f32[1024,1]{1,0:T(8,128)} %copy.79.log_ref), custom_call_target="tpu_custom_call" | custom-call | flops 25769803776 | bytes 58720256 | tf_op jit(solution)/shard_map/exit_backward/pallas_call | solution.py:2099
  328.3 34.3 %ff_backward.1 = (f32[1024,768]{1,0:T(8,128)}, bf16[1024,768]{1,0:T(8,128)(2,1)}, bf16[1024,768]{1,0:T(8,128)(2,1)}, bf16[1024,192]{1,0:T(8,128)(2,1)}, bf16[102...) custom-call(bf16[1024,768]{1,0:T(8,128)(2,1)} %get-tuple-element.83., ...), custom_call_target="tpu_custom_call" | custom-call | flops 9663676416 | bytes 26214400 | tf_op jit(solution)/shard_map/ff_backward/pallas_call | solution.py:1441
  362.6 2.9 convolution_convert_fusion.2
  365.5 1.1 convolution_convert_fusion.1
  368.4 1.1 convolution_convert_fusion
  369.8 4.2 copy.89
  374.0 0.7 reduce-scatter.5.cloned.1.call-update
  374.7 2.7 slice_bitcast_fusion.cq4_ref
  377.4 179.5 %layer_backward.1 = (f32[1024,768]{1,0:T(8,128)}, bf16[2048,768]{1,0:T(8,128)(2,1)}, bf16[1024,192]{1,0:T(8,128)(2,1)}, bf16[2048,384]{1,0:T(8,128)(2,1)}, bf16[...) custom-call(bf16[1024,192]{1,0:T(8,128)(2,1)} %get-tuple-element.88.gcr_ref, ...), custom_call_target="tpu_custom_call" | custom-call | tf_op jit(solution)/shard_map/layer_backward/pallas_call | solution.py:1958
  556.9 0.8 convert.59
  557.7 0.8 slice_reduce_fusion.4
  558.9 0.7 fusion.7
  559.6 0.9 copy.83
  560.5 2.1 convolution_convert_fusion.6
  562.6 0.9 copy.84
  564.2 0.7 convolution_convert_fusion.7
  565.0 0.9 copy.81
  565.9 3.8 fusion.6
  570.0 3.1 convolution_convert_fusion.4
  573.0 4.0 concatenate.36.x_ref
  577.1 17.0 %plane_scatter.1 = f32[96,1408]{1,0:T(8,128)S(1)} custom-call(bf16[8,96,1408]{2,1,0:T(8,128)(2,1)S(1)} %concatenate.36.x_ref), custom_call_target="tpu_custom_call" | custom-call | tf_op jit(solution)/shard_map/plane_scatter/pallas_call | solution.py:183
  594.1 0.8 fusion.10
  594.9 0.7 copy.85
  595.7 5.1 convert_element_type.30
  600.8 0.8 slice_reduce_fusion
  602.1 0.8 slice.114
  603.1 1.0 fusion.11
  604.2 0.8 copy.88
  605.2 0.8 copy.87
  606.1 0.8 copy.86
  607.5 3.2 convert_bitcast_fusion
  610.8 1.7 copy.97
  (85 shorter events, 6.8 us)
Async XLA Ops:
  7.2 6.7 %copy-start.6 = (bf16[96,192]{1,0:T(8,128)(2,1)S(1)}, bf16[96,192]{1,0:T(8,128)(2,1)}, u32[]{:S(2)}) copy-start(bf16[96,192]{1,0:T(8,128)(2,1)} %param.30) | copy-start | bytes 110596
  7.2 7.4 %copy-start.7 = (bf16[512,96]{0,1:T(8,128)(2,1)S(1)}, bf16[512,96]{0,1:T(8,128)(2,1)}, u32[]{:S(2)}) copy-start(bf16[512,96]{0,1:T(8,128)(2,1)} %param.36) | copy-start | bytes 294916
  7.2 7.4 %copy-start.8 = (bf16[96,512]{1,0:T(8,128)(2,1)S(1)}, bf16[96,512]{1,0:T(8,128)(2,1)}, u32[]{:S(2)}) copy-start(bf16[96,512]{1,0:T(8,128)(2,1)} %param.35) | copy-start | bytes 294916
  7.2 7.4 %copy-start.9 = (bf16[96,512]{1,0:T(8,128)(2,1)S(1)}, bf16[96,512]{1,0:T(8,128)(2,1)}, u32[]{:S(2)}) copy-start(bf16[96,512]{1,0:T(8,128)(2,1)} %param.34) | copy-start | bytes 294916
  7.2 8.1 %copy-start.13 = (bf16[96,192]{1,0:T(8,128)(2,1)S(1)}, bf16[96,192]{1,0:T(8,128)(2,1)}, u32[]{:S(2)}) copy-start(bf16[96,192]{1,0:T(8,128)(2,1)} %param.32) | copy-start | bytes 110596
  7.2 8.1 %copy-start.12 = (bf16[96,192]{1,0:T(8,128)(2,1)S(1)}, bf16[96,192]{1,0:T(8,128)(2,1)}, u32[]{:S(2)}) copy-start(bf16[96,192]{1,0:T(8,128)(2,1)} %param.31) | copy-start | bytes 110596
  7.3 8.1 %copy-start.11 = (bf16[96,192]{1,0:T(8,128)(2,1)S(1)}, bf16[96,192]{1,0:T(8,128)(2,1)}, u32[]{:S(2)}) copy-start(bf16[96,192]{1,0:T(8,128)(2,1)} %param.28) | copy-start | bytes 110596
  7.3 8.1 %copy-start.10 = (bf16[96,192]{1,0:T(8,128)(2,1)S(1)}, bf16[96,192]{1,0:T(8,128)(2,1)}, u32[]{:S(2)}) copy-start(bf16[96,192]{1,0:T(8,128)(2,1)} %param.27) | copy-start | bytes 110596
  7.3 8.1 %copy-start.14 = (bf16[96,192]{1,0:T(8,128)(2,1)S(1)}, bf16[96,192]{1,0:T(8,128)(2,1)}, u32[]{:S(2)}) copy-start(bf16[96,192]{1,0:T(8,128)(2,1)} %param.26) | copy-start | bytes 110596
  7.3 594.9 %reduce-scatter.7.cloned.1.call-start = ((), (), s32[]{:S(2)}) async-start(), calls=%async_computation.3 | async-start | bytes 3096576
  11.0 205.8 %copy-start = (s32[1024,1]{1,0:T(8,128)}, s32[1024,1]{1,0:T(8,128)S(1)}, u32[]{:S(2)}) copy-start(s32[1024,1]{1,0:T(8,128)S(1)} %copy.77.target_ref) | copy-start | bytes 12292
  216.8 1.4 copy-start.1
  362.6 2.9 copy-start.21
  362.6 2.9 copy-start.23
  365.5 1.4 copy-start.20
  365.5 1.5 copy-start.25
  366.6 1.5 copy-start.19
  366.6 1.8 copy-start.22
  374.0 233.5 %reduce-scatter.5.cloned.1.call-start = ((), (), s32[]{:S(2)}) async-start(), calls=%async_computation.2 | async-start | bytes 14155776 | tf_op jit(solution)/shard_map/reduce_scatter | solution.py:2292
  377.4 180.3 %copy-start.15 = (f32[8,768]{1,0:T(8,128)S(1)}, f32[8,768]{1,0:T(8,128)}, u32[]{:S(2)}) copy-start(f32[8,768]{1,0:T(8,128)} %get-tuple-element.105) | copy-start | bytes 73732
  377.4 181.2 %copy-start.2 = (f32[1024,768]{1,0:T(8,128)S(1)}, f32[1024,768]{1,0:T(8,128)}, u32[]{:S(2)}) copy-start(f32[1024,768]{1,0:T(8,128)} %get-tuple-element.97.as_ref) | copy-start | bytes 9437188
  556.9 2.0 copy-start.5
  558.8 1.7 copy-start.24
  560.5 3.3 copy-start.3
  560.5 3.7 copy-start.26
  595.7 5.8 copy-start.16
  595.7 5.8 copy-start.17
  595.7 5.8 copy-start.18
  605.9 4.8 copy-start.4
Sparse Core Ops, SparseCore 0:
  374.1 52.3 reduce-scatter.6
  430.4 109.1 reduce-scatter.4

commit v6 on v5

--- a/solution.py
+++ b/solution.py
@@ -84,121 +84,173 @@
     )
 
 
-def plane_gather_kernel(x_ref, out_ref, send, recv, core_send, core_recv):
-    f, c, t = here()
-    core = f % 2
-    chips = [(0, 1), (2, 0), (2, 1)]
-    peers = [(f ^ df, c ^ dc, t) for df, dc in chips]
-    partner = (f ^ 1, c, t)
-    greet(peers + [partner])
-
-    def slot(df, dc):
-        return (f ^ df) * 2 + (c ^ dc)
-
-    own = slot(0, 0)
-    copies = []
-    for j, peer in enumerate(peers):
-        copy = remote(x_ref, out_ref.at[own], send.at[j], recv.at[j], peer)
-        copy.start()
-        copies.append(copy)
-    passes = [remote(x_ref, out_ref.at[own], core_send.at[3], core_recv.at[3], partner)]
-    passes[0].start()
-    out_ref[own] = x_ref[...]
-    for j, (df, dc) in enumerate(chips):
-        copies[j].wait_recv()
-        there = slot(df, dc)
-        copy = remote(
-            out_ref.at[there], out_ref.at[there], core_send.at[j], core_recv.at[j], partner
-        )
-        copy.start()
-        passes.append(copy)
-    for copy in copies:
-        copy.wait_send()
-    for copy in passes:
-        copy.wait()
-
-
-def plane_gather(shard, collective_id):
-    if not small_plane():
-        return lax.all_gather(shard, PLANE, axis=0, tiled=True)
-    rows, columns = shard.shape
-    out = pl.pallas_call(
-        plane_gather_kernel,
-        in_specs=[pl.BlockSpec(memory_space=pltpu.VMEM)],
-        out_specs=pl.BlockSpec(memory_space=pltpu.VMEM),
-        out_shape=jax.ShapeDtypeStruct((8, rows, columns), shard.dtype),
-        scratch_shapes=[
-            pltpu.SemaphoreType.DMA((3,)),
-            pltpu.SemaphoreType.DMA((3,)),
-            pltpu.SemaphoreType.DMA((4,)),
-            pltpu.SemaphoreType.DMA((4,)),
-        ],
-        compiler_params=pltpu.CompilerParams(
-            collective_id=collective_id, has_side_effects=True, vmem_limit_bytes=VMEM_LIMIT
-        ),
-        name="plane_gather",
-    )(shard)
-    return out.reshape(8 * rows, columns)
-
-
-def plane_scatter_kernel(
-    x_ref, out_ref, chip, core_in, chip_in, send, recv, core_send, core_recv
+def weight_scatter_kernel(
+    enc_ref,
+    gkvc_ref,
+    tok_ref,
+    gkvs_ref,
+    gq_ref,
+    as_ref,
+    gcq_ref,
+    gsl_ref,
+    att_ref,
+    gains_ref,
+    norms_low_ref,
+    norms_ref,
+    out_ref,
+    hidden_one,
+    hidden_two,
+    norm_rows,
+    x_ref,
+    chip,
+    core_in,
+    chip_in,
+    send,
+    recv,
+    core_send,
+    core_recv,
 ):
     f, c, t = here()
-    core = f % 2
     chips = [(2, 1), (0, 1), (2, 0)]
     peers = [(f ^ df, c ^ dc, t) for df, dc in chips]
     partner = (f ^ 1, c, t)
     greet(peers + [partner])
+    features = x_ref.shape[0]
+    shard = features // 8
+    rows = tok_ref.shape[0]
+    kv, width = gkvs_ref.shape[1], gq_ref.shape[1]
     order = chips + [(0, 0)]
-    swaps = []
-    for j, (df, dc) in enumerate(order):
-        block = (f ^ df ^ 1) * 2 + (c ^ dc)
-        copy = remote(x_ref.at[block], core_in.at[j], core_send.at[j], core_recv.at[j], partner)
-        copy.start()
-        swaps.append(copy)
-    copies = []
-    for j, (df, dc) in enumerate(order):
-        swaps[j].wait_recv()
-        block = (f ^ df) * 2 + (c ^ dc)
-        total = x_ref[block].astype(F32) + core_in[j].astype(F32)
-        if j < 3:
-            chip[j] = total.astype(BF16)
-            copy = remote(chip.at[j], chip_in.at[j], send.at[j], recv.at[j], peers[j])
-            copy.start()
-            copies.append(copy)
-        else:
-            out_ref[...] = total
-    for copy in swaps:
-        copy.wait_send()
-    for j in range(3):
-        copies[j].wait()
-        out_ref[...] += chip_in[j].astype(F32)
-
-
-def plane_scatter(total, collective_id):
-    if not small_plane():
-        return lax.psum_scatter(total.astype(F32), PLANE, scatter_dimension=0, tiled=True)
-    rows, columns = total.shape[0] // 8, total.shape[1]
+    spans = [(0, kv), (kv, kv), (Q2 - 256, 256), (Q2, 2 * width)]
+
+    def block(df, dc):
+        slot = (f ^ df) * 2 + (c ^ dc)
+        return pl.ds(pl.multiple_of(slot * shard, shard), shard)
+
+    def swap_copy(g, j):
+        cols = pl.ds(*spans[g])
+        df, dc = order[j]
+        return remote(
+            x_ref.at[block(df ^ 1, dc), cols],
+            core_in.at[j, :, cols],
+            core_send.at[g, j],
+            core_recv.at[g, j],
+            partner,
+        )
+
+    def chip_copy(g, j):
+        cols = pl.ds(*spans[g])
+        return remote(
+            chip.at[j, :, cols], chip_in.at[j, :, cols], send.at[g, j], recv.at[g, j], peers[j]
+        )
+
+    def product(left, right, start, size):
+        @pl.loop(0, features // 256)
+        def _(n):
+            at = pl.ds(pl.multiple_of(n * 256, 256), 256)
+            x_ref[at, start : start + size] = mat_tn(left[:, at], right[...]).astype(BF16)
+
+    def swap_group(g):
+        for j in range(4):
+            swap_copy(g, j).start()
+
+    def chip_group(g):
+        cols = slice(spans[g][0], spans[g][0] + spans[g][1])
+        for j in range(4):
+            swap_copy(g, j).wait_recv()
+            total = x_ref[block(*order[j]), cols].astype(F32) + core_in[j, :, cols].astype(F32)
+            if j < 3:
+                chip[j, :, cols] = total.astype(BF16)
+                chip_copy(g, j).start()
+            else:
+                out_ref[:, cols] = total
+
+    def hidden(source, gain, target):
+        @pl.loop(0, rows // 256)
+        def _(n):
+            at = pl.ds(pl.multiple_of(n * 256, 256), 256)
+            value = source[at].astype(F32)
+            target[at] = (value * rms_scale(value) * gains_ref[gain : gain + 1]).astype(BF16)
+
+    product(enc_ref, gkvc_ref, 0, kv)
+    swap_group(0)
+    hidden(tok_ref, 0, hidden_one)
+    product(hidden_one, gkvs_ref, kv, kv)
+    swap_group(1)
+    chip_group(0)
+    product(hidden_one, gq_ref, 2 * kv, width)
+    norm_rows[...] = jnp.zeros_like(norm_rows)
+    norm_rows[0:2] = norms_low_ref[0:2]
+    norm_rows[2:3] = norms_ref[1:2]
+    norm_rows[3:4] = norms_ref[0:1]
+    x_ref[:, Q2 - 64 : Q2] = norm_rows[...].T.astype(BF16)
+    swap_group(2)
+    chip_group(1)
+    hidden(as_ref, 1, hidden_two)
+    product(hidden_two, gcq_ref, Q2, width)
+    product(gsl_ref, att_ref, Q2 + width, width)
+    swap_group(3)
+    chip_group(2)
+    chip_group(3)
+    for g in range(4):
+        cols = slice(spans[g][0], spans[g][0] + spans[g][1])
+        for j in range(3):
+            chip_copy(g, j).wait_recv()
+            out_ref[:, cols] += chip_in[j, :, cols].astype(F32)
+    for g in range(4):
+        for j in range(4):
+            swap_copy(g, j).wait_send()
+        for j in range(3):
+            chip_copy(g, j).wait_send()
+
+
+def weight_scatter(operands, collective_id):
+    features = operands[0].shape[1]
+    kv, width = operands[3].shape[1], operands[4].shape[1]
+    rows, shard, columns = operands[2].shape[0], features // 8, Q2 + 2 * width
     return pl.pallas_call(
-        plane_scatter_kernel,
-        in_specs=[pl.BlockSpec(memory_space=pltpu.VMEM)],
+        weight_scatter_kernel,
+        in_specs=[pl.BlockSpec(memory_space=pltpu.VMEM)] * len(operands),
         out_specs=pl.BlockSpec(memory_space=pltpu.VMEM),
-        out_shape=jax.ShapeDtypeStruct((rows, columns), F32),
+        out_shape=jax.ShapeDtypeStruct((shard, columns), F32),
         scratch_shapes=[
-            pltpu.VMEM((3, rows, columns), BF16),
-            pltpu.VMEM((4, rows, columns), BF16),
-            pltpu.VMEM((3, rows, columns), BF16),
-            pltpu.SemaphoreType.DMA((3,)),
-            pltpu.SemaphoreType.DMA((3,)),
-            pltpu.SemaphoreType.DMA((4,)),
-            pltpu.SemaphoreType.DMA((4,)),
+            pltpu.VMEM((rows, features), BF16),
+            pltpu.VMEM((rows, features), BF16),
+            pltpu.VMEM((64, features), F32),
+            pltpu.VMEM((features, columns), BF16),
+            pltpu.VMEM((3, shard, columns), BF16),
+            pltpu.VMEM((4, shard, columns), BF16),
+            pltpu.VMEM((3, shard, columns), BF16),
+            pltpu.SemaphoreType.DMA((4, 3)),
+            pltpu.SemaphoreType.DMA((4, 3)),
+            pltpu.SemaphoreType.DMA((4, 4)),
+            pltpu.SemaphoreType.DMA((4, 4)),
         ],
         compiler_params=pltpu.CompilerParams(
-            collective_id=collective_id, has_side_effects=True, vmem_limit_bytes=VMEM_LIMIT
+            collective_id=collective_id, has_side_effects=True, vmem_limit_bytes=VMEM_MOST
         ),
-        name="plane_scatter",
-    )(total.reshape(8, rows, columns))
+        name="weight_scatter",
+    )(*operands)
+
+
+def weight_scatter_plain(operands, collective_id):
+    enc, gkvc, tokens, gkvs, gq, after_self, gcq, gsl, attended, gains, norms_low, norms = operands
+    tok = tokens.astype(F32)
+    hidden_one = (tok * rms_scale(tok) * gains[0:1]).astype(BF16)
+    hidden_two = (after_self * rms_scale(after_self) * gains[1:2]).astype(BF16)
+    norm_block = jnp.pad(
+        jnp.stack([norms_low[0], norms_low[1], norms[1], norms[0]], axis=1), ((0, 0), (0, 60))
+    )
+    parts = [
+        mat_tn(enc, gkvc),
+        mat_tn(hidden_one, gkvs),
+        mat_tn(hidden_one, gq),
+        norm_block,
+        mat_tn(hidden_two, gcq),
+        mat_tn(gsl, attended),
+    ]
+    return lax.psum_scatter(
+        jnp.concatenate(parts, axis=1), PLANE, scatter_dimension=0, tiled=True
+    )
 
 
 def line_project_kernel(
@@ -973,43 +1025,42 @@
 
 
 def layer_forward_kernel(
-    count,
-    parents_ref,
-    tok_ref,
-    enc_ref,
-    heads_in,
-    op_in,
-    ff_in,
-    embed_in,
-    heads_all,
-    op_all,
-    ff_all,
-    embed_all,
-    gains_out,
-    bias,
-    q_out,
-    kvs,
-    kvc,
-    att,
-    tots,
-    cq,
-    crs,
-    totc,
-    as_out,
-    ac_out,
-    zop,
-    zff,
-    held_s,
-    held_c,
-    spread_send,
-    spread_recv,
-    line_right,
-    line_left,
-    line_recv,
-    ctx_send,
-    ctx_recv,
-    local_sem,
+    count, parents_ref, tok_ref, enc_ref, heads_in, op_in, ff_in, embed_in, *refs
 ):
+    ff_all, embed_all = refs[:2]
+    results, staged = refs[2:17], refs[17:32]
+    (
+        heads_all,
+        own_out,
+        query_all,
+        gains_out,
+        bias,
+        q_out,
+        kvs,
+        kvc,
+        att,
+        tots,
+        cq,
+        as_out,
+        crs,
+        totc,
+        ac_out,
+    ) = staged
+    (
+        op_all,
+        zop,
+        zff,
+        held_s,
+        held_c,
+        spread_send,
+        spread_recv,
+        line_right,
+        line_left,
+        line_recv,
+        ctx_send,
+        ctx_recv,
+        local_sem,
+    ) = refs[32:]
     f, c, t = here()
     right, left = (f, c, t + 1), (f, c, t - 1)
     x_peer, y_peer, core_peer = (f, 1 - c, t), (f ^ 2, c, t), (f ^ 1, c, t)
@@ -1196,14 +1247,30 @@
         "OS": out_self,
         "OC": out_cross,
     }
+    leaving = [
+        pltpu.make_async_copy(src, dst, local_sem.at[2 + j])
+        for j, (src, dst) in enumerate(zip(staged, results))
+    ]
+    ready = {("OS", 1), ("WC", 1), ("WC", 0), ("GE", "o")}
     for name, *rest in FORWARD_ORDER:
         steps[name](*rest)
+        if (name, *rest) in ready:
+            ready.remove((name, *rest))
+            if not ready:
+                own_out[...] = op_all[:2, t]
+                query_all[...] = op_all[2]
+                for copy in leaving[:12]:
+                    copy.start()
+    for copy in leaving[12:]:
+        copy.start()
     for one in list(spreads.values()) + [op_line, ff_line] + self_lines + cross_lines:
         one.finish()
     for copy in ctx_self + ctx_cross:
         copy.wait_send()
     ff_own.wait()
     embed_own.wait()
+    for copy in leaving:
+        copy.wait()
 
 
 def layer_forward(parents, tokens, encoder, heads_in, op_in, ff_in, embed_in, collective_id):
@@ -1223,29 +1290,31 @@
     def full(*shape):
         return jax.ShapeDtypeStruct(shape, F32)
 
-    return pl.pallas_call(
+    results = [
+        low(features, heads_in.shape[1]),
+        low(2, features, width),
+        low(count, features, width),
+        full(8, features),
+        low(MB, 2 * rows, rows),
+        low(tok_rows, width),
+        low(MB, 2 * rows, 2 * width),
+        low(MB, enc_rows, 2 * width),
+        low(tok_rows, width),
+        full(MB, nh, rows),
+        low(tok_rows, width),
+        full(tok_rows, features),
+        low(tok_rows, width),
+        full(MB, nh, rows),
+        full(tok_rows, features),
+    ]
+    outcome = pl.pallas_call(
         functools.partial(layer_forward_kernel, count),
         in_specs=[pl.BlockSpec(memory_space=pltpu.SMEM)] + [vmem] * 5 + [anywhere],
-        out_specs=[vmem, vmem, anywhere, anywhere] + [vmem] * 12,
-        out_shape=[
-            low(features, heads_in.shape[1]),
-            low(3, count, features, width),
-            low(features, count * ff_cols),
-            low(features, embed_in.shape[1]),
-            full(8, features),
-            low(MB, 2 * rows, rows),
-            low(tok_rows, width),
-            low(MB, 2 * rows, 2 * width),
-            low(MB, enc_rows, 2 * width),
-            low(tok_rows, width),
-            full(MB, nh, rows),
-            low(tok_rows, width),
-            low(tok_rows, width),
-            full(MB, nh, rows),
-            full(tok_rows, features),
-            full(tok_rows, features),
-        ],
-        scratch_shapes=[
+        out_specs=[anywhere] * 17,
+        out_shape=[low(features, count * ff_cols), low(features, embed_in.shape[1])] + results,
+        scratch_shapes=[pltpu.VMEM(r.shape, r.dtype) for r in results]
+        + [
+            pltpu.VMEM((3, count, features, width), BF16),
             pltpu.VMEM((3, count, shard, width), BF16),
             pltpu.VMEM((shard, count * ff_cols), BF16),
             pltpu.VMEM((count, tok_rows, width), BF16),
@@ -1257,13 +1326,17 @@
             pltpu.SemaphoreType.DMA((6, count)),
             pltpu.SemaphoreType.DMA((4,)),
             pltpu.SemaphoreType.DMA((4,)),
-            pltpu.SemaphoreType.DMA((2,)),
+            pltpu.SemaphoreType.DMA((17,)),
         ],
         compiler_params=pltpu.CompilerParams(
             collective_id=collective_id, has_side_effects=True, vmem_limit_bytes=VMEM_MOST
         ),
         name="layer_forward",
     )(parents, tokens, encoder, heads_in, op_in, ff_in, embed_in)
+    ff_all, embed_all, heads_all, own_out, query_all, gains, bias, q, kvs, kvc = outcome[:10]
+    att, tots, cq, after_self, crs, totc, after_cross = outcome[10:]
+    gathered = (heads_all, own_out, query_all, ff_all, embed_all, gains)
+    return gathered + (bias, q, kvs, kvc, att, tots, cq, crs, totc, after_self, after_cross)
 
 
 def ff_forward_kernel(
@@ -1272,7 +1345,7 @@
     step = pl.program_id(0)
     rows = ac_ref.shape[0]
     units = gate_ref.shape[1]
-    tile = min(rows, 256)
+    tile = min(rows, 512)
 
     @pl.loop(0, rows // tile)
     def _(n):
@@ -1368,7 +1441,7 @@
     last = pl.num_programs(0) - 1
     rows = ac_ref.shape[0]
     units = gate_ref.shape[1]
-    tile = min(rows, 256)
+    tile = min(rows, 512)
 
     @pl.when(step == 0)
     def _():
@@ -1522,7 +1595,8 @@
     after_cross = line_project(crossed, op_all[1], after_self, 3)
     return (
         heads_all,
-        op_all,
+        lax.dynamic_index_in_dim(op_all[:2], lax.axis_index("tp"), 1, False),
+        op_all[2],
         ff_all,
         embed_all,
         gains,
@@ -1726,49 +1800,29 @@
 
 
 def layer_backward_kernel(
-    count,
-    gcr_ref,
-    cq_ref,
-    kvc_ref,
-    totc_ref,
-    q_ref,
-    kvs_ref,
-    bias_ref,
-    tots_ref,
-    gac_ref,
-    as_ref,
-    tok_ref,
-    wo_ref,
-    cq4_ref,
-    heads_ref,
-    gains_ref,
-    gt_out,
-    enc_sum,
-    gcq,
-    gkvc,
-    gq,
-    gkvs,
-    gsl,
-    norms,
-    dkvc,
-    dkvc_in,
-    dkvs,
-    dkvs_in,
-    acc,
-    held,
-    gatt,
-    enc_part,
-    one_part,
-    one_sum,
-    enc_buffers,
-    one_buffers,
-    line_right,
-    line_left,
-    line_recv,
-    ctx_send,
-    ctx_recv,
-    sum_sems,
+    count, gcr_ref, cq_ref, kvc_ref, totc_ref, q_ref, tots_ref, wo_ref, gains_ref, *refs
 ):
+    late, outs, scratch = refs[:7], refs[7:15], refs[15:]
+    gt_out, enc_sum, gcq, gkvc, gq, gkvs, gsl, norms = outs
+    dkvc, dkvc_in, dkvs, dkvs_in, acc, held, gatt, enc_part, one_part, one_sum = scratch[:10]
+    enc_buffers, one_buffers = scratch[10:12]
+    landed = scratch[12:19]
+    line_right, line_left, line_recv, ctx_send, ctx_recv, sum_sems, load_sem = scratch[19:]
+    heads_ref, query_ref, as_ref, gac_ref, kvs_ref, bias_ref, tok_ref = landed
+    loads = [
+        pltpu.make_async_copy(src, dst, load_sem.at[j])
+        for j, (src, dst) in enumerate(zip(late, landed))
+    ]
+    for copy in loads:
+        copy.start()
+    waiting = list(range(len(loads)))
+
+    def need(*numbers):
+        for j in numbers:
+            if j in waiting:
+                waiting.remove(j)
+                loads[j].wait()
+
     f, c, t = here()
     right, left = (f, c, t + 1), (f, c, t - 1)
     x_peer = (f, 1 - c, t)
@@ -1857,9 +1911,9 @@
 
     def after_queries(i):
         def body(at, inner):
-            grad = mat_nt(held[0, at], cq4_ref[0])
+            grad = mat_nt(held[0, at], query_ref[0])
             for origin in range(1, count):
-                grad = grad + mat_nt(held[origin, at], cq4_ref[origin])
+                grad = grad + mat_nt(held[origin, at], query_ref[origin])
             value = as_ref[at]
             scale = rms_scale(value)
             normed = value * scale
@@ -1916,7 +1970,9 @@
         "OBN": lambda i, j: one_sums[i].back_near(j),
         "OBF": lambda i, j: one_sums[i].back_far(j),
     }
+    needs = {"EP": (0,), "AQ": (1, 2, 3), "S": (4, 5), "TP": (0,), "FT": (6,)}
     for name, *rest in BACKWARD_ORDER:
+        need(*needs.get(name, ()))
         steps[name](*rest)
     for one in query_lines + enc_sums + one_sums:
         one.finish()
@@ -1931,6 +1987,8 @@
     enc_tree = enc_rows // MB
     width = operands[0].shape[1]
     vmem = pl.BlockSpec(memory_space=pltpu.VMEM)
+    gcr, cq, kvc, totc, q, kvs, bias, tots, gac, after_self, tok, wo, query, heads, gains = operands
+    late = (heads, query, after_self, gac, kvs, bias, tok)
     outs = [
         ((tok_rows, features), F32),
         ((enc_rows, features), BF16),
@@ -1957,10 +2015,11 @@
     ]
     return pl.pallas_call(
         functools.partial(layer_backward_kernel, count),
-        in_specs=[vmem] * 15,
+        in_specs=[vmem] * 8 + [pl.BlockSpec(memory_space=pl.ANY)] * len(late),
         out_specs=[vmem] * len(outs),
         out_shape=[jax.ShapeDtypeStruct(shape, kind) for shape, kind in outs],
         scratch_shapes=[pltpu.VMEM(shape, kind) for shape, kind in scratch]
+        + [pltpu.VMEM(value.shape, value.dtype) for value in late]
         + [
             pltpu.SemaphoreType.DMA((MB, count)),
             pltpu.SemaphoreType.DMA((MB, count)),
@@ -1968,12 +2027,13 @@
             pltpu.SemaphoreType.DMA((2 * MB,)),
             pltpu.SemaphoreType.DMA((2 * MB,)),
             pltpu.SemaphoreType.DMA((2 * MB, 8, 4)),
+            pltpu.SemaphoreType.DMA((len(late),)),
         ],
         compiler_params=pltpu.CompilerParams(
             collective_id=collective_id, has_side_effects=True, vmem_limit_bytes=VMEM_MOST
         ),
         name="layer_backward",
-    )(*operands)
+    )(gcr, cq, kvc, totc, q, tots, wo, gains, *late)
 
 
 EXIT_ORDER = (
@@ -2254,7 +2314,8 @@
     forward = layer_forward if small_plane() else layer_forward_plain
     (
         heads_all,
-        op_all,
+        own_out,
+        query_all,
         ff_all,
         embed_t,
         gains,
@@ -2270,8 +2331,6 @@
         after_self,
         after_cross,
     ) = forward(parents, tokens, encoder, heads_in, op_in, ff_in, embed_in, 1)
-    gain_self, gain_cross = gains[0:1], gains[1:2]
-    own_out = lax.dynamic_index_in_dim(op_all[:2], t, 1, False)
     w_out_own, c_out_own = own_out[0], own_out[1]
     gate_pre, up_pre, mixed, mixed_low, exit_in, exit_in_t = ff_forward(
         after_cross, gains, ff_all, tp_count, shrink
@@ -2339,7 +2398,7 @@
             after_self,
             tokens,
             w_out_own,
-            op_all[2],
+            query_all,
             heads_all,
             gains,
         ),
@@ -2347,10 +2406,6 @@
         encoder.shape[0],
         6,
     )
-    tok = tokens.astype(F32)
-    hidden_one = (tok * rms_scale(tok) * gain_self).astype(BF16)
-    hidden_two = (after_self * rms_scale(after_self) * gain_cross).astype(BF16)
-
     ff_grads = jnp.concatenate(
         [
             mat_tn(hidden_three, grad_gate_own),
@@ -2361,22 +2416,22 @@
         axis=1,
     ).astype(BF16)
     ff_own = lax.psum_scatter(ff_grads, PLANE, scatter_dimension=0, tiled=True)
-    norm_block = jnp.pad(
-        jnp.stack([norms_low[0], norms_low[1], norms[1], norms[0]], axis=1),
-        ((0, 0), (0, 60)),
-    )
-    own = plane_scatter(
-        jnp.concatenate(
-            [
-                mat_tn(hidden_one, grad_kv_self),
-                mat_tn(encoder, grad_kv_cross),
-                mat_tn(hidden_one, grad_q),
-                norm_block,
-                mat_tn(hidden_two, grad_cq),
-                mat_tn(grad_self_low, attended),
-            ],
-            axis=1,
-        ).astype(BF16),
+    scatter = weight_scatter if small_plane() else weight_scatter_plain
+    own = scatter(
+        (
+            encoder,
+            grad_kv_cross,
+            tokens,
+            grad_kv_self,
+            grad_q,
+            after_self,
+            grad_cq,
+            grad_self_low,
+            attended,
+            gains,
+            norms_low,
+            norms,
+        ),
         9,
     )
 
@@ -2391,12 +2446,12 @@
         grad_tokens,
         grad_encoder.astype(F32),
         part(own, 4 * width, width),
+        part(own, 2 * width, width),
+        part(own, 3 * width, width),
+        part(own, Q2 + width, width).T,
+        part(own, Q2, width),
         part(own, 0, width),
         part(own, width, width),
-        part(own, Q2 + width, width).T,
-        part(own, Q2, width),
-        part(own, 2 * width, width),
-        part(own, 3 * width, width),
         part(ff_own, 3 * hidden_units, width).T,
         part(ff_own, 0, hidden_units),
         part(ff_own, hidden_units, hidden_units),

time: 630 us -> 597 us (0.948)
  local copies, waits for them, and re-layouts: 39.8 us -> 27.8 us
  matrix products: 15.9 us -> 5.53 us
  Pallas kernels: 533 us -> 525 us
    dot_general x9 -> x4, matrix products: 15.9 us -> 5.53 us  [mat_tn(): lax.dot_general(left, right, (((0,), (0,)), ((), ())), preferred_element_...]
    pallas_call x1, Pallas kernels: 17 us -> 25.6 us  [weight_scatter(): pl.pallas_call(weight_scatter_kernel, in_specs=[pl.BlockSpec(memory_space...]
    unnamed x67 -> x56, local copies, waits for them, and re-layouts: 14.1 us -> 14.3 us
  transfers between devices with their start and end apart: 2 -> 2, of which waited for: 0 -> 0; matrix products, arithmetic and copies ran while one was open for 6% -> 2% of each run, Pallas kernels for 32% -> 34%
where the time goes in v6:
time: 597 us; the launch traced here: 586 us
  Pallas kernels  525 us (88%)
  local copies, waits for them, and re-layouts  27.8 us (5%)
  between operations  14.6 us (2%)
  other arithmetic  12.2 us (2%)
    pallas_call x1, Pallas kernels, layer_backward(): pl.pallas_call(functools.partial(layer_backward_kernel, count), in_specs=...  173 us
    pallas_call x1, Pallas kernels, layer_forward(): pl.pallas_call(functools.partial(layer_forward_kernel, count), in_specs=[...  168 us
    pallas_call x1, Pallas kernels, exit_backward(): pl.pallas_call(functools.partial(exit_backward_kernel, count, valid), gri...  73.5 us
    pallas_call x1, Pallas kernels, ff_backward(): pl.pallas_call(functools.partial(ff_backward_kernel, shrink), grid=(count...  32.6 us
    pallas_call x1, Pallas kernels, weight_scatter(): pl.pallas_call(weight_scatter_kernel, in_specs=[pl.BlockSpec(memory_space...  25.6 us
    pallas_call x1, Pallas kernels, exit_forward(): pl.pallas_call(functools.partial(exit_forward_kernel, valid), grid=(padde...  24.4 us
    pallas_call x1, Pallas kernels, ff_forward(): pl.pallas_call(functools.partial(ff_forward_kernel, shrink), grid=(count,...  21.3 us
    unnamed x56, local copies, waits for them, and re-layouts  14.3 us
  transfers between devices with their start and end apart: 2, of which 0 were waited for; matrix products, arithmetic and copies ran while one was open for 2% of the time, Pallas kernels for 34%

profile of v6, /device:TPU:0, one launch (start us, length us, event | category | flops | bytes accessed | tf_op | source)
XLA Modules:
  0.0 586.3 jit_solution(1967179072596563096)
XLA Ops:
  7.2 0.7 pad_maximum_fusion.4
  8.0 0.1 copy.65
  8.1 0.9 copy.66
  9.0 0.9 copy.67
  9.9 0.7 and_select_fusion
  10.6 0.2 copy.68.target_ref
  10.9 2.9 pad.9.embed_in
  13.8 0.7 pad_maximum_fusion.2.op_in
  14.5 0.7 pad_maximum_fusion.1.ff_in
  15.3 0.8 concatenate.11.heads_in
  16.2 167.8 %layer_forward.1 = (bf16[768,6144]{1,0:T(8,128)(2,1)}, bf16[768,8192]{1,0:T(8,128)(2,1)}, bf16[768,1280]{1,0:T(8,128)(2,1)}, bf16[2,768,192]{2,1,0:T(8,128)(2,1)...) custom-call(s32[2,8]{1,0:T(2,128)} %parents_ref.1, ...), custom_call_target="tpu_custom_call" | custom-call | tf_op jit(solution)/shard_map/layer_forward/pallas_call | solution.py:1310
  184.0 2.1 slice_bitcast_fusion
  186.0 21.3 %ff_forward.1 = (f32[1024,2048]{1,0:T(8,128)}, f32[1024,2048]{1,0:T(8,128)}, f32[1024,768]{1,0:T(8,128)}, bf16[1024,768]{1,0:T(8,128)(2,1)}, bf16[1024,768]{1,0:T(8,128)(2,1)}, /*index=5*/bf16[768,1024]{1,0:T(8,128)(2,1)}) custom-call(f32[1024,768]{1,0:T(8,128)} %get-tuple-element.70.ac_ref, f32[8,768]{1,0:T(8,128)} %get-tuple-element.71.gains_ref, ...), custom_call_target="tpu_custom_call" | custom-call | flops 9663676416 | bytes 26214400 | tf_op jit(solution)/shard_map/ff_forward/pallas_call | solution.py:1389
  207.4 1.4 copy-done.1
  208.8 24.4 %exit_forward.1 = (f32[1024,8192]{1,0:T(8,128)}, f32[1024,1]{1,0:T(8,128)S(1)}, f32[1024,1]{1,0:T(8,128)S(1)}, f32[1024,1]{1,0:T(8,128)S(1)}) custom-call(bf16[1024,768]{1,0:T(8,128)(2,1)S(1)} %copy-done.1, bf16[768,8192]{1,0:T(8,128)(2,1)} %get-tuple-element.75.e_ref, s32[1024,1]{1,0:T(8,128)S(1)} %copy.68.target_ref), custom_call_target="tpu_custom_call" | custom-call | flops 12884901888 | bytes 46137344 | tf_op jit(solution)/shard_map/exit_forward/pallas_call | solution.py:661
  233.2 0.2 reduce
  233.4 0.2 reduce.1
  233.6 0.2 reduce.2
  233.8 0.6 pad_maximum_fusion.3.x_ref
  234.4 6.9 %share_stats.1 = (f32[8,128]{1,0:T(8,128)}, f32[8,128]{1,0:T(8,128)}, f32[8,128]{1,0:T(8,128)}) custom-call(f32[3,8,128]{2,1,0:T(8,128)} %pad_maximum_fusion.3.x_ref), custom_call_target="tpu_custom_call" | custom-call | tf_op jit(solution)/shard_map/share_stats/pallas_call | solution.py:556
  241.3 1.7 copy.70.log_ref
  243.0 73.5 %exit_backward.1 = (bf16[768,8192]{1,0:T(8,128)(2,1)}, bf16[1024,768]{1,0:T(8,128)(2,1)}) custom-call(f32[1024,8192]{1,0:T(8,128)} %get-tuple-element.82.logits_ref, bf16[768,8192]{1,0:T(8,128)(2,1)} %get-tuple-element.75.e_ref, bf16[768,1024]{1,0:T(8,128)(2,1)} %get-tuple-element.83.x_t_ref, s32[1024,1]{1,0:T(8,128)} %copy-done, f32[1024,1]{1,0:T(8,128)} %copy.70.log_ref), custom_call_target="tpu_custom_call" | custom-call | flops 25769803776 | bytes 58720256 | tf_op jit(solution)/shard_map/exit_backward/pallas_call | solution.py:2159
  316.5 32.6 %ff_backward.1 = (f32[1024,768]{1,0:T(8,128)}, bf16[1024,768]{1,0:T(8,128)(2,1)}, bf16[1024,768]{1,0:T(8,128)(2,1)}, bf16[1024,192]{1,0:T(8,128)(2,1)}, bf16[102...) custom-call(bf16[1024,768]{1,0:T(8,128)(2,1)} %get-tuple-element.84., ...), custom_call_target="tpu_custom_call" | custom-call | flops 9663676416 | bytes 26214400 | tf_op jit(solution)/shard_map/ff_backward/pallas_call | solution.py:1514
  349.2 2.9 convolution_convert_fusion.2
  352.1 1.1 convolution_convert_fusion.1
  353.2 0.3 copy-done.17
  353.6 0.5 convolution_convert_fusion.3
  354.1 0.9 copy-done.16
  355.0 0.3 copy-done.19
  355.3 1.1 convolution_convert_fusion
  356.3 0.3 pad_maximum_fusion
  356.7 4.2 copy.75
  360.9 0.7 reduce-scatter.5.cloned.1.call-update
  361.6 173.2 %layer_backward.1 = (f32[1024,768]{1,0:T(8,128)}, bf16[2048,768]{1,0:T(8,128)(2,1)}, bf16[1024,192]{1,0:T(8,128)(2,1)}, bf16[2048,384]{1,0:T(8,128)(2,1)}, bf16[...) custom-call(bf16[1024,192]{1,0:T(8,128)(2,1)} %get-tuple-element.89.gcr_ref, ...), custom_call_target="tpu_custom_call" | custom-call | tf_op jit(solution)/shard_map/layer_backward/pallas_call | solution.py:2016
  534.8 25.6 %weight_scatter.1 = f32[96,1408]{1,0:T(8,128)} custom-call(bf16[2048,768]{1,0:T(8,128)(2,1)} %enc_ref.3, bf16[2048,384]{1,0:T(8,128)(2,1)} %get-tuple-element.103.gkvc_ref, bf16[1024,768]{1,0:T(8,128)(2,1)} %tok_ref.3, bf16[1024,384]{1,0:T(8,128)(2,1)} %get-tuple-element.104.gkvs_ref, bf16[1024,192]{1,0:T(8,128)(2,1)} %get-tuple-element.105.gq_ref, ...), custom_call_target="tpu_custom_call" | custom-call | tf_op jit(solution)/shard_map/weight_scatter/pallas_call | solution.py:210
  560.4 2.1 fusion
  562.5 0.7 copy.71
  563.3 3.2 convert_element_type.10
  566.5 1.7 slice_reduce_fusion
  568.2 0.6 subtract_bitcast_fusion
  568.8 0.8 slice.72
  569.7 1.0 fusion.1
  570.9 0.8 copy.74
  571.8 0.8 copy.73
  572.7 0.8 copy.72
  573.5 0.6 convert_bitcast_fusion.2
  574.2 3.4 convert_bitcast_fusion
  577.6 1.7 copy.82
  (52 shorter events, 0.8 us)
Async XLA Ops:
  7.2 561.6 %reduce-scatter.7.cloned.1.call-start = ((), (), s32[]{:S(2)}) async-start(), calls=%async_computation.3 | async-start | bytes 3096576
  8.0 5.9 %copy-start.4 = (bf16[96,192]{1,0:T(8,128)(2,1)S(1)}, bf16[96,192]{1,0:T(8,128)(2,1)}, u32[]{:S(2)}) copy-start(bf16[96,192]{1,0:T(8,128)(2,1)} %param.30) | copy-start | bytes 110596
  10.6 3.9 copy-start.5
  10.6 3.9 copy-start.6
  10.6 3.9 copy-start.7
  10.8 196.6 %copy-start = (s32[1024,1]{1,0:T(8,128)}, s32[1024,1]{1,0:T(8,128)S(1)}, u32[]{:S(2)}) copy-start(s32[1024,1]{1,0:T(8,128)S(1)} %copy.68.target_ref) | copy-start | bytes 12292
  10.9 4.4 copy-start.8
  10.9 4.4 copy-start.9
  10.9 4.4 copy-start.10
  10.9 4.4 copy-start.11
  10.9 4.4 copy-start.12
  207.4 1.4 copy-start.1
  349.1 2.9 copy-start.18
  349.2 2.9 copy-start.20
  352.1 1.4 copy-start.17
  352.1 1.5 copy-start.21
  353.6 1.4 copy-start.16
  353.6 1.7 copy-start.19
  360.9 213.3 %reduce-scatter.5.cloned.1.call-start = ((), (), s32[]{:S(2)}) async-start(), calls=%async_computation.2 | async-start | bytes 14155776 | tf_op jit(solution)/shard_map/reduce_scatter | solution.py:2351
  534.8 28.4 %copy-start.3 = (bf16[2048,768]{1,0:T(8,128)(2,1)S(1)}, bf16[2048,768]{1,0:T(8,128)(2,1)}, u32[]{:S(2)}) copy-start(bf16[2048,768]{1,0:T(8,128)(2,1)} %get-tuple-element.102) | copy-start | bytes 9437188
  563.3 4.9 copy-start.13
  563.3 4.9 copy-start.14
  563.3 4.9 copy-start.15
  574.2 3.4 copy-start.2
Sparse Core Ops, SparseCore 0:
  361.0 54.4 reduce-scatter.6
  419.3 101.8 reduce-scatter.4

commit v7 on v6

--- a/solution.py
+++ b/solution.py
@@ -25,6 +25,7 @@
 EXIT_PIECES = 2
 EXIT_CHUNKS = 4
 EXIT_STEPS = 24
+FF_TILE = 512
 
 
 def mat(left, right):
@@ -1345,7 +1346,7 @@
     step = pl.program_id(0)
     rows = ac_ref.shape[0]
     units = gate_ref.shape[1]
-    tile = min(rows, 512)
+    tile = min(rows, FF_TILE)
 
     @pl.loop(0, rows // tile)
     def _(n):
@@ -1422,18 +1423,20 @@
     ac_ref,
     gains_ref,
     co_ref,
+    crs_ref,
     w_ref,
     gate_ref,
     up_ref,
     gac_ref,
+    gcr_ref,
+    grads_ref,
+    norms_ref,
     low_ref,
     gcl_ref,
-    gcr_ref,
     hid_ref,
     act_ref,
     gg_ref,
     gu_ref,
-    norms_ref,
     acc,
 ):
     step = pl.program_id(0)
@@ -1441,7 +1444,7 @@
     last = pl.num_programs(0) - 1
     rows = ac_ref.shape[0]
     units = gate_ref.shape[1]
-    tile = min(rows, 512)
+    tile = min(rows, FF_TILE)
 
     @pl.when(step == 0)
     def _():
@@ -1495,9 +1498,31 @@
             gcl_ref[at] = total.astype(BF16)
             gcr_ref[at] = mat(total.astype(BF16), co_ref[...]).astype(BF16)
 
+    @pl.when(step == last)
+    def _():
+        pairs = [(hid_ref, gg_ref), (hid_ref, gu_ref), (low_ref, act_ref), (gcl_ref, crs_ref)]
+        for k, (left, right) in enumerate(pairs):
+            cols = slice(k * units, k * units + right.shape[1])
+
+            @pl.loop(0, grads_ref.shape[0] // 256)
+            def _(n):
+                at = pl.ds(pl.multiple_of(n * 256, 256), 256)
+                grads_ref[at, cols] = mat_tn(left[:, at], right[...]).astype(BF16)
+
 
 def ff_backward(
-    grad_exit, mixed, cotangent, after_cross, gains, c_out_own, ff_all, gate, up, count, shrink
+    grad_exit,
+    mixed,
+    cotangent,
+    after_cross,
+    gains,
+    c_out_own,
+    crossed,
+    ff_all,
+    gate,
+    up,
+    count,
+    shrink,
 ):
     rows, features = after_cross.shape
     cols = ff_all.shape[1] // count
@@ -1518,26 +1543,26 @@
         + [
             fixed(8, features),
             fixed(features, width),
+            fixed(rows, width),
             pl.BlockSpec((features, cols), lambda i: (0, i)),
             moving,
             moving,
         ],
-        out_specs=[fixed(rows, features)] * 3
-        + [fixed(rows, width), fixed(rows, features)]
-        + [fixed(rows, units)] * 3
-        + [fixed(8, features)],
+        out_specs=[
+            fixed(rows, features),
+            fixed(rows, width),
+            fixed(features, cols + width),
+            fixed(8, features),
+        ],
         out_shape=[
             jax.ShapeDtypeStruct((rows, features), F32),
-            low(rows, features),
-            low(rows, features),
             low(rows, width),
-            low(rows, features),
-            low(rows, units),
-            low(rows, units),
-            low(rows, units),
+            low(features, cols + width),
             jax.ShapeDtypeStruct((8, features), F32),
         ],
-        scratch_shapes=[pltpu.VMEM((rows, features), F32)],
+        scratch_shapes=[pltpu.VMEM((rows, features), BF16)] * 3
+        + [pltpu.VMEM((rows, units), BF16)] * 3
+        + [pltpu.VMEM((rows, features), F32)],
         compiler_params=pltpu.CompilerParams(vmem_limit_bytes=VMEM_MOST),
         cost_estimate=pl.CostEstimate(
             flops=2 * rows * features * count * cols,
@@ -1545,7 +1570,7 @@
             transcendentals=rows * count * units,
         ),
         name="ff_backward",
-    )(grad_exit, mixed, cotangent, after_cross, gains, c_out_own, ff_all, gate, up)
+    )(grad_exit, mixed, cotangent, after_cross, gains, c_out_own, crossed, ff_all, gate, up)
 
 
 def layer_forward_plain(
@@ -2351,23 +2376,14 @@
         lax.psum_scatter(grad_embed, PLANE, scatter_dimension=0, tiled=True)
     )
 
-    (
-        grad_after_cross,
-        grad_mixed_low,
-        grad_cross_low,
-        grad_crossed,
-        hidden_three,
-        activated_own,
-        grad_gate_own,
-        grad_up_own,
-        norms,
-    ) = ff_backward(
+    grad_after_cross, grad_crossed, ff_grads, norms = ff_backward(
         grad_exit,
         mixed,
         cotangent,
         after_cross,
         gains,
         c_out_own,
+        crossed,
         ff_all,
         gate_pre,
         up_pre,
@@ -2406,15 +2422,6 @@
         encoder.shape[0],
         6,
     )
-    ff_grads = jnp.concatenate(
-        [
-            mat_tn(hidden_three, grad_gate_own),
-            mat_tn(hidden_three, grad_up_own),
-            mat_tn(grad_mixed_low, activated_own),
-            mat_tn(grad_cross_low, crossed),
-        ],
-        axis=1,
-    ).astype(BF16)
     ff_own = lax.psum_scatter(ff_grads, PLANE, scatter_dimension=0, tiled=True)
     scatter = weight_scatter if small_plane() else weight_scatter_plain
     own = scatter(

time: 597 us -> 587 us (0.983)
  local copies, waits for them, and re-layouts: 27.8 us -> 18.1 us
    unnamed x56 -> x37, local copies, waits for them, and re-layouts: 14.3 us -> 6.39 us
where the time goes in v7:
time: 587 us; the launch traced here: 577 us
  Pallas kernels  529 us (90%)
  local copies, waits for them, and re-layouts  18.1 us (3%)
  between operations  14.8 us (3%)
  other arithmetic  13.8 us (2%)
    pallas_call x1, Pallas kernels, layer_backward(): pl.pallas_call(functools.partial(layer_backward_kernel, count), in_specs=...  173 us
    pallas_call x1, Pallas kernels, layer_forward(): pl.pallas_call(functools.partial(layer_forward_kernel, count), in_specs=[...  168 us
    pallas_call x1, Pallas kernels, exit_backward(): pl.pallas_call(functools.partial(exit_backward_kernel, count, valid), gri...  73.8 us
    pallas_call x1, Pallas kernels, ff_backward(): pl.pallas_call(functools.partial(ff_backward_kernel, shrink), grid=(count...  36.6 us
    pallas_call x1, Pallas kernels, weight_scatter(): pl.pallas_call(weight_scatter_kernel, in_specs=[pl.BlockSpec(memory_space...  25.6 us
    pallas_call x1, Pallas kernels, exit_forward(): pl.pallas_call(functools.partial(exit_forward_kernel, valid), grid=(padde...  24.3 us
    pallas_call x1, Pallas kernels, ff_forward(): pl.pallas_call(functools.partial(ff_forward_kernel, shrink), grid=(count,...  21.3 us
  transfers between devices with their start and end apart: 2, of which 0 were waited for; matrix products, arithmetic and copies ran while one was open for 2% of the time, Pallas kernels for 34%

profile of v7, /device:TPU:0, one launch (start us, length us, event | category | flops | bytes accessed | tf_op | source)
XLA Modules:
  0.0 576.8 jit_solution(6175559934679995347)
XLA Ops:
  7.2 0.0 copy-start.4
  7.2 0.0 copy-start.5
  7.2 0.0 copy-start.6
  7.2 0.0 copy-start.7
  7.2 0.0 copy-start.11
  7.3 0.0 reduce-scatter.3.cloned.1.call-start
  7.3 0.8 pad_maximum_fusion.3
  8.2 0.1 copy.61
  8.3 0.9 copy.62
  9.2 0.9 copy.63
  10.1 0.7 and_select_fusion
  10.8 0.2 copy.64.target_ref
  11.0 0.0 copy-start
  11.0 2.9 pad.9.embed_in
  13.9 0.7 pad_maximum_fusion.1.op_in
  14.6 0.0 copy-done.5
  14.6 0.7 pad_maximum_fusion.ff_in
  15.4 0.8 concatenate.7.heads_in
  16.2 167.5 %layer_forward.1 = (bf16[768,6144]{1,0:T(8,128)(2,1)}, bf16[768,8192]{1,0:T(8,128)(2,1)}, bf16[768,1280]{1,0:T(8,128)(2,1)}, bf16[2,768,192]{2,1,0:T(8,128)(2,1)...) custom-call(s32[2,8]{1,0:T(2,128)} %parents_ref.1, ...), custom_call_target="tpu_custom_call" | custom-call | tf_op jit(solution)/shard_map/layer_forward/pallas_call | solution.py:1311
  183.8 2.1 slice_bitcast_fusion
  185.8 21.3 %ff_forward.1 = (f32[1024,2048]{1,0:T(8,128)}, f32[1024,2048]{1,0:T(8,128)}, f32[1024,768]{1,0:T(8,128)}, bf16[1024,768]{1,0:T(8,128)(2,1)}, bf16[1024,768]{1,0:T(8,128)(2,1)}, /*index=5*/bf16[768,1024]{1,0:T(8,128)(2,1)}) custom-call(f32[1024,768]{1,0:T(8,128)} %get-tuple-element.65.ac_ref, f32[8,768]{1,0:T(8,128)} %get-tuple-element.66.gains_ref, ...), custom_call_target="tpu_custom_call" | custom-call | flops 9663676416 | bytes 26214400 | tf_op jit(solution)/shard_map/ff_forward/pallas_call | solution.py:1390
  207.2 0.0 copy-start.1
  207.2 1.4 copy-done.1
  208.6 24.3 %exit_forward.1 = (f32[1024,8192]{1,0:T(8,128)}, f32[1024,1]{1,0:T(8,128)S(1)}, f32[1024,1]{1,0:T(8,128)S(1)}, f32[1024,1]{1,0:T(8,128)S(1)}) custom-call(bf16[1024,768]{1,0:T(8,128)(2,1)S(1)} %copy-done.1, bf16[768,8192]{1,0:T(8,128)(2,1)} %get-tuple-element.70.e_ref, s32[1024,1]{1,0:T(8,128)S(1)} %copy.64.target_ref), custom_call_target="tpu_custom_call" | custom-call | flops 12884901888 | bytes 46137344 | tf_op jit(solution)/shard_map/exit_forward/pallas_call | solution.py:662
  232.9 0.2 reduce
  233.1 0.2 reduce.1
  233.3 0.2 reduce.2
  233.5 0.6 pad_maximum_fusion.2.x_ref
  234.1 6.9 %share_stats.1 = (f32[8,128]{1,0:T(8,128)}, f32[8,128]{1,0:T(8,128)}, f32[8,128]{1,0:T(8,128)}) custom-call(f32[3,8,128]{2,1,0:T(8,128)} %pad_maximum_fusion.2.x_ref), custom_call_target="tpu_custom_call" | custom-call | tf_op jit(solution)/shard_map/share_stats/pallas_call | solution.py:557
  241.1 1.7 copy.66.log_ref
  242.8 73.8 %exit_backward.1 = (bf16[768,8192]{1,0:T(8,128)(2,1)}, bf16[1024,768]{1,0:T(8,128)(2,1)}) custom-call(f32[1024,8192]{1,0:T(8,128)} %get-tuple-element.77.logits_ref, bf16[768,8192]{1,0:T(8,128)(2,1)} %get-tuple-element.70.e_ref, bf16[768,1024]{1,0:T(8,128)(2,1)} %get-tuple-element.78.x_t_ref, s32[1024,1]{1,0:T(8,128)} %copy-done, f32[1024,1]{1,0:T(8,128)} %copy.66.log_ref), custom_call_target="tpu_custom_call" | custom-call | flops 25769803776 | bytes 58720256 | tf_op jit(solution)/shard_map/exit_backward/pallas_call | solution.py:2184
  316.5 36.6 %ff_backward.1 = (f32[1024,768]{1,0:T(8,128)}, bf16[1024,192]{1,0:T(8,128)(2,1)}, bf16[768,1728]{1,0:T(8,128)(2,1)}, f32[8,768]{1,0:T(8,128)}) custom-call(bf16[1024,768]{1,0:T(8,128)(2,1)} %get-tuple-element.79.ge_ref, f32[1024,768]{1,0:T(8,128)} %get-tuple-element.80.mixed_ref, bf16[1024,768]{1,0:T(8,128)(2,1)} %cot_ref.1, ...), custom_call_target="tpu_custom_call" | custom-call | flops 9663676416 | bytes 26214400 | tf_op jit(solution)/shard_map/ff_backward/pallas_call | solution.py:1539
  353.2 0.0 reduce-scatter.3.cloned.1.call-update
  353.2 0.0 reduce-scatter.5.cloned.1.call-start
  353.3 0.7 reduce-scatter.5.cloned.1.call-update
  354.0 173.1 %layer_backward.1 = (f32[1024,768]{1,0:T(8,128)}, bf16[2048,768]{1,0:T(8,128)(2,1)}, bf16[1024,192]{1,0:T(8,128)(2,1)}, bf16[2048,384]{1,0:T(8,128)(2,1)}, bf16[...) custom-call(bf16[1024,192]{1,0:T(8,128)(2,1)} %get-tuple-element.85.gcr_ref, ...), custom_call_target="tpu_custom_call" | custom-call | tf_op jit(solution)/shard_map/layer_backward/pallas_call | solution.py:2041
  527.1 25.6 %weight_scatter.1 = f32[96,1408]{1,0:T(8,128)} custom-call(bf16[2048,768]{1,0:T(8,128)(2,1)} %enc_ref.3, bf16[2048,384]{1,0:T(8,128)(2,1)} %get-tuple-element.99.gkvc_ref, bf16[1024,768]{1,0:T(8,128)(2,1)} %tok_ref.3, bf16[1024,384]{1,0:T(8,128)(2,1)} %get-tuple-element.100.gkvs_ref, bf16[1024,192]{1,0:T(8,128)(2,1)} %get-tuple-element.101.gq_ref, ...), custom_call_target="tpu_custom_call" | custom-call | tf_op jit(solution)/shard_map/weight_scatter/pallas_call | solution.py:211
  552.7 2.1 fusion
  554.8 0.7 copy.67
  555.6 3.2 convert_element_type.16
  558.8 1.8 slice_reduce_fusion
  560.6 0.0 copy-done.15
  560.6 0.6 subtract_bitcast_fusion
  561.2 0.8 convert_bitcast_fusion.2
  562.1 0.7 copy.68
  562.8 1.8 convert_bitcast_fusion.1
  564.6 3.2 convert_bitcast_fusion
  567.9 1.7 copy.70
  (26 shorter events, 0.1 us)
Async XLA Ops:
  7.2 6.7 %copy-start.4 = (bf16[96,192]{1,0:T(8,128)(2,1)S(1)}, bf16[96,192]{1,0:T(8,128)(2,1)}, u32[]{:S(2)}) copy-start(bf16[96,192]{1,0:T(8,128)(2,1)} %param.30) | copy-start | bytes 110596
  7.2 7.4 %copy-start.5 = (bf16[512,96]{0,1:T(8,128)(2,1)S(1)}, bf16[512,96]{0,1:T(8,128)(2,1)}, u32[]{:S(2)}) copy-start(bf16[512,96]{0,1:T(8,128)(2,1)} %param.36) | copy-start | bytes 294916
  7.2 7.4 %copy-start.6 = (bf16[96,512]{1,0:T(8,128)(2,1)S(1)}, bf16[96,512]{1,0:T(8,128)(2,1)}, u32[]{:S(2)}) copy-start(bf16[96,512]{1,0:T(8,128)(2,1)} %param.35) | copy-start | bytes 294916
  7.2 7.4 %copy-start.7 = (bf16[96,512]{1,0:T(8,128)(2,1)S(1)}, bf16[96,512]{1,0:T(8,128)(2,1)}, u32[]{:S(2)}) copy-start(bf16[96,512]{1,0:T(8,128)(2,1)} %param.34) | copy-start | bytes 294916
  7.2 8.1 %copy-start.11 = (bf16[96,192]{1,0:T(8,128)(2,1)S(1)}, bf16[96,192]{1,0:T(8,128)(2,1)}, u32[]{:S(2)}) copy-start(bf16[96,192]{1,0:T(8,128)(2,1)} %param.32) | copy-start | bytes 110596
  7.2 8.1 %copy-start.10 = (bf16[96,192]{1,0:T(8,128)(2,1)S(1)}, bf16[96,192]{1,0:T(8,128)(2,1)}, u32[]{:S(2)}) copy-start(bf16[96,192]{1,0:T(8,128)(2,1)} %param.31) | copy-start | bytes 110596
  7.3 8.1 %copy-start.9 = (bf16[96,192]{1,0:T(8,128)(2,1)S(1)}, bf16[96,192]{1,0:T(8,128)(2,1)}, u32[]{:S(2)}) copy-start(bf16[96,192]{1,0:T(8,128)(2,1)} %param.28) | copy-start | bytes 110596
  7.3 8.1 %copy-start.8 = (bf16[96,192]{1,0:T(8,128)(2,1)S(1)}, bf16[96,192]{1,0:T(8,128)(2,1)}, u32[]{:S(2)}) copy-start(bf16[96,192]{1,0:T(8,128)(2,1)} %param.27) | copy-start | bytes 110596
  7.3 8.1 %copy-start.12 = (bf16[96,192]{1,0:T(8,128)(2,1)S(1)}, bf16[96,192]{1,0:T(8,128)(2,1)}, u32[]{:S(2)}) copy-start(bf16[96,192]{1,0:T(8,128)(2,1)} %param.26) | copy-start | bytes 110596
  7.3 554.0 %reduce-scatter.3.cloned.1.call-start = ((), (), s32[]{:S(2)}) async-start(), calls=%async_computation.2 | async-start | bytes 3096576 | tf_op jit(solution)/shard_map/reduce_scatter | solution.py:2425
  11.0 196.1 %copy-start = (s32[1024,1]{1,0:T(8,128)}, s32[1024,1]{1,0:T(8,128)S(1)}, u32[]{:S(2)}) copy-start(s32[1024,1]{1,0:T(8,128)S(1)} %copy.64.target_ref) | copy-start | bytes 12292
  207.2 1.4 copy-start.1
  353.2 211.4 %reduce-scatter.5.cloned.1.call-start = ((), (), s32[]{:S(2)}) async-start(), calls=%async_computation.3 | async-start | bytes 14155776 | tf_op jit(solution)/shard_map/reduce_scatter | solution.py:2376
  527.1 28.5 %copy-start.3 = (bf16[2048,768]{1,0:T(8,128)(2,1)S(1)}, bf16[2048,768]{1,0:T(8,128)(2,1)}, u32[]{:S(2)}) copy-start(bf16[2048,768]{1,0:T(8,128)(2,1)} %get-tuple-element.98) | copy-start | bytes 9437188
  555.6 5.0 copy-start.13
  555.6 5.0 copy-start.14
  555.6 5.0 copy-start.15
  558.8 9.1 %copy-start.2 = (f32[1024,768]{1,0:T(8,128)S(1)}, f32[1024,768]{1,0:T(8,128)}, u32[]{:S(2)}) copy-start(f32[1024,768]{1,0:T(8,128)} %get-tuple-element.214) | copy-start | bytes 9437188
Sparse Core Ops, SparseCore 0:
  353.3 54.4 reduce-scatter.2
  411.7 101.7 reduce-scatter.4
